TPU v7x, 32 devices: a whole 2x2x4 slice. The times are simulated.
32 devices in a mesh: member: 2 (over y), lat: 4 (over z), lev: 2 (over x), fld: 2 (over core).
Axes of the slice: x: 2, y: 2, z: 4, core: 2. Of those that a mesh axis runs over, the one named last changes fastest.
Arguments:
- grid_state: bfloat16 [4, 48, 480, 1920], P(('member', 'fld'), 'lev', 'lat'), parts along dimension 0, may hold values from -6 to 6
- lat_order: int32 [480], replicated, may hold values from 0 to 479, each once
- slot_wave: int32 [384], replicated, may hold values from 0 to 383, each once
- truncation: int32 [384], replicated, may hold values from 288 to 383, as said below
- zonal_wind: float32 [480], replicated, may hold values from -3 to 3
- zonal_rate: float32 [480], replicated, may hold values from 0.0003 to 0.003
- quad_weight: float32 [480], replicated, may hold values from 0.02 to 0.09
- legendre: bfloat16 [384, 384, 480], P(('lat', 'lev')), may hold values from -5 to 5
- vert_modes: float32 [48, 48], replicated, may hold values from -0.875 to 0.875
- vert_project: float32 [48, 48], replicated, may hold values from -0.875 to 0.875
- mode_rates: float32 [48], replicated, may hold values from 0.5 to 8
- thermal_into_spread_matrix: float32 [48, 48], replicated, may hold values from -0.875 to 0.875
- pressure_balance_matrix: float32 [48, 48], replicated, may hold values from -0.875 to 0.875
Outputs:
- grid_new: bfloat16 [4, 48, 480, 1920], P(('member', 'fld'), 'lev', 'lat'), parts along dimension 0
There are 2 independent parts, one for each index of `member`. A program takes and returns all parts, laid end to end along the dimension named above; an argument that names none is the same for every part. Nothing has to cross between parts.
Inputs may be any that keep to these rules, and one draw needn't show every extreme that they name: `lat_order`: each latitude once. `slot_wave`: each wavenumber once. truncation[m] is never below m, and truncation[383] = 383.
All inputs are finite; a program needn't handle non-finite values.
Results may differ from a plain program's by a relative error of at most 0.0071.
Values may be sent and summed in bfloat16 or wider, within the bound.
No kernel may reach another device: no remote copies, remote signals or barrier semaphores. Data moves between devices by JAX's collectives and lax.ppermute only.
A program may use at most 128 MiB of HBM per device.

v0:
```python
import functools

import jax
import jax.numpy as jnp
from jax import lax
from jax.experimental import pallas as pl
from jax.experimental.pallas import tpu as pltpu
from jax.sharding import PartitionSpec as P


PRECISE = lax.Precision.HIGHEST
BF16 = jnp.bfloat16
F32 = jnp.float32


def dft_table(wavenums, nlon):
    columns = jnp.arange(nlon, dtype=jnp.int32)
    turns = columns[:, None] * wavenums[None, :] % nlon
    angles = turns.astype(jnp.float32) * (2.0 * jnp.pi / nlon)
    return jnp.stack([jnp.cos(angles), -jnp.sin(angles)], axis=1).astype(jnp.bfloat16)


def pick_values(idents, source_table):
    hits = idents[:, None] == jnp.arange(source_table.shape[0], dtype=jnp.int32)[None, :]
    return jnp.sum(jnp.where(hits, source_table[None, :], 0), axis=1)


def layer_eigen_basis(matrix, columns):
    return jnp.einsum("skcj,ij->skci", columns, matrix, precision=PRECISE)


def analyse(legendre, fourier_data):
    return jnp.einsum("skl,slx->skx", legendre, fourier_data, preferred_element_type=jnp.float32)


def synthesise(legendre, coeffs):
    return jnp.einsum("skl,skx->slx", legendre, coeffs, preferred_element_type=jnp.float32)


def local_general(
    grid_state,
    lat_order,
    slot_wave,
    truncation,
    zonal_wind,
    zonal_rate,
    quad_weight,
    legendre,
    vert_modes,
    vert_project,
    mode_rates,
    thermal_into_spread_matrix,
    pressure_balance_matrix,
):
    levd, latd, nlon = (grid_state.shape[1], grid_state.shape[2], grid_state.shape[3])
    slots = legendre.shape[0]
    nmodes = slot_wave.shape[0]
    nlat = lat_order.shape[0]
    nlev = vert_modes.shape[0]
    lat_count = lax.axis_size("lat")
    lev_count = lax.axis_size("lev")
    lat_index = lax.axis_index("lat")
    lev_index = lax.axis_index("lev")
    unknown_position = lax.axis_index("fld")
    my_lats = lax.dynamic_slice_in_dim(lat_order, lat_index * latd, latd)
    onehot = (my_lats[:, None] == jnp.arange(nlat, dtype=jnp.int32)[None, :]).astype(jnp.float32)
    per_lat = jnp.dot(
        onehot, jnp.stack([zonal_wind, zonal_rate, quad_weight], axis=1), precision=PRECISE
    )
    values = grid_state[0].astype(jnp.float32)
    flux = (values * (per_lat[None, :, 0][:, :, None] + values)).astype(jnp.bfloat16)
    count_rows = levd * latd
    stacked = jnp.concatenate(
        [grid_state[0].reshape(count_rows, nlon), flux.reshape(count_rows, nlon)], axis=0
    )
    table = dft_table(slot_wave, nlon).reshape(nlon, 2 * nmodes)
    spectra = lax.dot_general(
        table, stacked, (((0,), (1,)), ((), ())), preferred_element_type=jnp.float32
    ) * nlon ** (-0.5)
    spectra = spectra.reshape(2, nmodes, 2 * count_rows)
    plain = spectra[:, :, :count_rows]
    moved = spectra[:, :, count_rows:]
    rate_row = jnp.tile(per_lat[:, 1], levd)[None, :]
    weight_row = jnp.tile(per_lat[:, 2], levd)[None, :]
    wave_float = slot_wave.astype(jnp.float32)[:, None]
    factor = rate_row * wave_float
    real_part = (plain[0] + factor * moved[1]) * weight_row
    imag_part = (plain[1] - factor * moved[0]) * weight_row
    fourier = jnp.stack([real_part, imag_part], axis=0).astype(jnp.bfloat16)
    arrived = lax.all_to_all(fourier, ("lat", "lev"), split_axis=1, concat_axis=2, tiled=True)
    arrived = arrived.reshape(2, slots, lat_count, lev_count, levd, latd)
    arranged = jnp.transpose(arrived, (1, 2, 5, 0, 3, 4))
    arranged = arranged.reshape(slots, nlat, 2 * nlev)
    position = jnp.zeros((nlat,), jnp.int32).at[lat_order].set(jnp.arange(nlat, dtype=jnp.int32))
    ordered = jnp.take(arranged, position, axis=1)
    owner_index = lat_index * lev_count + lev_index
    my_waves = lax.dynamic_slice_in_dim(slot_wave, owner_index * slots, slots)
    limits = pick_values(my_waves, truncation)
    counts = limits - my_waves + 1
    degree = jnp.arange(nmodes, dtype=jnp.int32)
    valid = (degree[None, :] < counts[:, None])[:, :, None]
    own_spec = jnp.where(valid, analyse(legendre, ordered), jnp.float32(0.0))
    joined_harmonic_unknowns = lax.all_gather(own_spec, "fld", axis=2, tiled=True)
    joined_harmonic_unknowns = joined_harmonic_unknowns.reshape(slots, nmodes, 2, 2, nlev)
    outflow_rate_coeffs = joined_harmonic_unknowns[:, :, 0]
    thermal_coeffs = joined_harmonic_unknowns[:, :, 1]
    n_deg = (my_waves[:, None] + degree[None, :]).astype(jnp.float32)
    elliptic_inverse_scale = (n_deg * (n_deg + 1.0) / (nmodes * (nmodes - 1)))[:, :, None, None]
    outflow_rate_source = outflow_rate_coeffs + elliptic_inverse_scale * layer_eigen_basis(
        thermal_into_spread_matrix, thermal_coeffs
    )
    projected = layer_eigen_basis(vert_project, outflow_rate_source) / (
        1.0 + elliptic_inverse_scale * mode_rates
    )
    outflow_rate_next = layer_eigen_basis(vert_modes, projected)
    thermal_next = thermal_coeffs - layer_eigen_basis(pressure_balance_matrix, outflow_rate_next)
    own_new = (
        jnp.where(unknown_position == 0, outflow_rate_next, thermal_next)
        .astype(jnp.bfloat16)
        .reshape(slots, nmodes, 2 * nlev)
    )
    back = synthesise(legendre, own_new) * nmodes ** (-0.5)
    back = jnp.take(back, lat_order, axis=1).astype(jnp.bfloat16)
    shaped = back.reshape(slots, lat_count, latd, 2, lev_count, levd)
    outgoing = jnp.transpose(shaped, (3, 0, 1, 4, 5, 2)).reshape(
        2, slots, lat_count * lev_count * count_rows
    )
    returned = lax.all_to_all(outgoing, ("lat", "lev"), split_axis=2, concat_axis=1, tiled=True)
    leading = returned.reshape(2 * nmodes, count_rows)
    grid_out = lax.dot_general(
        leading, table, (((0,), (1,)), ((), ())), preferred_element_type=jnp.float32
    ) * nmodes ** (-0.5)
    return grid_out.astype(jnp.bfloat16).reshape(1, levd, latd, nlon)


LANES = 128
SHARES = (1, 1)


def xor_order(array, index, axis):
    size = array.shape[axis]
    bits = size.bit_length() - 1
    shape = array.shape[:axis] + (2,) * bits + array.shape[axis + 1 :]
    out = array.reshape(shape)
    for b in range(bits):
        ax = axis + bits - 1 - b
        out = jnp.where((index >> b) & 1 == 1, jnp.flip(out, ax), out)
    return out.reshape(array.shape)


def table_kernel(nblk, hi_c, hi_s, lo_c, lo_s, out):
    rows = hi_c.shape[0]
    cl, sl = lo_c[...], lo_s[...]
    for b in range(nblk):
        ch, sh = hi_c[:, b : b + 1], hi_s[:, b : b + 1]
        cols = slice(b * LANES, (b + 1) * LANES)
        out[:rows, cols] = (ch * cl - sh * sl).astype(BF16)
        out[rows:, cols] = (-(sh * cl + ch * sl)).astype(BF16)


def make_table(waves, nlon):
    nblk = nlon // LANES
    scale = 2.0 * jnp.pi / nlon
    step_lo = jnp.arange(LANES, dtype=jnp.int32)
    step_hi = jnp.arange(LANES, dtype=jnp.int32) * LANES
    lo = (waves[:, None] * step_lo[None, :] % nlon).astype(F32) * scale
    hi = (waves[:, None] * step_hi[None, :] % nlon).astype(F32) * scale
    rows = waves.shape[0]
    return pl.pallas_call(
        functools.partial(table_kernel, nblk),
        out_shape=jax.ShapeDtypeStruct((2 * rows, nlon), BF16),
        name="table",
    )(jnp.cos(hi), jnp.sin(hi), jnp.cos(lo), jnp.sin(lo))


def dft_kernel(groups, vb, latd, x_ref, t_ref, wind_ref, lat_ref, wave_ref, *rest):
    outs, (xf, scr) = rest[:groups], rest[groups:]
    rows = t_ref.shape[0]
    half = rows // 2
    per = half // groups
    nblk = x_ref.shape[2] // LANES

    @pl.when(pl.program_id(0) == 0)
    def _():
        xf[...] = jnp.zeros_like(xf)

    wind = jnp.concatenate([wind_ref[...]] * nblk, axis=1)
    rate = lat_ref[0:1, :]
    weight = lat_ref[1:2, :]

    def body(v, carry):
        xv = x_ref[v]
        x32 = xv.astype(F32)
        xf[0:latd, :] = xv
        xf[LANES : LANES + latd, :] = (x32 * (wind + x32)).astype(BF16)
        both = lax.dot_general(
            t_ref[...], xf[...], (((1,), (1,)), ((), ())), preferred_element_type=F32
        )
        plain, moved = both[:, :LANES], both[:, LANES:]
        factor = wave_ref[...] * rate
        real = (plain[:half] + factor * moved[half:]) * weight
        imag = (plain[half:] - factor * moved[:half]) * weight
        scr[pl.ds(v, half, stride=vb), :] = real
        scr[pl.ds(half * vb + v, half, stride=vb), :] = imag
        return carry

    lax.fori_loop(0, vb, body, 0, unroll=2)
    for g in range(groups):
        for c in range(2):
            start = (c * half + g * per) * vb
            piece = scr[start : start + per * vb, :].reshape(per, vb, LANES)
            outs[g][:, c] = piece[:, :, :latd].astype(BF16)


def dft(x, table, wind, latrow, waves, groups):
    levd, latd, nlon = x.shape
    rows = table.shape[0]
    half = rows // 2
    per = half // groups
    vb = 8
    const = lambda i: (0, 0)
    block = pl.BlockSpec((per, 2, vb, latd), lambda i: (0, 0, i, 0))
    return pl.pallas_call(
        functools.partial(dft_kernel, groups, vb, latd),
        out_shape=[jax.ShapeDtypeStruct((per, 2, levd, latd), BF16)] * groups,
        grid=(levd // vb,),
        in_specs=[
            pl.BlockSpec((vb, latd, nlon), lambda i: (i, 0, 0)),
            pl.BlockSpec((rows, nlon), const),
            pl.BlockSpec((latd, LANES), const),
            pl.BlockSpec((2, LANES), const),
            pl.BlockSpec((half, LANES), const),
        ],
        out_specs=[block] * groups,
        scratch_shapes=[
            pltpu.VMEM((2 * LANES, nlon), BF16),
            pltpu.VMEM((rows * vb, LANES), F32),
        ],
        cost_estimate=pl.CostEstimate(
            flops=4 * rows * levd * latd * nlon,
            bytes_accessed=2 * levd * latd * (nlon + rows) + 2 * rows * nlon,
            transcendentals=0,
        ),
        name="dft",
    )(x, table, wind, latrow, jnp.broadcast_to(waves.astype(F32)[:, None], (half, LANES)))


def split3_dot(w3, x):
    hi = x.astype(BF16)
    lo = (x - hi.astype(F32)).astype(BF16)
    return jnp.dot(w3, jnp.concatenate([hi, lo, hi], axis=0), preferred_element_type=F32)


def legendre_kernel(
    groups, levs, latd, nmodes, info, leg_ref, perm_ref, w1_ref, w2_ref, mr_ref, *rest
):
    own = rest[:groups]
    other = rest[groups]
    outs = rest[groups + 1 : 2 * groups + 1]
    give = rest[2 * groups + 1]
    acc = rest[2 * groups + 2]
    levd = own[0].shape[2]
    nlev = levs * levd
    t = pl.program_id(0)

    @pl.when(t == 0)
    def _():
        acc[...] = jnp.zeros_like(acc)

    for rel in range(groups):
        dz, dx = rel // levs, rel % levs
        lanes = slice(dz * LANES, dz * LANES + latd)
        for c in range(2):
            row = c * 2 * nlev + dx * levd
            acc[row : row + levd, lanes] = own[rel][0, c].astype(F32)
            row += nlev
            acc[row : row + levd, lanes] = other[rel, 0, c].astype(F32)
    data = acc[...].astype(BF16)
    leg = jnp.dot(perm_ref[...], leg_ref[0], preferred_element_type=F32).astype(BF16)
    spec = jnp.dot(data, leg, preferred_element_type=F32)
    k = lax.broadcasted_iota(jnp.int32, (1, nmodes), 1)
    wave, count, unknown = info[0, t], info[1, t], info[2, 0]
    n = (wave + k).astype(F32)
    h = n * (n + 1.0) / float(nmodes * (nmodes - 1))
    first = unknown == 0
    scale_own = jnp.where(first, 1.0, h)
    scale_other = jnp.where(first, h, 1.0)
    keep_own = jnp.where(first, 0.0, 1.0)
    keep_other = jnp.where(first, 1.0, 0.0)
    denom = 1.0 + h * mr_ref[...]
    spec = jnp.where(k < count, spec, 0.0)
    fresh = []
    for c in range(2):
        a = spec[c * 2 * nlev : c * 2 * nlev + nlev]
        b = spec[c * 2 * nlev + nlev : (c + 1) * 2 * nlev]
        src = split3_dot(w1_ref[...], jnp.concatenate([a * scale_own, b * scale_other], axis=0))
        q = src / denom
        new = split3_dot(w2_ref[...], q)
        fresh.append(new[:nlev] + keep_own * a)
        fresh.append(new[nlev:] + keep_other * b)
    fresh = jnp.concatenate(fresh, axis=0).astype(BF16)
    back = lax.dot_general(fresh, leg, (((1,), (1,)), ((), ())), preferred_element_type=F32)
    back = back * float(nmodes) ** (-0.5)
    for rel in range(groups):
        dz, dx = rel // levs, rel % levs
        lanes = slice(dz * LANES, dz * LANES + latd)
        for c in range(2):
            row = c * 2 * nlev + dx * levd
            outs[rel][0, c] = back[row : row + levd, lanes].astype(BF16)
            row += nlev
            give[rel, 0, c] = back[row : row + levd, lanes].astype(BF16)


def legendre_step(info, leg, perm, w1, w2, rates, own, other, levs, nmodes):
    groups = len(own)
    count, _, levd, latd = other.shape[1:]
    lanes, nlat = perm.shape
    nlev = levs * levd
    const = lambda t, s: (0, 0)
    piece = pl.BlockSpec((1, 2, levd, latd), lambda t, s: (t, 0, 0, 0))
    stack = pl.BlockSpec((groups, 1, 2, levd, latd), lambda t, s: (0, t, 0, 0, 0))
    flops = count * 2 * (2 * nlev * 2 * nmodes * lanes * 2 + nmodes * nlat * lanes)
    return pl.pallas_call(
        functools.partial(legendre_kernel, groups, levs, latd, nmodes),
        out_shape=[jax.ShapeDtypeStruct((2 * count, 2, levd, latd), BF16)] * groups
        + [jax.ShapeDtypeStruct((groups, count, 2, levd, latd), BF16)],
        grid_spec=pltpu.PrefetchScalarGridSpec(
            num_scalar_prefetch=1,
            grid=(count,),
            in_specs=[
                pl.BlockSpec((1, nlat, nmodes), lambda t, s: (s[3, 0] + t, 0, 0)),
                pl.BlockSpec((lanes, nlat), const),
                pl.BlockSpec(w1.shape, const),
                pl.BlockSpec(w2.shape, const),
                pl.BlockSpec(rates.shape, const),
            ]
            + [piece] * groups
            + [stack],
            out_specs=[piece] * groups + [stack],
            scratch_shapes=[pltpu.VMEM((4 * nlev, lanes), F32)],
        ),
        cost_estimate=pl.CostEstimate(
            flops=flops,
            bytes_accessed=count * 2 * (nmodes * nlat + 8 * nlev * lanes),
            transcendentals=0,
        ),
        name="legendre",
    )(info, leg, perm, w1, w2, rates, *own, other)


def gather_kernel(groups, *refs):
    ins, out = refs[:groups], refs[-1]
    for r in range(groups):
        out[r] = ins[r][...]


def gather_halves(blocks, after):
    groups = len(blocks)
    count, _, levd, latd = blocks[0].shape
    half = count // 2
    any_spec = pl.BlockSpec(memory_space=pl.ANY)
    return pl.pallas_call(
        functools.partial(gather_kernel, groups),
        out_shape=jax.ShapeDtypeStruct((groups, half, 2, levd, latd), BF16),
        grid=(1,),
        in_specs=[pl.BlockSpec((half, 2, levd, latd), lambda i: (1, 0, 0, 0))] * groups
        + [any_spec] * len(after),
        out_specs=pl.BlockSpec((groups, half, 2, levd, latd), lambda i: (0, 0, 0, 0, 0)),
        name="gather_halves",
    )(*blocks, *after)


def fill_kernel(groups, got, *refs):
    outs = refs[-groups:]
    for r in range(groups):
        outs[r][...] = got[r]


def fill_halves(blocks, got):
    groups, half, _, levd, latd = got.shape
    any_spec = pl.BlockSpec(memory_space=pl.ANY)
    return pl.pallas_call(
        functools.partial(fill_kernel, groups),
        out_shape=[jax.ShapeDtypeStruct(b.shape, b.dtype) for b in blocks],
        grid=(1,),
        in_specs=[pl.BlockSpec(got.shape, lambda i: (0, 0, 0, 0, 0))] + [any_spec] * groups,
        out_specs=[pl.BlockSpec((half, 2, levd, latd), lambda i: (1, 0, 0, 0))] * groups,
        input_output_aliases={r + 1: r for r in range(groups)},
        name="fill_halves",
    )(got, *blocks)


def inverse_kernel(spread, vb, latd, scale, add, t_ref, *rest):
    ins, rest = rest[: len(spread)], rest[len(spread) :]
    partial = rest[0] if add else None
    out, scr, lhs = rest[-3:]
    rows, nlon = t_ref.shape
    half = rows // 2
    for ref, (start, per) in zip(ins, spread):
        for c in range(2):
            at = (c * half + start) * vb
            scr[at : at + per * vb, :latd] = ref[:, c].astype(F32).reshape(per * vb, latd)
    for v in range(vb):
        col = scr[pl.ds(v, rows, stride=vb), :].astype(BF16)
        lhs[v * LANES : (v + 1) * LANES, :] = col.T
    step = 3 * LANES
    for j in range(0, nlon, step):
        cols = slice(j, j + step)
        grid = jnp.dot(lhs[...], t_ref[:, cols], preferred_element_type=F32) * scale
        for v in range(vb):
            piece = grid[v * LANES : v * LANES + latd]
            if partial is not None:
                piece = piece + partial[v, :, cols]
            out[v, :, cols] = piece.astype(out.dtype)


def inverse_dft(table, pieces, spread, partial, scale, out_dtype, after):
    levd, latd = pieces[0].shape[2:]
    rows, nlon = table.shape
    vb = 8
    grid_block = pl.BlockSpec((vb, latd, nlon), lambda i: (i, 0, 0))
    in_specs = [pl.BlockSpec((rows, nlon), lambda i: (0, 0))] + [
        pl.BlockSpec((p.shape[0], 2, vb, latd), lambda i: (0, 0, i, 0)) for p in pieces
    ]
    args = [table, *pieces]
    if partial is not None:
        in_specs.append(grid_block)
        args.append(partial)
    in_specs += [pl.BlockSpec(memory_space=pl.ANY)] * len(after)
    args += after
    return pl.pallas_call(
        functools.partial(inverse_kernel, spread, vb, latd, scale, partial is not None),
        out_shape=jax.ShapeDtypeStruct((levd, latd, nlon), out_dtype),
        grid=(levd // vb,),
        in_specs=in_specs,
        out_specs=grid_block,
        scratch_shapes=[
            pltpu.VMEM((rows * vb, LANES), F32),
            pltpu.VMEM((vb * LANES, rows), BF16),
        ],
        cost_estimate=pl.CostEstimate(
            flops=2 * rows * levd * latd * nlon,
            bytes_accessed=2 * levd * latd * (nlon + rows) + 2 * rows * nlon,
            transcendentals=0,
        ),
        name="inverse_dft",
    )(*args)


def local_fast(
    parts,
    grid_state,
    lat_order,
    slot_wave,
    truncation,
    zonal_wind,
    zonal_rate,
    quad_weight,
    legendre,
    vert_modes,
    vert_project,
    mode_rates,
    thermal_matrix,
    pressure_matrix,
):
    levd, latd, nlon = grid_state.shape[1:]
    slots = legendre.shape[0]
    nmodes = slot_wave.shape[0]
    nlat = lat_order.shape[0]
    nlev = vert_modes.shape[0]
    lats, levs = lax.axis_size("lat"), lax.axis_size("lev")
    groups = lats * levs
    z, x, f = lax.axis_index("lat"), lax.axis_index("lev"), lax.axis_index("fld")
    me = z * levs + x
    starts = [sum(parts[:i]) for i in range(len(parts))]

    waves = slot_wave.reshape(groups, 2, slots // 2)
    waves = xor_order(xor_order(waves, me, 0), f, 1)
    my_lats = lax.dynamic_slice_in_dim(lat_order, z * latd, latd)
    onehot = (my_lats[:, None] == jnp.arange(nlat, dtype=jnp.int32)[None, :]).astype(F32)
    per_lat = jnp.dot(
        onehot,
        jnp.stack([zonal_wind, zonal_rate, quad_weight * nlon ** (-0.5)], axis=1),
        precision=PRECISE,
    )
    wind = jnp.broadcast_to(per_lat[:, 0:1], (latd, LANES))
    latrow = jnp.pad(per_lat[:, 1:].T, ((0, 0), (0, LANES - latd)))

    first = f == 0
    mix = jnp.dot(vert_project, thermal_matrix, precision=PRECISE)
    drop = -jnp.dot(pressure_matrix, vert_modes, precision=PRECISE)
    by_col = lambda m: xor_order(m.reshape(nlev, levs, levd), x, 1).reshape(nlev, nlev)
    by_row = lambda m: xor_order(m.reshape(levs, levd, nlev), x, 0).reshape(nlev, nlev)
    w1 = by_col(jnp.where(first, vert_project, mix)), by_col(jnp.where(first, mix, vert_project))
    w1 = jnp.concatenate(w1, axis=1)
    w2 = by_row(jnp.where(first, vert_modes, drop)), by_row(jnp.where(first, drop, vert_modes))
    w2 = jnp.concatenate(w2, axis=0)

    def three(w):
        hi = lax.reduce_precision(w, 8, 7)
        lo = (w - hi).astype(BF16)
        hi = hi.astype(BF16)
        return jnp.concatenate([hi, hi, lo], axis=1)

    w1, w2 = three(w1), three(w2)
    rates = mode_rates[:, None]
    lat_rel = xor_order(lat_order.reshape(lats, latd), z, 0)
    lat_rel = jnp.pad(lat_rel, ((0, 0), (0, LANES - latd)), constant_values=-1).reshape(-1, 1)
    perm = (lat_rel == jnp.arange(nlat, dtype=jnp.int32)[None, :]).astype(BF16)
    my_waves = waves[0, 0]
    counts = pick_values(my_waves, truncation) - my_waves + 1

    lat_lev = ("lat", "lev")

    def exchange(blocks):
        return [
            b if r == 0 else lax.ppermute(b, lat_lev, [(i, i ^ r) for i in range(groups)])
            for r, b in enumerate(blocks)
        ]

    def swap(block):
        return lax.ppermute(block, "fld", [(0, 1), (1, 0)])

    tables, arrived = [], []
    for i, (at, part) in enumerate(zip(starts, parts)):
        w = waves[:, :, at : at + part].reshape(-1)
        tables.append(make_table(w, nlon))
        blocks = dft(grid_state[0], tables[i], wind, latrow, w, groups)
        arrived.append(exchange(blocks))
    legendre = jnp.swapaxes(legendre, 1, 2)
    returned = []
    after = [arrived[-1][0]]
    for i, (at, part) in enumerate(zip(starts, parts)):
        other = gather_halves(arrived[i], after)
        other = swap(other)
        info = jnp.stack(
            [
                my_waves[at : at + part],
                counts[at : at + part],
                jnp.full((part,), f, jnp.int32),
                jnp.full((part,), f * (slots // 2) + at, jnp.int32),
            ]
        )
        res = legendre_step(info, legendre, perm, w1, w2, rates, arrived[i], other, levs, nmodes)
        got = swap(res[groups])
        sent = fill_halves(res[:groups], got)
        after = [sent[0]]
        returned.append(exchange(sent))
    total = None
    for i, part in enumerate(parts):
        spread = tuple((r * 2 * part, 2 * part) for r in range(groups))
        last = i == len(parts) - 1
        total = inverse_dft(
            tables[i],
            returned[i],
            spread,
            total,
            float(nmodes) ** (-0.5),
            BF16 if last else F32,
            [] if last else after,
        )
    return total[None]


def power_of_two(n):
    return n & (n - 1) == 0


def solution(mesh):
    in_specs = (
        P(("member", "fld"), "lev", "lat", None),
        P(),
        P(),
        P(),
        P(),
        P(),
        P(),
        P(("lat", "lev"), None, None),
        P(),
        P(),
        P(),
        P(),
        P(),
    )
    out_specs = P(("member", "fld"), "lev", "lat", None)
    lats, levs = mesh.shape["lat"], mesh.shape["lev"]

    groups = lats * levs
    small = (
        mesh.shape["fld"] == 2 and power_of_two(lats) and power_of_two(levs) and 1 < groups <= 8
    )

    def local(grid_state, *rest):
        legendre = rest[6]
        levd, latd, nlon = grid_state.shape[1:]
        fits = (
            legendre.shape[0] % (2 * sum(SHARES)) == 0
            and levd % 8 == 0
            and latd % 8 == 0
            and latd <= LANES
            and nlon % (3 * LANES) == 0
        )
        if small and fits:
            unit = legendre.shape[0] // (2 * sum(SHARES))
            return local_fast([unit * n for n in SHARES], grid_state, *rest)
        return local_general(grid_state, *rest)

    return jax.shard_map(local, mesh=mesh, in_specs=in_specs, out_specs=out_specs, check_vma=False)
```

profile of v0, /device:TPU:12, one launch (start us, length us, event | category | flops | bytes accessed | tf_op | source)
XLA Modules:
  0.0 326.3 jit_solution(17921194043141841098)
XLA Ops:
  4.2 2.6 fusion.25
  6.8 3.0 table.3.t_ref
  11.2 16.6 %dft.3 = (bf16[24,2,24,120]{3,2,1,0:T(8,128)(2,1)}, bf16[24,2,24,120]{3,2,1,0:T(8,128)(2,1)}, bf16[24,2,24,120]{3,2,1,0:T(8,128)(2,1)}, bf16[24,2,24,120]{3,2,1,...) custom-call(bf16[24,120,1920]{2,1,0:T(8,128)(2,1)} %bitcast.57, ...), custom_call_target="tpu_custom_call" | custom-call | flops 8493465600 | bytes 14745600 | tf_op jit(solution)/shard_map/dft/pallas_call | solution.py:223
  27.8 1.5 collective-permute-start.7
  29.8 1.6 collective-permute-start.9
  31.4 2.6 collective-permute-start.10
  33.9 1.3 collective-permute-start.11
  36.1 3.0 table.2.t_ref
  39.9 16.6 %dft.2 = (bf16[24,2,24,120]{3,2,1,0:T(8,128)(2,1)}, bf16[24,2,24,120]{3,2,1,0:T(8,128)(2,1)}, bf16[24,2,24,120]{3,2,1,0:T(8,128)(2,1)}, bf16[24,2,24,120]{3,2,1,...) custom-call(bf16[24,120,1920]{2,1,0:T(8,128)(2,1)} %bitcast.58, ...), custom_call_target="tpu_custom_call" | custom-call | flops 8493465600 | bytes 14745600 | tf_op jit(solution)/shard_map/dft/pallas_call | solution.py:223
  57.3 1.6 collective-permute-start.12
  61.3 17.4 %collective-permute-done.12.refs_6_.rest_6_ = bf16[24,2,24,120]{3,2,1,0:T(8,128)(2,1)S(1)} collective-permute-done((bf16[24,2,24,120]{3,2,1,0:T(8,128)(2,1)S(1)}, bf16[24,2,24,120]{3,2,1,0:T(8,128)(2,1)S(1)}, u32[]{:S(2)}, u32[]{:S(2)}) %collective-permute-start.12) | collective-permute-done | bytes 276512 | tf_op jit(solution)/shard_map/ppermute | solution.py:517
  78.7 5.9 %collective-permute-done.13.refs_7_.rest_7_ = bf16[24,2,24,120]{3,2,1,0:T(8,128)(2,1)S(1)} collective-permute-done((bf16[24,2,24,120]{3,2,1,0:T(8,128)(2,1)S(1)}, bf16[24,2,24,120]{3,2,1,0:T(8,128)(2,1)S(1)}, u32[]{:S(2)}, u32[]{:S(2)}) %collective-permute-start.13) | collective-permute-done | bytes 276512 | tf_op jit(solution)/shard_map/ppermute | solution.py:517
  85.3 2.5 gather_halves.2
  89.6 1.3 collective-permute-done.14.rest_8_
  90.9 1.0 copy-done.2
  91.9 20.2 %legendre.2 = (bf16[24,2,24,120]{3,2,1,0:T(8,128)(2,1)}, bf16[24,2,24,120]{3,2,1,0:T(8,128)(2,1)}, bf16[24,2,24,120]{3,2,1,0:T(8,128)(2,1)}, bf16[24,2,24,120]{3...) custom-call(s32[4,12]{1,0:T(4,128)} %get-tuple-element.129.info, ...), custom_call_target="tpu_custom_call" | custom-call | flops 4076863488 | bytes 9142272 | tf_op jit(solution)/shard_map/legendre/pallas_call | solution.py:323
  113.1 2.7 collective-permute-start.2
  115.9 2.1 collective-permute-start.3
  118.0 3.7 %collective-permute-done.refs_1_.rest_1_ = bf16[24,2,24,120]{3,2,1,0:T(8,128)(2,1)S(1)} collective-permute-done((bf16[24,2,24,120]{3,2,1,0:T(8,128)(2,1)S(1)}, bf16[24,2,24,120]{3,2,1,0:T(8,128)(2,1)S(1)}, u32[]{:S(2)}, u32[]{:S(2)}) %collective-permute-start) | collective-permute-done | bytes 276512 | tf_op jit(solution)/shard_map/ppermute | solution.py:517
  121.7 10.2 %collective-permute-done.1.refs_2_.rest_2_ = bf16[24,2,24,120]{3,2,1,0:T(8,128)(2,1)S(1)} collective-permute-done((bf16[24,2,24,120]{3,2,1,0:T(8,128)(2,1)S(1)}, bf16[24,2,24,120]{3,2,1,0:T(8,128)(2,1)S(1)}, u32[]{:S(2)}, u32[]{:S(2)}) %collective-permute-start.1) | collective-permute-done | bytes 276512 | tf_op jit(solution)/shard_map/ppermute | solution.py:517
  132.4 3.1 collective-permute-start.6
  135.5 2.5 fill_halves.2
  138.1 19.3 %collective-permute-done.4.refs_5_.rest_5_ = bf16[24,2,24,120]{3,2,1,0:T(8,128)(2,1)S(1)} collective-permute-done((bf16[24,2,24,120]{3,2,1,0:T(8,128)(2,1)}, bf16[24,2,24,120]{3,2,1,0:T(8,128)(2,1)S(1)}, u32[]{:S(2)}, u32[]{:S(2)}) %collective-permute-start.4) | collective-permute-done | bytes 276512 | tf_op jit(solution)/shard_map/ppermute | solution.py:517
  157.3 6.7 %collective-permute-done.5.refs_6_.rest_6_ = bf16[24,2,24,120]{3,2,1,0:T(8,128)(2,1)S(1)} collective-permute-done((bf16[24,2,24,120]{3,2,1,0:T(8,128)(2,1)}, bf16[24,2,24,120]{3,2,1,0:T(8,128)(2,1)S(1)}, u32[]{:S(2)}, u32[]{:S(2)}) %collective-permute-start.5) | collective-permute-done | bytes 276512 | tf_op jit(solution)/shard_map/ppermute | solution.py:517
  164.0 5.7 %collective-permute-done.6.refs_7_.rest_7_ = bf16[24,2,24,120]{3,2,1,0:T(8,128)(2,1)S(1)} collective-permute-done((bf16[24,2,24,120]{3,2,1,0:T(8,128)(2,1)}, bf16[24,2,24,120]{3,2,1,0:T(8,128)(2,1)S(1)}, u32[]{:S(2)}, u32[]{:S(2)}) %collective-permute-start.6) | collective-permute-done | bytes 276512 | tf_op jit(solution)/shard_map/ppermute | solution.py:517
  170.4 2.5 gather_halves.3
  173.0 3.1 collective-permute-done.16.rest_8_
  176.0 1.0 copy-done.3
  177.1 20.2 %legendre.3 = (bf16[24,2,24,120]{3,2,1,0:T(8,128)(2,1)}, bf16[24,2,24,120]{3,2,1,0:T(8,128)(2,1)}, bf16[24,2,24,120]{3,2,1,0:T(8,128)(2,1)}, bf16[24,2,24,120]{3...) custom-call(s32[4,12]{1,0:T(4,128)} %get-tuple-element.130.info, ...), custom_call_target="tpu_custom_call" | custom-call | flops 4076863488 | bytes 9142272 | tf_op jit(solution)/shard_map/legendre/pallas_call | solution.py:323
  197.6 1.5 collective-permute-start.25
  199.1 2.0 collective-permute-start.27
  201.1 1.0 collective-permute-start.28
  202.1 2.9 collective-permute-start.29
  205.0 2.6 fill_halves.3
  207.6 1.5 collective-permute-start.30
  209.1 9.3 %collective-permute-done.26.rest_2_ = bf16[24,2,24,120]{3,2,1,0:T(8,128)(2,1)} collective-permute-done((bf16[24,2,24,120]{3,2,1,0:T(8,128)(2,1)S(1)}, bf16[24,2,24,120]{3,2,1,0:T(8,128)(2,1)}, u32[]{:S(2)}, u32[]{:S(2)}) %collective-permute-start.26) | collective-permute-done | bytes 276512 | tf_op jit(solution)/shard_map/ppermute | solution.py:517
  218.4 5.7 %collective-permute-done.27.rest_3_ = bf16[24,2,24,120]{3,2,1,0:T(8,128)(2,1)} collective-permute-done((bf16[24,2,24,120]{3,2,1,0:T(8,128)(2,1)S(1)}, bf16[24,2,24,120]{3,2,1,0:T(8,128)(2,1)}, u32[]{:S(2)}, u32[]{:S(2)}) %collective-permute-start.27) | collective-permute-done | bytes 276512 | tf_op jit(solution)/shard_map/ppermute | solution.py:517
  224.2 4.0 %collective-permute-start.19 = (bf16[24,2,24,120]{3,2,1,0:T(8,128)(2,1)}, bf16[24,2,24,120]{3,2,1,0:T(8,128)(2,1)S(1)}, u32[]{:S(2)}, u32[]{:S(2)}) collective-permute-start(bf16[24,2,24,120]{3,2,1,0:T(8,128)(2,1)} %get-tuple-element.92), channel_id=1, source_target_pairs={{0,4},{2,6},{4,0},{6,2},{8,12},{10,14},{12,8},{14,10},{1,5},{3,7},... | collective-permute-start | bytes 829448 | tf_op jit(solution)/shard_map/ppermute | solution.py:517
  228.2 12.9 %collective-permute-done.29.rest_5_ = bf16[24,2,24,120]{3,2,1,0:T(8,128)(2,1)} collective-permute-done((bf16[24,2,24,120]{3,2,1,0:T(8,128)(2,1)S(1)}, bf16[24,2,24,120]{3,2,1,0:T(8,128)(2,1)}, u32[]{:S(2)}, u32[]{:S(2)}) %collective-permute-start.29) | collective-permute-done | bytes 276512 | tf_op jit(solution)/shard_map/ppermute | solution.py:517
  241.1 3.5 %collective-permute-start.20 = (bf16[24,2,24,120]{3,2,1,0:T(8,128)(2,1)}, bf16[24,2,24,120]{3,2,1,0:T(8,128)(2,1)S(1)}, u32[]{:S(2)}, u32[]{:S(2)}) collective-permute-start(bf16[24,2,24,120]{3,2,1,0:T(8,128)(2,1)} %get-tuple-element.93), channel_id=1, source_target_pairs={{0,6},{2,4},{4,2},{6,0},{8,14},{10,12},{12,10},{14,8},{1,7},{3,5},... | collective-permute-start | bytes 829448 | tf_op jit(solution)/shard_map/ppermute | solution.py:517
  244.6 3.9 %collective-permute-done.30.rest_6_ = bf16[24,2,24,120]{3,2,1,0:T(8,128)(2,1)S(1)} collective-permute-done((bf16[24,2,24,120]{3,2,1,0:T(8,128)(2,1)S(1)}, bf16[24,2,24,120]{3,2,1,0:T(8,128)(2,1)S(1)}, u32[]{:S(2)}, u32[]{:S(2)}) %collective-permute-start.30) | collective-permute-done | bytes 276512 | tf_op jit(solution)/shard_map/ppermute | solution.py:517
  248.4 20.8 %collective-permute-done.31.rest_7_ = bf16[24,2,24,120]{3,2,1,0:T(8,128)(2,1)S(1)} collective-permute-done((bf16[24,2,24,120]{3,2,1,0:T(8,128)(2,1)S(1)}, bf16[24,2,24,120]{3,2,1,0:T(8,128)(2,1)S(1)}, u32[]{:S(2)}, u32[]{:S(2)}) %collective-permute-start.31) | collective-permute-done | bytes 276512 | tf_op jit(solution)/shard_map/ppermute | solution.py:517
  269.3 6.7 %collective-permute-start.24 = (bf16[24,2,24,120]{3,2,1,0:T(8,128)(2,1)}, bf16[24,2,24,120]{3,2,1,0:T(8,128)(2,1)S(1)}, u32[]{:S(2)}, u32[]{:S(2)}) collective-permute-start(bf16[24,2,24,120]{3,2,1,0:T(8,128)(2,1)} %get-tuple-element.97), channel_id=1, source_target_pairs={{0,14},{2,12},{4,10},{6,8},{8,6},{10,4},{12,2},{14,0},{1,15},{3,13... | collective-permute-start | bytes 829448 | tf_op jit(solution)/shard_map/ppermute | solution.py:517
  276.0 13.5 %inverse_dft.2.rest_8_ = f32[24,120,1920]{2,1,0:T(8,128)} custom-call(bf16[384,1920]{1,0:T(8,128)(2,1)} %table.3.t_ref, bf16[24,2,24,120]{3,2,1,0:T(8,128)(2,1)} %get-tuple-element.80.refs_8_.rest_0_, bf16[24,2,24,120]{3,2,1,0:T(8,128)(2,1)} %collective-permute-done.25.rest_1_, bf16[24,2,24,120]{3,2,1,0:T(8,128)(2,1)} %collective-permute-done.26.rest_2_, ...), custom_call_target="tpu_custom_call" | custom-call | flops 4246732800 | bytes 14745600 | tf_op jit(solution)/shard_map/inverse_dft/pallas_call | solution.py:431
  289.6 5.1 %collective-permute-done.22.rest_5_ = bf16[24,2,24,120]{3,2,1,0:T(8,128)(2,1)S(1)} collective-permute-done((bf16[24,2,24,120]{3,2,1,0:T(8,128)(2,1)}, bf16[24,2,24,120]{3,2,1,0:T(8,128)(2,1)S(1)}, u32[]{:S(2)}, u32[]{:S(2)}) %collective-permute-start.22) | collective-permute-done | bytes 276512 | tf_op jit(solution)/shard_map/ppermute | solution.py:517
  294.7 7.7 %collective-permute-done.23.rest_6_ = bf16[24,2,24,120]{3,2,1,0:T(8,128)(2,1)S(1)} collective-permute-done((bf16[24,2,24,120]{3,2,1,0:T(8,128)(2,1)}, bf16[24,2,24,120]{3,2,1,0:T(8,128)(2,1)S(1)}, u32[]{:S(2)}, u32[]{:S(2)}) %collective-permute-start.23) | collective-permute-done | bytes 276512 | tf_op jit(solution)/shard_map/ppermute | solution.py:517
  302.4 5.5 %collective-permute-done.24.rest_7_ = bf16[24,2,24,120]{3,2,1,0:T(8,128)(2,1)S(1)} collective-permute-done((bf16[24,2,24,120]{3,2,1,0:T(8,128)(2,1)}, bf16[24,2,24,120]{3,2,1,0:T(8,128)(2,1)S(1)}, u32[]{:S(2)}, u32[]{:S(2)}) %collective-permute-start.24) | collective-permute-done | bytes 276512 | tf_op jit(solution)/shard_map/ppermute | solution.py:517
  308.6 17.5 %inverse_dft.3 = bf16[24,120,1920]{2,1,0:T(8,128)(2,1)} custom-call(bf16[384,1920]{1,0:T(8,128)(2,1)} %table.2.t_ref, bf16[24,2,24,120]{3,2,1,0:T(8,128)(2,1)} %get-tuple-element.90.rest_8_.rest_0_, bf16[24,2,24,120]{3,2,1,0:T(8,128)(2,1)} %copy-done.20, bf16[24,2,24,120]{3,2,1,0:T(8,128)(2,1)} %copy-done.21, bf16[24,2,24,120]{3,2,1,0:T(8,128)(2,1)} %copy-done.22, ...), custom_call_target="tpu_custom_call" | custom-call | flops 4246732800 | bytes 14745600 | tf_op jit(solution)/shard_map/inverse_dft/pallas_call | solution.py:431
  (170 shorter events, 16.5 us)
Async XLA Ops:
  0.0 35.3 %copy-start = (f32[48,48]{1,0:T(8,128)S(1)}, f32[48,48]{1,0:T(8,128)}, u32[]{:S(2)}) copy-start(f32[48,48]{1,0:T(8,128)} %param.24) | copy-start | bytes 27652
  11.2 24.0 %copy-start.40 = (s32[480]{0:T(512)S(1)}, s32[480]{0:T(512)}, u32[]{:S(2)}) copy-start(s32[480]{0:T(512)} %param.14) | copy-start | bytes 5764
  11.2 24.1 %copy-start.36 = (f32[48,48]{1,0:T(8,128)S(1)}, f32[48,48]{1,0:T(8,128)}, u32[]{:S(2)}) copy-start(f32[48,48]{1,0:T(8,128)} %param.22) | copy-start | bytes 27652
  11.2 24.6 %copy-start.37 = (f32[48,48]{1,0:T(8,128)S(1)}, f32[48,48]{1,0:T(8,128)}, u32[]{:S(2)}) copy-start(f32[48,48]{1,0:T(8,128)} %param.21) | copy-start | bytes 27652
  11.2 24.6 %copy-start.38 = (f32[48,48]{1,0:T(8,128)S(1)}, f32[48,48]{1,0:T(8,128)}, u32[]{:S(2)}) copy-start(f32[48,48]{1,0:T(8,128)} %param.25) | copy-start | bytes 27652
  27.8 29.4 %collective-permute-start.7 = (bf16[24,2,24,120]{3,2,1,0:T(8,128)(2,1)}, bf16[24,2,24,120]{3,2,1,0:T(8,128)(2,1)S(1)}, u32[]{:S(2)}, u32[]{:S(2)}) collective-permute-start(bf16[24,2,24,120]{3,2,1,0:T(8,128)(2,1)} %get-tuple-element.64), channel_id=1, source_target_pairs={{0,2},{2,0},{4,6},{6,4},{8,10},{10,8},{12,14},{14,12},{1,3},{3,1},... | collective-permute-start | bytes 829448 | tf_op jit(solution)/shard_map/ppermute | solution.py:517
  29.4 29.5 %collective-permute-start.8 = (bf16[24,2,24,120]{3,2,1,0:T(8,128)(2,1)}, bf16[24,2,24,120]{3,2,1,0:T(8,128)(2,1)S(1)}, u32[]{:S(2)}, u32[]{:S(2)}) collective-permute-start(bf16[24,2,24,120]{3,2,1,0:T(8,128)(2,1)} %get-tuple-element.65), channel_id=1, source_target_pairs={{0,4},{2,6},{4,0},{6,2},{8,12},{10,14},{12,8},{14,10},{1,5},{3,7},... | collective-permute-start | bytes 829448 | tf_op jit(solution)/shard_map/ppermute | solution.py:517
  29.8 31.4 %collective-permute-start.9 = (bf16[24,2,24,120]{3,2,1,0:T(8,128)(2,1)}, bf16[24,2,24,120]{3,2,1,0:T(8,128)(2,1)S(1)}, u32[]{:S(2)}, u32[]{:S(2)}) collective-permute-start(bf16[24,2,24,120]{3,2,1,0:T(8,128)(2,1)} %get-tuple-element.66), channel_id=1, source_target_pairs={{0,6},{2,4},{4,2},{6,0},{8,14},{10,12},{12,10},{14,8},{1,7},{3,5},... | collective-permute-start | bytes 829448 | tf_op jit(solution)/shard_map/ppermute | solution.py:517
  31.4 29.9 %collective-permute-start.10 = (bf16[24,2,24,120]{3,2,1,0:T(8,128)(2,1)}, bf16[24,2,24,120]{3,2,1,0:T(8,128)(2,1)S(1)}, u32[]{:S(2)}, u32[]{:S(2)}) collective-permute-start(bf16[24,2,24,120]{3,2,1,0:T(8,128)(2,1)} %get-tuple-element.67), channel_id=1, source_target_pairs={{0,8},{2,10},{4,12},{6,14},{8,0},{10,2},{12,4},{14,6},{1,9},{3,11}... | collective-permute-start | bytes 829448 | tf_op jit(solution)/shard_map/ppermute | solution.py:517
  33.9 27.3 %collective-permute-start.11 = (bf16[24,2,24,120]{3,2,1,0:T(8,128)(2,1)}, bf16[24,2,24,120]{3,2,1,0:T(8,128)(2,1)S(1)}, u32[]{:S(2)}, u32[]{:S(2)}) collective-permute-start(bf16[24,2,24,120]{3,2,1,0:T(8,128)(2,1)} %get-tuple-element.68), channel_id=1, source_target_pairs={{0,10},{2,8},{4,14},{6,12},{8,2},{10,0},{12,6},{14,4},{1,11},{3,9}... | collective-permute-start | bytes 829448 | tf_op jit(solution)/shard_map/ppermute | solution.py:517
  57.2 27.3 %copy-start.6 = (bf16[24,2,24,120]{3,2,1,0:T(8,128)(2,1)}, bf16[24,2,24,120]{3,2,1,0:T(8,128)(2,1)S(1)}, u32[]{:S(2)}) copy-start(bf16[24,2,24,120]{3,2,1,0:T(8,128)(2,1)S(1)} %collective-permute-done.7.refs_1_.rest_1_) | copy-start | bytes 829444
  57.3 21.5 %collective-permute-start.12 = (bf16[24,2,24,120]{3,2,1,0:T(8,128)(2,1)S(1)}, bf16[24,2,24,120]{3,2,1,0:T(8,128)(2,1)S(1)}, u32[]{:S(2)}, u32[]{:S(2)}) collective-permute-start(bf16[24,2,24,120]{3,2,1,0:T(8,128)(2,1)S(1)} %copy-done.43), channel_id=1, source_target_pairs={{0,12},{2,14},{4,8},{6,10},{8,4},{10,6},{12,0},{14,2},{1,13},{3,15... | collective-permute-start | bytes 829448 | tf_op jit(solution)/shard_map/ppermute | solution.py:517
  58.9 25.7 %copy-start.7 = (bf16[24,2,24,120]{3,2,1,0:T(8,128)(2,1)}, bf16[24,2,24,120]{3,2,1,0:T(8,128)(2,1)S(1)}, u32[]{:S(2)}) copy-start(bf16[24,2,24,120]{3,2,1,0:T(8,128)(2,1)S(1)} %collective-permute-done.8.refs_2_.rest_2_) | copy-start | bytes 829444
  58.9 25.7 %collective-permute-start.13 = (bf16[24,2,24,120]{3,2,1,0:T(8,128)(2,1)S(1)}, bf16[24,2,24,120]{3,2,1,0:T(8,128)(2,1)S(1)}, u32[]{:S(2)}, u32[]{:S(2)}) collective-permute-start(bf16[24,2,24,120]{3,2,1,0:T(8,128)(2,1)S(1)} %copy-done.42), channel_id=1, source_target_pairs={{0,14},{2,12},{4,10},{6,8},{8,6},{10,4},{12,2},{14,0},{1,15},{3,13... | collective-permute-start | bytes 829448 | tf_op jit(solution)/shard_map/ppermute | solution.py:517
  61.2 23.4 %copy-start.8 = (bf16[24,2,24,120]{3,2,1,0:T(8,128)(2,1)}, bf16[24,2,24,120]{3,2,1,0:T(8,128)(2,1)S(1)}, u32[]{:S(2)}) copy-start(bf16[24,2,24,120]{3,2,1,0:T(8,128)(2,1)S(1)} %collective-permute-done.9.refs_3_.rest_3_) | copy-start | bytes 829444
  61.2 23.4 %copy-start.9 = (bf16[24,2,24,120]{3,2,1,0:T(8,128)(2,1)}, bf16[24,2,24,120]{3,2,1,0:T(8,128)(2,1)S(1)}, u32[]{:S(2)}) copy-start(bf16[24,2,24,120]{3,2,1,0:T(8,128)(2,1)S(1)} %collective-permute-done.10.refs_4_.rest_4_) | copy-start | bytes 829444
  87.8 3.1 collective-permute-start.14
  112.2 20.2 %collective-permute-start.15 = (bf16[8,12,2,24,120]{4,3,2,1,0:T(8,128)(2,1)}, bf16[8,12,2,24,120]{4,3,2,1,0:T(8,128)(2,1)S(1)}, u32[]{:S(2)}, u32[]{:S(2)}) collective-permute-start(bf16[8,12,2,24,120]{4,3,2,1,0:T(8,128)(2,1)} %get-tuple-element.71), channel_id=1, source_target_pairs={{0,1},{1,0},{2,3},{3,2},{4,5},{5,4},{6,7},{7,6},{8,9},{9,8},{10,11... | collective-permute-start | bytes 3317768 | tf_op jit(solution)/shard_map/ppermute | solution.py:522
  112.4 9.3 %collective-permute-start = (bf16[24,2,24,120]{3,2,1,0:T(8,128)(2,1)S(1)}, bf16[24,2,24,120]{3,2,1,0:T(8,128)(2,1)S(1)}, u32[]{:S(2)}, u32[]{:S(2)}) collective-permute-start(bf16[24,2,24,120]{3,2,1,0:T(8,128)(2,1)S(1)} %copy-done.45), channel_id=1, source_target_pairs={{0,2},{2,0},{4,6},{6,4},{8,10},{10,8},{12,14},{14,12},{1,3},{3,1},... | collective-permute-start | bytes 829448 | tf_op jit(solution)/shard_map/ppermute | solution.py:517
  113.1 18.7 %collective-permute-start.1 = (bf16[24,2,24,120]{3,2,1,0:T(8,128)(2,1)S(1)}, bf16[24,2,24,120]{3,2,1,0:T(8,128)(2,1)S(1)}, u32[]{:S(2)}, u32[]{:S(2)}) collective-permute-start(bf16[24,2,24,120]{3,2,1,0:T(8,128)(2,1)S(1)} %copy-done.44), channel_id=1, source_target_pairs={{0,4},{2,6},{4,0},{6,2},{8,12},{10,14},{12,8},{14,10},{1,5},{3,7},... | collective-permute-start | bytes 829448 | tf_op jit(solution)/shard_map/ppermute | solution.py:517
  113.1 24.9 %collective-permute-start.2 = (bf16[24,2,24,120]{3,2,1,0:T(8,128)(2,1)}, bf16[24,2,24,120]{3,2,1,0:T(8,128)(2,1)S(1)}, u32[]{:S(2)}, u32[]{:S(2)}) collective-permute-start(bf16[24,2,24,120]{3,2,1,0:T(8,128)(2,1)} %get-tuple-element.58), channel_id=1, source_target_pairs={{0,6},{2,4},{4,2},{6,0},{8,14},{10,12},{12,10},{14,8},{1,7},{3,5},... | collective-permute-start | bytes 829448 | tf_op jit(solution)/shard_map/ppermute | solution.py:517
  115.9 22.2 %collective-permute-start.3 = (bf16[24,2,24,120]{3,2,1,0:T(8,128)(2,1)}, bf16[24,2,24,120]{3,2,1,0:T(8,128)(2,1)S(1)}, u32[]{:S(2)}, u32[]{:S(2)}) collective-permute-start(bf16[24,2,24,120]{3,2,1,0:T(8,128)(2,1)} %get-tuple-element.59), channel_id=1, source_target_pairs={{0,8},{2,10},{4,12},{6,14},{8,0},{10,2},{12,4},{14,6},{1,9},{3,11}... | collective-permute-start | bytes 829448 | tf_op jit(solution)/shard_map/ppermute | solution.py:517
  121.6 48.1 %copy-start.11 = (bf16[24,2,24,120]{3,2,1,0:T(8,128)(2,1)}, bf16[24,2,24,120]{3,2,1,0:T(8,128)(2,1)S(1)}, u32[]{:S(2)}) copy-start(bf16[24,2,24,120]{3,2,1,0:T(8,128)(2,1)S(1)} %collective-permute-done.refs_1_.rest_1_) | copy-start | bytes 829444
  121.7 35.7 %collective-permute-start.4 = (bf16[24,2,24,120]{3,2,1,0:T(8,128)(2,1)}, bf16[24,2,24,120]{3,2,1,0:T(8,128)(2,1)S(1)}, u32[]{:S(2)}, u32[]{:S(2)}) collective-permute-start(bf16[24,2,24,120]{3,2,1,0:T(8,128)(2,1)} %get-tuple-element.60), channel_id=1, source_target_pairs={{0,10},{2,8},{4,14},{6,12},{8,2},{10,0},{12,6},{14,4},{1,11},{3,9}... | collective-permute-start | bytes 829448 | tf_op jit(solution)/shard_map/ppermute | solution.py:517
  131.8 37.9 %copy-start.12 = (bf16[24,2,24,120]{3,2,1,0:T(8,128)(2,1)}, bf16[24,2,24,120]{3,2,1,0:T(8,128)(2,1)S(1)}, u32[]{:S(2)}) copy-start(bf16[24,2,24,120]{3,2,1,0:T(8,128)(2,1)S(1)} %collective-permute-done.1.refs_2_.rest_2_) | copy-start | bytes 829444
  131.8 32.2 %collective-permute-start.5 = (bf16[24,2,24,120]{3,2,1,0:T(8,128)(2,1)}, bf16[24,2,24,120]{3,2,1,0:T(8,128)(2,1)S(1)}, u32[]{:S(2)}, u32[]{:S(2)}) collective-permute-start(bf16[24,2,24,120]{3,2,1,0:T(8,128)(2,1)} %get-tuple-element.61), channel_id=1, source_target_pairs={{0,12},{2,14},{4,8},{6,10},{8,4},{10,6},{12,0},{14,2},{1,13},{3,15... | collective-permute-start | bytes 829448 | tf_op jit(solution)/shard_map/ppermute | solution.py:517
  132.4 37.3 %collective-permute-start.6 = (bf16[24,2,24,120]{3,2,1,0:T(8,128)(2,1)}, bf16[24,2,24,120]{3,2,1,0:T(8,128)(2,1)S(1)}, u32[]{:S(2)}, u32[]{:S(2)}) collective-permute-start(bf16[24,2,24,120]{3,2,1,0:T(8,128)(2,1)} %get-tuple-element.62), channel_id=1, source_target_pairs={{0,14},{2,12},{4,10},{6,8},{8,6},{10,4},{12,2},{14,0},{1,15},{3,13... | collective-permute-start | bytes 829448 | tf_op jit(solution)/shard_map/ppermute | solution.py:517
  138.0 31.7 %copy-start.14 = (bf16[24,2,24,120]{3,2,1,0:T(8,128)(2,1)}, bf16[24,2,24,120]{3,2,1,0:T(8,128)(2,1)S(1)}, u32[]{:S(2)}) copy-start(bf16[24,2,24,120]{3,2,1,0:T(8,128)(2,1)S(1)} %collective-permute-done.2.refs_3_.rest_3_) | copy-start | bytes 829444
  138.0 31.7 %copy-start.15 = (bf16[24,2,24,120]{3,2,1,0:T(8,128)(2,1)}, bf16[24,2,24,120]{3,2,1,0:T(8,128)(2,1)S(1)}, u32[]{:S(2)}) copy-start(bf16[24,2,24,120]{3,2,1,0:T(8,128)(2,1)S(1)} %collective-permute-done.3.refs_4_.rest_4_) | copy-start | bytes 829444
  173.0 3.1 collective-permute-start.16
  177.1 24.0 %copy-start.30 = (bf16[24,2,24,120]{3,2,1,0:T(8,128)(2,1)S(1)}, bf16[24,2,24,120]{3,2,1,0:T(8,128)(2,1)}, u32[]{:S(2)}) copy-start(bf16[24,2,24,120]{3,2,1,0:T(8,128)(2,1)} %get-tuple-element.101) | copy-start | bytes 829444
  177.1 25.0 %copy-start.31 = (bf16[24,2,24,120]{3,2,1,0:T(8,128)(2,1)S(1)}, bf16[24,2,24,120]{3,2,1,0:T(8,128)(2,1)}, u32[]{:S(2)}) copy-start(bf16[24,2,24,120]{3,2,1,0:T(8,128)(2,1)} %get-tuple-element.102) | copy-start | bytes 829444
  197.4 4.7 %collective-permute-start.17 = (bf16[8,12,2,24,120]{4,3,2,1,0:T(8,128)(2,1)}, bf16[8,12,2,24,120]{4,3,2,1,0:T(8,128)(2,1)S(1)}, u32[]{:S(2)}, u32[]{:S(2)}) collective-permute-start(bf16[8,12,2,24,120]{4,3,2,1,0:T(8,128)(2,1)} %get-tuple-element.81), channel_id=1, source_target_pairs={{0,1},{1,0},{2,3},{3,2},{4,5},{5,4},{6,7},{7,6},{8,9},{9,8},{10,11... | collective-permute-start | bytes 3317768 | tf_op jit(solution)/shard_map/ppermute | solution.py:522
  197.6 10.0 %collective-permute-start.25 = (bf16[24,2,24,120]{3,2,1,0:T(8,128)(2,1)S(1)}, bf16[24,2,24,120]{3,2,1,0:T(8,128)(2,1)}, u32[]{:S(2)}, u32[]{:S(2)}) collective-permute-start(bf16[24,2,24,120]{3,2,1,0:T(8,128)(2,1)S(1)} %copy-done.27), channel_id=1, source_target_pairs={{0,2},{2,0},{4,6},{6,4},{8,10},{10,8},{12,14},{14,12},{1,3},{3,1},... | collective-permute-start | bytes 829448 | tf_op jit(solution)/shard_map/ppermute | solution.py:517
  199.0 19.3 %collective-permute-start.26 = (bf16[24,2,24,120]{3,2,1,0:T(8,128)(2,1)S(1)}, bf16[24,2,24,120]{3,2,1,0:T(8,128)(2,1)}, u32[]{:S(2)}, u32[]{:S(2)}) collective-permute-start(bf16[24,2,24,120]{3,2,1,0:T(8,128)(2,1)S(1)} %copy-done.28), channel_id=1, source_target_pairs={{0,4},{2,6},{4,0},{6,2},{8,12},{10,14},{12,8},{14,10},{1,5},{3,7},... | collective-permute-start | bytes 829448 | tf_op jit(solution)/shard_map/ppermute | solution.py:517
  199.1 25.1 %collective-permute-start.27 = (bf16[24,2,24,120]{3,2,1,0:T(8,128)(2,1)S(1)}, bf16[24,2,24,120]{3,2,1,0:T(8,128)(2,1)}, u32[]{:S(2)}, u32[]{:S(2)}) collective-permute-start(bf16[24,2,24,120]{3,2,1,0:T(8,128)(2,1)S(1)} %copy-done.29), channel_id=1, source_target_pairs={{0,6},{2,4},{4,2},{6,0},{8,14},{10,12},{12,10},{14,8},{1,7},{3,5},... | collective-permute-start | bytes 829448 | tf_op jit(solution)/shard_map/ppermute | solution.py:517
  201.1 23.1 %collective-permute-start.28 = (bf16[24,2,24,120]{3,2,1,0:T(8,128)(2,1)S(1)}, bf16[24,2,24,120]{3,2,1,0:T(8,128)(2,1)}, u32[]{:S(2)}, u32[]{:S(2)}) collective-permute-start(bf16[24,2,24,120]{3,2,1,0:T(8,128)(2,1)S(1)} %copy-done.30), channel_id=1, source_target_pairs={{0,8},{2,10},{4,12},{6,14},{8,0},{10,2},{12,4},{14,6},{1,9},{3,11}... | collective-permute-start | bytes 829448 | tf_op jit(solution)/shard_map/ppermute | solution.py:517
  202.1 39.0 %collective-permute-start.29 = (bf16[24,2,24,120]{3,2,1,0:T(8,128)(2,1)S(1)}, bf16[24,2,24,120]{3,2,1,0:T(8,128)(2,1)}, u32[]{:S(2)}, u32[]{:S(2)}) collective-permute-start(bf16[24,2,24,120]{3,2,1,0:T(8,128)(2,1)S(1)} %copy-done.31), channel_id=1, source_target_pairs={{0,10},{2,8},{4,14},{6,12},{8,2},{10,0},{12,6},{14,4},{1,11},{3,9}... | collective-permute-start | bytes 829448 | tf_op jit(solution)/shard_map/ppermute | solution.py:517
  207.6 40.9 %collective-permute-start.30 = (bf16[24,2,24,120]{3,2,1,0:T(8,128)(2,1)S(1)}, bf16[24,2,24,120]{3,2,1,0:T(8,128)(2,1)S(1)}, u32[]{:S(2)}, u32[]{:S(2)}) collective-permute-start(bf16[24,2,24,120]{3,2,1,0:T(8,128)(2,1)S(1)} %copy-done.32), channel_id=1, source_target_pairs={{0,12},{2,14},{4,8},{6,10},{8,4},{10,6},{12,0},{14,2},{1,13},{3,15... | collective-permute-start | bytes 829448 | tf_op jit(solution)/shard_map/ppermute | solution.py:517
  218.4 50.9 %collective-permute-start.31 = (bf16[24,2,24,120]{3,2,1,0:T(8,128)(2,1)S(1)}, bf16[24,2,24,120]{3,2,1,0:T(8,128)(2,1)S(1)}, u32[]{:S(2)}, u32[]{:S(2)}) collective-permute-start(bf16[24,2,24,120]{3,2,1,0:T(8,128)(2,1)S(1)} %copy-done.33), channel_id=1, source_target_pairs={{0,14},{2,12},{4,10},{6,8},{8,6},{10,4},{12,2},{14,0},{1,15},{3,13... | collective-permute-start | bytes 829448 | tf_op jit(solution)/shard_map/ppermute | solution.py:517
  224.1 45.1 %collective-permute-start.18 = (bf16[24,2,24,120]{3,2,1,0:T(8,128)(2,1)}, bf16[24,2,24,120]{3,2,1,0:T(8,128)(2,1)S(1)}, u32[]{:S(2)}, u32[]{:S(2)}) collective-permute-start(bf16[24,2,24,120]{3,2,1,0:T(8,128)(2,1)} %get-tuple-element.91), channel_id=1, source_target_pairs={{0,2},{2,0},{4,6},{6,4},{8,10},{10,8},{12,14},{14,12},{1,3},{3,1},... | collective-permute-start | bytes 829448 | tf_op jit(solution)/shard_map/ppermute | solution.py:517
  224.2 45.2 %collective-permute-start.19 = (bf16[24,2,24,120]{3,2,1,0:T(8,128)(2,1)}, bf16[24,2,24,120]{3,2,1,0:T(8,128)(2,1)S(1)}, u32[]{:S(2)}, u32[]{:S(2)}) collective-permute-start(bf16[24,2,24,120]{3,2,1,0:T(8,128)(2,1)} %get-tuple-element.92), channel_id=1, source_target_pairs={{0,4},{2,6},{4,0},{6,2},{8,12},{10,14},{12,8},{14,10},{1,5},{3,7},... | collective-permute-start | bytes 829448 | tf_op jit(solution)/shard_map/ppermute | solution.py:517
  241.1 48.5 %collective-permute-start.20 = (bf16[24,2,24,120]{3,2,1,0:T(8,128)(2,1)}, bf16[24,2,24,120]{3,2,1,0:T(8,128)(2,1)S(1)}, u32[]{:S(2)}, u32[]{:S(2)}) collective-permute-start(bf16[24,2,24,120]{3,2,1,0:T(8,128)(2,1)} %get-tuple-element.93), channel_id=1, source_target_pairs={{0,6},{2,4},{4,2},{6,0},{8,14},{10,12},{12,10},{14,8},{1,7},{3,5},... | collective-permute-start | bytes 829448 | tf_op jit(solution)/shard_map/ppermute | solution.py:517
  248.4 27.6 %copy-start.34 = (bf16[24,2,24,120]{3,2,1,0:T(8,128)(2,1)}, bf16[24,2,24,120]{3,2,1,0:T(8,128)(2,1)S(1)}, u32[]{:S(2)}) copy-start(bf16[24,2,24,120]{3,2,1,0:T(8,128)(2,1)S(1)} %collective-permute-done.30.rest_6_) | copy-start | bytes 829444
  248.4 41.2 %collective-permute-start.21 = (bf16[24,2,24,120]{3,2,1,0:T(8,128)(2,1)}, bf16[24,2,24,120]{3,2,1,0:T(8,128)(2,1)S(1)}, u32[]{:S(2)}, u32[]{:S(2)}) collective-permute-start(bf16[24,2,24,120]{3,2,1,0:T(8,128)(2,1)} %get-tuple-element.94), channel_id=1, source_target_pairs={{0,8},{2,10},{4,12},{6,14},{8,0},{10,2},{12,4},{14,6},{1,9},{3,11}... | collective-permute-start | bytes 829448 | tf_op jit(solution)/shard_map/ppermute | solution.py:517
  269.2 25.4 %collective-permute-start.22 = (bf16[24,2,24,120]{3,2,1,0:T(8,128)(2,1)}, bf16[24,2,24,120]{3,2,1,0:T(8,128)(2,1)S(1)}, u32[]{:S(2)}, u32[]{:S(2)}) collective-permute-start(bf16[24,2,24,120]{3,2,1,0:T(8,128)(2,1)} %get-tuple-element.95), channel_id=1, source_target_pairs={{0,10},{2,8},{4,14},{6,12},{8,2},{10,0},{12,6},{14,4},{1,11},{3,9}... | collective-permute-start | bytes 829448 | tf_op jit(solution)/shard_map/ppermute | solution.py:517
  269.2 33.1 %collective-permute-start.23 = (bf16[24,2,24,120]{3,2,1,0:T(8,128)(2,1)}, bf16[24,2,24,120]{3,2,1,0:T(8,128)(2,1)S(1)}, u32[]{:S(2)}, u32[]{:S(2)}) collective-permute-start(bf16[24,2,24,120]{3,2,1,0:T(8,128)(2,1)} %get-tuple-element.96), channel_id=1, source_target_pairs={{0,12},{2,14},{4,8},{6,10},{8,4},{10,6},{12,0},{14,2},{1,13},{3,15... | collective-permute-start | bytes 829448 | tf_op jit(solution)/shard_map/ppermute | solution.py:517
  269.3 38.5 %collective-permute-start.24 = (bf16[24,2,24,120]{3,2,1,0:T(8,128)(2,1)}, bf16[24,2,24,120]{3,2,1,0:T(8,128)(2,1)S(1)}, u32[]{:S(2)}, u32[]{:S(2)}) collective-permute-start(bf16[24,2,24,120]{3,2,1,0:T(8,128)(2,1)} %get-tuple-element.97), channel_id=1, source_target_pairs={{0,14},{2,12},{4,10},{6,8},{8,6},{10,4},{12,2},{14,0},{1,15},{3,13... | collective-permute-start | bytes 829448 | tf_op jit(solution)/shard_map/ppermute | solution.py:517
  (30 other events, 377.1 us)
where the time goes:
time: 327 us; the launch traced here: 326 us
  waiting for transfers between devices  144 us (44%)
  Pallas kernels  121 us (37%)
  starting transfers between devices  42.4 us (13%)
  local copies, waits for them, and re-layouts  10.4 us (3%)
  other arithmetic  6.6 us (2%)
    ppermute x28, waiting for transfers between devices, exchange(): lax.ppermute(b, lat_lev, [(i, i ^ r) for i in range(groups)])  140 us
    ppermute x28, starting transfers between devices, exchange(): lax.ppermute(b, lat_lev, [(i, i ^ r) for i in range(groups)])  42 us
    pallas_call x2, Pallas kernels, legendre_step(): pl.pallas_call(functools.partial(legendre_kernel, groups, levs, latd, nmo...  40.5 us
    pallas_call x2, Pallas kernels, dft(): pl.pallas_call(functools.partial(dft_kernel, groups, vb, latd), out_shape...  33.2 us
    pallas_call x2, Pallas kernels, inverse_dft(): pl.pallas_call(functools.partial(inverse_kernel, spread, vb, latd, scale,...  31.1 us
  transfers between devices with their start and end apart: 32, of which 17 were waited for; matrix products, arithmetic and copies ran while one was open for 2% of the time, Pallas kernels for 12%

commit v1 on v0

--- a/solution.py
+++ b/solution.py
@@ -261,54 +261,59 @@
     acc = rest[2 * groups + 2]
     levd = own[0].shape[2]
     nlev = levs * levd
+    count = leg_ref.shape[0]
     t = pl.program_id(0)
 
     @pl.when(t == 0)
     def _():
         acc[...] = jnp.zeros_like(acc)
 
+    k = lax.broadcasted_iota(jnp.int32, (1, nmodes), 1)
+    first = info[2, 0] == 0
+    keep_own = jnp.where(first, 0.0, 1.0)
+    keep_other = jnp.where(first, 1.0, 0.0)
+    where = []
     for rel in range(groups):
         dz, dx = rel // levs, rel % levs
-        lanes = slice(dz * LANES, dz * LANES + latd)
         for c in range(2):
             row = c * 2 * nlev + dx * levd
-            acc[row : row + levd, lanes] = own[rel][0, c].astype(F32)
-            row += nlev
-            acc[row : row + levd, lanes] = other[rel, 0, c].astype(F32)
-    data = acc[...].astype(BF16)
-    leg = jnp.dot(perm_ref[...], leg_ref[0], preferred_element_type=F32).astype(BF16)
-    spec = jnp.dot(data, leg, preferred_element_type=F32)
-    k = lax.broadcasted_iota(jnp.int32, (1, nmodes), 1)
-    wave, count, unknown = info[0, t], info[1, t], info[2, 0]
-    n = (wave + k).astype(F32)
-    h = n * (n + 1.0) / float(nmodes * (nmodes - 1))
-    first = unknown == 0
-    scale_own = jnp.where(first, 1.0, h)
-    scale_other = jnp.where(first, h, 1.0)
-    keep_own = jnp.where(first, 0.0, 1.0)
-    keep_other = jnp.where(first, 1.0, 0.0)
-    denom = 1.0 + h * mr_ref[...]
-    spec = jnp.where(k < count, spec, 0.0)
+            where.append((rel, c, row, slice(dz * LANES, dz * LANES + latd)))
+    for j in range(count):
+        for rel, c, row, lanes in where:
+            acc[j, row : row + levd, lanes] = own[rel][j, c].astype(F32)
+            acc[j, row + nlev : row + nlev + levd, lanes] = other[rel, j, c].astype(F32)
+    legs = [
+        jnp.dot(perm_ref[...], leg_ref[j], preferred_element_type=F32).astype(BF16)
+        for j in range(count)
+    ]
     fresh = []
-    for c in range(2):
-        a = spec[c * 2 * nlev : c * 2 * nlev + nlev]
-        b = spec[c * 2 * nlev + nlev : (c + 1) * 2 * nlev]
-        src = split3_dot(w1_ref[...], jnp.concatenate([a * scale_own, b * scale_other], axis=0))
-        q = src / denom
-        new = split3_dot(w2_ref[...], q)
-        fresh.append(new[:nlev] + keep_own * a)
-        fresh.append(new[nlev:] + keep_other * b)
-    fresh = jnp.concatenate(fresh, axis=0).astype(BF16)
-    back = lax.dot_general(fresh, leg, (((1,), (1,)), ((), ())), preferred_element_type=F32)
-    back = back * float(nmodes) ** (-0.5)
-    for rel in range(groups):
-        dz, dx = rel // levs, rel % levs
-        lanes = slice(dz * LANES, dz * LANES + latd)
+    for j in range(count):
+        wave, terms = info[0, t * count + j], info[1, t * count + j]
+        n = (wave + k).astype(F32)
+        h = n * (n + 1.0) / float(nmodes * (nmodes - 1))
+        scale_own = jnp.where(first, 1.0, h)
+        scale_other = jnp.where(first, h, 1.0)
+        denom = 1.0 + h * mr_ref[...]
+        spec = jnp.dot(acc[j].astype(BF16), legs[j], preferred_element_type=F32)
+        spec = jnp.where(k < terms, spec, 0.0)
+        new = []
         for c in range(2):
-            row = c * 2 * nlev + dx * levd
-            outs[rel][0, c] = back[row : row + levd, lanes].astype(BF16)
-            row += nlev
-            give[rel, 0, c] = back[row : row + levd, lanes].astype(BF16)
+            a = spec[c * 2 * nlev : c * 2 * nlev + nlev]
+            b = spec[c * 2 * nlev + nlev : (c + 1) * 2 * nlev]
+            src = jnp.concatenate([a * scale_own, b * scale_other], axis=0)
+            q = split3_dot(w1_ref[...], src) / denom
+            both = split3_dot(w2_ref[...], q)
+            new.append(both[:nlev] + keep_own * a)
+            new.append(both[nlev:] + keep_other * b)
+        fresh.append(jnp.concatenate(new, axis=0).astype(BF16))
+    for j in range(count):
+        back = lax.dot_general(
+            fresh[j], legs[j], (((1,), (1,)), ((), ())), preferred_element_type=F32
+        )
+        back = (back * float(nmodes) ** (-0.5)).astype(BF16)
+        for rel, c, row, lanes in where:
+            outs[rel][j, c] = back[row : row + levd, lanes]
+            give[rel, j, c] = back[row + nlev : row + nlev + levd, lanes]
 
 
 def legendre_step(info, leg, perm, w1, w2, rates, own, other, levs, nmodes):
@@ -317,8 +322,9 @@
     lanes, nlat = perm.shape
     nlev = levs * levd
     const = lambda t, s: (0, 0)
-    piece = pl.BlockSpec((1, 2, levd, latd), lambda t, s: (t, 0, 0, 0))
-    stack = pl.BlockSpec((groups, 1, 2, levd, latd), lambda t, s: (0, t, 0, 0, 0))
+    step = 2 if count % 2 == 0 else 1
+    piece = pl.BlockSpec((step, 2, levd, latd), lambda t, s: (t, 0, 0, 0))
+    stack = pl.BlockSpec((groups, step, 2, levd, latd), lambda t, s: (0, t, 0, 0, 0))
     flops = count * 2 * (2 * nlev * 2 * nmodes * lanes * 2 + nmodes * nlat * lanes)
     return pl.pallas_call(
         functools.partial(legendre_kernel, groups, levs, latd, nmodes),
@@ -326,9 +332,9 @@
         + [jax.ShapeDtypeStruct((groups, count, 2, levd, latd), BF16)],
         grid_spec=pltpu.PrefetchScalarGridSpec(
             num_scalar_prefetch=1,
-            grid=(count,),
+            grid=(count // step,),
             in_specs=[
-                pl.BlockSpec((1, nlat, nmodes), lambda t, s: (s[3, 0] + t, 0, 0)),
+                pl.BlockSpec((step, nlat, nmodes), lambda t, s: (s[3, 0] // step + t, 0, 0)),
                 pl.BlockSpec((lanes, nlat), const),
                 pl.BlockSpec(w1.shape, const),
                 pl.BlockSpec(w2.shape, const),
@@ -337,7 +343,7 @@
             + [piece] * groups
             + [stack],
             out_specs=[piece] * groups + [stack],
-            scratch_shapes=[pltpu.VMEM((4 * nlev, lanes), F32)],
+            scratch_shapes=[pltpu.VMEM((step, 4 * nlev, lanes), F32)],
         ),
         cost_estimate=pl.CostEstimate(
             flops=flops,
@@ -390,23 +396,38 @@
     )(got, *blocks)
 
 
-def inverse_kernel(spread, vb, latd, scale, add, t_ref, *rest):
-    ins, rest = rest[: len(spread)], rest[len(spread) :]
-    partial = rest[0] if add else None
-    out, scr, lhs = rest[-3:]
-    rows, nlon = t_ref.shape
-    half = rows // 2
-    for ref, (start, per) in zip(ins, spread):
-        for c in range(2):
-            at = (c * half + start) * vb
-            scr[at : at + per * vb, :latd] = ref[:, c].astype(F32).reshape(per * vb, latd)
+def inverse_kernel(counts, vb, latd, scale, add, *refs):
+    tabs, refs = refs[: len(counts)], refs[len(counts) :]
+    pieces, refs = refs[: sum(counts)], refs[sum(counts) :]
+    partial = refs[0] if add else None
+    out, scr, lhs = refs[-3:]
+    nlon = tabs[0].shape[1]
+    base, depth = 0, 0
+    for tab, number in zip(tabs, counts):
+        rows = tab.shape[0]
+        per = rows // (2 * number)
+        for g in range(number):
+            for c in range(2):
+                at = (base + c * (rows // 2) + g * per) * vb
+                part = pieces[depth + g][:, c].astype(F32)
+                scr[at : at + per * vb, :latd] = part.reshape(per * vb, latd)
+        base += rows
+        depth += number
     for v in range(vb):
-        col = scr[pl.ds(v, rows, stride=vb), :].astype(BF16)
+        col = scr[pl.ds(v, base, stride=vb), :].astype(BF16)
         lhs[v * LANES : (v + 1) * LANES, :] = col.T
     step = 3 * LANES
     for j in range(0, nlon, step):
         cols = slice(j, j + step)
-        grid = jnp.dot(lhs[...], t_ref[:, cols], preferred_element_type=F32) * scale
+        grid, base = None, 0
+        for tab in tabs:
+            rows = tab.shape[0]
+            term = jnp.dot(
+                lhs[:, base : base + rows], tab[:, cols], preferred_element_type=F32
+            )
+            grid = term if grid is None else grid + term
+            base += rows
+        grid = grid * scale
         for v in range(vb):
             piece = grid[v * LANES : v * LANES + latd]
             if partial is not None:
@@ -414,22 +435,26 @@
             out[v, :, cols] = piece.astype(out.dtype)
 
 
-def inverse_dft(table, pieces, spread, partial, scale, out_dtype, after):
+def inverse_dft(sets, partial, scale, out_dtype, after):
+    tabs = [tab for tab, _ in sets]
+    pieces = [p for _, group in sets for p in group]
     levd, latd = pieces[0].shape[2:]
-    rows, nlon = table.shape
+    nlon = tabs[0].shape[1]
+    rows = sum(tab.shape[0] for tab in tabs)
     vb = 8
     grid_block = pl.BlockSpec((vb, latd, nlon), lambda i: (i, 0, 0))
-    in_specs = [pl.BlockSpec((rows, nlon), lambda i: (0, 0))] + [
+    in_specs = [pl.BlockSpec(tab.shape, lambda i: (0, 0)) for tab in tabs] + [
         pl.BlockSpec((p.shape[0], 2, vb, latd), lambda i: (0, 0, i, 0)) for p in pieces
     ]
-    args = [table, *pieces]
+    args = [*tabs, *pieces]
     if partial is not None:
         in_specs.append(grid_block)
         args.append(partial)
     in_specs += [pl.BlockSpec(memory_space=pl.ANY)] * len(after)
     args += after
+    counts = tuple(len(group) for _, group in sets)
     return pl.pallas_call(
-        functools.partial(inverse_kernel, spread, vb, latd, scale, partial is not None),
+        functools.partial(inverse_kernel, counts, vb, latd, scale, partial is not None),
         out_shape=jax.ShapeDtypeStruct((levd, latd, nlon), out_dtype),
         grid=(levd // vb,),
         in_specs=in_specs,
@@ -512,21 +537,28 @@
 
     lat_lev = ("lat", "lev")
 
-    def exchange(blocks):
-        return [
-            b if r == 0 else lax.ppermute(b, lat_lev, [(i, i ^ r) for i in range(groups)])
-            for r, b in enumerate(blocks)
-        ]
+    def exchange(blocks, order):
+        out = list(blocks)
+        for r in order:
+            if r:
+                pairs = [(i, i ^ r) for i in range(groups)]
+                out[r] = lax.ppermute(blocks[r], lat_lev, pairs)
+        return out
 
     def swap(block):
         return lax.ppermute(block, "fld", [(0, 1), (1, 0)])
 
+    far, near = far_near(groups)
     tables, arrived = [], []
     for i, (at, part) in enumerate(zip(starts, parts)):
-        w = waves[:, :, at : at + part].reshape(-1)
-        tables.append(make_table(w, nlon))
-        blocks = dft(grid_state[0], tables[i], wind, latrow, w, groups)
-        arrived.append(exchange(blocks))
+        blocks = [None] * groups
+        tables.append({})
+        for rels in (far, near) if i == 0 else (near, far):
+            w = waves[rels[0] : rels[-1] + 1, :, at : at + part].reshape(-1)
+            tables[i][rels] = make_table(w, nlon)
+            got = dft(grid_state[0], tables[i][rels], wind, latrow, w, len(rels))
+            blocks[rels[0] : rels[-1] + 1] = got
+        arrived.append(exchange(blocks, far + near))
     legendre = jnp.swapaxes(legendre, 1, 2)
     returned = []
     after = [arrived[-1][0]]
@@ -545,21 +577,21 @@
         got = swap(res[groups])
         sent = fill_halves(res[:groups], got)
         after = [sent[0]]
-        returned.append(exchange(sent))
+        returned.append(exchange(sent, near + far))
     total = None
-    for i, part in enumerate(parts):
-        spread = tuple((r * 2 * part, 2 * part) for r in range(groups))
-        last = i == len(parts) - 1
-        total = inverse_dft(
-            tables[i],
-            returned[i],
-            spread,
-            total,
-            float(nmodes) ** (-0.5),
-            BF16 if last else F32,
-            [] if last else after,
-        )
+    last = len(parts) - 1
+    scale = float(nmodes) ** (-0.5)
+    one = lambda i, rels: (tables[i][rels], [returned[i][r] for r in rels])
+    for i in range(last):
+        total = inverse_dft([one(i, near), one(i, far)], total, scale, F32, after)
+    total = inverse_dft([one(last, near)], total, scale, F32, [])
+    total = inverse_dft([one(last, far)], total, scale, BF16, [])
     return total[None]
+
+
+def far_near(groups):
+    rels = tuple(range(groups))
+    return rels[groups // 2 :], rels[: groups // 2]
 
 
 def power_of_two(n):
@@ -594,7 +626,7 @@
         legendre = rest[6]
         levd, latd, nlon = grid_state.shape[1:]
         fits = (
-            legendre.shape[0] % (2 * sum(SHARES)) == 0
+            legendre.shape[0] % (4 * sum(SHARES)) == 0
             and levd % 8 == 0
             and latd % 8 == 0
             and latd <= LANES

time: 327 us -> 363 us (1.11)
  Pallas kernels: 121 us -> 154 us
    pallas_call x2 -> x4, Pallas kernels: 33.2 us -> 53 us  [dft(): pl.pallas_call(functools.partial(dft_kernel, groups, vb, latd), out_shape...]
    pallas_call x2 -> x3, Pallas kernels: 31.1 us -> 48 us  [inverse_dft(): pl.pallas_call(functools.partial(inverse_kernel, counts, vb, latd, scale,...]
    pallas_call x2, Pallas kernels: 40.5 us -> 33.9 us  [legendre_step(): pl.pallas_call(functools.partial(legendre_kernel, groups, levs, latd, nmo...]
    pallas_call x2 -> x4, Pallas kernels: 6.04 us -> 8.86 us  [make_table(): pl.pallas_call(functools.partial(table_kernel, nblk), out_shape=jax.Shape...]
  transfers between devices with their start and end apart: 32 -> 32, of which waited for: 17 -> 16; matrix products, arithmetic and copies ran while one was open for 2% -> 2% of each run, Pallas kernels for 12% -> 24%
where the time goes in v1:
time: 363 us; the launch traced here: 359 us
  Pallas kernels  154 us (42%)
  waiting for transfers between devices  142 us (39%)
  starting transfers between devices  41.1 us (11%)
  local copies, waits for them, and re-layouts  13.6 us (4%)
  other arithmetic  6.75 us (2%)
    ppermute x28, waiting for transfers between devices, exchange(): out[r] = lax.ppermute(blocks[r], lat_lev, pairs)  137 us
    pallas_call x4, Pallas kernels, dft(): pl.pallas_call(functools.partial(dft_kernel, groups, vb, latd), out_shape...  53 us
    pallas_call x3, Pallas kernels, inverse_dft(): pl.pallas_call(functools.partial(inverse_kernel, counts, vb, latd, scale,...  48 us
    ppermute x28, starting transfers between devices, exchange(): out[r] = lax.ppermute(blocks[r], lat_lev, pairs)  40.7 us
    pallas_call x2, Pallas kernels, legendre_step(): pl.pallas_call(functools.partial(legendre_kernel, groups, levs, latd, nmo...  33.9 us
    pallas_call x4, Pallas kernels, make_table(): pl.pallas_call(functools.partial(table_kernel, nblk), out_shape=jax.Shape...  8.86 us
  transfers between devices with their start and end apart: 32, of which 16 were waited for; matrix products, arithmetic and copies ran while one was open for 2% of the time, Pallas kernels for 24%

profile of v1, /device:TPU:12, one launch (start us, length us, event | category | flops | bytes accessed | tf_op | source)
XLA Modules:
  0.0 358.8 jit_solution(8910063405006469903)
XLA Ops:
  4.4 2.6 fusion.26
  7.0 2.2 table.6.t_ref.refs_0_
  10.6 13.2 %dft.6 = (bf16[24,2,24,120]{3,2,1,0:T(8,128)(2,1)}, bf16[24,2,24,120]{3,2,1,0:T(8,128)(2,1)}, bf16[24,2,24,120]{3,2,1,0:T(8,128)(2,1)}, bf16[24,2,24,120]{3,2,1,0:T(8,128)(2,1)}) custom-call(bf16[24,120,1920]{2,1,0:T(8,128)(2,1)} %bitcast.57, bf16[192,1920]{1,0:T(8,128)(2,1)} %table.6.t_ref.refs_0_, f32[120,128]{1,0:T(8,128)} %broadcast_in_dim.32.wind_ref, ...), custom_call_target="tpu_custom_call" | custom-call | flops 4246732800 | bytes 12902400 | tf_op jit(solution)/shard_map/dft/pallas_call | solution.py:223
  23.8 1.5 collective-permute-start.7
  25.8 1.6 collective-permute-start.9
  27.3 2.2 table.7.t_ref.refs_1_
  30.3 13.3 %dft.7 = (bf16[24,2,24,120]{3,2,1,0:T(8,128)(2,1)}, bf16[24,2,24,120]{3,2,1,0:T(8,128)(2,1)}, bf16[24,2,24,120]{3,2,1,0:T(8,128)(2,1)}, bf16[24,2,24,120]{3,2,1,0:T(8,128)(2,1)}) custom-call(bf16[24,120,1920]{2,1,0:T(8,128)(2,1)} %bitcast.58, bf16[192,1920]{1,0:T(8,128)(2,1)} %table.7.t_ref.refs_1_, f32[120,128]{1,0:T(8,128)} %broadcast_in_dim.32.wind_ref, ...), custom_call_target="tpu_custom_call" | custom-call | flops 4246732800 | bytes 12902400 | tf_op jit(solution)/shard_map/dft/pallas_call | solution.py:223
  43.6 2.7 collective-permute-start.10
  46.3 1.3 collective-permute-start.11
  50.1 2.2 table.5.t_ref.refs_0_
  53.2 1.6 collective-permute-start.12
  56.1 13.3 %dft.4 = (bf16[24,2,24,120]{3,2,1,0:T(8,128)(2,1)}, bf16[24,2,24,120]{3,2,1,0:T(8,128)(2,1)}, bf16[24,2,24,120]{3,2,1,0:T(8,128)(2,1)}, bf16[24,2,24,120]{3,2,1,0:T(8,128)(2,1)}) custom-call(bf16[24,120,1920]{2,1,0:T(8,128)(2,1)} %bitcast.59, bf16[192,1920]{1,0:T(8,128)(2,1)} %table.5.t_ref.refs_0_, f32[120,128]{1,0:T(8,128)} %broadcast_in_dim.32.wind_ref, ...), custom_call_target="tpu_custom_call" | custom-call | flops 4246732800 | bytes 12902400 | tf_op jit(solution)/shard_map/dft/pallas_call | solution.py:223
  69.4 7.9 %collective-permute-done.10.refs_4_.rest_4_ = bf16[24,2,24,120]{3,2,1,0:T(8,128)(2,1)S(1)} collective-permute-done((bf16[24,2,24,120]{3,2,1,0:T(8,128)(2,1)}, bf16[24,2,24,120]{3,2,1,0:T(8,128)(2,1)S(1)}, u32[]{:S(2)}, u32[]{:S(2)}) %collective-permute-start.10) | collective-permute-done | bytes 276512 | tf_op jit(solution)/shard_map/ppermute | solution.py:545
  77.3 6.3 %collective-permute-done.11.refs_5_.rest_5_ = bf16[24,2,24,120]{3,2,1,0:T(8,128)(2,1)S(1)} collective-permute-done((bf16[24,2,24,120]{3,2,1,0:T(8,128)(2,1)}, bf16[24,2,24,120]{3,2,1,0:T(8,128)(2,1)S(1)}, u32[]{:S(2)}, u32[]{:S(2)}) %collective-permute-start.11) | collective-permute-done | bytes 276512 | tf_op jit(solution)/shard_map/ppermute | solution.py:545
  83.6 7.1 %collective-permute-done.12.refs_6_.rest_6_ = bf16[24,2,24,120]{3,2,1,0:T(8,128)(2,1)S(1)} collective-permute-done((bf16[24,2,24,120]{3,2,1,0:T(8,128)(2,1)S(1)}, bf16[24,2,24,120]{3,2,1,0:T(8,128)(2,1)S(1)}, u32[]{:S(2)}, u32[]{:S(2)}) %collective-permute-start.12) | collective-permute-done | bytes 276512 | tf_op jit(solution)/shard_map/ppermute | solution.py:545
  90.7 6.1 %collective-permute-done.13.refs_7_.rest_7_ = bf16[24,2,24,120]{3,2,1,0:T(8,128)(2,1)S(1)} collective-permute-done((bf16[24,2,24,120]{3,2,1,0:T(8,128)(2,1)S(1)}, bf16[24,2,24,120]{3,2,1,0:T(8,128)(2,1)S(1)}, u32[]{:S(2)}, u32[]{:S(2)}) %collective-permute-start.13) | collective-permute-done | bytes 276512 | tf_op jit(solution)/shard_map/ppermute | solution.py:545
  97.6 2.6 gather_halves.2
  101.9 1.2 collective-permute-done.14.rest_8_
  104.2 16.9 %legendre.2 = (bf16[24,2,24,120]{3,2,1,0:T(8,128)(2,1)}, bf16[24,2,24,120]{3,2,1,0:T(8,128)(2,1)}, bf16[24,2,24,120]{3,2,1,0:T(8,128)(2,1)}, bf16[24,2,24,120]{3...) custom-call(s32[4,12]{1,0:T(4,128)} %get-tuple-element.141.info, ...), custom_call_target="tpu_custom_call" | custom-call | flops 4076863488 | bytes 9142272 | tf_op jit(solution)/shard_map/legendre/pallas_call | solution.py:329
  121.2 2.2 table.4.t_ref.refs_0_
  124.1 13.2 %dft.5 = (bf16[24,2,24,120]{3,2,1,0:T(8,128)(2,1)}, bf16[24,2,24,120]{3,2,1,0:T(8,128)(2,1)}, bf16[24,2,24,120]{3,2,1,0:T(8,128)(2,1)}, bf16[24,2,24,120]{3,2,1,0:T(8,128)(2,1)}) custom-call(bf16[24,120,1920]{2,1,0:T(8,128)(2,1)} %bitcast.60, bf16[192,1920]{1,0:T(8,128)(2,1)} %table.4.t_ref.refs_0_, f32[120,128]{1,0:T(8,128)} %broadcast_in_dim.32.wind_ref, ...), custom_call_target="tpu_custom_call" | custom-call | flops 4246732800 | bytes 12902400 | tf_op jit(solution)/shard_map/dft/pallas_call | solution.py:223
  137.4 3.0 collective-permute-start.4
  140.4 2.5 collective-permute-start.5
  143.8 26.6 %collective-permute-done.3.refs_4_.rest_4_ = bf16[24,2,24,120]{3,2,1,0:T(8,128)(2,1)S(1)} collective-permute-done((bf16[24,2,24,120]{3,2,1,0:T(8,128)(2,1)}, bf16[24,2,24,120]{3,2,1,0:T(8,128)(2,1)S(1)}, u32[]{:S(2)}, u32[]{:S(2)}) %collective-permute-start.3) | collective-permute-done | bytes 276512 | tf_op jit(solution)/shard_map/ppermute | solution.py:545
  171.0 5.6 %collective-permute-done.4.refs_5_.rest_5_ = bf16[24,2,24,120]{3,2,1,0:T(8,128)(2,1)S(1)} collective-permute-done((bf16[24,2,24,120]{3,2,1,0:T(8,128)(2,1)}, bf16[24,2,24,120]{3,2,1,0:T(8,128)(2,1)S(1)}, u32[]{:S(2)}, u32[]{:S(2)}) %collective-permute-start.4) | collective-permute-done | bytes 276512 | tf_op jit(solution)/shard_map/ppermute | solution.py:545
  176.7 4.3 %collective-permute-start.1 = (bf16[24,2,24,120]{3,2,1,0:T(8,128)(2,1)}, bf16[24,2,24,120]{3,2,1,0:T(8,128)(2,1)S(1)}, u32[]{:S(2)}, u32[]{:S(2)}) collective-permute-start(bf16[24,2,24,120]{3,2,1,0:T(8,128)(2,1)} %get-tuple-element.57), channel_id=1, source_target_pairs={{0,4},{2,6},{4,0},{6,2},{8,12},{10,14},{12,8},{14,10},{1,5},{3,7},... | collective-permute-start | bytes 829448 | tf_op jit(solution)/shard_map/ppermute | solution.py:545
  182.1 2.5 fill_halves.2
  184.6 1.2 collective-permute-done.5.refs_6_.rest_6_
  185.8 9.4 %collective-permute-done.6.refs_7_.rest_7_ = bf16[24,2,24,120]{3,2,1,0:T(8,128)(2,1)S(1)} collective-permute-done((bf16[24,2,24,120]{3,2,1,0:T(8,128)(2,1)}, bf16[24,2,24,120]{3,2,1,0:T(8,128)(2,1)S(1)}, u32[]{:S(2)}, u32[]{:S(2)}) %collective-permute-start.6) | collective-permute-done | bytes 276512 | tf_op jit(solution)/shard_map/ppermute | solution.py:545
  195.2 3.0 collective-permute-done.2.refs_3_.rest_3_
  199.0 2.6 gather_halves.3
  201.5 3.1 collective-permute-done.16.rest_8_
  205.6 17.0 %legendre.3 = (bf16[24,2,24,120]{3,2,1,0:T(8,128)(2,1)}, bf16[24,2,24,120]{3,2,1,0:T(8,128)(2,1)}, bf16[24,2,24,120]{3,2,1,0:T(8,128)(2,1)}, bf16[24,2,24,120]{3...) custom-call(s32[4,12]{1,0:T(4,128)} %get-tuple-element.142.info, ...), custom_call_target="tpu_custom_call" | custom-call | flops 4076863488 | bytes 9142272 | tf_op jit(solution)/shard_map/legendre/pallas_call | solution.py:329
  222.9 1.5 collective-permute-start.25
  224.4 2.0 collective-permute-start.27
  226.4 3.9 %collective-permute-start.29 = (bf16[24,2,24,120]{3,2,1,0:T(8,128)(2,1)S(1)}, bf16[24,2,24,120]{3,2,1,0:T(8,128)(2,1)}, u32[]{:S(2)}, u32[]{:S(2)}) collective-permute-start(bf16[24,2,24,120]{3,2,1,0:T(8,128)(2,1)S(1)} %copy-done.28), channel_id=1, source_target_pairs={{0,10},{2,8},{4,14},{6,12},{8,2},{10,0},{12,6},{14,4},{1,11},{3,9}... | collective-permute-start | bytes 829448 | tf_op jit(solution)/shard_map/ppermute | solution.py:545
  230.3 2.6 fill_halves.3
  233.0 9.1 %collective-permute-done.26.refs_4_ = bf16[24,2,24,120]{3,2,1,0:T(8,128)(2,1)} collective-permute-done((bf16[24,2,24,120]{3,2,1,0:T(8,128)(2,1)S(1)}, bf16[24,2,24,120]{3,2,1,0:T(8,128)(2,1)}, u32[]{:S(2)}, u32[]{:S(2)}) %collective-permute-start.26) | collective-permute-done | bytes 276512 | tf_op jit(solution)/shard_map/ppermute | solution.py:545
  242.8 5.0 %collective-permute-done.27.refs_5_ = bf16[24,2,24,120]{3,2,1,0:T(8,128)(2,1)} collective-permute-done((bf16[24,2,24,120]{3,2,1,0:T(8,128)(2,1)S(1)}, bf16[24,2,24,120]{3,2,1,0:T(8,128)(2,1)}, u32[]{:S(2)}, u32[]{:S(2)}) %collective-permute-start.27) | collective-permute-done | bytes 276512 | tf_op jit(solution)/shard_map/ppermute | solution.py:545
  247.8 4.0 %collective-permute-start.23 = (bf16[24,2,24,120]{3,2,1,0:T(8,128)(2,1)}, bf16[24,2,24,120]{3,2,1,0:T(8,128)(2,1)S(1)}, u32[]{:S(2)}, u32[]{:S(2)}) collective-permute-start(bf16[24,2,24,120]{3,2,1,0:T(8,128)(2,1)} %get-tuple-element.96), channel_id=1, source_target_pairs={{0,4},{2,6},{4,0},{6,2},{8,12},{10,14},{12,8},{14,10},{1,5},{3,7},... | collective-permute-start | bytes 829448 | tf_op jit(solution)/shard_map/ppermute | solution.py:545
  251.8 13.4 %collective-permute-done.29.refs_7_ = bf16[24,2,24,120]{3,2,1,0:T(8,128)(2,1)} collective-permute-done((bf16[24,2,24,120]{3,2,1,0:T(8,128)(2,1)S(1)}, bf16[24,2,24,120]{3,2,1,0:T(8,128)(2,1)}, u32[]{:S(2)}, u32[]{:S(2)}) %collective-permute-start.29) | collective-permute-done | bytes 276512 | tf_op jit(solution)/shard_map/ppermute | solution.py:545
  265.3 4.6 %collective-permute-start.18 = (bf16[24,2,24,120]{3,2,1,0:T(8,128)(2,1)}, bf16[24,2,24,120]{3,2,1,0:T(8,128)(2,1)S(1)}, u32[]{:S(2)}, u32[]{:S(2)}) collective-permute-start(bf16[24,2,24,120]{3,2,1,0:T(8,128)(2,1)} %get-tuple-element.90), channel_id=1, source_target_pairs={{0,8},{2,10},{4,12},{6,14},{8,0},{10,2},{12,4},{14,6},{1,9},{3,11}... | collective-permute-start | bytes 829448 | tf_op jit(solution)/shard_map/ppermute | solution.py:545
  269.8 10.2 %collective-permute-done.30.refs_8_ = bf16[24,2,24,120]{3,2,1,0:T(8,128)(2,1)S(1)} collective-permute-done((bf16[24,2,24,120]{3,2,1,0:T(8,128)(2,1)S(1)}, bf16[24,2,24,120]{3,2,1,0:T(8,128)(2,1)S(1)}, u32[]{:S(2)}, u32[]{:S(2)}) %collective-permute-start.30) | collective-permute-done | bytes 276512 | tf_op jit(solution)/shard_map/ppermute | solution.py:545
  280.1 26.2 %collective-permute-done.31.refs_9_ = bf16[24,2,24,120]{3,2,1,0:T(8,128)(2,1)S(1)} collective-permute-done((bf16[24,2,24,120]{3,2,1,0:T(8,128)(2,1)S(1)}, bf16[24,2,24,120]{3,2,1,0:T(8,128)(2,1)S(1)}, u32[]{:S(2)}, u32[]{:S(2)}) %collective-permute-start.31) | collective-permute-done | bytes 276512 | tf_op jit(solution)/shard_map/ppermute | solution.py:545
  306.7 1.5 collective-permute-start.21
  308.3 15.3 %inverse_dft.3.refs_5_ = f32[24,120,1920]{2,1,0:T(8,128)} custom-call(bf16[192,1920]{1,0:T(8,128)(2,1)} %table.6.t_ref.refs_0_, bf16[192,1920]{1,0:T(8,128)(2,1)} %table.7.t_ref.refs_1_, bf16[24,2,24,120]{3,2,1,0:T(8,128)(2,1)} %get-tuple-element.80.refs_8_.refs_2_, bf16[24,2,24,120]{3,2,1,0:T(8,128)(2,1)} %collective-permute-done.25.refs_3_, ...), custom_call_target="tpu_custom_call" | custom-call | flops 4246732800 | bytes 14745600 | tf_op jit(solution)/shard_map/inverse_dft/pallas_call | solution.py:456
  324.3 18.1 %inverse_dft.4.refs_5_ = f32[24,120,1920]{2,1,0:T(8,128)} custom-call(bf16[192,1920]{1,0:T(8,128)(2,1)} %table.5.t_ref.refs_0_, bf16[24,2,24,120]{3,2,1,0:T(8,128)(2,1)} %get-tuple-element.94.refs_10_.refs_1_, bf16[24,2,24,120]{3,2,1,0:T(8,128)(2,1)} %copy-done.33, bf16[24,2,24,120]{3,2,1,0:T(8,128)(2,1)} %copy-done.34, bf16[24,2,24,120]{3,2,1,0:T(8,128)(2,1)} %copy-done.35, ...), custom_call_target="tpu_custom_call" | custom-call | flops 2123366400 | bytes 12902400 | tf_op jit(solution)/shard_map/inverse_dft/pallas_call | solution.py:456
  344.1 14.6 %inverse_dft.5 = bf16[24,120,1920]{2,1,0:T(8,128)(2,1)} custom-call(bf16[192,1920]{1,0:T(8,128)(2,1)} %table.4.t_ref.refs_0_, bf16[24,2,24,120]{3,2,1,0:T(8,128)(2,1)} %copy-done.20, bf16[24,2,24,120]{3,2,1,0:T(8,128)(2,1)} %copy-done.21, bf16[24,2,24,120]{3,2,1,0:T(8,128)(2,1)} %copy-done.22, bf16[24,2,24,120]{3,2,1,0:T(8,128)(2,1)} %copy-done.23, ...), custom_call_target="tpu_custom_call" | custom-call | flops 2123366400 | bytes 12902400 | tf_op jit(solution)/shard_map/inverse_dft/pallas_call | solution.py:456
  (177 shorter events, 24.2 us)
Async XLA Ops:
  0.0 47.6 %copy-start = (f32[48,48]{1,0:T(8,128)S(1)}, f32[48,48]{1,0:T(8,128)}, u32[]{:S(2)}) copy-start(f32[48,48]{1,0:T(8,128)} %param.24) | copy-start | bytes 27652
  23.8 29.4 %collective-permute-start.7 = (bf16[24,2,24,120]{3,2,1,0:T(8,128)(2,1)}, bf16[24,2,24,120]{3,2,1,0:T(8,128)(2,1)S(1)}, u32[]{:S(2)}, u32[]{:S(2)}) collective-permute-start(bf16[24,2,24,120]{3,2,1,0:T(8,128)(2,1)} %get-tuple-element.64), channel_id=1, source_target_pairs={{0,2},{2,0},{4,6},{6,4},{8,10},{10,8},{12,14},{14,12},{1,3},{3,1},... | collective-permute-start | bytes 829448 | tf_op jit(solution)/shard_map/ppermute | solution.py:545
  25.3 29.5 %collective-permute-start.8 = (bf16[24,2,24,120]{3,2,1,0:T(8,128)(2,1)}, bf16[24,2,24,120]{3,2,1,0:T(8,128)(2,1)S(1)}, u32[]{:S(2)}, u32[]{:S(2)}) collective-permute-start(bf16[24,2,24,120]{3,2,1,0:T(8,128)(2,1)} %get-tuple-element.65), channel_id=1, source_target_pairs={{0,4},{2,6},{4,0},{6,2},{8,12},{10,14},{12,8},{14,10},{1,5},{3,7},... | collective-permute-start | bytes 829448 | tf_op jit(solution)/shard_map/ppermute | solution.py:545
  25.8 43.6 %collective-permute-start.9 = (bf16[24,2,24,120]{3,2,1,0:T(8,128)(2,1)}, bf16[24,2,24,120]{3,2,1,0:T(8,128)(2,1)S(1)}, u32[]{:S(2)}, u32[]{:S(2)}) collective-permute-start(bf16[24,2,24,120]{3,2,1,0:T(8,128)(2,1)} %get-tuple-element.66), channel_id=1, source_target_pairs={{0,6},{2,4},{4,2},{6,0},{8,14},{10,12},{12,10},{14,8},{1,7},{3,5},... | collective-permute-start | bytes 829448 | tf_op jit(solution)/shard_map/ppermute | solution.py:545
  30.3 17.3 %copy-start.40 = (s32[480]{0:T(512)S(1)}, s32[480]{0:T(512)}, u32[]{:S(2)}) copy-start(s32[480]{0:T(512)} %param.14) | copy-start | bytes 5764
  30.3 17.4 %copy-start.36 = (f32[48,48]{1,0:T(8,128)S(1)}, f32[48,48]{1,0:T(8,128)}, u32[]{:S(2)}) copy-start(f32[48,48]{1,0:T(8,128)} %param.22) | copy-start | bytes 27652
  30.3 17.9 %copy-start.37 = (f32[48,48]{1,0:T(8,128)S(1)}, f32[48,48]{1,0:T(8,128)}, u32[]{:S(2)}) copy-start(f32[48,48]{1,0:T(8,128)} %param.21) | copy-start | bytes 27652
  30.3 17.9 %copy-start.38 = (f32[48,48]{1,0:T(8,128)S(1)}, f32[48,48]{1,0:T(8,128)}, u32[]{:S(2)}) copy-start(f32[48,48]{1,0:T(8,128)} %param.25) | copy-start | bytes 27652
  30.3 19.1 %copy-start.41 = (f32[48]{0:T(128)S(1)}, f32[48]{0:T(128)}, u32[]{:S(2)}) copy-start(f32[48]{0:T(128)} %param.23) | copy-start | bytes 580
  43.6 33.7 %collective-permute-start.10 = (bf16[24,2,24,120]{3,2,1,0:T(8,128)(2,1)}, bf16[24,2,24,120]{3,2,1,0:T(8,128)(2,1)S(1)}, u32[]{:S(2)}, u32[]{:S(2)}) collective-permute-start(bf16[24,2,24,120]{3,2,1,0:T(8,128)(2,1)} %get-tuple-element.67), channel_id=1, source_target_pairs={{0,8},{2,10},{4,12},{6,14},{8,0},{10,2},{12,4},{14,6},{1,9},{3,11}... | collective-permute-start | bytes 829448 | tf_op jit(solution)/shard_map/ppermute | solution.py:545
  46.3 37.3 %collective-permute-start.11 = (bf16[24,2,24,120]{3,2,1,0:T(8,128)(2,1)}, bf16[24,2,24,120]{3,2,1,0:T(8,128)(2,1)S(1)}, u32[]{:S(2)}, u32[]{:S(2)}) collective-permute-start(bf16[24,2,24,120]{3,2,1,0:T(8,128)(2,1)} %get-tuple-element.68), channel_id=1, source_target_pairs={{0,10},{2,8},{4,14},{6,12},{8,2},{10,0},{12,6},{14,4},{1,11},{3,9}... | collective-permute-start | bytes 829448 | tf_op jit(solution)/shard_map/ppermute | solution.py:545
  53.2 37.5 %collective-permute-start.12 = (bf16[24,2,24,120]{3,2,1,0:T(8,128)(2,1)S(1)}, bf16[24,2,24,120]{3,2,1,0:T(8,128)(2,1)S(1)}, u32[]{:S(2)}, u32[]{:S(2)}) collective-permute-start(bf16[24,2,24,120]{3,2,1,0:T(8,128)(2,1)S(1)} %copy-done.43), channel_id=1, source_target_pairs={{0,12},{2,14},{4,8},{6,10},{8,4},{10,6},{12,0},{14,2},{1,13},{3,15... | collective-permute-start | bytes 829448 | tf_op jit(solution)/shard_map/ppermute | solution.py:545
  54.9 42.0 %collective-permute-start.13 = (bf16[24,2,24,120]{3,2,1,0:T(8,128)(2,1)S(1)}, bf16[24,2,24,120]{3,2,1,0:T(8,128)(2,1)S(1)}, u32[]{:S(2)}, u32[]{:S(2)}) collective-permute-start(bf16[24,2,24,120]{3,2,1,0:T(8,128)(2,1)S(1)} %copy-done.42), channel_id=1, source_target_pairs={{0,14},{2,12},{4,10},{6,8},{8,6},{10,4},{12,2},{14,0},{1,15},{3,13... | collective-permute-start | bytes 829448 | tf_op jit(solution)/shard_map/ppermute | solution.py:545
  69.3 27.5 %copy-start.8 = (bf16[24,2,24,120]{3,2,1,0:T(8,128)(2,1)}, bf16[24,2,24,120]{3,2,1,0:T(8,128)(2,1)S(1)}, u32[]{:S(2)}) copy-start(bf16[24,2,24,120]{3,2,1,0:T(8,128)(2,1)S(1)} %collective-permute-done.9.refs_3_.rest_3_) | copy-start | bytes 829444
  77.3 19.6 %copy-start.9 = (bf16[24,2,24,120]{3,2,1,0:T(8,128)(2,1)}, bf16[24,2,24,120]{3,2,1,0:T(8,128)(2,1)S(1)}, u32[]{:S(2)}) copy-start(bf16[24,2,24,120]{3,2,1,0:T(8,128)(2,1)S(1)} %collective-permute-done.10.refs_4_.rest_4_) | copy-start | bytes 829444
  100.1 3.1 collective-permute-start.14
  121.0 60.0 %collective-permute-start.15 = (bf16[8,12,2,24,120]{4,3,2,1,0:T(8,128)(2,1)}, bf16[8,12,2,24,120]{4,3,2,1,0:T(8,128)(2,1)S(1)}, u32[]{:S(2)}, u32[]{:S(2)}) collective-permute-start(bf16[8,12,2,24,120]{4,3,2,1,0:T(8,128)(2,1)} %get-tuple-element.71), channel_id=1, source_target_pairs={{0,1},{1,0},{2,3},{3,2},{4,5},{5,4},{6,7},{7,6},{8,9},{9,8},{10,11... | collective-permute-start | bytes 3317768 | tf_op jit(solution)/shard_map/ppermute | solution.py:549
  137.4 33.0 %collective-permute-start.3 = (bf16[24,2,24,120]{3,2,1,0:T(8,128)(2,1)}, bf16[24,2,24,120]{3,2,1,0:T(8,128)(2,1)S(1)}, u32[]{:S(2)}, u32[]{:S(2)}) collective-permute-start(bf16[24,2,24,120]{3,2,1,0:T(8,128)(2,1)} %get-tuple-element.59), channel_id=1, source_target_pairs={{0,8},{2,10},{4,12},{6,14},{8,0},{10,2},{12,4},{14,6},{1,9},{3,11}... | collective-permute-start | bytes 829448 | tf_op jit(solution)/shard_map/ppermute | solution.py:545
  137.4 39.3 %collective-permute-start.4 = (bf16[24,2,24,120]{3,2,1,0:T(8,128)(2,1)}, bf16[24,2,24,120]{3,2,1,0:T(8,128)(2,1)S(1)}, u32[]{:S(2)}, u32[]{:S(2)}) collective-permute-start(bf16[24,2,24,120]{3,2,1,0:T(8,128)(2,1)} %get-tuple-element.60), channel_id=1, source_target_pairs={{0,10},{2,8},{4,14},{6,12},{8,2},{10,0},{12,6},{14,4},{1,11},{3,9}... | collective-permute-start | bytes 829448 | tf_op jit(solution)/shard_map/ppermute | solution.py:545
  140.4 45.4 %collective-permute-start.5 = (bf16[24,2,24,120]{3,2,1,0:T(8,128)(2,1)}, bf16[24,2,24,120]{3,2,1,0:T(8,128)(2,1)S(1)}, u32[]{:S(2)}, u32[]{:S(2)}) collective-permute-start(bf16[24,2,24,120]{3,2,1,0:T(8,128)(2,1)} %get-tuple-element.61), channel_id=1, source_target_pairs={{0,12},{2,14},{4,8},{6,10},{8,4},{10,6},{12,0},{14,2},{1,13},{3,15... | collective-permute-start | bytes 829448 | tf_op jit(solution)/shard_map/ppermute | solution.py:545
  142.9 52.4 %collective-permute-start.6 = (bf16[24,2,24,120]{3,2,1,0:T(8,128)(2,1)}, bf16[24,2,24,120]{3,2,1,0:T(8,128)(2,1)S(1)}, u32[]{:S(2)}, u32[]{:S(2)}) collective-permute-start(bf16[24,2,24,120]{3,2,1,0:T(8,128)(2,1)} %get-tuple-element.62), channel_id=1, source_target_pairs={{0,14},{2,12},{4,10},{6,8},{8,6},{10,4},{12,2},{14,0},{1,15},{3,13... | collective-permute-start | bytes 829448 | tf_op jit(solution)/shard_map/ppermute | solution.py:545
  170.4 27.9 %copy-start.11 = (bf16[24,2,24,120]{3,2,1,0:T(8,128)(2,1)}, bf16[24,2,24,120]{3,2,1,0:T(8,128)(2,1)S(1)}, u32[]{:S(2)}) copy-start(bf16[24,2,24,120]{3,2,1,0:T(8,128)(2,1)S(1)} %collective-permute-done.3.refs_4_.rest_4_) | copy-start | bytes 829444
  170.4 24.8 %collective-permute-start = (bf16[24,2,24,120]{3,2,1,0:T(8,128)(2,1)}, bf16[24,2,24,120]{3,2,1,0:T(8,128)(2,1)S(1)}, u32[]{:S(2)}, u32[]{:S(2)}) collective-permute-start(bf16[24,2,24,120]{3,2,1,0:T(8,128)(2,1)} %get-tuple-element.56), channel_id=1, source_target_pairs={{0,2},{2,0},{4,6},{6,4},{8,10},{10,8},{12,14},{14,12},{1,3},{3,1},... | collective-permute-start | bytes 829448 | tf_op jit(solution)/shard_map/ppermute | solution.py:545
  176.7 21.6 %copy-start.12 = (bf16[24,2,24,120]{3,2,1,0:T(8,128)(2,1)}, bf16[24,2,24,120]{3,2,1,0:T(8,128)(2,1)S(1)}, u32[]{:S(2)}) copy-start(bf16[24,2,24,120]{3,2,1,0:T(8,128)(2,1)S(1)} %collective-permute-done.4.refs_5_.rest_5_) | copy-start | bytes 829444
  176.7 18.5 %collective-permute-start.1 = (bf16[24,2,24,120]{3,2,1,0:T(8,128)(2,1)}, bf16[24,2,24,120]{3,2,1,0:T(8,128)(2,1)S(1)}, u32[]{:S(2)}, u32[]{:S(2)}) collective-permute-start(bf16[24,2,24,120]{3,2,1,0:T(8,128)(2,1)} %get-tuple-element.57), channel_id=1, source_target_pairs={{0,4},{2,6},{4,0},{6,2},{8,12},{10,14},{12,8},{14,10},{1,5},{3,7},... | collective-permute-start | bytes 829448 | tf_op jit(solution)/shard_map/ppermute | solution.py:545
  181.0 17.2 %collective-permute-start.2 = (bf16[24,2,24,120]{3,2,1,0:T(8,128)(2,1)}, bf16[24,2,24,120]{3,2,1,0:T(8,128)(2,1)S(1)}, u32[]{:S(2)}, u32[]{:S(2)}) collective-permute-start(bf16[24,2,24,120]{3,2,1,0:T(8,128)(2,1)} %get-tuple-element.58), channel_id=1, source_target_pairs={{0,6},{2,4},{4,2},{6,0},{8,14},{10,12},{12,10},{14,8},{1,7},{3,5},... | collective-permute-start | bytes 829448 | tf_op jit(solution)/shard_map/ppermute | solution.py:545
  201.5 3.1 collective-permute-start.16
  205.6 17.3 %copy-start.24 = (bf16[24,2,24,120]{3,2,1,0:T(8,128)(2,1)S(1)}, bf16[24,2,24,120]{3,2,1,0:T(8,128)(2,1)}, u32[]{:S(2)}) copy-start(bf16[24,2,24,120]{3,2,1,0:T(8,128)(2,1)} %get-tuple-element.98) | copy-start | bytes 829444
  205.6 18.8 %copy-start.25 = (bf16[24,2,24,120]{3,2,1,0:T(8,128)(2,1)S(1)}, bf16[24,2,24,120]{3,2,1,0:T(8,128)(2,1)}, u32[]{:S(2)}) copy-start(bf16[24,2,24,120]{3,2,1,0:T(8,128)(2,1)} %get-tuple-element.99) | copy-start | bytes 829444
  205.6 18.8 %copy-start.26 = (bf16[24,2,24,120]{3,2,1,0:T(8,128)(2,1)S(1)}, bf16[24,2,24,120]{3,2,1,0:T(8,128)(2,1)}, u32[]{:S(2)}) copy-start(bf16[24,2,24,120]{3,2,1,0:T(8,128)(2,1)} %get-tuple-element.100) | copy-start | bytes 829444
  205.6 20.8 %copy-start.27 = (bf16[24,2,24,120]{3,2,1,0:T(8,128)(2,1)S(1)}, bf16[24,2,24,120]{3,2,1,0:T(8,128)(2,1)}, u32[]{:S(2)}) copy-start(bf16[24,2,24,120]{3,2,1,0:T(8,128)(2,1)} %get-tuple-element.101) | copy-start | bytes 829444
  205.6 20.8 %copy-start.28 = (bf16[24,2,24,120]{3,2,1,0:T(8,128)(2,1)S(1)}, bf16[24,2,24,120]{3,2,1,0:T(8,128)(2,1)}, u32[]{:S(2)}) copy-start(bf16[24,2,24,120]{3,2,1,0:T(8,128)(2,1)} %get-tuple-element.102) | copy-start | bytes 829444
  222.7 3.7 %collective-permute-start.17 = (bf16[8,12,2,24,120]{4,3,2,1,0:T(8,128)(2,1)}, bf16[8,12,2,24,120]{4,3,2,1,0:T(8,128)(2,1)S(1)}, u32[]{:S(2)}, u32[]{:S(2)}) collective-permute-start(bf16[8,12,2,24,120]{4,3,2,1,0:T(8,128)(2,1)} %get-tuple-element.81), channel_id=1, source_target_pairs={{0,1},{1,0},{2,3},{3,2},{4,5},{5,4},{6,7},{7,6},{8,9},{9,8},{10,11... | collective-permute-start | bytes 3317768 | tf_op jit(solution)/shard_map/ppermute | solution.py:549
  222.9 10.0 %collective-permute-start.25 = (bf16[24,2,24,120]{3,2,1,0:T(8,128)(2,1)S(1)}, bf16[24,2,24,120]{3,2,1,0:T(8,128)(2,1)}, u32[]{:S(2)}, u32[]{:S(2)}) collective-permute-start(bf16[24,2,24,120]{3,2,1,0:T(8,128)(2,1)S(1)} %copy-done.24), channel_id=1, source_target_pairs={{0,2},{2,0},{4,6},{6,4},{8,10},{10,8},{12,14},{14,12},{1,3},{3,1},... | collective-permute-start | bytes 829448 | tf_op jit(solution)/shard_map/ppermute | solution.py:545
  224.4 17.7 %collective-permute-start.26 = (bf16[24,2,24,120]{3,2,1,0:T(8,128)(2,1)S(1)}, bf16[24,2,24,120]{3,2,1,0:T(8,128)(2,1)}, u32[]{:S(2)}, u32[]{:S(2)}) collective-permute-start(bf16[24,2,24,120]{3,2,1,0:T(8,128)(2,1)S(1)} %copy-done.25), channel_id=1, source_target_pairs={{0,4},{2,6},{4,0},{6,2},{8,12},{10,14},{12,8},{14,10},{1,5},{3,7},... | collective-permute-start | bytes 829448 | tf_op jit(solution)/shard_map/ppermute | solution.py:545
  224.4 23.4 %collective-permute-start.27 = (bf16[24,2,24,120]{3,2,1,0:T(8,128)(2,1)S(1)}, bf16[24,2,24,120]{3,2,1,0:T(8,128)(2,1)}, u32[]{:S(2)}, u32[]{:S(2)}) collective-permute-start(bf16[24,2,24,120]{3,2,1,0:T(8,128)(2,1)S(1)} %copy-done.26), channel_id=1, source_target_pairs={{0,6},{2,4},{4,2},{6,0},{8,14},{10,12},{12,10},{14,8},{1,7},{3,5},... | collective-permute-start | bytes 829448 | tf_op jit(solution)/shard_map/ppermute | solution.py:545
  226.4 21.4 %collective-permute-start.28 = (bf16[24,2,24,120]{3,2,1,0:T(8,128)(2,1)S(1)}, bf16[24,2,24,120]{3,2,1,0:T(8,128)(2,1)}, u32[]{:S(2)}, u32[]{:S(2)}) collective-permute-start(bf16[24,2,24,120]{3,2,1,0:T(8,128)(2,1)S(1)} %copy-done.27), channel_id=1, source_target_pairs={{0,8},{2,10},{4,12},{6,14},{8,0},{10,2},{12,4},{14,6},{1,9},{3,11}... | collective-permute-start | bytes 829448 | tf_op jit(solution)/shard_map/ppermute | solution.py:545
  226.4 38.9 %collective-permute-start.29 = (bf16[24,2,24,120]{3,2,1,0:T(8,128)(2,1)S(1)}, bf16[24,2,24,120]{3,2,1,0:T(8,128)(2,1)}, u32[]{:S(2)}, u32[]{:S(2)}) collective-permute-start(bf16[24,2,24,120]{3,2,1,0:T(8,128)(2,1)S(1)} %copy-done.28), channel_id=1, source_target_pairs={{0,10},{2,8},{4,14},{6,12},{8,2},{10,0},{12,6},{14,4},{1,11},{3,9}... | collective-permute-start | bytes 829448 | tf_op jit(solution)/shard_map/ppermute | solution.py:545
  232.9 47.2 %collective-permute-start.30 = (bf16[24,2,24,120]{3,2,1,0:T(8,128)(2,1)S(1)}, bf16[24,2,24,120]{3,2,1,0:T(8,128)(2,1)S(1)}, u32[]{:S(2)}, u32[]{:S(2)}) collective-permute-start(bf16[24,2,24,120]{3,2,1,0:T(8,128)(2,1)S(1)} %copy-done.29), channel_id=1, source_target_pairs={{0,12},{2,14},{4,8},{6,10},{8,4},{10,6},{12,0},{14,2},{1,13},{3,15... | collective-permute-start | bytes 829448 | tf_op jit(solution)/shard_map/ppermute | solution.py:545
  242.1 64.2 %collective-permute-start.31 = (bf16[24,2,24,120]{3,2,1,0:T(8,128)(2,1)S(1)}, bf16[24,2,24,120]{3,2,1,0:T(8,128)(2,1)S(1)}, u32[]{:S(2)}, u32[]{:S(2)}) collective-permute-start(bf16[24,2,24,120]{3,2,1,0:T(8,128)(2,1)S(1)} %copy-done.30), channel_id=1, source_target_pairs={{0,14},{2,12},{4,10},{6,8},{8,6},{10,4},{12,2},{14,0},{1,15},{3,13... | collective-permute-start | bytes 829448 | tf_op jit(solution)/shard_map/ppermute | solution.py:545
  247.8 59.0 %collective-permute-start.22 = (bf16[24,2,24,120]{3,2,1,0:T(8,128)(2,1)}, bf16[24,2,24,120]{3,2,1,0:T(8,128)(2,1)S(1)}, u32[]{:S(2)}, u32[]{:S(2)}) collective-permute-start(bf16[24,2,24,120]{3,2,1,0:T(8,128)(2,1)} %get-tuple-element.95), channel_id=1, source_target_pairs={{0,2},{2,0},{4,6},{6,4},{8,10},{10,8},{12,14},{14,12},{1,3},{3,1},... | collective-permute-start | bytes 829448 | tf_op jit(solution)/shard_map/ppermute | solution.py:545
  247.8 60.5 %collective-permute-start.23 = (bf16[24,2,24,120]{3,2,1,0:T(8,128)(2,1)}, bf16[24,2,24,120]{3,2,1,0:T(8,128)(2,1)S(1)}, u32[]{:S(2)}, u32[]{:S(2)}) collective-permute-start(bf16[24,2,24,120]{3,2,1,0:T(8,128)(2,1)} %get-tuple-element.96), channel_id=1, source_target_pairs={{0,4},{2,6},{4,0},{6,2},{8,12},{10,14},{12,8},{14,10},{1,5},{3,7},... | collective-permute-start | bytes 829448 | tf_op jit(solution)/shard_map/ppermute | solution.py:545
  265.3 77.2 %collective-permute-start.18 = (bf16[24,2,24,120]{3,2,1,0:T(8,128)(2,1)}, bf16[24,2,24,120]{3,2,1,0:T(8,128)(2,1)S(1)}, u32[]{:S(2)}, u32[]{:S(2)}) collective-permute-start(bf16[24,2,24,120]{3,2,1,0:T(8,128)(2,1)} %get-tuple-element.90), channel_id=1, source_target_pairs={{0,8},{2,10},{4,12},{6,14},{8,0},{10,2},{12,4},{14,6},{1,9},{3,11}... | collective-permute-start | bytes 829448 | tf_op jit(solution)/shard_map/ppermute | solution.py:545
  280.1 28.2 %copy-start.31 = (bf16[24,2,24,120]{3,2,1,0:T(8,128)(2,1)}, bf16[24,2,24,120]{3,2,1,0:T(8,128)(2,1)S(1)}, u32[]{:S(2)}) copy-start(bf16[24,2,24,120]{3,2,1,0:T(8,128)(2,1)S(1)} %collective-permute-done.30.refs_8_) | copy-start | bytes 829444
  280.1 62.4 %collective-permute-start.19 = (bf16[24,2,24,120]{3,2,1,0:T(8,128)(2,1)}, bf16[24,2,24,120]{3,2,1,0:T(8,128)(2,1)S(1)}, u32[]{:S(2)}, u32[]{:S(2)}) collective-permute-start(bf16[24,2,24,120]{3,2,1,0:T(8,128)(2,1)} %get-tuple-element.91), channel_id=1, source_target_pairs={{0,10},{2,8},{4,14},{6,12},{8,2},{10,0},{12,6},{14,4},{1,11},{3,9}... | collective-permute-start | bytes 829448 | tf_op jit(solution)/shard_map/ppermute | solution.py:545
  306.2 36.2 %collective-permute-start.20 = (bf16[24,2,24,120]{3,2,1,0:T(8,128)(2,1)}, bf16[24,2,24,120]{3,2,1,0:T(8,128)(2,1)S(1)}, u32[]{:S(2)}, u32[]{:S(2)}) collective-permute-start(bf16[24,2,24,120]{3,2,1,0:T(8,128)(2,1)} %get-tuple-element.92), channel_id=1, source_target_pairs={{0,12},{2,14},{4,8},{6,10},{8,4},{10,6},{12,0},{14,2},{1,13},{3,15... | collective-permute-start | bytes 829448 | tf_op jit(solution)/shard_map/ppermute | solution.py:545
  306.7 35.8 %collective-permute-start.21 = (bf16[24,2,24,120]{3,2,1,0:T(8,128)(2,1)}, bf16[24,2,24,120]{3,2,1,0:T(8,128)(2,1)S(1)}, u32[]{:S(2)}, u32[]{:S(2)}) collective-permute-start(bf16[24,2,24,120]{3,2,1,0:T(8,128)(2,1)} %get-tuple-element.93), channel_id=1, source_target_pairs={{0,14},{2,12},{4,10},{6,8},{8,6},{10,4},{12,2},{14,0},{1,15},{3,13... | collective-permute-start | bytes 829448 | tf_op jit(solution)/shard_map/ppermute | solution.py:545
  308.3 15.3 %collective-permute-start.24 = (bf16[24,2,24,120]{3,2,1,0:T(8,128)(2,1)}, bf16[24,2,24,120]{3,2,1,0:T(8,128)(2,1)S(1)}, u32[]{:S(2)}, u32[]{:S(2)}) collective-permute-start(bf16[24,2,24,120]{3,2,1,0:T(8,128)(2,1)} %get-tuple-element.97), channel_id=1, source_target_pairs={{0,6},{2,4},{4,2},{6,0},{8,14},{10,12},{12,10},{14,8},{1,7},{3,5},... | collective-permute-start | bytes 829448 | tf_op jit(solution)/shard_map/ppermute | solution.py:545
  (28 other events, 177.6 us)

commit v2 on v1

--- a/solution.py
+++ b/solution.py
@@ -134,6 +134,7 @@
 
 
 LANES = 128
+UNROLL = 2
 SHARES = (1, 1)
 
 
@@ -173,76 +174,111 @@
     )(jnp.cos(hi), jnp.sin(hi), jnp.cos(lo), jnp.sin(lo))
 
 
-def dft_kernel(groups, vb, latd, x_ref, t_ref, wind_ref, lat_ref, wave_ref, *rest):
+def column_table_kernel(nlon, wave_ref, out):
+    width = wave_ref.shape[1]
+    nblk = nlon // LANES
+    wave = wave_ref[...]
+
+    def angles(rows, step):
+        index = lax.broadcasted_iota(jnp.int32, (rows, width), 0) * step
+        turns = index.astype(F32) * wave
+        turns = turns - nlon * jnp.floor(turns * (1.0 / nlon))
+        turns = jnp.where(turns < 0.0, turns + nlon, turns)
+        turns = jnp.where(turns >= nlon, turns - nlon, turns)
+        return turns * (2.0 * jnp.pi / nlon)
+
+    lo = angles(LANES, 1)
+    cl, sl = jnp.cos(lo), jnp.sin(lo)
+    hi = angles(16, LANES)
+    ch, sh = jnp.cos(hi), jnp.sin(hi)
+    for b in range(nblk):
+        c, s = ch[b : b + 1], sh[b : b + 1]
+        rows = slice(b * LANES, (b + 1) * LANES)
+        out[rows, :width] = (c * cl - s * sl).astype(BF16)
+        out[rows, width:] = (-(s * cl + c * sl)).astype(BF16)
+
+
+def make_column_table(wave_row, nlon):
+    width = wave_row.shape[1]
+    return pl.pallas_call(
+        functools.partial(column_table_kernel, nlon),
+        out_shape=jax.ShapeDtypeStruct((nlon, 2 * width), BF16),
+        name="column_table",
+    )(wave_row)
+
+
+def dft_kernel(groups, vb, latd, slots, x_ref, t_ref, lat_ref, wave_ref, *rest):
     outs, (xf, scr) = rest[:groups], rest[groups:]
-    rows = t_ref.shape[0]
-    half = rows // 2
-    per = half // groups
-    nblk = x_ref.shape[2] // LANES
+    width = t_ref.shape[1] // 2
+    per = slots // groups
 
     @pl.when(pl.program_id(0) == 0)
     def _():
         xf[...] = jnp.zeros_like(xf)
 
-    wind = jnp.concatenate([wind_ref[...]] * nblk, axis=1)
-    rate = lat_ref[0:1, :]
-    weight = lat_ref[1:2, :]
-
-    def body(v, carry):
-        xv = x_ref[v]
-        x32 = xv.astype(F32)
-        xf[0:latd, :] = xv
-        xf[LANES : LANES + latd, :] = (x32 * (wind + x32)).astype(BF16)
-        both = lax.dot_general(
-            t_ref[...], xf[...], (((1,), (1,)), ((), ())), preferred_element_type=F32
-        )
-        plain, moved = both[:, :LANES], both[:, LANES:]
-        factor = wave_ref[...] * rate
-        real = (plain[:half] + factor * moved[half:]) * weight
-        imag = (plain[half:] - factor * moved[:half]) * weight
-        scr[pl.ds(v, half, stride=vb), :] = real
-        scr[pl.ds(half * vb + v, half, stride=vb), :] = imag
+    wind = lat_ref[:, 0:1]
+    factor = lat_ref[:, 1:2] * wave_ref[...]
+    weight = lat_ref[:, 2:3]
+    pair = 2
+
+    def body(p, carry):
+        for u in range(pair):
+            xv = x_ref[p * pair + u]
+            x32 = xv.astype(F32)
+            at = u * 2 * LANES
+            xf[at : at + latd, :] = xv
+            xf[at + LANES : at + LANES + latd, :] = (x32 * (wind + x32)).astype(BF16)
+        both = jnp.dot(xf[...], t_ref[...], preferred_element_type=F32)
+        for u in range(pair):
+            v = p * pair + u
+            at = u * 2 * LANES
+            plain = both[at : at + latd]
+            moved = both[at + LANES : at + LANES + latd]
+            real = (plain[:, :width] + factor * moved[:, width:]) * weight
+            imag = (plain[:, width:] - factor * moved[:, :width]) * weight
+            pad = jnp.zeros((LANES - latd, width), F32)
+            real = jnp.concatenate([real, pad], axis=0).T
+            imag = jnp.concatenate([imag, pad], axis=0).T
+            scr[pl.ds(v, slots, stride=vb), :] = real[:slots]
+            scr[pl.ds(slots * vb + v, slots, stride=vb), :] = imag[:slots]
         return carry
 
-    lax.fori_loop(0, vb, body, 0, unroll=2)
+    lax.fori_loop(0, vb // pair, body, 0, unroll=UNROLL)
     for g in range(groups):
         for c in range(2):
-            start = (c * half + g * per) * vb
+            start = (c * slots + g * per) * vb
             piece = scr[start : start + per * vb, :].reshape(per, vb, LANES)
             outs[g][:, c] = piece[:, :, :latd].astype(BF16)
 
 
-def dft(x, table, wind, latrow, waves, groups):
+def dft(x, table, per_lat, wave_row, slots, groups):
     levd, latd, nlon = x.shape
-    rows = table.shape[0]
-    half = rows // 2
-    per = half // groups
+    per = slots // groups
     vb = 8
     const = lambda i: (0, 0)
     block = pl.BlockSpec((per, 2, vb, latd), lambda i: (0, 0, i, 0))
     return pl.pallas_call(
-        functools.partial(dft_kernel, groups, vb, latd),
+        functools.partial(dft_kernel, groups, vb, latd, slots),
         out_shape=[jax.ShapeDtypeStruct((per, 2, levd, latd), BF16)] * groups,
         grid=(levd // vb,),
         in_specs=[
             pl.BlockSpec((vb, latd, nlon), lambda i: (i, 0, 0)),
-            pl.BlockSpec((rows, nlon), const),
-            pl.BlockSpec((latd, LANES), const),
-            pl.BlockSpec((2, LANES), const),
-            pl.BlockSpec((half, LANES), const),
+            pl.BlockSpec(table.shape, const),
+            pl.BlockSpec(per_lat.shape, const),
+            pl.BlockSpec(wave_row.shape, const),
         ],
         out_specs=[block] * groups,
         scratch_shapes=[
-            pltpu.VMEM((2 * LANES, nlon), BF16),
-            pltpu.VMEM((rows * vb, LANES), F32),
+            pltpu.VMEM((4 * LANES, nlon), BF16),
+            pltpu.VMEM((2 * slots * vb, LANES), F32),
         ],
         cost_estimate=pl.CostEstimate(
-            flops=4 * rows * levd * latd * nlon,
-            bytes_accessed=2 * levd * latd * (nlon + rows) + 2 * rows * nlon,
+            flops=8 * slots * levd * latd * nlon,
+            bytes_accessed=2 * levd * latd * (nlon + 2 * slots) + 4 * slots * nlon,
             transcendentals=0,
         ),
         name="dft",
-    )(x, table, wind, latrow, jnp.broadcast_to(waves.astype(F32)[:, None], (half, LANES)))
+    )(x, table, per_lat, wave_row)
 
 
 def split3_dot(w3, x):
@@ -502,14 +538,9 @@
     waves = slot_wave.reshape(groups, 2, slots // 2)
     waves = xor_order(xor_order(waves, me, 0), f, 1)
     my_lats = lax.dynamic_slice_in_dim(lat_order, z * latd, latd)
-    onehot = (my_lats[:, None] == jnp.arange(nlat, dtype=jnp.int32)[None, :]).astype(F32)
-    per_lat = jnp.dot(
-        onehot,
-        jnp.stack([zonal_wind, zonal_rate, quad_weight * nlon ** (-0.5)], axis=1),
-        precision=PRECISE,
-    )
-    wind = jnp.broadcast_to(per_lat[:, 0:1], (latd, LANES))
-    latrow = jnp.pad(per_lat[:, 1:].T, ((0, 0), (0, LANES - latd)))
+    hits = my_lats[:, None, None] == jnp.arange(nlat, dtype=jnp.int32)[None, None, :]
+    zonal = jnp.stack([zonal_wind, zonal_rate, quad_weight * nlon ** (-0.5)], axis=0)
+    per_lat = jnp.sum(jnp.where(hits, zonal[None], 0.0), axis=2)
 
     first = f == 0
     mix = jnp.dot(vert_project, thermal_matrix, precision=PRECISE)
@@ -550,15 +581,13 @@
 
     far, near = far_near(groups)
     tables, arrived = [], []
-    for i, (at, part) in enumerate(zip(starts, parts)):
-        blocks = [None] * groups
-        tables.append({})
-        for rels in (far, near) if i == 0 else (near, far):
-            w = waves[rels[0] : rels[-1] + 1, :, at : at + part].reshape(-1)
-            tables[i][rels] = make_table(w, nlon)
-            got = dft(grid_state[0], tables[i][rels], wind, latrow, w, len(rels))
-            blocks[rels[0] : rels[-1] + 1] = got
+    for at, part in zip(starts, parts):
+        w = waves[:, :, at : at + part].reshape(-1)
+        row = jnp.pad(w.astype(F32), (0, -w.shape[0] % LANES))[None, :]
+        columns = make_column_table(row, nlon)
+        blocks = dft(grid_state[0], columns, per_lat, row, w.shape[0], groups)
         arrived.append(exchange(blocks, far + near))
+        tables.append(make_table(w, nlon))
     legendre = jnp.swapaxes(legendre, 1, 2)
     returned = []
     after = [arrived[-1][0]]
@@ -580,12 +609,14 @@
         returned.append(exchange(sent, near + far))
     total = None
     last = len(parts) - 1
-    scale = float(nmodes) ** (-0.5)
-    one = lambda i, rels: (tables[i][rels], [returned[i][r] for r in rels])
-    for i in range(last):
-        total = inverse_dft([one(i, near), one(i, far)], total, scale, F32, after)
-    total = inverse_dft([one(last, near)], total, scale, F32, [])
-    total = inverse_dft([one(last, far)], total, scale, BF16, [])
+    for i in range(len(parts)):
+        total = inverse_dft(
+            [(tables[i], returned[i])],
+            total,
+            float(nmodes) ** (-0.5),
+            BF16 if i == last else F32,
+            [] if i == last else after,
+        )
     return total[None]
 
 

time: 363 us -> 321 us (0.88); the launches traced: 359 us -> 321 us
  Pallas kernels: 154 us -> 126 us
  waiting for transfers between devices: 142 us -> 135 us
    pallas_call x3 -> x2, Pallas kernels: 48 us -> 30.9 us  [inverse_dft(): pl.pallas_call(functools.partial(inverse_kernel, counts, vb, latd, scale,...]
    pallas_call x4, Pallas kernels: 53 us -> 45 us  [the longest x2 38.9 us: dft(): pl.pallas_call(functools.partial(dft_kernel, groups, vb, latd, slots), ou...]
    ppermute x28, waiting for transfers between devices: 137 us -> 130 us  [exchange(): out[r] = lax.ppermute(blocks[r], lat_lev, pairs)]
    pallas_call x4 -> x2, Pallas kernels: 8.86 us -> 6.12 us  [make_table(): pl.pallas_call(functools.partial(table_kernel, nblk), out_shape=jax.Shape...]
  transfers between devices with their start and end apart: 32 -> 32, of which waited for: 16 -> 20; matrix products, arithmetic and copies ran while one was open for 2% -> 3% of each run, Pallas kernels for 24% -> 15%
where the time goes in v2:
time: 321 us
  waiting for transfers between devices  135 us (42%)
  Pallas kernels  126 us (39%)
  starting transfers between devices  40.7 us (13%)
  local copies, waits for them, and re-layouts  10.6 us (3%)
  other arithmetic  7.64 us (2%)
    ppermute x28, waiting for transfers between devices, exchange(): out[r] = lax.ppermute(blocks[r], lat_lev, pairs)  130 us
    ppermute x28, starting transfers between devices, exchange(): out[r] = lax.ppermute(blocks[r], lat_lev, pairs)  40.3 us
    pallas_call x2, Pallas kernels, dft(): pl.pallas_call(functools.partial(dft_kernel, groups, vb, latd, slots), ou...  38.9 us
    pallas_call x2, Pallas kernels, legendre_step(): pl.pallas_call(functools.partial(legendre_kernel, groups, levs, latd, nmo...  34 us
    pallas_call x2, Pallas kernels, inverse_dft(): pl.pallas_call(functools.partial(inverse_kernel, counts, vb, latd, scale,...  30.9 us
  transfers between devices with their start and end apart: 32, of which 20 were waited for; matrix products, arithmetic and copies ran while one was open for 3% of the time, Pallas kernels for 15%

profile of v2, /device:TPU:12, one launch (start us, length us, event | category | flops | bytes accessed | tf_op | source)
XLA Modules:
  0.0 320.6 jit_solution(14266158126628126175)
XLA Ops:
  4.8 3.0 column_table.3.t_ref
  7.8 19.4 %dft.3 = (bf16[24,2,24,120]{3,2,1,0:T(8,128)(2,1)}, bf16[24,2,24,120]{3,2,1,0:T(8,128)(2,1)}, bf16[24,2,24,120]{3,2,1,0:T(8,128)(2,1)}, bf16[24,2,24,120]{3,2,1,...) custom-call(bf16[24,120,1920]{2,1,0:T(8,128)(2,1)} %bitcast.61, ...), custom_call_target="tpu_custom_call" | custom-call | flops 8493465600 | bytes 14745600 | tf_op jit(solution)/shard_map/dft/pallas_call | solution.py:260
  27.3 1.5 collective-permute-start.7
  29.2 1.6 collective-permute-start.9
  30.8 2.6 collective-permute-start.10
  35.9 3.0 column_table.2.t_ref
  39.0 19.5 %dft.2 = (bf16[24,2,24,120]{3,2,1,0:T(8,128)(2,1)}, bf16[24,2,24,120]{3,2,1,0:T(8,128)(2,1)}, bf16[24,2,24,120]{3,2,1,0:T(8,128)(2,1)}, bf16[24,2,24,120]{3,2,1,...) custom-call(bf16[24,120,1920]{2,1,0:T(8,128)(2,1)} %bitcast.62, ...), custom_call_target="tpu_custom_call" | custom-call | flops 8493465600 | bytes 14745600 | tf_op jit(solution)/shard_map/dft/pallas_call | solution.py:260
  59.5 1.6 collective-permute-start.12
  63.5 17.1 %collective-permute-done.12.refs_6_.rest_6_ = bf16[24,2,24,120]{3,2,1,0:T(8,128)(2,1)S(1)} collective-permute-done((bf16[24,2,24,120]{3,2,1,0:T(8,128)(2,1)S(1)}, bf16[24,2,24,120]{3,2,1,0:T(8,128)(2,1)S(1)}, u32[]{:S(2)}, u32[]{:S(2)}) %collective-permute-start.12) | collective-permute-done | bytes 276512 | tf_op jit(solution)/shard_map/ppermute | solution.py:576
  80.7 5.2 %collective-permute-done.13.refs_7_.rest_7_ = bf16[24,2,24,120]{3,2,1,0:T(8,128)(2,1)S(1)} collective-permute-done((bf16[24,2,24,120]{3,2,1,0:T(8,128)(2,1)S(1)}, bf16[24,2,24,120]{3,2,1,0:T(8,128)(2,1)S(1)}, u32[]{:S(2)}, u32[]{:S(2)}) %collective-permute-start.13) | collective-permute-done | bytes 276512 | tf_op jit(solution)/shard_map/ppermute | solution.py:576
  86.6 2.6 gather_halves.2
  90.9 1.3 collective-permute-done.14.rest_8_
  93.2 17.0 %legendre.2 = (bf16[24,2,24,120]{3,2,1,0:T(8,128)(2,1)}, bf16[24,2,24,120]{3,2,1,0:T(8,128)(2,1)}, bf16[24,2,24,120]{3,2,1,0:T(8,128)(2,1)}, bf16[24,2,24,120]{3...) custom-call(s32[4,12]{1,0:T(4,128)} %get-tuple-element.129.info, ...), custom_call_target="tpu_custom_call" | custom-call | flops 4076863488 | bytes 9142272 | tf_op jit(solution)/shard_map/legendre/pallas_call | solution.py:365
  110.4 1.5 collective-permute-start
  111.9 2.0 collective-permute-start.2
  114.9 4.7 %collective-permute-done.refs_1_.rest_1_ = bf16[24,2,24,120]{3,2,1,0:T(8,128)(2,1)S(1)} collective-permute-done((bf16[24,2,24,120]{3,2,1,0:T(8,128)(2,1)S(1)}, bf16[24,2,24,120]{3,2,1,0:T(8,128)(2,1)S(1)}, u32[]{:S(2)}, u32[]{:S(2)}) %collective-permute-start) | collective-permute-done | bytes 276512 | tf_op jit(solution)/shard_map/ppermute | solution.py:576
  119.7 11.8 %collective-permute-done.1.refs_2_.rest_2_ = bf16[24,2,24,120]{3,2,1,0:T(8,128)(2,1)S(1)} collective-permute-done((bf16[24,2,24,120]{3,2,1,0:T(8,128)(2,1)S(1)}, bf16[24,2,24,120]{3,2,1,0:T(8,128)(2,1)S(1)}, u32[]{:S(2)}, u32[]{:S(2)}) %collective-permute-start.1) | collective-permute-done | bytes 276512 | tf_op jit(solution)/shard_map/ppermute | solution.py:576
  133.1 2.5 fill_halves.2
  135.6 1.8 collective-permute-done.2.refs_3_.rest_3_
  137.4 16.9 %collective-permute-done.4.refs_5_.rest_5_ = bf16[24,2,24,120]{3,2,1,0:T(8,128)(2,1)S(1)} collective-permute-done((bf16[24,2,24,120]{3,2,1,0:T(8,128)(2,1)}, bf16[24,2,24,120]{3,2,1,0:T(8,128)(2,1)S(1)}, u32[]{:S(2)}, u32[]{:S(2)}) %collective-permute-start.4) | collective-permute-done | bytes 276512 | tf_op jit(solution)/shard_map/ppermute | solution.py:576
  154.3 6.5 %collective-permute-done.5.refs_6_.rest_6_ = bf16[24,2,24,120]{3,2,1,0:T(8,128)(2,1)S(1)} collective-permute-done((bf16[24,2,24,120]{3,2,1,0:T(8,128)(2,1)}, bf16[24,2,24,120]{3,2,1,0:T(8,128)(2,1)S(1)}, u32[]{:S(2)}, u32[]{:S(2)}) %collective-permute-start.5) | collective-permute-done | bytes 276512 | tf_op jit(solution)/shard_map/ppermute | solution.py:576
  160.8 6.8 %collective-permute-done.6.refs_7_.rest_7_ = bf16[24,2,24,120]{3,2,1,0:T(8,128)(2,1)S(1)} collective-permute-done((bf16[24,2,24,120]{3,2,1,0:T(8,128)(2,1)}, bf16[24,2,24,120]{3,2,1,0:T(8,128)(2,1)S(1)}, u32[]{:S(2)}, u32[]{:S(2)}) %collective-permute-start.6) | collective-permute-done | bytes 276512 | tf_op jit(solution)/shard_map/ppermute | solution.py:576
  168.3 2.6 gather_halves.3
  170.9 3.1 collective-permute-done.16.rest_8_
  175.0 17.0 %legendre.3 = (bf16[24,2,24,120]{3,2,1,0:T(8,128)(2,1)}, bf16[24,2,24,120]{3,2,1,0:T(8,128)(2,1)}, bf16[24,2,24,120]{3,2,1,0:T(8,128)(2,1)}, bf16[24,2,24,120]{3...) custom-call(s32[4,12]{1,0:T(4,128)} %get-tuple-element.130.info, ...), custom_call_target="tpu_custom_call" | custom-call | flops 4076863488 | bytes 9142272 | tf_op jit(solution)/shard_map/legendre/pallas_call | solution.py:365
  192.7 3.0 collective-permute-start.27
  196.7 2.0 collective-permute-start.29
  198.7 2.6 fill_halves.3
  201.6 1.5 collective-permute-start.30
  203.1 8.5 %collective-permute-done.26.refs_3_ = bf16[24,2,24,120]{3,2,1,0:T(8,128)(2,1)} collective-permute-done((bf16[24,2,24,120]{3,2,1,0:T(8,128)(2,1)S(1)}, bf16[24,2,24,120]{3,2,1,0:T(8,128)(2,1)}, u32[]{:S(2)}, u32[]{:S(2)}) %collective-permute-start.26) | collective-permute-done | bytes 276512 | tf_op jit(solution)/shard_map/ppermute | solution.py:576
  211.6 2.4 collective-permute-start.31
  214.0 3.3 %collective-permute-done.27.refs_4_ = bf16[24,2,24,120]{3,2,1,0:T(8,128)(2,1)} collective-permute-done((bf16[24,2,24,120]{3,2,1,0:T(8,128)(2,1)S(1)}, bf16[24,2,24,120]{3,2,1,0:T(8,128)(2,1)}, u32[]{:S(2)}, u32[]{:S(2)}) %collective-permute-start.27) | collective-permute-done | bytes 276512 | tf_op jit(solution)/shard_map/ppermute | solution.py:576
  217.3 2.0 collective-permute-start.18
  219.3 2.1 collective-permute-start.19
  221.4 2.6 fusion.23
  223.9 3.1 table.2.refs_0_
  227.1 3.0 table.3.refs_0_
  230.1 5.6 %collective-permute-done.29.refs_6_ = bf16[24,2,24,120]{3,2,1,0:T(8,128)(2,1)} collective-permute-done((bf16[24,2,24,120]{3,2,1,0:T(8,128)(2,1)S(1)}, bf16[24,2,24,120]{3,2,1,0:T(8,128)(2,1)}, u32[]{:S(2)}, u32[]{:S(2)}) %collective-permute-start.29) | collective-permute-done | bytes 276512 | tf_op jit(solution)/shard_map/ppermute | solution.py:576
  235.7 3.5 %collective-permute-start.20 = (bf16[24,2,24,120]{3,2,1,0:T(8,128)(2,1)S(1)}, bf16[24,2,24,120]{3,2,1,0:T(8,128)(2,1)S(1)}, u32[]{:S(2)}, u32[]{:S(2)}) collective-permute-start(bf16[24,2,24,120]{3,2,1,0:T(8,128)(2,1)S(1)} %copy-done.34), channel_id=1, source_target_pairs={{0,6},{2,4},{4,2},{6,0},{8,14},{10,12},{12,10},{14,8},{1,7},{3,5},... | collective-permute-start | bytes 829448 | tf_op jit(solution)/shard_map/ppermute | solution.py:576
  239.2 3.8 %collective-permute-done.30.refs_7_ = bf16[24,2,24,120]{3,2,1,0:T(8,128)(2,1)S(1)} collective-permute-done((bf16[24,2,24,120]{3,2,1,0:T(8,128)(2,1)S(1)}, bf16[24,2,24,120]{3,2,1,0:T(8,128)(2,1)S(1)}, u32[]{:S(2)}, u32[]{:S(2)}) %collective-permute-start.30) | collective-permute-done | bytes 276512 | tf_op jit(solution)/shard_map/ppermute | solution.py:576
  243.1 16.0 %collective-permute-done.31.refs_8_ = bf16[24,2,24,120]{3,2,1,0:T(8,128)(2,1)S(1)} collective-permute-done((bf16[24,2,24,120]{3,2,1,0:T(8,128)(2,1)S(1)}, bf16[24,2,24,120]{3,2,1,0:T(8,128)(2,1)S(1)}, u32[]{:S(2)}, u32[]{:S(2)}) %collective-permute-start.31) | collective-permute-done | bytes 276512 | tf_op jit(solution)/shard_map/ppermute | solution.py:576
  259.8 7.3 %collective-permute-start.23 = (bf16[24,2,24,120]{3,2,1,0:T(8,128)(2,1)S(1)}, bf16[24,2,24,120]{3,2,1,0:T(8,128)(2,1)S(1)}, u32[]{:S(2)}, u32[]{:S(2)}) collective-permute-start(bf16[24,2,24,120]{3,2,1,0:T(8,128)(2,1)S(1)} %copy-done.37), channel_id=1, source_target_pairs={{0,12},{2,14},{4,8},{6,10},{8,4},{10,6},{12,0},{14,2},{1,13},{3,15... | collective-permute-start | bytes 829448 | tf_op jit(solution)/shard_map/ppermute | solution.py:576
  267.2 13.4 %inverse_dft.2.refs_9_ = f32[24,120,1920]{2,1,0:T(8,128)} custom-call(bf16[384,1920]{1,0:T(8,128)(2,1)} %table.3.refs_0_, bf16[24,2,24,120]{3,2,1,0:T(8,128)(2,1)} %get-tuple-element.80.refs_8_.refs_1_, bf16[24,2,24,120]{3,2,1,0:T(8,128)(2,1)} %collective-permute-done.25.refs_2_, bf16[24,2,24,120]{3,2,1,0:T(8,128)(2,1)} %collective-permute-done.26.refs_3_, ...), custom_call_target="tpu_custom_call" | custom-call | flops 4246732800 | bytes 14745600 | tf_op jit(solution)/shard_map/inverse_dft/pallas_call | solution.py:492
  280.6 1.7 collective-permute-done.21.refs_5_
  282.3 6.3 %collective-permute-done.22.refs_6_ = bf16[24,2,24,120]{3,2,1,0:T(8,128)(2,1)S(1)} collective-permute-done((bf16[24,2,24,120]{3,2,1,0:T(8,128)(2,1)S(1)}, bf16[24,2,24,120]{3,2,1,0:T(8,128)(2,1)S(1)}, u32[]{:S(2)}, u32[]{:S(2)}) %collective-permute-start.22) | collective-permute-done | bytes 276512 | tf_op jit(solution)/shard_map/ppermute | solution.py:576
  288.6 7.8 %collective-permute-done.23.refs_7_ = bf16[24,2,24,120]{3,2,1,0:T(8,128)(2,1)S(1)} collective-permute-done((bf16[24,2,24,120]{3,2,1,0:T(8,128)(2,1)S(1)}, bf16[24,2,24,120]{3,2,1,0:T(8,128)(2,1)S(1)}, u32[]{:S(2)}, u32[]{:S(2)}) %collective-permute-start.23) | collective-permute-done | bytes 276512 | tf_op jit(solution)/shard_map/ppermute | solution.py:576
  296.4 5.8 %collective-permute-done.24.refs_8_ = bf16[24,2,24,120]{3,2,1,0:T(8,128)(2,1)S(1)} collective-permute-done((bf16[24,2,24,120]{3,2,1,0:T(8,128)(2,1)}, bf16[24,2,24,120]{3,2,1,0:T(8,128)(2,1)S(1)}, u32[]{:S(2)}, u32[]{:S(2)}) %collective-permute-start.24) | collective-permute-done | bytes 276512 | tf_op jit(solution)/shard_map/ppermute | solution.py:576
  302.9 17.5 %inverse_dft.3 = bf16[24,120,1920]{2,1,0:T(8,128)(2,1)} custom-call(bf16[384,1920]{1,0:T(8,128)(2,1)} %table.2.refs_0_, bf16[24,2,24,120]{3,2,1,0:T(8,128)(2,1)} %get-tuple-element.90.refs_9_.refs_1_, bf16[24,2,24,120]{3,2,1,0:T(8,128)(2,1)} %copy-done.20, bf16[24,2,24,120]{3,2,1,0:T(8,128)(2,1)} %copy-done.21, bf16[24,2,24,120]{3,2,1,0:T(8,128)(2,1)} %copy-done.22, ...), custom_call_target="tpu_custom_call" | custom-call | flops 4246732800 | bytes 14745600 | tf_op jit(solution)/shard_map/inverse_dft/pallas_call | solution.py:492
  (179 shorter events, 22.6 us)
Async XLA Ops:
  0.0 35.4 %copy-start = (f32[48,48]{1,0:T(8,128)S(1)}, f32[48,48]{1,0:T(8,128)}, u32[]{:S(2)}) copy-start(f32[48,48]{1,0:T(8,128)} %param.24) | copy-start | bytes 27652
  7.8 26.8 %copy-start.44 = (s32[480]{0:T(512)S(1)}, s32[480]{0:T(512)}, u32[]{:S(2)}) copy-start(s32[480]{0:T(512)} %param.14) | copy-start | bytes 5764
  7.8 27.6 %copy-start.40 = (f32[48,48]{1,0:T(8,128)S(1)}, f32[48,48]{1,0:T(8,128)}, u32[]{:S(2)}) copy-start(f32[48,48]{1,0:T(8,128)} %param.22) | copy-start | bytes 27652
  27.3 32.2 %collective-permute-start.7 = (bf16[24,2,24,120]{3,2,1,0:T(8,128)(2,1)}, bf16[24,2,24,120]{3,2,1,0:T(8,128)(2,1)S(1)}, u32[]{:S(2)}, u32[]{:S(2)}) collective-permute-start(bf16[24,2,24,120]{3,2,1,0:T(8,128)(2,1)} %get-tuple-element.64), channel_id=1, source_target_pairs={{0,2},{2,0},{4,6},{6,4},{8,10},{10,8},{12,14},{14,12},{1,3},{3,1},... | collective-permute-start | bytes 829448 | tf_op jit(solution)/shard_map/ppermute | solution.py:576
  28.8 32.3 %collective-permute-start.8 = (bf16[24,2,24,120]{3,2,1,0:T(8,128)(2,1)}, bf16[24,2,24,120]{3,2,1,0:T(8,128)(2,1)S(1)}, u32[]{:S(2)}, u32[]{:S(2)}) collective-permute-start(bf16[24,2,24,120]{3,2,1,0:T(8,128)(2,1)} %get-tuple-element.65), channel_id=1, source_target_pairs={{0,4},{2,6},{4,0},{6,2},{8,12},{10,14},{12,8},{14,10},{1,5},{3,7},... | collective-permute-start | bytes 829448 | tf_op jit(solution)/shard_map/ppermute | solution.py:576
  29.2 34.2 %collective-permute-start.9 = (bf16[24,2,24,120]{3,2,1,0:T(8,128)(2,1)}, bf16[24,2,24,120]{3,2,1,0:T(8,128)(2,1)S(1)}, u32[]{:S(2)}, u32[]{:S(2)}) collective-permute-start(bf16[24,2,24,120]{3,2,1,0:T(8,128)(2,1)} %get-tuple-element.66), channel_id=1, source_target_pairs={{0,6},{2,4},{4,2},{6,0},{8,14},{10,12},{12,10},{14,8},{1,7},{3,5},... | collective-permute-start | bytes 829448 | tf_op jit(solution)/shard_map/ppermute | solution.py:576
  30.8 32.7 %collective-permute-start.10 = (bf16[24,2,24,120]{3,2,1,0:T(8,128)(2,1)}, bf16[24,2,24,120]{3,2,1,0:T(8,128)(2,1)S(1)}, u32[]{:S(2)}, u32[]{:S(2)}) collective-permute-start(bf16[24,2,24,120]{3,2,1,0:T(8,128)(2,1)} %get-tuple-element.67), channel_id=1, source_target_pairs={{0,8},{2,10},{4,12},{6,14},{8,0},{10,2},{12,4},{14,6},{1,9},{3,11}... | collective-permute-start | bytes 829448 | tf_op jit(solution)/shard_map/ppermute | solution.py:576
  33.4 30.1 %collective-permute-start.11 = (bf16[24,2,24,120]{3,2,1,0:T(8,128)(2,1)}, bf16[24,2,24,120]{3,2,1,0:T(8,128)(2,1)S(1)}, u32[]{:S(2)}, u32[]{:S(2)}) collective-permute-start(bf16[24,2,24,120]{3,2,1,0:T(8,128)(2,1)} %get-tuple-element.68), channel_id=1, source_target_pairs={{0,10},{2,8},{4,14},{6,12},{8,2},{10,0},{12,6},{14,4},{1,11},{3,9}... | collective-permute-start | bytes 829448 | tf_op jit(solution)/shard_map/ppermute | solution.py:576
  38.9 22.9 %copy-start.45 = (f32[48]{0:T(128)S(1)}, f32[48]{0:T(128)}, u32[]{:S(2)}) copy-start(f32[48]{0:T(128)} %param.23) | copy-start | bytes 580
  39.0 24.3 %copy-start.43 = (s32[384]{0:T(512)S(1)}, s32[384]{0:T(512)}, u32[]{:S(2)}) copy-start(s32[384]{0:T(512)} %param.16) | copy-start | bytes 4612
  59.5 26.4 %copy-start.6 = (bf16[24,2,24,120]{3,2,1,0:T(8,128)(2,1)}, bf16[24,2,24,120]{3,2,1,0:T(8,128)(2,1)S(1)}, u32[]{:S(2)}) copy-start(bf16[24,2,24,120]{3,2,1,0:T(8,128)(2,1)S(1)} %collective-permute-done.7.refs_1_.rest_1_) | copy-start | bytes 829444
  59.5 21.2 %collective-permute-start.12 = (bf16[24,2,24,120]{3,2,1,0:T(8,128)(2,1)S(1)}, bf16[24,2,24,120]{3,2,1,0:T(8,128)(2,1)S(1)}, u32[]{:S(2)}, u32[]{:S(2)}) collective-permute-start(bf16[24,2,24,120]{3,2,1,0:T(8,128)(2,1)S(1)} %copy-done.49), channel_id=1, source_target_pairs={{0,12},{2,14},{4,8},{6,10},{8,4},{10,6},{12,0},{14,2},{1,13},{3,15... | collective-permute-start | bytes 829448 | tf_op jit(solution)/shard_map/ppermute | solution.py:576
  61.1 24.7 %copy-start.7 = (bf16[24,2,24,120]{3,2,1,0:T(8,128)(2,1)}, bf16[24,2,24,120]{3,2,1,0:T(8,128)(2,1)S(1)}, u32[]{:S(2)}) copy-start(bf16[24,2,24,120]{3,2,1,0:T(8,128)(2,1)S(1)} %collective-permute-done.8.refs_2_.rest_2_) | copy-start | bytes 829444
  61.1 24.7 %collective-permute-start.13 = (bf16[24,2,24,120]{3,2,1,0:T(8,128)(2,1)S(1)}, bf16[24,2,24,120]{3,2,1,0:T(8,128)(2,1)S(1)}, u32[]{:S(2)}, u32[]{:S(2)}) collective-permute-start(bf16[24,2,24,120]{3,2,1,0:T(8,128)(2,1)S(1)} %copy-done.48), channel_id=1, source_target_pairs={{0,14},{2,12},{4,10},{6,8},{8,6},{10,4},{12,2},{14,0},{1,15},{3,13... | collective-permute-start | bytes 829448 | tf_op jit(solution)/shard_map/ppermute | solution.py:576
  63.5 22.4 %copy-start.8 = (bf16[24,2,24,120]{3,2,1,0:T(8,128)(2,1)}, bf16[24,2,24,120]{3,2,1,0:T(8,128)(2,1)S(1)}, u32[]{:S(2)}) copy-start(bf16[24,2,24,120]{3,2,1,0:T(8,128)(2,1)S(1)} %collective-permute-done.9.refs_3_.rest_3_) | copy-start | bytes 829444
  63.5 22.4 %copy-start.9 = (bf16[24,2,24,120]{3,2,1,0:T(8,128)(2,1)}, bf16[24,2,24,120]{3,2,1,0:T(8,128)(2,1)S(1)}, u32[]{:S(2)}) copy-start(bf16[24,2,24,120]{3,2,1,0:T(8,128)(2,1)S(1)} %collective-permute-done.10.refs_4_.rest_4_) | copy-start | bytes 829444
  89.1 3.1 collective-permute-start.14
  110.2 21.9 %collective-permute-start.15 = (bf16[8,12,2,24,120]{4,3,2,1,0:T(8,128)(2,1)}, bf16[8,12,2,24,120]{4,3,2,1,0:T(8,128)(2,1)S(1)}, u32[]{:S(2)}, u32[]{:S(2)}) collective-permute-start(bf16[8,12,2,24,120]{4,3,2,1,0:T(8,128)(2,1)} %get-tuple-element.71), channel_id=1, source_target_pairs={{0,1},{1,0},{2,3},{3,2},{4,5},{5,4},{6,7},{7,6},{8,9},{9,8},{10,11... | collective-permute-start | bytes 3317768 | tf_op jit(solution)/shard_map/ppermute | solution.py:580
  110.4 9.3 %collective-permute-start = (bf16[24,2,24,120]{3,2,1,0:T(8,128)(2,1)S(1)}, bf16[24,2,24,120]{3,2,1,0:T(8,128)(2,1)S(1)}, u32[]{:S(2)}, u32[]{:S(2)}) collective-permute-start(bf16[24,2,24,120]{3,2,1,0:T(8,128)(2,1)S(1)} %copy-done.47), channel_id=1, source_target_pairs={{0,2},{2,0},{4,6},{6,4},{8,10},{10,8},{12,14},{14,12},{1,3},{3,1},... | collective-permute-start | bytes 829448 | tf_op jit(solution)/shard_map/ppermute | solution.py:576
  111.9 19.6 %collective-permute-start.1 = (bf16[24,2,24,120]{3,2,1,0:T(8,128)(2,1)S(1)}, bf16[24,2,24,120]{3,2,1,0:T(8,128)(2,1)S(1)}, u32[]{:S(2)}, u32[]{:S(2)}) collective-permute-start(bf16[24,2,24,120]{3,2,1,0:T(8,128)(2,1)S(1)} %copy-done.46), channel_id=1, source_target_pairs={{0,4},{2,6},{4,0},{6,2},{8,12},{10,14},{12,8},{14,10},{1,5},{3,7},... | collective-permute-start | bytes 829448 | tf_op jit(solution)/shard_map/ppermute | solution.py:576
  111.9 25.5 %collective-permute-start.2 = (bf16[24,2,24,120]{3,2,1,0:T(8,128)(2,1)}, bf16[24,2,24,120]{3,2,1,0:T(8,128)(2,1)S(1)}, u32[]{:S(2)}, u32[]{:S(2)}) collective-permute-start(bf16[24,2,24,120]{3,2,1,0:T(8,128)(2,1)} %get-tuple-element.58), channel_id=1, source_target_pairs={{0,6},{2,4},{4,2},{6,0},{8,14},{10,12},{12,10},{14,8},{1,7},{3,5},... | collective-permute-start | bytes 829448 | tf_op jit(solution)/shard_map/ppermute | solution.py:576
  113.9 23.5 %collective-permute-start.3 = (bf16[24,2,24,120]{3,2,1,0:T(8,128)(2,1)}, bf16[24,2,24,120]{3,2,1,0:T(8,128)(2,1)S(1)}, u32[]{:S(2)}, u32[]{:S(2)}) collective-permute-start(bf16[24,2,24,120]{3,2,1,0:T(8,128)(2,1)} %get-tuple-element.59), channel_id=1, source_target_pairs={{0,8},{2,10},{4,12},{6,14},{8,0},{10,2},{12,4},{14,6},{1,9},{3,11}... | collective-permute-start | bytes 829448 | tf_op jit(solution)/shard_map/ppermute | solution.py:576
  119.7 47.9 %copy-start.11 = (bf16[24,2,24,120]{3,2,1,0:T(8,128)(2,1)}, bf16[24,2,24,120]{3,2,1,0:T(8,128)(2,1)S(1)}, u32[]{:S(2)}) copy-start(bf16[24,2,24,120]{3,2,1,0:T(8,128)(2,1)S(1)} %collective-permute-done.refs_1_.rest_1_) | copy-start | bytes 829444
  119.7 34.6 %collective-permute-start.4 = (bf16[24,2,24,120]{3,2,1,0:T(8,128)(2,1)}, bf16[24,2,24,120]{3,2,1,0:T(8,128)(2,1)S(1)}, u32[]{:S(2)}, u32[]{:S(2)}) collective-permute-start(bf16[24,2,24,120]{3,2,1,0:T(8,128)(2,1)} %get-tuple-element.60), channel_id=1, source_target_pairs={{0,10},{2,8},{4,14},{6,12},{8,2},{10,0},{12,6},{14,4},{1,11},{3,9}... | collective-permute-start | bytes 829448 | tf_op jit(solution)/shard_map/ppermute | solution.py:576
  131.5 36.1 %copy-start.12 = (bf16[24,2,24,120]{3,2,1,0:T(8,128)(2,1)}, bf16[24,2,24,120]{3,2,1,0:T(8,128)(2,1)S(1)}, u32[]{:S(2)}) copy-start(bf16[24,2,24,120]{3,2,1,0:T(8,128)(2,1)S(1)} %collective-permute-done.1.refs_2_.rest_2_) | copy-start | bytes 829444
  131.5 29.2 %collective-permute-start.5 = (bf16[24,2,24,120]{3,2,1,0:T(8,128)(2,1)}, bf16[24,2,24,120]{3,2,1,0:T(8,128)(2,1)S(1)}, u32[]{:S(2)}, u32[]{:S(2)}) collective-permute-start(bf16[24,2,24,120]{3,2,1,0:T(8,128)(2,1)} %get-tuple-element.61), channel_id=1, source_target_pairs={{0,12},{2,14},{4,8},{6,10},{8,4},{10,6},{12,0},{14,2},{1,13},{3,15... | collective-permute-start | bytes 829448 | tf_op jit(solution)/shard_map/ppermute | solution.py:576
  132.1 35.5 %collective-permute-start.6 = (bf16[24,2,24,120]{3,2,1,0:T(8,128)(2,1)}, bf16[24,2,24,120]{3,2,1,0:T(8,128)(2,1)S(1)}, u32[]{:S(2)}, u32[]{:S(2)}) collective-permute-start(bf16[24,2,24,120]{3,2,1,0:T(8,128)(2,1)} %get-tuple-element.62), channel_id=1, source_target_pairs={{0,14},{2,12},{4,10},{6,8},{8,6},{10,4},{12,2},{14,0},{1,15},{3,13... | collective-permute-start | bytes 829448 | tf_op jit(solution)/shard_map/ppermute | solution.py:576
  137.3 30.3 %copy-start.14 = (bf16[24,2,24,120]{3,2,1,0:T(8,128)(2,1)}, bf16[24,2,24,120]{3,2,1,0:T(8,128)(2,1)S(1)}, u32[]{:S(2)}) copy-start(bf16[24,2,24,120]{3,2,1,0:T(8,128)(2,1)S(1)} %collective-permute-done.2.refs_3_.rest_3_) | copy-start | bytes 829444
  137.3 30.3 %copy-start.15 = (bf16[24,2,24,120]{3,2,1,0:T(8,128)(2,1)}, bf16[24,2,24,120]{3,2,1,0:T(8,128)(2,1)S(1)}, u32[]{:S(2)}) copy-start(bf16[24,2,24,120]{3,2,1,0:T(8,128)(2,1)S(1)} %collective-permute-done.3.refs_4_.rest_4_) | copy-start | bytes 829444
  170.9 3.1 collective-permute-start.16
  192.0 4.7 %collective-permute-start.17 = (bf16[8,12,2,24,120]{4,3,2,1,0:T(8,128)(2,1)}, bf16[8,12,2,24,120]{4,3,2,1,0:T(8,128)(2,1)S(1)}, u32[]{:S(2)}, u32[]{:S(2)}) collective-permute-start(bf16[8,12,2,24,120]{4,3,2,1,0:T(8,128)(2,1)} %get-tuple-element.81), channel_id=1, source_target_pairs={{0,1},{1,0},{2,3},{3,2},{4,5},{5,4},{6,7},{7,6},{8,9},{9,8},{10,11... | collective-permute-start | bytes 3317768 | tf_op jit(solution)/shard_map/ppermute | solution.py:580
  192.2 9.4 %collective-permute-start.25 = (bf16[24,2,24,120]{3,2,1,0:T(8,128)(2,1)S(1)}, bf16[24,2,24,120]{3,2,1,0:T(8,128)(2,1)}, u32[]{:S(2)}, u32[]{:S(2)}) collective-permute-start(bf16[24,2,24,120]{3,2,1,0:T(8,128)(2,1)S(1)} %copy-done.27), channel_id=1, source_target_pairs={{0,2},{2,0},{4,6},{6,4},{8,10},{10,8},{12,14},{14,12},{1,3},{3,1},... | collective-permute-start | bytes 829448 | tf_op jit(solution)/shard_map/ppermute | solution.py:576
  192.7 18.8 %collective-permute-start.26 = (bf16[24,2,24,120]{3,2,1,0:T(8,128)(2,1)S(1)}, bf16[24,2,24,120]{3,2,1,0:T(8,128)(2,1)}, u32[]{:S(2)}, u32[]{:S(2)}) collective-permute-start(bf16[24,2,24,120]{3,2,1,0:T(8,128)(2,1)S(1)} %copy-done.28), channel_id=1, source_target_pairs={{0,4},{2,6},{4,0},{6,2},{8,12},{10,14},{12,8},{14,10},{1,5},{3,7},... | collective-permute-start | bytes 829448 | tf_op jit(solution)/shard_map/ppermute | solution.py:576
  192.7 24.6 %collective-permute-start.27 = (bf16[24,2,24,120]{3,2,1,0:T(8,128)(2,1)S(1)}, bf16[24,2,24,120]{3,2,1,0:T(8,128)(2,1)}, u32[]{:S(2)}, u32[]{:S(2)}) collective-permute-start(bf16[24,2,24,120]{3,2,1,0:T(8,128)(2,1)S(1)} %copy-done.29), channel_id=1, source_target_pairs={{0,6},{2,4},{4,2},{6,0},{8,14},{10,12},{12,10},{14,8},{1,7},{3,5},... | collective-permute-start | bytes 829448 | tf_op jit(solution)/shard_map/ppermute | solution.py:576
  195.7 23.6 %collective-permute-start.28 = (bf16[24,2,24,120]{3,2,1,0:T(8,128)(2,1)S(1)}, bf16[24,2,24,120]{3,2,1,0:T(8,128)(2,1)}, u32[]{:S(2)}, u32[]{:S(2)}) collective-permute-start(bf16[24,2,24,120]{3,2,1,0:T(8,128)(2,1)S(1)} %copy-done.30), channel_id=1, source_target_pairs={{0,8},{2,10},{4,12},{6,14},{8,0},{10,2},{12,4},{14,6},{1,9},{3,11}... | collective-permute-start | bytes 829448 | tf_op jit(solution)/shard_map/ppermute | solution.py:576
  196.7 39.0 %collective-permute-start.29 = (bf16[24,2,24,120]{3,2,1,0:T(8,128)(2,1)S(1)}, bf16[24,2,24,120]{3,2,1,0:T(8,128)(2,1)}, u32[]{:S(2)}, u32[]{:S(2)}) collective-permute-start(bf16[24,2,24,120]{3,2,1,0:T(8,128)(2,1)S(1)} %copy-done.31), channel_id=1, source_target_pairs={{0,10},{2,8},{4,14},{6,12},{8,2},{10,0},{12,6},{14,4},{1,11},{3,9}... | collective-permute-start | bytes 829448 | tf_op jit(solution)/shard_map/ppermute | solution.py:576
  201.6 41.5 %collective-permute-start.30 = (bf16[24,2,24,120]{3,2,1,0:T(8,128)(2,1)S(1)}, bf16[24,2,24,120]{3,2,1,0:T(8,128)(2,1)S(1)}, u32[]{:S(2)}, u32[]{:S(2)}) collective-permute-start(bf16[24,2,24,120]{3,2,1,0:T(8,128)(2,1)S(1)} %copy-done.32), channel_id=1, source_target_pairs={{0,12},{2,14},{4,8},{6,10},{8,4},{10,6},{12,0},{14,2},{1,13},{3,15... | collective-permute-start | bytes 829448 | tf_op jit(solution)/shard_map/ppermute | solution.py:576
  211.6 47.5 %collective-permute-start.31 = (bf16[24,2,24,120]{3,2,1,0:T(8,128)(2,1)S(1)}, bf16[24,2,24,120]{3,2,1,0:T(8,128)(2,1)S(1)}, u32[]{:S(2)}, u32[]{:S(2)}) collective-permute-start(bf16[24,2,24,120]{3,2,1,0:T(8,128)(2,1)S(1)} %copy-done.33), channel_id=1, source_target_pairs={{0,14},{2,12},{4,10},{6,8},{8,6},{10,4},{12,2},{14,0},{1,15},{3,13... | collective-permute-start | bytes 829448 | tf_op jit(solution)/shard_map/ppermute | solution.py:576
  217.3 41.8 %collective-permute-start.18 = (bf16[24,2,24,120]{3,2,1,0:T(8,128)(2,1)}, bf16[24,2,24,120]{3,2,1,0:T(8,128)(2,1)S(1)}, u32[]{:S(2)}, u32[]{:S(2)}) collective-permute-start(bf16[24,2,24,120]{3,2,1,0:T(8,128)(2,1)} %get-tuple-element.91), channel_id=1, source_target_pairs={{0,2},{2,0},{4,6},{6,4},{8,10},{10,8},{12,14},{14,12},{1,3},{3,1},... | collective-permute-start | bytes 829448 | tf_op jit(solution)/shard_map/ppermute | solution.py:576
  219.3 47.8 %collective-permute-start.19 = (bf16[24,2,24,120]{3,2,1,0:T(8,128)(2,1)}, bf16[24,2,24,120]{3,2,1,0:T(8,128)(2,1)S(1)}, u32[]{:S(2)}, u32[]{:S(2)}) collective-permute-start(bf16[24,2,24,120]{3,2,1,0:T(8,128)(2,1)} %get-tuple-element.92), channel_id=1, source_target_pairs={{0,4},{2,6},{4,0},{6,2},{8,12},{10,14},{12,8},{14,10},{1,5},{3,7},... | collective-permute-start | bytes 829448 | tf_op jit(solution)/shard_map/ppermute | solution.py:576
  223.9 35.2 %copy-start.36 = (bf16[24,2,24,120]{3,2,1,0:T(8,128)(2,1)S(1)}, bf16[24,2,24,120]{3,2,1,0:T(8,128)(2,1)}, u32[]{:S(2)}) copy-start(bf16[24,2,24,120]{3,2,1,0:T(8,128)(2,1)} %get-tuple-element.95) | copy-start | bytes 829444
  223.9 35.9 %copy-start.37 = (bf16[24,2,24,120]{3,2,1,0:T(8,128)(2,1)S(1)}, bf16[24,2,24,120]{3,2,1,0:T(8,128)(2,1)}, u32[]{:S(2)}) copy-start(bf16[24,2,24,120]{3,2,1,0:T(8,128)(2,1)} %get-tuple-element.96) | copy-start | bytes 829444
  235.7 44.9 %collective-permute-start.20 = (bf16[24,2,24,120]{3,2,1,0:T(8,128)(2,1)S(1)}, bf16[24,2,24,120]{3,2,1,0:T(8,128)(2,1)S(1)}, u32[]{:S(2)}, u32[]{:S(2)}) collective-permute-start(bf16[24,2,24,120]{3,2,1,0:T(8,128)(2,1)S(1)} %copy-done.34), channel_id=1, source_target_pairs={{0,6},{2,4},{4,2},{6,0},{8,14},{10,12},{12,10},{14,8},{1,7},{3,5},... | collective-permute-start | bytes 829448 | tf_op jit(solution)/shard_map/ppermute | solution.py:576
  243.1 24.0 %copy-start.38 = (bf16[24,2,24,120]{3,2,1,0:T(8,128)(2,1)}, bf16[24,2,24,120]{3,2,1,0:T(8,128)(2,1)S(1)}, u32[]{:S(2)}) copy-start(bf16[24,2,24,120]{3,2,1,0:T(8,128)(2,1)S(1)} %collective-permute-done.30.refs_7_) | copy-start | bytes 829444
  243.1 39.2 %collective-permute-start.21 = (bf16[24,2,24,120]{3,2,1,0:T(8,128)(2,1)S(1)}, bf16[24,2,24,120]{3,2,1,0:T(8,128)(2,1)S(1)}, u32[]{:S(2)}, u32[]{:S(2)}) collective-permute-start(bf16[24,2,24,120]{3,2,1,0:T(8,128)(2,1)S(1)} %copy-done.35), channel_id=1, source_target_pairs={{0,8},{2,10},{4,12},{6,14},{8,0},{10,2},{12,4},{14,6},{1,9},{3,11}... | collective-permute-start | bytes 829448 | tf_op jit(solution)/shard_map/ppermute | solution.py:576
  259.1 29.5 %collective-permute-start.22 = (bf16[24,2,24,120]{3,2,1,0:T(8,128)(2,1)S(1)}, bf16[24,2,24,120]{3,2,1,0:T(8,128)(2,1)S(1)}, u32[]{:S(2)}, u32[]{:S(2)}) collective-permute-start(bf16[24,2,24,120]{3,2,1,0:T(8,128)(2,1)S(1)} %copy-done.36), channel_id=1, source_target_pairs={{0,10},{2,8},{4,14},{6,12},{8,2},{10,0},{12,6},{14,4},{1,11},{3,9}... | collective-permute-start | bytes 829448 | tf_op jit(solution)/shard_map/ppermute | solution.py:576
  259.8 36.6 %collective-permute-start.23 = (bf16[24,2,24,120]{3,2,1,0:T(8,128)(2,1)S(1)}, bf16[24,2,24,120]{3,2,1,0:T(8,128)(2,1)S(1)}, u32[]{:S(2)}, u32[]{:S(2)}) collective-permute-start(bf16[24,2,24,120]{3,2,1,0:T(8,128)(2,1)S(1)} %copy-done.37), channel_id=1, source_target_pairs={{0,12},{2,14},{4,8},{6,10},{8,4},{10,6},{12,0},{14,2},{1,13},{3,15... | collective-permute-start | bytes 829448 | tf_op jit(solution)/shard_map/ppermute | solution.py:576
  267.1 35.1 %collective-permute-start.24 = (bf16[24,2,24,120]{3,2,1,0:T(8,128)(2,1)}, bf16[24,2,24,120]{3,2,1,0:T(8,128)(2,1)S(1)}, u32[]{:S(2)}, u32[]{:S(2)}) collective-permute-start(bf16[24,2,24,120]{3,2,1,0:T(8,128)(2,1)} %get-tuple-element.97), channel_id=1, source_target_pairs={{0,14},{2,12},{4,10},{6,8},{8,6},{10,4},{12,2},{14,0},{1,15},{3,13... | collective-permute-start | bytes 829448 | tf_op jit(solution)/shard_map/ppermute | solution.py:576
  (34 other events, 428.4 us)

commit v3 on v2

--- a/solution.py
+++ b/solution.py
@@ -134,7 +134,6 @@
 
 
 LANES = 128
-UNROLL = 2
 SHARES = (1, 1)
 
 
@@ -174,9 +173,9 @@
     )(jnp.cos(hi), jnp.sin(hi), jnp.cos(lo), jnp.sin(lo))
 
 
-def column_table_kernel(nlon, wave_ref, out):
+def column_table_kernel(nlon, wave_ref, cos_ref, sin_ref):
     width = wave_ref.shape[1]
-    nblk = nlon // LANES
+    depth = cos_ref.shape[0]
     wave = wave_ref[...]
 
     def angles(rows, step):
@@ -189,61 +188,88 @@
 
     lo = angles(LANES, 1)
     cl, sl = jnp.cos(lo), jnp.sin(lo)
-    hi = angles(16, LANES)
+    hi = angles(8 * -(-depth // (8 * LANES)), LANES)
     ch, sh = jnp.cos(hi), jnp.sin(hi)
-    for b in range(nblk):
+    row = lax.broadcasted_iota(jnp.int32, (LANES, width), 0)
+    for b in range(depth // LANES):
         c, s = ch[b : b + 1], sh[b : b + 1]
+        at = row + b * LANES
+        share = jnp.where((at == 0) | (at == nlon // 2), 0.5, 1.0)
+        share = jnp.where(at > nlon // 2, 0.0, share)
         rows = slice(b * LANES, (b + 1) * LANES)
-        out[rows, :width] = (c * cl - s * sl).astype(BF16)
-        out[rows, width:] = (-(s * cl + c * sl)).astype(BF16)
-
-
-def make_column_table(wave_row, nlon):
+        cos_ref[rows, :] = (share * (c * cl - s * sl)).astype(BF16)
+        sin_ref[rows, :] = (-share * (s * cl + c * sl)).astype(BF16)
+
+
+def make_column_tables(wave_row, nlon):
     width = wave_row.shape[1]
+    depth = (nlon // 2 // LANES + 1) * LANES
     return pl.pallas_call(
         functools.partial(column_table_kernel, nlon),
-        out_shape=jax.ShapeDtypeStruct((nlon, 2 * width), BF16),
+        out_shape=[jax.ShapeDtypeStruct((depth, width), BF16)] * 2,
         name="column_table",
     )(wave_row)
 
 
-def dft_kernel(groups, vb, latd, slots, x_ref, t_ref, lat_ref, wave_ref, *rest):
-    outs, (xf, scr) = rest[:groups], rest[groups:]
-    width = t_ref.shape[1] // 2
+def dft_kernel(groups, vb, latd, slots, x_ref, cos_ref, sin_ref, lat_ref, wave_ref, *rest):
+    outs, (sums, difs, scr) = rest[:groups], rest[groups:]
+    width = cos_ref.shape[1]
+    depth = cos_ref.shape[0]
     per = slots // groups
+    nblk = x_ref.shape[2] // LANES
+    pair = 2
 
     @pl.when(pl.program_id(0) == 0)
     def _():
-        xf[...] = jnp.zeros_like(xf)
+        sums[...] = jnp.zeros_like(sums)
+        difs[...] = jnp.zeros_like(difs)
 
     wind = lat_ref[:, 0:1]
     factor = lat_ref[:, 1:2] * wave_ref[...]
     weight = lat_ref[:, 2:3]
-    pair = 2
-
-    def body(p, carry):
+    lane = lax.broadcasted_iota(jnp.int32, (latd, LANES), 1)
+    mirror = (LANES - lane) % LANES
+    first = lane == 0
+    wind = jnp.broadcast_to(wind, (latd, LANES))
+
+    def moved_of(x):
+        return (x * (wind + x)).astype(BF16).astype(F32)
+
+    def fold(p):
         for u in range(pair):
-            xv = x_ref[p * pair + u]
-            x32 = xv.astype(F32)
             at = u * 2 * LANES
-            xf[at : at + latd, :] = xv
-            xf[at + LANES : at + LANES + latd, :] = (x32 * (wind + x32)).astype(BF16)
-        both = jnp.dot(xf[...], t_ref[...], preferred_element_type=F32)
+            xs = [
+                x_ref[p * pair + u, :, b * LANES : (b + 1) * LANES].astype(F32)
+                for b in range(nblk)
+            ]
+            for b in range(depth // LANES):
+                cols = slice(b * LANES, (b + 1) * LANES)
+                x = xs[b]
+                turned = jnp.take_along_axis(xs[nblk - 1 - b], mirror, axis=1)
+                y = jnp.where(first, xs[(nblk - b) % nblk], turned)
+                f, g = moved_of(x), moved_of(y)
+                sums[p % 2, at : at + latd, cols] = (x + y).astype(BF16)
+                difs[p % 2, at : at + latd, cols] = (x - y).astype(BF16)
+                sums[p % 2, at + LANES : at + LANES + latd, cols] = (f + g).astype(BF16)
+                difs[p % 2, at + LANES : at + LANES + latd, cols] = (f - g).astype(BF16)
+
+    fold(0)
+    for p in range(vb // pair):
+        if p + 1 < vb // pair:
+            fold(p + 1)
+        even = jnp.dot(sums[p % 2], cos_ref[...], preferred_element_type=F32)
+        odd = jnp.dot(difs[p % 2], sin_ref[...], preferred_element_type=F32)
         for u in range(pair):
             v = p * pair + u
-            at = u * 2 * LANES
-            plain = both[at : at + latd]
-            moved = both[at + LANES : at + LANES + latd]
-            real = (plain[:, :width] + factor * moved[:, width:]) * weight
-            imag = (plain[:, width:] - factor * moved[:, :width]) * weight
+            plain = slice(u * 2 * LANES, u * 2 * LANES + latd)
+            moved = slice(u * 2 * LANES + LANES, u * 2 * LANES + LANES + latd)
+            real = (even[plain] + factor * odd[moved]) * weight
+            imag = (odd[plain] - factor * even[moved]) * weight
             pad = jnp.zeros((LANES - latd, width), F32)
             real = jnp.concatenate([real, pad], axis=0).T
             imag = jnp.concatenate([imag, pad], axis=0).T
             scr[pl.ds(v, slots, stride=vb), :] = real[:slots]
             scr[pl.ds(slots * vb + v, slots, stride=vb), :] = imag[:slots]
-        return carry
-
-    lax.fori_loop(0, vb // pair, body, 0, unroll=UNROLL)
     for g in range(groups):
         for c in range(2):
             start = (c * slots + g * per) * vb
@@ -251,34 +277,37 @@
             outs[g][:, c] = piece[:, :, :latd].astype(BF16)
 
 
-def dft(x, table, per_lat, wave_row, slots, groups):
+def dft(x, tables, per_lat, wave_row, slots, groups):
     levd, latd, nlon = x.shape
     per = slots // groups
     vb = 8
     const = lambda i: (0, 0)
     block = pl.BlockSpec((per, 2, vb, latd), lambda i: (0, 0, i, 0))
+    shape = tables[0].shape
     return pl.pallas_call(
         functools.partial(dft_kernel, groups, vb, latd, slots),
         out_shape=[jax.ShapeDtypeStruct((per, 2, levd, latd), BF16)] * groups,
         grid=(levd // vb,),
         in_specs=[
             pl.BlockSpec((vb, latd, nlon), lambda i: (i, 0, 0)),
-            pl.BlockSpec(table.shape, const),
+            pl.BlockSpec(shape, const),
+            pl.BlockSpec(shape, const),
             pl.BlockSpec(per_lat.shape, const),
             pl.BlockSpec(wave_row.shape, const),
         ],
         out_specs=[block] * groups,
         scratch_shapes=[
-            pltpu.VMEM((4 * LANES, nlon), BF16),
+            pltpu.VMEM((2, 4 * LANES, shape[0]), BF16),
+            pltpu.VMEM((2, 4 * LANES, shape[0]), BF16),
             pltpu.VMEM((2 * slots * vb, LANES), F32),
         ],
         cost_estimate=pl.CostEstimate(
-            flops=8 * slots * levd * latd * nlon,
+            flops=4 * slots * levd * latd * nlon,
             bytes_accessed=2 * levd * latd * (nlon + 2 * slots) + 4 * slots * nlon,
             transcendentals=0,
         ),
         name="dft",
-    )(x, table, per_lat, wave_row)
+    )(x, *tables, per_lat, wave_row)
 
 
 def split3_dot(w3, x):
@@ -584,7 +613,7 @@
     for at, part in zip(starts, parts):
         w = waves[:, :, at : at + part].reshape(-1)
         row = jnp.pad(w.astype(F32), (0, -w.shape[0] % LANES))[None, :]
-        columns = make_column_table(row, nlon)
+        columns = make_column_tables(row, nlon)
         blocks = dft(grid_state[0], columns, per_lat, row, w.shape[0], groups)
         arrived.append(exchange(blocks, far + near))
         tables.append(make_table(w, nlon))
@@ -662,6 +691,7 @@
             and latd % 8 == 0
             and latd <= LANES
             and nlon % (3 * LANES) == 0
+            and nlon % 2 == 0
         )
         if small and fits:
             unit = legendre.shape[0] // (2 * sum(SHARES))

time: 321 us -> 319 us (level)
  transfers between devices with their start and end apart: 32 -> 32, of which waited for: 20 -> 19; matrix products, arithmetic and copies ran while one was open for 3% -> 3% of each run, Pallas kernels for 15% -> 14%
where the time goes in v3:
time: 319 us; the launch traced here: 318 us
  waiting for transfers between devices  134 us (42%)
  Pallas kernels  124 us (39%)
  starting transfers between devices  41.9 us (13%)
  local copies, waits for them, and re-layouts  10.1 us (3%)
  other arithmetic  7.87 us (2%)
    ppermute x28, waiting for transfers between devices, exchange(): out[r] = lax.ppermute(blocks[r], lat_lev, pairs)  129 us
    ppermute x28, starting transfers between devices, exchange(): out[r] = lax.ppermute(blocks[r], lat_lev, pairs)  41.5 us
    pallas_call x2, Pallas kernels, dft(): pl.pallas_call(functools.partial(dft_kernel, groups, vb, latd, slots), ou...  37.4 us
    pallas_call x2, Pallas kernels, legendre_step(): pl.pallas_call(functools.partial(legendre_kernel, groups, levs, latd, nmo...  34.1 us
    pallas_call x2, Pallas kernels, inverse_dft(): pl.pallas_call(functools.partial(inverse_kernel, counts, vb, latd, scale,...  30.9 us
  transfers between devices with their start and end apart: 32, of which 19 were waited for; matrix products, arithmetic and copies ran while one was open for 3% of the time, Pallas kernels for 14%

profile of v3, /device:TPU:12, one launch (start us, length us, event | category | flops | bytes accessed | tf_op | source)
XLA Modules:
  0.0 318.1 jit_solution(10351968321489560669)
XLA Ops:
  4.8 2.5 column_table.3
  7.3 18.7 %dft.3 = (bf16[24,2,24,120]{3,2,1,0:T(8,128)(2,1)}, bf16[24,2,24,120]{3,2,1,0:T(8,128)(2,1)}, bf16[24,2,24,120]{3,2,1,0:T(8,128)(2,1)}, bf16[24,2,24,120]{3,2,1,...) custom-call(bf16[24,120,1920]{2,1,0:T(8,128)(2,1)} %bitcast.61, ...), custom_call_target="tpu_custom_call" | custom-call | flops 4246732800 | bytes 14745600 | tf_op jit(solution)/shard_map/dft/pallas_call | solution.py:287
  26.0 1.6 collective-permute-start.7
  28.0 1.5 collective-permute-start.9
  29.5 2.6 collective-permute-start.10
  36.6 2.5 column_table.2
  40.0 1.6 collective-permute-start.12
  41.7 5.6 %collective-permute-done.8.refs_2_.rest_2_ = bf16[24,2,24,120]{3,2,1,0:T(8,128)(2,1)S(1)} collective-permute-done((bf16[24,2,24,120]{3,2,1,0:T(8,128)(2,1)}, bf16[24,2,24,120]{3,2,1,0:T(8,128)(2,1)S(1)}, u32[]{:S(2)}, u32[]{:S(2)}) %collective-permute-start.8) | collective-permute-done | bytes 276512 | tf_op jit(solution)/shard_map/ppermute | solution.py:605
  47.6 18.7 %dft.2 = (bf16[24,2,24,120]{3,2,1,0:T(8,128)(2,1)}, bf16[24,2,24,120]{3,2,1,0:T(8,128)(2,1)}, bf16[24,2,24,120]{3,2,1,0:T(8,128)(2,1)}, bf16[24,2,24,120]{3,2,1,...) custom-call(bf16[24,120,1920]{2,1,0:T(8,128)(2,1)} %bitcast.62, ...), custom_call_target="tpu_custom_call" | custom-call | flops 4246732800 | bytes 14745600 | tf_op jit(solution)/shard_map/dft/pallas_call | solution.py:287
  66.4 5.1 %collective-permute-done.11.refs_5_.rest_5_ = bf16[24,2,24,120]{3,2,1,0:T(8,128)(2,1)S(1)} collective-permute-done((bf16[24,2,24,120]{3,2,1,0:T(8,128)(2,1)}, bf16[24,2,24,120]{3,2,1,0:T(8,128)(2,1)S(1)}, u32[]{:S(2)}, u32[]{:S(2)}) %collective-permute-start.11) | collective-permute-done | bytes 276512 | tf_op jit(solution)/shard_map/ppermute | solution.py:605
  71.4 6.3 %collective-permute-done.12.refs_6_.rest_6_ = bf16[24,2,24,120]{3,2,1,0:T(8,128)(2,1)S(1)} collective-permute-done((bf16[24,2,24,120]{3,2,1,0:T(8,128)(2,1)}, bf16[24,2,24,120]{3,2,1,0:T(8,128)(2,1)S(1)}, u32[]{:S(2)}, u32[]{:S(2)}) %collective-permute-start.12) | collective-permute-done | bytes 276512 | tf_op jit(solution)/shard_map/ppermute | solution.py:605
  77.8 5.0 %collective-permute-done.13.refs_7_.rest_7_ = bf16[24,2,24,120]{3,2,1,0:T(8,128)(2,1)S(1)} collective-permute-done((bf16[24,2,24,120]{3,2,1,0:T(8,128)(2,1)}, bf16[24,2,24,120]{3,2,1,0:T(8,128)(2,1)S(1)}, u32[]{:S(2)}, u32[]{:S(2)}) %collective-permute-start.13) | collective-permute-done | bytes 276512 | tf_op jit(solution)/shard_map/ppermute | solution.py:605
  83.5 2.6 gather_halves.2
  87.8 1.3 collective-permute-done.14.rest_8_
  90.1 17.0 %legendre.2 = (bf16[24,2,24,120]{3,2,1,0:T(8,128)(2,1)}, bf16[24,2,24,120]{3,2,1,0:T(8,128)(2,1)}, bf16[24,2,24,120]{3,2,1,0:T(8,128)(2,1)}, bf16[24,2,24,120]{3...) custom-call(s32[4,12]{1,0:T(4,128)} %get-tuple-element.137.info, ...), custom_call_target="tpu_custom_call" | custom-call | flops 4076863488 | bytes 9142272 | tf_op jit(solution)/shard_map/legendre/pallas_call | solution.py:394
  108.2 2.6 collective-permute-start.2
  110.8 2.1 collective-permute-start.3
  112.9 3.7 %collective-permute-done.refs_1_.rest_1_ = bf16[24,2,24,120]{3,2,1,0:T(8,128)(2,1)S(1)} collective-permute-done((bf16[24,2,24,120]{3,2,1,0:T(8,128)(2,1)S(1)}, bf16[24,2,24,120]{3,2,1,0:T(8,128)(2,1)S(1)}, u32[]{:S(2)}, u32[]{:S(2)}) %collective-permute-start) | collective-permute-done | bytes 276512 | tf_op jit(solution)/shard_map/ppermute | solution.py:605
  116.6 10.3 %collective-permute-done.1.refs_2_.rest_2_ = bf16[24,2,24,120]{3,2,1,0:T(8,128)(2,1)S(1)} collective-permute-done((bf16[24,2,24,120]{3,2,1,0:T(8,128)(2,1)S(1)}, bf16[24,2,24,120]{3,2,1,0:T(8,128)(2,1)S(1)}, u32[]{:S(2)}, u32[]{:S(2)}) %collective-permute-start.1) | collective-permute-done | bytes 276512 | tf_op jit(solution)/shard_map/ppermute | solution.py:605
  127.5 3.0 collective-permute-start.6
  130.4 2.5 fill_halves.2
  133.0 19.3 %collective-permute-done.4.refs_5_.rest_5_ = bf16[24,2,24,120]{3,2,1,0:T(8,128)(2,1)S(1)} collective-permute-done((bf16[24,2,24,120]{3,2,1,0:T(8,128)(2,1)}, bf16[24,2,24,120]{3,2,1,0:T(8,128)(2,1)S(1)}, u32[]{:S(2)}, u32[]{:S(2)}) %collective-permute-start.4) | collective-permute-done | bytes 276512 | tf_op jit(solution)/shard_map/ppermute | solution.py:605
  152.3 6.7 %collective-permute-done.5.refs_6_.rest_6_ = bf16[24,2,24,120]{3,2,1,0:T(8,128)(2,1)S(1)} collective-permute-done((bf16[24,2,24,120]{3,2,1,0:T(8,128)(2,1)}, bf16[24,2,24,120]{3,2,1,0:T(8,128)(2,1)S(1)}, u32[]{:S(2)}, u32[]{:S(2)}) %collective-permute-start.5) | collective-permute-done | bytes 276512 | tf_op jit(solution)/shard_map/ppermute | solution.py:605
  159.0 5.7 %collective-permute-done.6.refs_7_.rest_7_ = bf16[24,2,24,120]{3,2,1,0:T(8,128)(2,1)S(1)} collective-permute-done((bf16[24,2,24,120]{3,2,1,0:T(8,128)(2,1)}, bf16[24,2,24,120]{3,2,1,0:T(8,128)(2,1)S(1)}, u32[]{:S(2)}, u32[]{:S(2)}) %collective-permute-start.6) | collective-permute-done | bytes 276512 | tf_op jit(solution)/shard_map/ppermute | solution.py:605
  165.4 2.6 gather_halves.3
  167.9 3.1 collective-permute-done.16.rest_8_
  172.0 17.0 %legendre.3 = (bf16[24,2,24,120]{3,2,1,0:T(8,128)(2,1)}, bf16[24,2,24,120]{3,2,1,0:T(8,128)(2,1)}, bf16[24,2,24,120]{3,2,1,0:T(8,128)(2,1)}, bf16[24,2,24,120]{3...) custom-call(s32[4,12]{1,0:T(4,128)} %get-tuple-element.138.info, ...), custom_call_target="tpu_custom_call" | custom-call | flops 4076863488 | bytes 9142272 | tf_op jit(solution)/shard_map/legendre/pallas_call | solution.py:394
  189.3 1.5 collective-permute-start.25
  190.8 2.0 collective-permute-start.27
  193.8 2.9 collective-permute-start.29
  196.7 2.6 fill_halves.3
  199.3 1.5 collective-permute-start.30
  200.8 9.3 %collective-permute-done.26.refs_3_ = bf16[24,2,24,120]{3,2,1,0:T(8,128)(2,1)} collective-permute-done((bf16[24,2,24,120]{3,2,1,0:T(8,128)(2,1)S(1)}, bf16[24,2,24,120]{3,2,1,0:T(8,128)(2,1)}, u32[]{:S(2)}, u32[]{:S(2)}) %collective-permute-start.26) | collective-permute-done | bytes 276512 | tf_op jit(solution)/shard_map/ppermute | solution.py:605
  210.2 5.7 %collective-permute-done.27.refs_4_ = bf16[24,2,24,120]{3,2,1,0:T(8,128)(2,1)} collective-permute-done((bf16[24,2,24,120]{3,2,1,0:T(8,128)(2,1)S(1)}, bf16[24,2,24,120]{3,2,1,0:T(8,128)(2,1)}, u32[]{:S(2)}, u32[]{:S(2)}) %collective-permute-start.27) | collective-permute-done | bytes 276512 | tf_op jit(solution)/shard_map/ppermute | solution.py:605
  215.9 4.0 %collective-permute-start.19 = (bf16[24,2,24,120]{3,2,1,0:T(8,128)(2,1)}, bf16[24,2,24,120]{3,2,1,0:T(8,128)(2,1)S(1)}, u32[]{:S(2)}, u32[]{:S(2)}) collective-permute-start(bf16[24,2,24,120]{3,2,1,0:T(8,128)(2,1)} %get-tuple-element.100), channel_id=1, source_target_pairs={{0,4},{2,6},{4,0},{6,2},{8,12},{10,14},{12,8},{14,10},{1,5},{3,7},... | collective-permute-start | bytes 829448 | tf_op jit(solution)/shard_map/ppermute | solution.py:605
  219.9 2.8 fusion.23
  222.7 3.0 table.2.refs_0_
  225.7 3.1 table.3.refs_0_
  228.8 4.0 %collective-permute-done.29.refs_6_ = bf16[24,2,24,120]{3,2,1,0:T(8,128)(2,1)} collective-permute-done((bf16[24,2,24,120]{3,2,1,0:T(8,128)(2,1)S(1)}, bf16[24,2,24,120]{3,2,1,0:T(8,128)(2,1)}, u32[]{:S(2)}, u32[]{:S(2)}) %collective-permute-start.29) | collective-permute-done | bytes 276512 | tf_op jit(solution)/shard_map/ppermute | solution.py:605
  232.8 3.5 %collective-permute-start.20 = (bf16[24,2,24,120]{3,2,1,0:T(8,128)(2,1)S(1)}, bf16[24,2,24,120]{3,2,1,0:T(8,128)(2,1)S(1)}, u32[]{:S(2)}, u32[]{:S(2)}) collective-permute-start(bf16[24,2,24,120]{3,2,1,0:T(8,128)(2,1)S(1)} %copy-done.34), channel_id=1, source_target_pairs={{0,6},{2,4},{4,2},{6,0},{8,14},{10,12},{12,10},{14,8},{1,7},{3,5},... | collective-permute-start | bytes 829448 | tf_op jit(solution)/shard_map/ppermute | solution.py:605
  236.3 3.8 %collective-permute-done.30.refs_7_ = bf16[24,2,24,120]{3,2,1,0:T(8,128)(2,1)S(1)} collective-permute-done((bf16[24,2,24,120]{3,2,1,0:T(8,128)(2,1)S(1)}, bf16[24,2,24,120]{3,2,1,0:T(8,128)(2,1)S(1)}, u32[]{:S(2)}, u32[]{:S(2)}) %collective-permute-start.30) | collective-permute-done | bytes 276512 | tf_op jit(solution)/shard_map/ppermute | solution.py:605
  240.2 20.9 %collective-permute-done.31.refs_8_ = bf16[24,2,24,120]{3,2,1,0:T(8,128)(2,1)S(1)} collective-permute-done((bf16[24,2,24,120]{3,2,1,0:T(8,128)(2,1)S(1)}, bf16[24,2,24,120]{3,2,1,0:T(8,128)(2,1)S(1)}, u32[]{:S(2)}, u32[]{:S(2)}) %collective-permute-start.31) | collective-permute-done | bytes 276512 | tf_op jit(solution)/shard_map/ppermute | solution.py:605
  261.9 6.5 %collective-permute-start.24 = (bf16[24,2,24,120]{3,2,1,0:T(8,128)(2,1)}, bf16[24,2,24,120]{3,2,1,0:T(8,128)(2,1)S(1)}, u32[]{:S(2)}, u32[]{:S(2)}) collective-permute-start(bf16[24,2,24,120]{3,2,1,0:T(8,128)(2,1)} %get-tuple-element.105), channel_id=1, source_target_pairs={{0,14},{2,12},{4,10},{6,8},{8,6},{10,4},{12,2},{14,0},{1,15},{3,13... | collective-permute-start | bytes 829448 | tf_op jit(solution)/shard_map/ppermute | solution.py:605
  268.4 13.3 %inverse_dft.2.refs_9_ = f32[24,120,1920]{2,1,0:T(8,128)} custom-call(bf16[384,1920]{1,0:T(8,128)(2,1)} %table.3.refs_0_, bf16[24,2,24,120]{3,2,1,0:T(8,128)(2,1)} %get-tuple-element.88.refs_8_.refs_1_, bf16[24,2,24,120]{3,2,1,0:T(8,128)(2,1)} %collective-permute-done.25.refs_2_, bf16[24,2,24,120]{3,2,1,0:T(8,128)(2,1)} %collective-permute-done.26.refs_3_, ...), custom_call_target="tpu_custom_call" | custom-call | flops 4246732800 | bytes 14745600 | tf_op jit(solution)/shard_map/inverse_dft/pallas_call | solution.py:521
  281.8 4.5 %collective-permute-done.22.refs_6_ = bf16[24,2,24,120]{3,2,1,0:T(8,128)(2,1)S(1)} collective-permute-done((bf16[24,2,24,120]{3,2,1,0:T(8,128)(2,1)S(1)}, bf16[24,2,24,120]{3,2,1,0:T(8,128)(2,1)S(1)}, u32[]{:S(2)}, u32[]{:S(2)}) %collective-permute-start.22) | collective-permute-done | bytes 276512 | tf_op jit(solution)/shard_map/ppermute | solution.py:605
  286.3 7.8 %collective-permute-done.23.refs_7_ = bf16[24,2,24,120]{3,2,1,0:T(8,128)(2,1)S(1)} collective-permute-done((bf16[24,2,24,120]{3,2,1,0:T(8,128)(2,1)S(1)}, bf16[24,2,24,120]{3,2,1,0:T(8,128)(2,1)S(1)}, u32[]{:S(2)}, u32[]{:S(2)}) %collective-permute-start.23) | collective-permute-done | bytes 276512 | tf_op jit(solution)/shard_map/ppermute | solution.py:605
  294.1 5.5 %collective-permute-done.24.refs_8_ = bf16[24,2,24,120]{3,2,1,0:T(8,128)(2,1)S(1)} collective-permute-done((bf16[24,2,24,120]{3,2,1,0:T(8,128)(2,1)}, bf16[24,2,24,120]{3,2,1,0:T(8,128)(2,1)S(1)}, u32[]{:S(2)}, u32[]{:S(2)}) %collective-permute-start.24) | collective-permute-done | bytes 276512 | tf_op jit(solution)/shard_map/ppermute | solution.py:605
  300.3 17.5 %inverse_dft.3 = bf16[24,120,1920]{2,1,0:T(8,128)(2,1)} custom-call(bf16[384,1920]{1,0:T(8,128)(2,1)} %table.2.refs_0_, bf16[24,2,24,120]{3,2,1,0:T(8,128)(2,1)} %get-tuple-element.98.refs_9_.refs_1_, bf16[24,2,24,120]{3,2,1,0:T(8,128)(2,1)} %copy-done.20, bf16[24,2,24,120]{3,2,1,0:T(8,128)(2,1)} %copy-done.21, bf16[24,2,24,120]{3,2,1,0:T(8,128)(2,1)} %copy-done.22, ...), custom_call_target="tpu_custom_call" | custom-call | flops 4246732800 | bytes 14745600 | tf_op jit(solution)/shard_map/inverse_dft/pallas_call | solution.py:521
  (175 shorter events, 20.5 us)
Async XLA Ops:
  0.0 33.5 %copy-start = (f32[48,48]{1,0:T(8,128)S(1)}, f32[48,48]{1,0:T(8,128)}, u32[]{:S(2)}) copy-start(f32[48,48]{1,0:T(8,128)} %param.24) | copy-start | bytes 27652
  7.3 26.1 %copy-start.44 = (s32[480]{0:T(512)S(1)}, s32[480]{0:T(512)}, u32[]{:S(2)}) copy-start(s32[480]{0:T(512)} %param.14) | copy-start | bytes 5764
  7.3 26.2 %copy-start.40 = (f32[48,48]{1,0:T(8,128)S(1)}, f32[48,48]{1,0:T(8,128)}, u32[]{:S(2)}) copy-start(f32[48,48]{1,0:T(8,128)} %param.22) | copy-start | bytes 27652
  7.3 26.7 %copy-start.41 = (f32[48,48]{1,0:T(8,128)S(1)}, f32[48,48]{1,0:T(8,128)}, u32[]{:S(2)}) copy-start(f32[48,48]{1,0:T(8,128)} %param.21) | copy-start | bytes 27652
  7.3 26.7 %copy-start.42 = (f32[48,48]{1,0:T(8,128)S(1)}, f32[48,48]{1,0:T(8,128)}, u32[]{:S(2)}) copy-start(f32[48,48]{1,0:T(8,128)} %param.25) | copy-start | bytes 27652
  7.3 28.6 %copy-start.45 = (f32[48]{0:T(128)S(1)}, f32[48]{0:T(128)}, u32[]{:S(2)}) copy-start(f32[48]{0:T(128)} %param.23) | copy-start | bytes 580
  7.3 32.5 %copy-start.43 = (s32[384]{0:T(512)S(1)}, s32[384]{0:T(512)}, u32[]{:S(2)}) copy-start(s32[384]{0:T(512)} %param.16) | copy-start | bytes 4612
  26.0 14.0 %collective-permute-start.7 = (bf16[24,2,24,120]{3,2,1,0:T(8,128)(2,1)}, bf16[24,2,24,120]{3,2,1,0:T(8,128)(2,1)S(1)}, u32[]{:S(2)}, u32[]{:S(2)}) collective-permute-start(bf16[24,2,24,120]{3,2,1,0:T(8,128)(2,1)} %get-tuple-element.72), channel_id=1, source_target_pairs={{0,2},{2,0},{4,6},{6,4},{8,10},{10,8},{12,14},{14,12},{1,3},{3,1},... | collective-permute-start | bytes 829448 | tf_op jit(solution)/shard_map/ppermute | solution.py:605
  27.5 19.7 %collective-permute-start.8 = (bf16[24,2,24,120]{3,2,1,0:T(8,128)(2,1)}, bf16[24,2,24,120]{3,2,1,0:T(8,128)(2,1)S(1)}, u32[]{:S(2)}, u32[]{:S(2)}) collective-permute-start(bf16[24,2,24,120]{3,2,1,0:T(8,128)(2,1)} %get-tuple-element.73), channel_id=1, source_target_pairs={{0,4},{2,6},{4,0},{6,2},{8,12},{10,14},{12,8},{14,10},{1,5},{3,7},... | collective-permute-start | bytes 829448 | tf_op jit(solution)/shard_map/ppermute | solution.py:605
  28.0 38.3 %collective-permute-start.9 = (bf16[24,2,24,120]{3,2,1,0:T(8,128)(2,1)}, bf16[24,2,24,120]{3,2,1,0:T(8,128)(2,1)S(1)}, u32[]{:S(2)}, u32[]{:S(2)}) collective-permute-start(bf16[24,2,24,120]{3,2,1,0:T(8,128)(2,1)} %get-tuple-element.74), channel_id=1, source_target_pairs={{0,6},{2,4},{4,2},{6,0},{8,14},{10,12},{12,10},{14,8},{1,7},{3,5},... | collective-permute-start | bytes 829448 | tf_op jit(solution)/shard_map/ppermute | solution.py:605
  29.5 36.8 %collective-permute-start.10 = (bf16[24,2,24,120]{3,2,1,0:T(8,128)(2,1)}, bf16[24,2,24,120]{3,2,1,0:T(8,128)(2,1)S(1)}, u32[]{:S(2)}, u32[]{:S(2)}) collective-permute-start(bf16[24,2,24,120]{3,2,1,0:T(8,128)(2,1)} %get-tuple-element.75), channel_id=1, source_target_pairs={{0,8},{2,10},{4,12},{6,14},{8,0},{10,2},{12,4},{14,6},{1,9},{3,11}... | collective-permute-start | bytes 829448 | tf_op jit(solution)/shard_map/ppermute | solution.py:605
  32.1 39.3 %collective-permute-start.11 = (bf16[24,2,24,120]{3,2,1,0:T(8,128)(2,1)}, bf16[24,2,24,120]{3,2,1,0:T(8,128)(2,1)S(1)}, u32[]{:S(2)}, u32[]{:S(2)}) collective-permute-start(bf16[24,2,24,120]{3,2,1,0:T(8,128)(2,1)} %get-tuple-element.76), channel_id=1, source_target_pairs={{0,10},{2,8},{4,14},{6,12},{8,2},{10,0},{12,6},{14,4},{1,11},{3,9}... | collective-permute-start | bytes 829448 | tf_op jit(solution)/shard_map/ppermute | solution.py:605
  40.0 26.3 %copy-start.6 = (bf16[24,2,24,120]{3,2,1,0:T(8,128)(2,1)}, bf16[24,2,24,120]{3,2,1,0:T(8,128)(2,1)S(1)}, u32[]{:S(2)}) copy-start(bf16[24,2,24,120]{3,2,1,0:T(8,128)(2,1)S(1)} %collective-permute-done.7.refs_1_.rest_1_) | copy-start | bytes 829444
  40.0 37.7 %collective-permute-start.12 = (bf16[24,2,24,120]{3,2,1,0:T(8,128)(2,1)}, bf16[24,2,24,120]{3,2,1,0:T(8,128)(2,1)S(1)}, u32[]{:S(2)}, u32[]{:S(2)}) collective-permute-start(bf16[24,2,24,120]{3,2,1,0:T(8,128)(2,1)} %get-tuple-element.77), channel_id=1, source_target_pairs={{0,12},{2,14},{4,8},{6,10},{8,4},{10,6},{12,0},{14,2},{1,13},{3,15... | collective-permute-start | bytes 829448 | tf_op jit(solution)/shard_map/ppermute | solution.py:605
  47.2 35.5 %collective-permute-start.13 = (bf16[24,2,24,120]{3,2,1,0:T(8,128)(2,1)}, bf16[24,2,24,120]{3,2,1,0:T(8,128)(2,1)S(1)}, u32[]{:S(2)}, u32[]{:S(2)}) collective-permute-start(bf16[24,2,24,120]{3,2,1,0:T(8,128)(2,1)} %get-tuple-element.78), channel_id=1, source_target_pairs={{0,14},{2,12},{4,10},{6,8},{8,6},{10,4},{12,2},{14,0},{1,15},{3,13... | collective-permute-start | bytes 829448 | tf_op jit(solution)/shard_map/ppermute | solution.py:605
  86.0 3.1 collective-permute-start.14
  107.1 20.3 %collective-permute-start.15 = (bf16[8,12,2,24,120]{4,3,2,1,0:T(8,128)(2,1)}, bf16[8,12,2,24,120]{4,3,2,1,0:T(8,128)(2,1)S(1)}, u32[]{:S(2)}, u32[]{:S(2)}) collective-permute-start(bf16[8,12,2,24,120]{4,3,2,1,0:T(8,128)(2,1)} %get-tuple-element.79), channel_id=1, source_target_pairs={{0,1},{1,0},{2,3},{3,2},{4,5},{5,4},{6,7},{7,6},{8,9},{9,8},{10,11... | collective-permute-start | bytes 3317768 | tf_op jit(solution)/shard_map/ppermute | solution.py:609
  107.3 9.3 %collective-permute-start = (bf16[24,2,24,120]{3,2,1,0:T(8,128)(2,1)S(1)}, bf16[24,2,24,120]{3,2,1,0:T(8,128)(2,1)S(1)}, u32[]{:S(2)}, u32[]{:S(2)}) collective-permute-start(bf16[24,2,24,120]{3,2,1,0:T(8,128)(2,1)S(1)} %copy-done.47), channel_id=1, source_target_pairs={{0,2},{2,0},{4,6},{6,4},{8,10},{10,8},{12,14},{14,12},{1,3},{3,1},... | collective-permute-start | bytes 829448 | tf_op jit(solution)/shard_map/ppermute | solution.py:605
  108.2 18.7 %collective-permute-start.1 = (bf16[24,2,24,120]{3,2,1,0:T(8,128)(2,1)S(1)}, bf16[24,2,24,120]{3,2,1,0:T(8,128)(2,1)S(1)}, u32[]{:S(2)}, u32[]{:S(2)}) collective-permute-start(bf16[24,2,24,120]{3,2,1,0:T(8,128)(2,1)S(1)} %copy-done.46), channel_id=1, source_target_pairs={{0,4},{2,6},{4,0},{6,2},{8,12},{10,14},{12,8},{14,10},{1,5},{3,7},... | collective-permute-start | bytes 829448 | tf_op jit(solution)/shard_map/ppermute | solution.py:605
  108.2 24.8 %collective-permute-start.2 = (bf16[24,2,24,120]{3,2,1,0:T(8,128)(2,1)}, bf16[24,2,24,120]{3,2,1,0:T(8,128)(2,1)S(1)}, u32[]{:S(2)}, u32[]{:S(2)}) collective-permute-start(bf16[24,2,24,120]{3,2,1,0:T(8,128)(2,1)} %get-tuple-element.64), channel_id=1, source_target_pairs={{0,6},{2,4},{4,2},{6,0},{8,14},{10,12},{12,10},{14,8},{1,7},{3,5},... | collective-permute-start | bytes 829448 | tf_op jit(solution)/shard_map/ppermute | solution.py:605
  110.8 22.2 %collective-permute-start.3 = (bf16[24,2,24,120]{3,2,1,0:T(8,128)(2,1)}, bf16[24,2,24,120]{3,2,1,0:T(8,128)(2,1)S(1)}, u32[]{:S(2)}, u32[]{:S(2)}) collective-permute-start(bf16[24,2,24,120]{3,2,1,0:T(8,128)(2,1)} %get-tuple-element.65), channel_id=1, source_target_pairs={{0,8},{2,10},{4,12},{6,14},{8,0},{10,2},{12,4},{14,6},{1,9},{3,11}... | collective-permute-start | bytes 829448 | tf_op jit(solution)/shard_map/ppermute | solution.py:605
  116.6 48.1 %copy-start.11 = (bf16[24,2,24,120]{3,2,1,0:T(8,128)(2,1)}, bf16[24,2,24,120]{3,2,1,0:T(8,128)(2,1)S(1)}, u32[]{:S(2)}) copy-start(bf16[24,2,24,120]{3,2,1,0:T(8,128)(2,1)S(1)} %collective-permute-done.refs_1_.rest_1_) | copy-start | bytes 829444
  116.6 35.7 %collective-permute-start.4 = (bf16[24,2,24,120]{3,2,1,0:T(8,128)(2,1)}, bf16[24,2,24,120]{3,2,1,0:T(8,128)(2,1)S(1)}, u32[]{:S(2)}, u32[]{:S(2)}) collective-permute-start(bf16[24,2,24,120]{3,2,1,0:T(8,128)(2,1)} %get-tuple-element.66), channel_id=1, source_target_pairs={{0,10},{2,8},{4,14},{6,12},{8,2},{10,0},{12,6},{14,4},{1,11},{3,9}... | collective-permute-start | bytes 829448 | tf_op jit(solution)/shard_map/ppermute | solution.py:605
  126.9 37.8 %copy-start.12 = (bf16[24,2,24,120]{3,2,1,0:T(8,128)(2,1)}, bf16[24,2,24,120]{3,2,1,0:T(8,128)(2,1)S(1)}, u32[]{:S(2)}) copy-start(bf16[24,2,24,120]{3,2,1,0:T(8,128)(2,1)S(1)} %collective-permute-done.1.refs_2_.rest_2_) | copy-start | bytes 829444
  126.9 32.1 %collective-permute-start.5 = (bf16[24,2,24,120]{3,2,1,0:T(8,128)(2,1)}, bf16[24,2,24,120]{3,2,1,0:T(8,128)(2,1)S(1)}, u32[]{:S(2)}, u32[]{:S(2)}) collective-permute-start(bf16[24,2,24,120]{3,2,1,0:T(8,128)(2,1)} %get-tuple-element.67), channel_id=1, source_target_pairs={{0,12},{2,14},{4,8},{6,10},{8,4},{10,6},{12,0},{14,2},{1,13},{3,15... | collective-permute-start | bytes 829448 | tf_op jit(solution)/shard_map/ppermute | solution.py:605
  127.5 37.2 %collective-permute-start.6 = (bf16[24,2,24,120]{3,2,1,0:T(8,128)(2,1)}, bf16[24,2,24,120]{3,2,1,0:T(8,128)(2,1)S(1)}, u32[]{:S(2)}, u32[]{:S(2)}) collective-permute-start(bf16[24,2,24,120]{3,2,1,0:T(8,128)(2,1)} %get-tuple-element.68), channel_id=1, source_target_pairs={{0,14},{2,12},{4,10},{6,8},{8,6},{10,4},{12,2},{14,0},{1,15},{3,13... | collective-permute-start | bytes 829448 | tf_op jit(solution)/shard_map/ppermute | solution.py:605
  133.0 31.7 %copy-start.13 = (bf16[24,2,24,120]{3,2,1,0:T(8,128)(2,1)}, bf16[24,2,24,120]{3,2,1,0:T(8,128)(2,1)S(1)}, u32[]{:S(2)}) copy-start(bf16[24,2,24,120]{3,2,1,0:T(8,128)(2,1)S(1)} %collective-permute-done.2.refs_3_.rest_3_) | copy-start | bytes 829444
  133.0 31.7 %copy-start.14 = (bf16[24,2,24,120]{3,2,1,0:T(8,128)(2,1)}, bf16[24,2,24,120]{3,2,1,0:T(8,128)(2,1)S(1)}, u32[]{:S(2)}) copy-start(bf16[24,2,24,120]{3,2,1,0:T(8,128)(2,1)S(1)} %collective-permute-done.3.refs_4_.rest_4_) | copy-start | bytes 829444
  167.9 3.1 collective-permute-start.16
  172.0 21.8 %copy-start.31 = (bf16[24,2,24,120]{3,2,1,0:T(8,128)(2,1)S(1)}, bf16[24,2,24,120]{3,2,1,0:T(8,128)(2,1)}, u32[]{:S(2)}) copy-start(bf16[24,2,24,120]{3,2,1,0:T(8,128)(2,1)} %get-tuple-element.110) | copy-start | bytes 829444
  189.1 4.7 %collective-permute-start.17 = (bf16[8,12,2,24,120]{4,3,2,1,0:T(8,128)(2,1)}, bf16[8,12,2,24,120]{4,3,2,1,0:T(8,128)(2,1)S(1)}, u32[]{:S(2)}, u32[]{:S(2)}) collective-permute-start(bf16[8,12,2,24,120]{4,3,2,1,0:T(8,128)(2,1)} %get-tuple-element.89), channel_id=1, source_target_pairs={{0,1},{1,0},{2,3},{3,2},{4,5},{5,4},{6,7},{7,6},{8,9},{9,8},{10,11... | collective-permute-start | bytes 3317768 | tf_op jit(solution)/shard_map/ppermute | solution.py:609
  189.3 10.0 %collective-permute-start.25 = (bf16[24,2,24,120]{3,2,1,0:T(8,128)(2,1)S(1)}, bf16[24,2,24,120]{3,2,1,0:T(8,128)(2,1)}, u32[]{:S(2)}, u32[]{:S(2)}) collective-permute-start(bf16[24,2,24,120]{3,2,1,0:T(8,128)(2,1)S(1)} %copy-done.27), channel_id=1, source_target_pairs={{0,2},{2,0},{4,6},{6,4},{8,10},{10,8},{12,14},{14,12},{1,3},{3,1},... | collective-permute-start | bytes 829448 | tf_op jit(solution)/shard_map/ppermute | solution.py:605
  190.8 19.3 %collective-permute-start.26 = (bf16[24,2,24,120]{3,2,1,0:T(8,128)(2,1)S(1)}, bf16[24,2,24,120]{3,2,1,0:T(8,128)(2,1)}, u32[]{:S(2)}, u32[]{:S(2)}) collective-permute-start(bf16[24,2,24,120]{3,2,1,0:T(8,128)(2,1)S(1)} %copy-done.28), channel_id=1, source_target_pairs={{0,4},{2,6},{4,0},{6,2},{8,12},{10,14},{12,8},{14,10},{1,5},{3,7},... | collective-permute-start | bytes 829448 | tf_op jit(solution)/shard_map/ppermute | solution.py:605
  190.8 25.0 %collective-permute-start.27 = (bf16[24,2,24,120]{3,2,1,0:T(8,128)(2,1)S(1)}, bf16[24,2,24,120]{3,2,1,0:T(8,128)(2,1)}, u32[]{:S(2)}, u32[]{:S(2)}) collective-permute-start(bf16[24,2,24,120]{3,2,1,0:T(8,128)(2,1)S(1)} %copy-done.29), channel_id=1, source_target_pairs={{0,6},{2,4},{4,2},{6,0},{8,14},{10,12},{12,10},{14,8},{1,7},{3,5},... | collective-permute-start | bytes 829448 | tf_op jit(solution)/shard_map/ppermute | solution.py:605
  192.8 23.1 %collective-permute-start.28 = (bf16[24,2,24,120]{3,2,1,0:T(8,128)(2,1)S(1)}, bf16[24,2,24,120]{3,2,1,0:T(8,128)(2,1)}, u32[]{:S(2)}, u32[]{:S(2)}) collective-permute-start(bf16[24,2,24,120]{3,2,1,0:T(8,128)(2,1)S(1)} %copy-done.30), channel_id=1, source_target_pairs={{0,8},{2,10},{4,12},{6,14},{8,0},{10,2},{12,4},{14,6},{1,9},{3,11}... | collective-permute-start | bytes 829448 | tf_op jit(solution)/shard_map/ppermute | solution.py:605
  193.8 39.0 %collective-permute-start.29 = (bf16[24,2,24,120]{3,2,1,0:T(8,128)(2,1)S(1)}, bf16[24,2,24,120]{3,2,1,0:T(8,128)(2,1)}, u32[]{:S(2)}, u32[]{:S(2)}) collective-permute-start(bf16[24,2,24,120]{3,2,1,0:T(8,128)(2,1)S(1)} %copy-done.31), channel_id=1, source_target_pairs={{0,10},{2,8},{4,14},{6,12},{8,2},{10,0},{12,6},{14,4},{1,11},{3,9}... | collective-permute-start | bytes 829448 | tf_op jit(solution)/shard_map/ppermute | solution.py:605
  199.3 40.9 %collective-permute-start.30 = (bf16[24,2,24,120]{3,2,1,0:T(8,128)(2,1)S(1)}, bf16[24,2,24,120]{3,2,1,0:T(8,128)(2,1)S(1)}, u32[]{:S(2)}, u32[]{:S(2)}) collective-permute-start(bf16[24,2,24,120]{3,2,1,0:T(8,128)(2,1)S(1)} %copy-done.32), channel_id=1, source_target_pairs={{0,12},{2,14},{4,8},{6,10},{8,4},{10,6},{12,0},{14,2},{1,13},{3,15... | collective-permute-start | bytes 829448 | tf_op jit(solution)/shard_map/ppermute | solution.py:605
  210.1 51.0 %collective-permute-start.31 = (bf16[24,2,24,120]{3,2,1,0:T(8,128)(2,1)S(1)}, bf16[24,2,24,120]{3,2,1,0:T(8,128)(2,1)S(1)}, u32[]{:S(2)}, u32[]{:S(2)}) collective-permute-start(bf16[24,2,24,120]{3,2,1,0:T(8,128)(2,1)S(1)} %copy-done.33), channel_id=1, source_target_pairs={{0,14},{2,12},{4,10},{6,8},{8,6},{10,4},{12,2},{14,0},{1,15},{3,13... | collective-permute-start | bytes 829448 | tf_op jit(solution)/shard_map/ppermute | solution.py:605
  215.8 45.3 %collective-permute-start.18 = (bf16[24,2,24,120]{3,2,1,0:T(8,128)(2,1)}, bf16[24,2,24,120]{3,2,1,0:T(8,128)(2,1)S(1)}, u32[]{:S(2)}, u32[]{:S(2)}) collective-permute-start(bf16[24,2,24,120]{3,2,1,0:T(8,128)(2,1)} %get-tuple-element.99), channel_id=1, source_target_pairs={{0,2},{2,0},{4,6},{6,4},{8,10},{10,8},{12,14},{14,12},{1,3},{3,1},... | collective-permute-start | bytes 829448 | tf_op jit(solution)/shard_map/ppermute | solution.py:605
  215.9 46.0 %collective-permute-start.19 = (bf16[24,2,24,120]{3,2,1,0:T(8,128)(2,1)}, bf16[24,2,24,120]{3,2,1,0:T(8,128)(2,1)S(1)}, u32[]{:S(2)}, u32[]{:S(2)}) collective-permute-start(bf16[24,2,24,120]{3,2,1,0:T(8,128)(2,1)} %get-tuple-element.100), channel_id=1, source_target_pairs={{0,4},{2,6},{4,0},{6,2},{8,12},{10,14},{12,8},{14,10},{1,5},{3,7},... | collective-permute-start | bytes 829448 | tf_op jit(solution)/shard_map/ppermute | solution.py:605
  225.7 35.4 %copy-start.36 = (bf16[24,2,24,120]{3,2,1,0:T(8,128)(2,1)S(1)}, bf16[24,2,24,120]{3,2,1,0:T(8,128)(2,1)}, u32[]{:S(2)}) copy-start(bf16[24,2,24,120]{3,2,1,0:T(8,128)(2,1)} %get-tuple-element.103) | copy-start | bytes 829444
  225.7 36.1 %copy-start.37 = (bf16[24,2,24,120]{3,2,1,0:T(8,128)(2,1)S(1)}, bf16[24,2,24,120]{3,2,1,0:T(8,128)(2,1)}, u32[]{:S(2)}) copy-start(bf16[24,2,24,120]{3,2,1,0:T(8,128)(2,1)} %get-tuple-element.104) | copy-start | bytes 829444
  232.8 48.9 %collective-permute-start.20 = (bf16[24,2,24,120]{3,2,1,0:T(8,128)(2,1)S(1)}, bf16[24,2,24,120]{3,2,1,0:T(8,128)(2,1)S(1)}, u32[]{:S(2)}, u32[]{:S(2)}) collective-permute-start(bf16[24,2,24,120]{3,2,1,0:T(8,128)(2,1)S(1)} %copy-done.34), channel_id=1, source_target_pairs={{0,6},{2,4},{4,2},{6,0},{8,14},{10,12},{12,10},{14,8},{1,7},{3,5},... | collective-permute-start | bytes 829448 | tf_op jit(solution)/shard_map/ppermute | solution.py:605
  240.2 21.7 %copy-start.38 = (bf16[24,2,24,120]{3,2,1,0:T(8,128)(2,1)}, bf16[24,2,24,120]{3,2,1,0:T(8,128)(2,1)S(1)}, u32[]{:S(2)}) copy-start(bf16[24,2,24,120]{3,2,1,0:T(8,128)(2,1)S(1)} %collective-permute-done.30.refs_7_) | copy-start | bytes 829444
  240.2 41.6 %collective-permute-start.21 = (bf16[24,2,24,120]{3,2,1,0:T(8,128)(2,1)S(1)}, bf16[24,2,24,120]{3,2,1,0:T(8,128)(2,1)S(1)}, u32[]{:S(2)}, u32[]{:S(2)}) collective-permute-start(bf16[24,2,24,120]{3,2,1,0:T(8,128)(2,1)S(1)} %copy-done.35), channel_id=1, source_target_pairs={{0,8},{2,10},{4,12},{6,14},{8,0},{10,2},{12,4},{14,6},{1,9},{3,11}... | collective-permute-start | bytes 829448 | tf_op jit(solution)/shard_map/ppermute | solution.py:605
  261.1 25.2 %collective-permute-start.22 = (bf16[24,2,24,120]{3,2,1,0:T(8,128)(2,1)S(1)}, bf16[24,2,24,120]{3,2,1,0:T(8,128)(2,1)S(1)}, u32[]{:S(2)}, u32[]{:S(2)}) collective-permute-start(bf16[24,2,24,120]{3,2,1,0:T(8,128)(2,1)S(1)} %copy-done.36), channel_id=1, source_target_pairs={{0,10},{2,8},{4,14},{6,12},{8,2},{10,0},{12,6},{14,4},{1,11},{3,9}... | collective-permute-start | bytes 829448 | tf_op jit(solution)/shard_map/ppermute | solution.py:605
  261.8 32.3 %collective-permute-start.23 = (bf16[24,2,24,120]{3,2,1,0:T(8,128)(2,1)S(1)}, bf16[24,2,24,120]{3,2,1,0:T(8,128)(2,1)S(1)}, u32[]{:S(2)}, u32[]{:S(2)}) collective-permute-start(bf16[24,2,24,120]{3,2,1,0:T(8,128)(2,1)S(1)} %copy-done.37), channel_id=1, source_target_pairs={{0,12},{2,14},{4,8},{6,10},{8,4},{10,6},{12,0},{14,2},{1,13},{3,15... | collective-permute-start | bytes 829448 | tf_op jit(solution)/shard_map/ppermute | solution.py:605
  261.9 37.8 %collective-permute-start.24 = (bf16[24,2,24,120]{3,2,1,0:T(8,128)(2,1)}, bf16[24,2,24,120]{3,2,1,0:T(8,128)(2,1)S(1)}, u32[]{:S(2)}, u32[]{:S(2)}) collective-permute-start(bf16[24,2,24,120]{3,2,1,0:T(8,128)(2,1)} %get-tuple-element.105), channel_id=1, source_target_pairs={{0,14},{2,12},{4,10},{6,8},{8,6},{10,4},{12,2},{14,0},{1,15},{3,13... | collective-permute-start | bytes 829448 | tf_op jit(solution)/shard_map/ppermute | solution.py:605
  (32 other events, 357.5 us)

commit v4 on v1

--- a/solution.py
+++ b/solution.py
@@ -134,7 +134,8 @@
 
 
 LANES = 128
-SHARES = (1, 1)
+LEVELS = 8
+SHARES = (1, 1, 1)
 
 
 def xor_order(array, index, axis):
@@ -148,33 +149,61 @@
     return out.reshape(array.shape)
 
 
-def table_kernel(nblk, hi_c, hi_s, lo_c, lo_s, out):
-    rows = hi_c.shape[0]
-    cl, sl = lo_c[...], lo_s[...]
+def packed_rows():
+    return 2 * LEVELS - 1
+
+
+def spare_lanes(row, last, latd):
+    index, values = row
+    share = LANES - latd
+    lane = lax.broadcasted_iota(jnp.int32, values.shape, 1)
+    turned = pltpu.roll(last, (latd - share * index) % LANES, 1)
+    return jnp.where(lane < latd, values, turned)
+
+
+def last_row(rows, latd):
+    share = LANES - latd
+    lane = lax.broadcasted_iota(jnp.int32, rows[0].shape, 1)
+    out = jnp.zeros_like(rows[0])
+    for i, row in enumerate(rows):
+        turned = pltpu.roll(row, (share * i - latd) % LANES, 1)
+        out = jnp.where((lane >= share * i) & (lane < share * (i + 1)), turned, out)
+    return out
+
+
+def table_kernel(nlon, wave_ref, out):
+    rows = wave_ref.shape[0]
+    nblk = nlon // LANES
+    wave = wave_ref[...]
+    lane = lax.broadcasted_iota(jnp.int32, (rows, LANES), 1)
+
+    def sincos(step):
+        turns = (lane * step).astype(F32) * wave
+        turns = turns - nlon * jnp.floor(turns * (1.0 / nlon))
+        turns = jnp.where(turns < 0.0, turns + nlon, turns)
+        turns = jnp.where(turns >= nlon, turns - nlon, turns)
+        angle = turns * (2.0 * jnp.pi / nlon)
+        return jnp.cos(angle), jnp.sin(angle)
+
+    cl, sl = sincos(1)
+    ch, sh = sincos(LANES)
     for b in range(nblk):
-        ch, sh = hi_c[:, b : b + 1], hi_s[:, b : b + 1]
+        c, s = ch[:, b : b + 1], sh[:, b : b + 1]
         cols = slice(b * LANES, (b + 1) * LANES)
-        out[:rows, cols] = (ch * cl - sh * sl).astype(BF16)
-        out[rows:, cols] = (-(sh * cl + ch * sl)).astype(BF16)
-
-
-def make_table(waves, nlon):
-    nblk = nlon // LANES
-    scale = 2.0 * jnp.pi / nlon
-    step_lo = jnp.arange(LANES, dtype=jnp.int32)
-    step_hi = jnp.arange(LANES, dtype=jnp.int32) * LANES
-    lo = (waves[:, None] * step_lo[None, :] % nlon).astype(F32) * scale
-    hi = (waves[:, None] * step_hi[None, :] % nlon).astype(F32) * scale
-    rows = waves.shape[0]
+        out[:rows, cols] = (c * cl - s * sl).astype(BF16)
+        out[rows:, cols] = (-(s * cl + c * sl)).astype(BF16)
+
+
+def make_table(wave_lanes, nlon):
     return pl.pallas_call(
-        functools.partial(table_kernel, nblk),
-        out_shape=jax.ShapeDtypeStruct((2 * rows, nlon), BF16),
+        functools.partial(table_kernel, nlon),
+        out_shape=jax.ShapeDtypeStruct((2 * wave_lanes.shape[0], nlon), BF16),
         name="table",
-    )(jnp.cos(hi), jnp.sin(hi), jnp.cos(lo), jnp.sin(lo))
-
-
-def dft_kernel(groups, vb, latd, x_ref, t_ref, wind_ref, lat_ref, wave_ref, *rest):
-    outs, (xf, scr) = rest[:groups], rest[groups:]
+    )(wave_lanes)
+
+
+def dft_kernel(groups, latd, x_ref, t_ref, lat_ref, wave_ref, *rest):
+    outs, (xf,) = rest[:groups], rest[groups:]
     rows = t_ref.shape[0]
     half = rows // 2
     per = half // groups
@@ -184,65 +213,67 @@
     def _():
         xf[...] = jnp.zeros_like(xf)
 
-    wind = jnp.concatenate([wind_ref[...]] * nblk, axis=1)
-    rate = lat_ref[0:1, :]
-    weight = lat_ref[1:2, :]
-
-    def body(v, carry):
+    wind = jnp.broadcast_to(lat_ref[...].T[:latd, 0:1], (latd, LANES))
+    wind = jnp.concatenate([wind] * nblk, axis=1)
+    weight = lat_ref[2:3, :]
+    factor = wave_ref[...] * lat_ref[1:2, :]
+
+    def load(v):
         xv = x_ref[v]
         x32 = xv.astype(F32)
-        xf[0:latd, :] = xv
-        xf[LANES : LANES + latd, :] = (x32 * (wind + x32)).astype(BF16)
+        xf[v % 2, 0:latd, :] = xv
+        xf[v % 2, LANES : LANES + latd, :] = (x32 * (wind + x32)).astype(BF16)
+
+    last = None
+    load(LEVELS - 1)
+    order = [LEVELS - 1, *range(LEVELS - 1)]
+    for at, v in enumerate(order):
+        if at + 1 < LEVELS:
+            load(order[at + 1])
         both = lax.dot_general(
-            t_ref[...], xf[...], (((1,), (1,)), ((), ())), preferred_element_type=F32
+            t_ref[...], xf[v % 2], (((1,), (1,)), ((), ())), preferred_element_type=F32
         )
         plain, moved = both[:, :LANES], both[:, LANES:]
-        factor = wave_ref[...] * rate
         real = (plain[:half] + factor * moved[half:]) * weight
         imag = (plain[half:] - factor * moved[:half]) * weight
-        scr[pl.ds(v, half, stride=vb), :] = real
-        scr[pl.ds(half * vb + v, half, stride=vb), :] = imag
-        return carry
-
-    lax.fori_loop(0, vb, body, 0, unroll=2)
-    for g in range(groups):
-        for c in range(2):
-            start = (c * half + g * per) * vb
-            piece = scr[start : start + per * vb, :].reshape(per, vb, LANES)
-            outs[g][:, c] = piece[:, :, :latd].astype(BF16)
-
-
-def dft(x, table, wind, latrow, waves, groups):
+        parts = [(v, real)]
+        if last is None:
+            last = imag
+        else:
+            parts.append((LEVELS + v, imag))
+        for index, values in parts:
+            full = spare_lanes((index, values), last, latd).astype(BF16)
+            for g in range(groups):
+                outs[g][index] = full[g * per : (g + 1) * per]
+
+
+def dft(x, table, lat_rows, wave_lanes, groups):
     levd, latd, nlon = x.shape
     rows = table.shape[0]
     half = rows // 2
     per = half // groups
-    vb = 8
+    packed = packed_rows()
     const = lambda i: (0, 0)
-    block = pl.BlockSpec((per, 2, vb, latd), lambda i: (0, 0, i, 0))
+    block = pl.BlockSpec((packed, per, LANES), lambda i: (i, 0, 0))
     return pl.pallas_call(
-        functools.partial(dft_kernel, groups, vb, latd),
-        out_shape=[jax.ShapeDtypeStruct((per, 2, levd, latd), BF16)] * groups,
-        grid=(levd // vb,),
+        functools.partial(dft_kernel, groups, latd),
+        out_shape=[jax.ShapeDtypeStruct((levd // LEVELS * packed, per, LANES), BF16)] * groups,
+        grid=(levd // LEVELS,),
         in_specs=[
-            pl.BlockSpec((vb, latd, nlon), lambda i: (i, 0, 0)),
+            pl.BlockSpec((LEVELS, latd, nlon), lambda i: (i, 0, 0)),
             pl.BlockSpec((rows, nlon), const),
-            pl.BlockSpec((latd, LANES), const),
-            pl.BlockSpec((2, LANES), const),
+            pl.BlockSpec(lat_rows.shape, const),
             pl.BlockSpec((half, LANES), const),
         ],
         out_specs=[block] * groups,
-        scratch_shapes=[
-            pltpu.VMEM((2 * LANES, nlon), BF16),
-            pltpu.VMEM((rows * vb, LANES), F32),
-        ],
+        scratch_shapes=[pltpu.VMEM((2, 2 * LANES, nlon), BF16)],
         cost_estimate=pl.CostEstimate(
             flops=4 * rows * levd * latd * nlon,
             bytes_accessed=2 * levd * latd * (nlon + rows) + 2 * rows * nlon,
             transcendentals=0,
         ),
         name="dft",
-    )(x, table, wind, latrow, jnp.broadcast_to(waves.astype(F32)[:, None], (half, LANES)))
+    )(x, table, lat_rows, wave_lanes)
 
 
 def split3_dot(w3, x):
@@ -252,49 +283,78 @@
 
 
 def legendre_kernel(
-    groups, levs, latd, nmodes, info, leg_ref, perm_ref, w1_ref, w2_ref, mr_ref, *rest
+    groups, levs, levd, latd, nmodes, info, leg_ref, perm_ref, w1_ref, w2_ref, mr_ref, *rest
 ):
     own = rest[:groups]
     other = rest[groups]
     outs = rest[groups + 1 : 2 * groups + 1]
     give = rest[2 * groups + 1]
-    acc = rest[2 * groups + 2]
-    levd = own[0].shape[2]
+    data, fresh_data = rest[2 * groups + 2 :]
+    slots = other.shape[2]
+    lats = groups // levs
     nlev = levs * levd
+    total = 4 * nlev
     count = leg_ref.shape[0]
+    packed = packed_rows()
     t = pl.program_id(0)
+
+    def each_group(move):
+        def body(group, carry):
+            for rel in range(groups):
+                dz, dx = rel // levs, rel % levs
+                for field in range(2):
+                    base = field * nlev + dx * levd + group * LEVELS
+                    rows = [
+                        base + (i // LEVELS) * 2 * nlev + i % LEVELS for i in range(packed + 1)
+                    ]
+                    move(rel, field, dz, group * packed, rows)
+            return carry
+
+        lax.fori_loop(0, levd // LEVELS, body, 0)
+
+    def unpack(rel, field, dz, at, rows):
+        values = []
+        for i in range(packed):
+            value = own[rel][at + i, :slots] if field == 0 else other[rel, at + i]
+            values.append(value.astype(F32))
+        values.append(last_row(values, latd))
+        for row, value in zip(rows, values):
+            data[dz, pl.ds(row, slots, stride=total), :] = value
+
+    def pack(rel, field, dz, at, rows):
+        last = fresh_data[dz, pl.ds(rows[-1], slots, stride=total), :]
+        for i in range(packed):
+            value = fresh_data[dz, pl.ds(rows[i], slots, stride=total), :]
+            full = spare_lanes((i, value), last, latd).astype(BF16)
+            if field == 0:
+                outs[rel][at + i] = full
+            else:
+                give[rel, at + i] = full
 
     @pl.when(t == 0)
     def _():
-        acc[...] = jnp.zeros_like(acc)
+        each_group(unpack)
 
     k = lax.broadcasted_iota(jnp.int32, (1, nmodes), 1)
     first = info[2, 0] == 0
     keep_own = jnp.where(first, 0.0, 1.0)
     keep_other = jnp.where(first, 1.0, 0.0)
-    where = []
-    for rel in range(groups):
-        dz, dx = rel // levs, rel % levs
-        for c in range(2):
-            row = c * 2 * nlev + dx * levd
-            where.append((rel, c, row, slice(dz * LANES, dz * LANES + latd)))
-    for j in range(count):
-        for rel, c, row, lanes in where:
-            acc[j, row : row + levd, lanes] = own[rel][j, c].astype(F32)
-            acc[j, row + nlev : row + nlev + levd, lanes] = other[rel, j, c].astype(F32)
     legs = [
         jnp.dot(perm_ref[...], leg_ref[j], preferred_element_type=F32).astype(BF16)
         for j in range(count)
     ]
     fresh = []
     for j in range(count):
-        wave, terms = info[0, t * count + j], info[1, t * count + j]
+        slot = t * count + j
+        wave, terms = info[0, slot], info[1, slot]
         n = (wave + k).astype(F32)
         h = n * (n + 1.0) / float(nmodes * (nmodes - 1))
         scale_own = jnp.where(first, 1.0, h)
         scale_other = jnp.where(first, h, 1.0)
         denom = 1.0 + h * mr_ref[...]
-        spec = jnp.dot(acc[j].astype(BF16), legs[j], preferred_element_type=F32)
+        here = pl.ds(pl.multiple_of(slot * total, total), total)
+        lined = jnp.concatenate([data[dz, here, :].astype(BF16) for dz in range(lats)], axis=1)
+        spec = jnp.dot(lined, legs[j], preferred_element_type=F32)
         spec = jnp.where(k < terms, spec, 0.0)
         new = []
         for c in range(2):
@@ -310,26 +370,30 @@
         back = lax.dot_general(
             fresh[j], legs[j], (((1,), (1,)), ((), ())), preferred_element_type=F32
         )
-        back = (back * float(nmodes) ** (-0.5)).astype(BF16)
-        for rel, c, row, lanes in where:
-            outs[rel][j, c] = back[row : row + levd, lanes]
-            give[rel, j, c] = back[row + nlev : row + nlev + levd, lanes]
-
-
-def legendre_step(info, leg, perm, w1, w2, rates, own, other, levs, nmodes):
-    groups = len(own)
-    count, _, levd, latd = other.shape[1:]
+        here = pl.ds(pl.multiple_of((t * count + j) * total, total), total)
+        back = back * float(nmodes) ** (-0.5)
+        for dz in range(lats):
+            fresh_data[dz, here, :] = back[:, dz * LANES : (dz + 1) * LANES]
+
+    @pl.when(t == pl.num_programs(0) - 1)
+    def _():
+        each_group(pack)
+
+
+def legendre_step(info, leg, perm, w1, w2, rates, own, other, levs, levd, latd):
+    groups, packed, count, _ = other.shape
+    nmodes = leg.shape[2]
     lanes, nlat = perm.shape
     nlev = levs * levd
     const = lambda t, s: (0, 0)
     step = 2 if count % 2 == 0 else 1
-    piece = pl.BlockSpec((step, 2, levd, latd), lambda t, s: (t, 0, 0, 0))
-    stack = pl.BlockSpec((groups, step, 2, levd, latd), lambda t, s: (0, t, 0, 0, 0))
+    piece = pl.BlockSpec((packed, count, LANES), lambda t, s: (0, 0, 0))
+    stack = pl.BlockSpec((groups, packed, count, LANES), lambda t, s: (0, 0, 0, 0))
     flops = count * 2 * (2 * nlev * 2 * nmodes * lanes * 2 + nmodes * nlat * lanes)
     return pl.pallas_call(
-        functools.partial(legendre_kernel, groups, levs, latd, nmodes),
-        out_shape=[jax.ShapeDtypeStruct((2 * count, 2, levd, latd), BF16)] * groups
-        + [jax.ShapeDtypeStruct((groups, count, 2, levd, latd), BF16)],
+        functools.partial(legendre_kernel, groups, levs, levd, latd, nmodes),
+        out_shape=[jax.ShapeDtypeStruct((packed, 2 * count, LANES), BF16)] * groups
+        + [jax.ShapeDtypeStruct(other.shape, BF16)],
         grid_spec=pltpu.PrefetchScalarGridSpec(
             num_scalar_prefetch=1,
             grid=(count // step,),
@@ -343,7 +407,7 @@
             + [piece] * groups
             + [stack],
             out_specs=[piece] * groups + [stack],
-            scratch_shapes=[pltpu.VMEM((step, 4 * nlev, lanes), F32)],
+            scratch_shapes=[pltpu.VMEM((groups // levs, count * 4 * nlev, LANES), F32)] * 2,
         ),
         cost_estimate=pl.CostEstimate(
             flops=flops,
@@ -360,20 +424,18 @@
         out[r] = ins[r][...]
 
 
-def gather_halves(blocks, after):
+def gather_halves(blocks):
     groups = len(blocks)
-    count, _, levd, latd = blocks[0].shape
+    packed, count, _ = blocks[0].shape
     half = count // 2
-    any_spec = pl.BlockSpec(memory_space=pl.ANY)
     return pl.pallas_call(
         functools.partial(gather_kernel, groups),
-        out_shape=jax.ShapeDtypeStruct((groups, half, 2, levd, latd), BF16),
+        out_shape=jax.ShapeDtypeStruct((groups, packed, half, LANES), BF16),
         grid=(1,),
-        in_specs=[pl.BlockSpec((half, 2, levd, latd), lambda i: (1, 0, 0, 0))] * groups
-        + [any_spec] * len(after),
-        out_specs=pl.BlockSpec((groups, half, 2, levd, latd), lambda i: (0, 0, 0, 0, 0)),
+        in_specs=[pl.BlockSpec((packed, half, LANES), lambda i: (0, 1, 0))] * groups,
+        out_specs=pl.BlockSpec((groups, packed, half, LANES), lambda i: (0, 0, 0, 0)),
         name="gather_halves",
-    )(*blocks, *after)
+    )(*blocks)
 
 
 def fill_kernel(groups, got, *refs):
@@ -383,39 +445,44 @@
 
 
 def fill_halves(blocks, got):
-    groups, half, _, levd, latd = got.shape
+    groups, packed, half, _ = got.shape
     any_spec = pl.BlockSpec(memory_space=pl.ANY)
     return pl.pallas_call(
         functools.partial(fill_kernel, groups),
         out_shape=[jax.ShapeDtypeStruct(b.shape, b.dtype) for b in blocks],
         grid=(1,),
-        in_specs=[pl.BlockSpec(got.shape, lambda i: (0, 0, 0, 0, 0))] + [any_spec] * groups,
-        out_specs=[pl.BlockSpec((half, 2, levd, latd), lambda i: (1, 0, 0, 0))] * groups,
+        in_specs=[pl.BlockSpec(got.shape, lambda i: (0, 0, 0, 0))] + [any_spec] * groups,
+        out_specs=[pl.BlockSpec((packed, half, LANES), lambda i: (0, 1, 0))] * groups,
         input_output_aliases={r + 1: r for r in range(groups)},
         name="fill_halves",
     )(got, *blocks)
 
 
-def inverse_kernel(counts, vb, latd, scale, add, *refs):
+def inverse_kernel(counts, latd, scale, add, *refs):
     tabs, refs = refs[: len(counts)], refs[len(counts) :]
     pieces, refs = refs[: sum(counts)], refs[sum(counts) :]
     partial = refs[0] if add else None
-    out, scr, lhs = refs[-3:]
+    out, lhs = refs[-2:]
     nlon = tabs[0].shape[1]
+    packed = packed_rows()
     base, depth = 0, 0
     for tab, number in zip(tabs, counts):
-        rows = tab.shape[0]
-        per = rows // (2 * number)
-        for g in range(number):
-            for c in range(2):
-                at = (base + c * (rows // 2) + g * per) * vb
-                part = pieces[depth + g][:, c].astype(F32)
-                scr[at : at + per * vb, :latd] = part.reshape(per * vb, latd)
-        base += rows
+        half = tab.shape[0] // 2
+        group = pieces[depth : depth + number]
+        for i in range(packed):
+            v, c = i % LEVELS, i // LEVELS
+            rows = jnp.concatenate([ref[i] for ref in group], axis=0)
+            at = base + c * half
+            lhs[v * LANES : (v + 1) * LANES, at : at + half] = rows.T
+        rows = [
+            jnp.concatenate([ref[i].astype(F32) for ref in group], axis=0) for i in range(packed)
+        ]
+        v = LEVELS - 1
+        lhs[v * LANES : (v + 1) * LANES, base + half : base + 2 * half] = (
+            last_row(rows, latd).astype(BF16).T
+        )
+        base += 2 * half
         depth += number
-    for v in range(vb):
-        col = scr[pl.ds(v, base, stride=vb), :].astype(BF16)
-        lhs[v * LANES : (v + 1) * LANES, :] = col.T
     step = 3 * LANES
     for j in range(0, nlon, step):
         cols = slice(j, j + step)
@@ -428,41 +495,35 @@
             grid = term if grid is None else grid + term
             base += rows
         grid = grid * scale
-        for v in range(vb):
+        for v in range(LEVELS):
             piece = grid[v * LANES : v * LANES + latd]
             if partial is not None:
                 piece = piece + partial[v, :, cols]
             out[v, :, cols] = piece.astype(out.dtype)
 
 
-def inverse_dft(sets, partial, scale, out_dtype, after):
+def inverse_dft(sets, shape, partial, scale, out_dtype):
     tabs = [tab for tab, _ in sets]
     pieces = [p for _, group in sets for p in group]
-    levd, latd = pieces[0].shape[2:]
-    nlon = tabs[0].shape[1]
+    levd, latd, nlon = shape
     rows = sum(tab.shape[0] for tab in tabs)
-    vb = 8
-    grid_block = pl.BlockSpec((vb, latd, nlon), lambda i: (i, 0, 0))
+    packed = packed_rows()
+    grid_block = pl.BlockSpec((LEVELS, latd, nlon), lambda i: (i, 0, 0))
     in_specs = [pl.BlockSpec(tab.shape, lambda i: (0, 0)) for tab in tabs] + [
-        pl.BlockSpec((p.shape[0], 2, vb, latd), lambda i: (0, 0, i, 0)) for p in pieces
+        pl.BlockSpec((packed, p.shape[1], LANES), lambda i: (i, 0, 0)) for p in pieces
     ]
     args = [*tabs, *pieces]
     if partial is not None:
         in_specs.append(grid_block)
         args.append(partial)
-    in_specs += [pl.BlockSpec(memory_space=pl.ANY)] * len(after)
-    args += after
     counts = tuple(len(group) for _, group in sets)
     return pl.pallas_call(
-        functools.partial(inverse_kernel, counts, vb, latd, scale, partial is not None),
+        functools.partial(inverse_kernel, counts, latd, scale, partial is not None),
         out_shape=jax.ShapeDtypeStruct((levd, latd, nlon), out_dtype),
-        grid=(levd // vb,),
+        grid=(levd // LEVELS,),
         in_specs=in_specs,
         out_specs=grid_block,
-        scratch_shapes=[
-            pltpu.VMEM((rows * vb, LANES), F32),
-            pltpu.VMEM((vb * LANES, rows), BF16),
-        ],
+        scratch_shapes=[pltpu.VMEM((LEVELS * LANES, rows), BF16)],
         cost_estimate=pl.CostEstimate(
             flops=2 * rows * levd * latd * nlon,
             bytes_accessed=2 * levd * latd * (nlon + rows) + 2 * rows * nlon,
@@ -501,15 +562,12 @@
 
     waves = slot_wave.reshape(groups, 2, slots // 2)
     waves = xor_order(xor_order(waves, me, 0), f, 1)
-    my_lats = lax.dynamic_slice_in_dim(lat_order, z * latd, latd)
-    onehot = (my_lats[:, None] == jnp.arange(nlat, dtype=jnp.int32)[None, :]).astype(F32)
-    per_lat = jnp.dot(
-        onehot,
-        jnp.stack([zonal_wind, zonal_rate, quad_weight * nlon ** (-0.5)], axis=1),
-        precision=PRECISE,
-    )
-    wind = jnp.broadcast_to(per_lat[:, 0:1], (latd, LANES))
-    latrow = jnp.pad(per_lat[:, 1:].T, ((0, 0), (0, LANES - latd)))
+    lat_rel = xor_order(lat_order.reshape(lats, latd), z, 0)
+    lat_rel = jnp.pad(lat_rel, ((0, 0), (0, LANES - latd)), constant_values=-1)
+    hits = lat_rel[0][None, :, None] == jnp.arange(nlat, dtype=jnp.int32)[None, None, :]
+    zonal = jnp.stack([zonal_wind, zonal_rate, quad_weight * nlon ** (-0.5)], axis=0)
+    lat_rows = jnp.sum(jnp.where(hits, zonal[:, None, :], 0.0), axis=2)
+    lat_rows = jnp.pad(lat_rows, ((0, 5), (0, 0)))
 
     first = f == 0
     mix = jnp.dot(vert_project, thermal_matrix, precision=PRECISE)
@@ -529,9 +587,7 @@
 
     w1, w2 = three(w1), three(w2)
     rates = mode_rates[:, None]
-    lat_rel = xor_order(lat_order.reshape(lats, latd), z, 0)
-    lat_rel = jnp.pad(lat_rel, ((0, 0), (0, LANES - latd)), constant_values=-1).reshape(-1, 1)
-    perm = (lat_rel == jnp.arange(nlat, dtype=jnp.int32)[None, :]).astype(BF16)
+    perm = (lat_rel.reshape(-1, 1) == jnp.arange(nlat, dtype=jnp.int32)[None, :]).astype(BF16)
     my_waves = waves[0, 0]
     counts = pick_values(my_waves, truncation) - my_waves + 1
 
@@ -551,19 +607,15 @@
     far, near = far_near(groups)
     tables, arrived = [], []
     for i, (at, part) in enumerate(zip(starts, parts)):
-        blocks = [None] * groups
-        tables.append({})
-        for rels in (far, near) if i == 0 else (near, far):
-            w = waves[rels[0] : rels[-1] + 1, :, at : at + part].reshape(-1)
-            tables[i][rels] = make_table(w, nlon)
-            got = dft(grid_state[0], tables[i][rels], wind, latrow, w, len(rels))
-            blocks[rels[0] : rels[-1] + 1] = got
+        w = waves[:, :, at : at + part].reshape(-1)
+        lanes = jnp.broadcast_to(w.astype(F32)[:, None], (w.shape[0], LANES))
+        tables.append(make_table(lanes, nlon))
+        blocks = dft(grid_state[0], tables[i], lat_rows, lanes, groups)
         arrived.append(exchange(blocks, far + near))
     legendre = jnp.swapaxes(legendre, 1, 2)
     returned = []
-    after = [arrived[-1][0]]
     for i, (at, part) in enumerate(zip(starts, parts)):
-        other = gather_halves(arrived[i], after)
+        other = gather_halves(arrived[i])
         other = swap(other)
         info = jnp.stack(
             [
@@ -573,19 +625,17 @@
                 jnp.full((part,), f * (slots // 2) + at, jnp.int32),
             ]
         )
-        res = legendre_step(info, legendre, perm, w1, w2, rates, arrived[i], other, levs, nmodes)
+        res = legendre_step(
+            info, legendre, perm, w1, w2, rates, arrived[i], other, levs, levd, latd
+        )
         got = swap(res[groups])
         sent = fill_halves(res[:groups], got)
-        after = [sent[0]]
         returned.append(exchange(sent, near + far))
-    total = None
-    last = len(parts) - 1
+    sets = list(zip(tables, returned))
     scale = float(nmodes) ** (-0.5)
-    one = lambda i, rels: (tables[i][rels], [returned[i][r] for r in rels])
-    for i in range(last):
-        total = inverse_dft([one(i, near), one(i, far)], total, scale, F32, after)
-    total = inverse_dft([one(last, near)], total, scale, F32, [])
-    total = inverse_dft([one(last, far)], total, scale, BF16, [])
+    shape = (levd, latd, nlon)
+    total = inverse_dft(sets[:-1], shape, None, scale, F32)
+    total = inverse_dft(sets[-1:], shape, total, scale, BF16)
     return total[None]
 
 
@@ -625,11 +675,13 @@
     def local(grid_state, *rest):
         legendre = rest[6]
         levd, latd, nlon = grid_state.shape[1:]
+        share = LANES - latd
         fits = (
-            legendre.shape[0] % (4 * sum(SHARES)) == 0
-            and levd % 8 == 0
+            legendre.shape[0] % (2 * 8 * sum(SHARES)) == 0
+            and levd % LEVELS == 0
             and latd % 8 == 0
-            and latd <= LANES
+            and share > 0
+            and share * (2 * LEVELS - 1) == latd
             and nlon % (3 * LANES) == 0
         )
         if small and fits:

time: 363 us -> 335 us (0.923)
  waiting for transfers between devices: 142 us -> 109 us
  starting transfers between devices: 41.1 us -> 66.6 us
  Pallas kernels: 154 us -> 140 us
    ppermute x28 -> x42, waiting for transfers between devices: 137 us -> 109 us  [exchange(): out[r] = lax.ppermute(blocks[r], lat_lev, pairs)]
    ppermute x28 -> x42, starting transfers between devices: 40.7 us -> 65.6 us  [exchange(): out[r] = lax.ppermute(blocks[r], lat_lev, pairs)]
    pallas_call x13 -> x11, Pallas kernels: 144 us -> 128 us  [the longest x3 50.6 us: legendre_step(): pl.pallas_call(functools.partial(legendre_kernel, groups, levs, levd, lat...]
    ppermute x4 -> x6, waiting for transfers between devices: 4.28 us -> 0.02 us  [swap(): return lax.ppermute(block, 'fld', [(0, 1), (1, 0)])]
  transfers between devices with their start and end apart: 32 -> 48, of which waited for: 16 -> 19; matrix products, arithmetic and copies ran while one was open for 2% -> 2% of each run, Pallas kernels for 24% -> 33%
where the time goes in v4:
time: 335 us; the launch traced here: 334 us
  Pallas kernels  140 us (42%)
  waiting for transfers between devices  109 us (33%)
  starting transfers between devices  66.6 us (20%)
  local copies, waits for them, and re-layouts  12.5 us (4%)
  other arithmetic  5.17 us (2%)
    ppermute x42, waiting for transfers between devices, exchange(): out[r] = lax.ppermute(blocks[r], lat_lev, pairs)  109 us
    ppermute x42, starting transfers between devices, exchange(): out[r] = lax.ppermute(blocks[r], lat_lev, pairs)  65.6 us
    pallas_call x3, Pallas kernels, legendre_step(): pl.pallas_call(functools.partial(legendre_kernel, groups, levs, levd, lat...  50.6 us
    pallas_call x3, Pallas kernels, dft(): pl.pallas_call(functools.partial(dft_kernel, groups, latd), out_shape=[ja...  39.2 us
    pallas_call x2, Pallas kernels, inverse_dft(): pl.pallas_call(functools.partial(inverse_kernel, counts, latd, scale, par...  29.3 us
    pallas_call x3, Pallas kernels, make_table(): pl.pallas_call(functools.partial(table_kernel, nlon), out_shape=jax.Shape...  8.61 us
  transfers between devices with their start and end apart: 48, of which 19 were waited for; matrix products, arithmetic and copies ran while one was open for 2% of the time, Pallas kernels for 33%

profile of v4, /device:TPU:12, one launch (start us, length us, event | category | flops | bytes accessed | tf_op | source)
XLA Modules:
  0.0 334.2 jit_solution(13946372149800763577)
XLA Ops:
  3.3 2.8 table.3.t_ref.refs_0_
  7.8 13.0 %dft.3 = (bf16[45,16,128]{2,1,0:T(8,128)(2,1)}, bf16[45,16,128]{2,1,0:T(8,128)(2,1)}, bf16[45,16,128]{2,1,0:T(8,128)(2,1)}, bf16[45,16,128]{2,1,0:T(8,128)(2,1)}...) custom-call(bf16[24,120,1920]{2,1,0:T(8,128)(2,1)} %bitcast.64, ...), custom_call_target="tpu_custom_call" | custom-call | flops 5662310400 | bytes 13516800 | tf_op jit(solution)/shard_map/dft/pallas_call | solution.py:258
  24.3 2.6 collective-permute-start.3
  29.5 2.9 table.5.t_ref.refs_1_
  33.2 2.8 table.4.t_ref.refs_0_
  36.0 13.1 %dft.4 = (bf16[45,16,128]{2,1,0:T(8,128)(2,1)}, bf16[45,16,128]{2,1,0:T(8,128)(2,1)}, bf16[45,16,128]{2,1,0:T(8,128)(2,1)}, bf16[45,16,128]{2,1,0:T(8,128)(2,1)}...) custom-call(bf16[24,120,1920]{2,1,0:T(8,128)(2,1)} %bitcast.65, ...), custom_call_target="tpu_custom_call" | custom-call | flops 5662310400 | bytes 13516800 | tf_op jit(solution)/shard_map/dft/pallas_call | solution.py:258
  49.1 13.1 %dft.5 = (bf16[45,16,128]{2,1,0:T(8,128)(2,1)}, bf16[45,16,128]{2,1,0:T(8,128)(2,1)}, bf16[45,16,128]{2,1,0:T(8,128)(2,1)}, bf16[45,16,128]{2,1,0:T(8,128)(2,1)}...) custom-call(bf16[24,120,1920]{2,1,0:T(8,128)(2,1)} %bitcast.66, ...), custom_call_target="tpu_custom_call" | custom-call | flops 5662310400 | bytes 13516800 | tf_op jit(solution)/shard_map/dft/pallas_call | solution.py:258
  63.6 1.6 collective-permute-start.5
  65.8 1.5 collective-permute-start.16
  67.3 2.3 collective-permute-start.17
  69.8 7.9 %collective-permute-done.5.refs_6_.rest_6_ = bf16[45,16,128]{2,1,0:T(8,128)(2,1)S(1)} collective-permute-done((bf16[45,16,128]{2,1,0:T(8,128)(2,1)S(1)}, bf16[45,16,128]{2,1,0:T(8,128)(2,1)S(1)}, u32[]{:S(2)}, u32[]{:S(2)}) %collective-permute-start.5) | collective-permute-done | bytes 184352 | tf_op jit(solution)/shard_map/ppermute | solution.py:601
  77.7 6.0 %collective-permute-done.6.refs_7_.rest_7_ = bf16[45,16,128]{2,1,0:T(8,128)(2,1)S(1)} collective-permute-done((bf16[45,16,128]{2,1,0:T(8,128)(2,1)S(1)}, bf16[45,16,128]{2,1,0:T(8,128)(2,1)S(1)}, u32[]{:S(2)}, u32[]{:S(2)}) %collective-permute-start.6) | collective-permute-done | bytes 184352 | tf_op jit(solution)/shard_map/ppermute | solution.py:601
  83.7 3.0 collective-permute-start.21
  87.8 2.1 gather_halves.3
  90.5 11.0 %collective-permute-done.19.refs_4_.rest_4_ = bf16[45,16,128]{2,1,0:T(8,128)(2,1)S(1)} collective-permute-done((bf16[45,16,128]{2,1,0:T(8,128)(2,1)}, bf16[45,16,128]{2,1,0:T(8,128)(2,1)S(1)}, u32[]{:S(2)}, u32[]{:S(2)}) %collective-permute-start.19) | collective-permute-done | bytes 184352 | tf_op jit(solution)/shard_map/ppermute | solution.py:601
  101.6 1.6 collective-permute-start.33
  103.2 2.2 collective-permute-done.20.refs_5_.rest_5_
  105.4 2.6 collective-permute-start.34
  108.0 1.6 collective-permute-done.21.refs_6_.rest_6_
  109.6 8.3 %collective-permute-done.22.refs_7_.rest_7_ = bf16[45,16,128]{2,1,0:T(8,128)(2,1)S(1)} collective-permute-done((bf16[45,16,128]{2,1,0:T(8,128)(2,1)S(1)}, bf16[45,16,128]{2,1,0:T(8,128)(2,1)S(1)}, u32[]{:S(2)}, u32[]{:S(2)}) %collective-permute-start.22) | collective-permute-done | bytes 184352 | tf_op jit(solution)/shard_map/ppermute | solution.py:601
  118.7 2.1 gather_halves.4
  120.9 1.8 collective-permute-start.37
  124.9 13.1 %collective-permute-done.36.refs_5_.rest_5_ = bf16[45,16,128]{2,1,0:T(8,128)(2,1)S(1)} collective-permute-done((bf16[45,16,128]{2,1,0:T(8,128)(2,1)}, bf16[45,16,128]{2,1,0:T(8,128)(2,1)S(1)}, u32[]{:S(2)}, u32[]{:S(2)}) %collective-permute-start.36) | collective-permute-done | bytes 184352 | tf_op jit(solution)/shard_map/ppermute | solution.py:601
  138.0 6.0 %collective-permute-done.37.refs_6_.rest_6_ = bf16[45,16,128]{2,1,0:T(8,128)(2,1)S(1)} collective-permute-done((bf16[45,16,128]{2,1,0:T(8,128)(2,1)}, bf16[45,16,128]{2,1,0:T(8,128)(2,1)S(1)}, u32[]{:S(2)}, u32[]{:S(2)}) %collective-permute-start.37) | collective-permute-done | bytes 184352 | tf_op jit(solution)/shard_map/ppermute | solution.py:601
  144.0 4.1 %collective-permute-done.38.refs_7_.rest_7_ = bf16[45,16,128]{2,1,0:T(8,128)(2,1)S(1)} collective-permute-done((bf16[45,16,128]{2,1,0:T(8,128)(2,1)}, bf16[45,16,128]{2,1,0:T(8,128)(2,1)S(1)}, u32[]{:S(2)}, u32[]{:S(2)}) %collective-permute-start.38) | collective-permute-done | bytes 184352 | tf_op jit(solution)/shard_map/ppermute | solution.py:601
  148.9 2.1 gather_halves.5
  154.2 16.9 %legendre.3 = (bf16[45,16,128]{2,1,0:T(8,128)(2,1)}, bf16[45,16,128]{2,1,0:T(8,128)(2,1)}, bf16[45,16,128]{2,1,0:T(8,128)(2,1)}, bf16[45,16,128]{2,1,0:T(8,128)(...) custom-call(s32[4,8]{1,0:T(4,128)} %get-tuple-element.171.info, ...), custom_call_target="tpu_custom_call" | custom-call | flops 2717908992 | bytes 6094848 | tf_op jit(solution)/shard_map/legendre/pallas_call | solution.py:393
  172.5 16.9 %legendre.4 = (bf16[45,16,128]{2,1,0:T(8,128)(2,1)}, bf16[45,16,128]{2,1,0:T(8,128)(2,1)}, bf16[45,16,128]{2,1,0:T(8,128)(2,1)}, bf16[45,16,128]{2,1,0:T(8,128)(...) custom-call(s32[4,8]{1,0:T(4,128)} %get-tuple-element.170.info, ...), custom_call_target="tpu_custom_call" | custom-call | flops 2717908992 | bytes 6094848 | tf_op jit(solution)/shard_map/legendre/pallas_call | solution.py:393
  190.2 16.8 %legendre.5 = (bf16[45,16,128]{2,1,0:T(8,128)(2,1)}, bf16[45,16,128]{2,1,0:T(8,128)(2,1)}, bf16[45,16,128]{2,1,0:T(8,128)(2,1)}, bf16[45,16,128]{2,1,0:T(8,128)(...) custom-call(s32[4,8]{1,0:T(4,128)} %get-tuple-element.169.info, ...), custom_call_target="tpu_custom_call" | custom-call | flops 2717908992 | bytes 6094848 | tf_op jit(solution)/shard_map/legendre/pallas_call | solution.py:393
  208.4 2.1 fill_halves.3
  211.9 2.1 fill_halves.4
  215.5 2.0 collective-permute-start.26
  219.3 2.1 fill_halves.5
  221.3 2.2 collective-permute-start.29
  224.1 3.7 %collective-permute-done.26.refs_4_ = bf16[45,16,128]{2,1,0:T(8,128)(2,1)S(1)} collective-permute-done((bf16[45,16,128]{2,1,0:T(8,128)(2,1)}, bf16[45,16,128]{2,1,0:T(8,128)(2,1)S(1)}, u32[]{:S(2)}, u32[]{:S(2)}) %collective-permute-start.26) | collective-permute-done | bytes 184352 | tf_op jit(solution)/shard_map/ppermute | solution.py:601
  231.2 10.9 %collective-permute-start.42 = (bf16[45,16,128]{2,1,0:T(8,128)(2,1)}, bf16[45,16,128]{2,1,0:T(8,128)(2,1)S(1)}, u32[]{:S(2)}, u32[]{:S(2)}) collective-permute-start(bf16[45,16,128]{2,1,0:T(8,128)(2,1)} %get-tuple-element.149), channel_id=1, source_target_pairs={{0,4},{2,6},{4,0},{6,2},{8,12},{10,14},{12,8},{14,10},{1,5},{3,7},... | collective-permute-start | bytes 552968 | tf_op jit(solution)/shard_map/ppermute | solution.py:601
  242.0 1.9 collective-permute-done.29.refs_7_
  243.9 4.2 %collective-permute-start.43 = (bf16[45,16,128]{2,1,0:T(8,128)(2,1)}, bf16[45,16,128]{2,1,0:T(8,128)(2,1)S(1)}, u32[]{:S(2)}, u32[]{:S(2)}) collective-permute-start(bf16[45,16,128]{2,1,0:T(8,128)(2,1)} %get-tuple-element.150), channel_id=1, source_target_pairs={{0,6},{2,4},{4,2},{6,0},{8,14},{10,12},{12,10},{14,8},{1,7},{3,5},... | collective-permute-start | bytes 552968 | tf_op jit(solution)/shard_map/ppermute | solution.py:601
  248.1 1.6 collective-permute-done.30.refs_8_
  249.7 16.1 %collective-permute-done.31.refs_9_ = bf16[45,16,128]{2,1,0:T(8,128)(2,1)S(1)} collective-permute-done((bf16[45,16,128]{2,1,0:T(8,128)(2,1)}, bf16[45,16,128]{2,1,0:T(8,128)(2,1)S(1)}, u32[]{:S(2)}, u32[]{:S(2)}) %collective-permute-start.31) | collective-permute-done | bytes 184352 | tf_op jit(solution)/shard_map/ppermute | solution.py:601
  267.1 4.6 %collective-permute-start.11 = (bf16[45,16,128]{2,1,0:T(8,128)(2,1)}, bf16[45,16,128]{2,1,0:T(8,128)(2,1)S(1)}, u32[]{:S(2)}, u32[]{:S(2)}) collective-permute-start(bf16[45,16,128]{2,1,0:T(8,128)(2,1)} %get-tuple-element.100), channel_id=1, source_target_pairs={{0,6},{2,4},{4,2},{6,0},{8,14},{10,12},{12,10},{14,8},{1,7},{3,5},... | collective-permute-start | bytes 552968 | tf_op jit(solution)/shard_map/ppermute | solution.py:601
  271.7 1.9 collective-permute-start.12
  273.6 13.1 %collective-permute-done.45.refs_15_ = bf16[45,16,128]{2,1,0:T(8,128)(2,1)S(1)} collective-permute-done((bf16[45,16,128]{2,1,0:T(8,128)(2,1)}, bf16[45,16,128]{2,1,0:T(8,128)(2,1)S(1)}, u32[]{:S(2)}, u32[]{:S(2)}) %collective-permute-start.45) | collective-permute-done | bytes 184352 | tf_op jit(solution)/shard_map/ppermute | solution.py:601
  286.7 4.2 %collective-permute-start.13 = (bf16[45,16,128]{2,1,0:T(8,128)(2,1)}, bf16[45,16,128]{2,1,0:T(8,128)(2,1)S(1)}, u32[]{:S(2)}, u32[]{:S(2)}) collective-permute-start(bf16[45,16,128]{2,1,0:T(8,128)(2,1)} %get-tuple-element.102), channel_id=1, source_target_pairs={{0,10},{2,8},{4,14},{6,12},{8,2},{10,0},{12,6},{14,4},{1,11},{3,9}... | collective-permute-start | bytes 552968 | tf_op jit(solution)/shard_map/ppermute | solution.py:601
  291.2 1.8 collective-permute-start.14
  293.0 9.8 %collective-permute-done.47.refs_17_ = bf16[45,16,128]{2,1,0:T(8,128)(2,1)S(1)} collective-permute-done((bf16[45,16,128]{2,1,0:T(8,128)(2,1)}, bf16[45,16,128]{2,1,0:T(8,128)(2,1)S(1)}, u32[]{:S(2)}, u32[]{:S(2)}) %collective-permute-start.47) | collective-permute-done | bytes 184352 | tf_op jit(solution)/shard_map/ppermute | solution.py:601
  303.9 14.3 %inverse_dft.2.refs_9_ = f32[24,120,1920]{2,1,0:T(8,128)} custom-call(bf16[256,1920]{1,0:T(8,128)(2,1)} %table.4.t_ref.refs_0_, bf16[256,1920]{1,0:T(8,128)(2,1)} %table.5.t_ref.refs_1_, bf16[45,16,128]{2,1,0:T(8,128)(2,1)} %get-tuple-element.122.refs_2_, bf16[45,16,128]{2,1,0:T(8,128)(2,1)} %copy-done.29, bf16[45,16,128]{2,1,0:T(8,128)(2,1)} %copy-done.30, ...), custom_call_target="tpu_custom_call" | custom-call | flops 5662310400 | bytes 15974400 | tf_op jit(solution)/shard_map/inverse_dft/pallas_call | solution.py:520
  319.1 14.9 %inverse_dft.3 = bf16[24,120,1920]{2,1,0:T(8,128)(2,1)} custom-call(bf16[256,1920]{1,0:T(8,128)(2,1)} %table.3.t_ref.refs_0_, bf16[45,16,128]{2,1,0:T(8,128)(2,1)} %get-tuple-element.97.refs_1_, bf16[45,16,128]{2,1,0:T(8,128)(2,1)} %copy-done.43, bf16[45,16,128]{2,1,0:T(8,128)(2,1)} %copy-done.44, bf16[45,16,128]{2,1,0:T(8,128)(2,1)} %copy-done.45, ...), custom_call_target="tpu_custom_call" | custom-call | flops 2831155200 | bytes 13516800 | tf_op jit(solution)/shard_map/inverse_dft/pallas_call | solution.py:520
  (233 shorter events, 37.7 us)
Async XLA Ops:
  20.7 42.9 %collective-permute-start = (bf16[45,16,128]{2,1,0:T(8,128)(2,1)}, bf16[45,16,128]{2,1,0:T(8,128)(2,1)S(1)}, u32[]{:S(2)}, u32[]{:S(2)}) collective-permute-start(bf16[45,16,128]{2,1,0:T(8,128)(2,1)} %get-tuple-element.81), channel_id=1, source_target_pairs={{0,2},{2,0},{4,6},{6,4},{8,10},{10,8},{12,14},{14,12},{1,3},{3,1},... | collective-permute-start | bytes 552968 | tf_op jit(solution)/shard_map/ppermute | solution.py:601
  22.3 43.0 %collective-permute-start.1 = (bf16[45,16,128]{2,1,0:T(8,128)(2,1)}, bf16[45,16,128]{2,1,0:T(8,128)(2,1)S(1)}, u32[]{:S(2)}, u32[]{:S(2)}) collective-permute-start(bf16[45,16,128]{2,1,0:T(8,128)(2,1)} %get-tuple-element.82), channel_id=1, source_target_pairs={{0,4},{2,6},{4,0},{6,2},{8,12},{10,14},{12,8},{14,10},{1,5},{3,7},... | collective-permute-start | bytes 552968 | tf_op jit(solution)/shard_map/ppermute | solution.py:601
  22.7 43.1 %collective-permute-start.2 = (bf16[45,16,128]{2,1,0:T(8,128)(2,1)}, bf16[45,16,128]{2,1,0:T(8,128)(2,1)S(1)}, u32[]{:S(2)}, u32[]{:S(2)}) collective-permute-start(bf16[45,16,128]{2,1,0:T(8,128)(2,1)} %get-tuple-element.83), channel_id=1, source_target_pairs={{0,6},{2,4},{4,2},{6,0},{8,14},{10,12},{12,10},{14,8},{1,7},{3,5},... | collective-permute-start | bytes 552968 | tf_op jit(solution)/shard_map/ppermute | solution.py:601
  24.3 43.1 %collective-permute-start.3 = (bf16[45,16,128]{2,1,0:T(8,128)(2,1)}, bf16[45,16,128]{2,1,0:T(8,128)(2,1)S(1)}, u32[]{:S(2)}, u32[]{:S(2)}) collective-permute-start(bf16[45,16,128]{2,1,0:T(8,128)(2,1)} %get-tuple-element.84), channel_id=1, source_target_pairs={{0,8},{2,10},{4,12},{6,14},{8,0},{10,2},{12,4},{14,6},{1,9},{3,11}... | collective-permute-start | bytes 552968 | tf_op jit(solution)/shard_map/ppermute | solution.py:601
  26.8 42.9 %collective-permute-start.4 = (bf16[45,16,128]{2,1,0:T(8,128)(2,1)}, bf16[45,16,128]{2,1,0:T(8,128)(2,1)S(1)}, u32[]{:S(2)}, u32[]{:S(2)}) collective-permute-start(bf16[45,16,128]{2,1,0:T(8,128)(2,1)} %get-tuple-element.85), channel_id=1, source_target_pairs={{0,10},{2,8},{4,14},{6,12},{8,2},{10,0},{12,6},{14,4},{1,11},{3,9}... | collective-permute-start | bytes 552968 | tf_op jit(solution)/shard_map/ppermute | solution.py:601
  63.6 14.0 %collective-permute-start.5 = (bf16[45,16,128]{2,1,0:T(8,128)(2,1)S(1)}, bf16[45,16,128]{2,1,0:T(8,128)(2,1)S(1)}, u32[]{:S(2)}, u32[]{:S(2)}) collective-permute-start(bf16[45,16,128]{2,1,0:T(8,128)(2,1)S(1)} %copy-done.54), channel_id=1, source_target_pairs={{0,12},{2,14},{4,8},{6,10},{8,4},{10,6},{12,0},{14,2},{1,13},{3,15... | collective-permute-start | bytes 552968 | tf_op jit(solution)/shard_map/ppermute | solution.py:601
  65.3 18.4 %collective-permute-start.6 = (bf16[45,16,128]{2,1,0:T(8,128)(2,1)S(1)}, bf16[45,16,128]{2,1,0:T(8,128)(2,1)S(1)}, u32[]{:S(2)}, u32[]{:S(2)}) collective-permute-start(bf16[45,16,128]{2,1,0:T(8,128)(2,1)S(1)} %copy-done.53), channel_id=1, source_target_pairs={{0,14},{2,12},{4,10},{6,8},{8,6},{10,4},{12,2},{14,0},{1,15},{3,13... | collective-permute-start | bytes 552968 | tf_op jit(solution)/shard_map/ppermute | solution.py:601
  65.8 17.9 %collective-permute-start.16 = (bf16[45,16,128]{2,1,0:T(8,128)(2,1)S(1)}, bf16[45,16,128]{2,1,0:T(8,128)(2,1)S(1)}, u32[]{:S(2)}, u32[]{:S(2)}) collective-permute-start(bf16[45,16,128]{2,1,0:T(8,128)(2,1)S(1)} %copy-done.59), channel_id=1, source_target_pairs={{0,2},{2,0},{4,6},{6,4},{8,10},{10,8},{12,14},{14,12},{1,3},{3,1},... | collective-permute-start | bytes 552968 | tf_op jit(solution)/shard_map/ppermute | solution.py:601
  67.3 19.4 %collective-permute-start.17 = (bf16[45,16,128]{2,1,0:T(8,128)(2,1)S(1)}, bf16[45,16,128]{2,1,0:T(8,128)(2,1)S(1)}, u32[]{:S(2)}, u32[]{:S(2)}) collective-permute-start(bf16[45,16,128]{2,1,0:T(8,128)(2,1)S(1)} %copy-done.58), channel_id=1, source_target_pairs={{0,4},{2,6},{4,0},{6,2},{8,12},{10,14},{12,8},{14,10},{1,5},{3,7},... | collective-permute-start | bytes 552968 | tf_op jit(solution)/shard_map/ppermute | solution.py:601
  69.7 20.2 %collective-permute-start.18 = (bf16[45,16,128]{2,1,0:T(8,128)(2,1)}, bf16[45,16,128]{2,1,0:T(8,128)(2,1)S(1)}, u32[]{:S(2)}, u32[]{:S(2)}) collective-permute-start(bf16[45,16,128]{2,1,0:T(8,128)(2,1)} %get-tuple-element.108), channel_id=1, source_target_pairs={{0,6},{2,4},{4,2},{6,0},{8,14},{10,12},{12,10},{14,8},{1,7},{3,5},... | collective-permute-start | bytes 552968 | tf_op jit(solution)/shard_map/ppermute | solution.py:601
  77.7 23.9 %collective-permute-start.19 = (bf16[45,16,128]{2,1,0:T(8,128)(2,1)}, bf16[45,16,128]{2,1,0:T(8,128)(2,1)S(1)}, u32[]{:S(2)}, u32[]{:S(2)}) collective-permute-start(bf16[45,16,128]{2,1,0:T(8,128)(2,1)} %get-tuple-element.109), channel_id=1, source_target_pairs={{0,8},{2,10},{4,12},{6,14},{8,0},{10,2},{12,4},{14,6},{1,9},{3,11}... | collective-permute-start | bytes 552968 | tf_op jit(solution)/shard_map/ppermute | solution.py:601
  83.7 21.8 %collective-permute-start.20 = (bf16[45,16,128]{2,1,0:T(8,128)(2,1)S(1)}, bf16[45,16,128]{2,1,0:T(8,128)(2,1)S(1)}, u32[]{:S(2)}, u32[]{:S(2)}) collective-permute-start(bf16[45,16,128]{2,1,0:T(8,128)(2,1)S(1)} %copy-done.57), channel_id=1, source_target_pairs={{0,10},{2,8},{4,14},{6,12},{8,2},{10,0},{12,6},{14,4},{1,11},{3,9}... | collective-permute-start | bytes 552968 | tf_op jit(solution)/shard_map/ppermute | solution.py:601
  83.7 25.9 %collective-permute-start.21 = (bf16[45,16,128]{2,1,0:T(8,128)(2,1)S(1)}, bf16[45,16,128]{2,1,0:T(8,128)(2,1)S(1)}, u32[]{:S(2)}, u32[]{:S(2)}) collective-permute-start(bf16[45,16,128]{2,1,0:T(8,128)(2,1)S(1)} %copy-done.56), channel_id=1, source_target_pairs={{0,12},{2,14},{4,8},{6,10},{8,4},{10,6},{12,0},{14,2},{1,13},{3,15... | collective-permute-start | bytes 552968 | tf_op jit(solution)/shard_map/ppermute | solution.py:601
  86.7 31.3 %collective-permute-start.22 = (bf16[45,16,128]{2,1,0:T(8,128)(2,1)S(1)}, bf16[45,16,128]{2,1,0:T(8,128)(2,1)S(1)}, u32[]{:S(2)}, u32[]{:S(2)}) collective-permute-start(bf16[45,16,128]{2,1,0:T(8,128)(2,1)S(1)} %copy-done.55), channel_id=1, source_target_pairs={{0,14},{2,12},{4,10},{6,8},{8,6},{10,4},{12,2},{14,0},{1,15},{3,13... | collective-permute-start | bytes 552968 | tf_op jit(solution)/shard_map/ppermute | solution.py:601
  89.9 30.8 %collective-permute-start.32 = (bf16[45,16,128]{2,1,0:T(8,128)(2,1)}, bf16[45,16,128]{2,1,0:T(8,128)(2,1)S(1)}, u32[]{:S(2)}, u32[]{:S(2)}) collective-permute-start(bf16[45,16,128]{2,1,0:T(8,128)(2,1)} %get-tuple-element.131), channel_id=1, source_target_pairs={{0,2},{2,0},{4,6},{6,4},{8,10},{10,8},{12,14},{14,12},{1,3},{3,1},... | collective-permute-start | bytes 552968 | tf_op jit(solution)/shard_map/ppermute | solution.py:601
  101.6 19.3 %collective-permute-start.33 = (bf16[45,16,128]{2,1,0:T(8,128)(2,1)}, bf16[45,16,128]{2,1,0:T(8,128)(2,1)S(1)}, u32[]{:S(2)}, u32[]{:S(2)}) collective-permute-start(bf16[45,16,128]{2,1,0:T(8,128)(2,1)} %get-tuple-element.132), channel_id=1, source_target_pairs={{0,4},{2,6},{4,0},{6,2},{8,12},{10,14},{12,8},{14,10},{1,5},{3,7},... | collective-permute-start | bytes 552968 | tf_op jit(solution)/shard_map/ppermute | solution.py:601
  105.4 17.2 %collective-permute-start.34 = (bf16[45,16,128]{2,1,0:T(8,128)(2,1)}, bf16[45,16,128]{2,1,0:T(8,128)(2,1)S(1)}, u32[]{:S(2)}, u32[]{:S(2)}) collective-permute-start(bf16[45,16,128]{2,1,0:T(8,128)(2,1)} %get-tuple-element.133), channel_id=1, source_target_pairs={{0,6},{2,4},{4,2},{6,0},{8,14},{10,12},{12,10},{14,8},{1,7},{3,5},... | collective-permute-start | bytes 552968 | tf_op jit(solution)/shard_map/ppermute | solution.py:601
  109.6 14.4 %collective-permute-start.35 = (bf16[45,16,128]{2,1,0:T(8,128)(2,1)}, bf16[45,16,128]{2,1,0:T(8,128)(2,1)S(1)}, u32[]{:S(2)}, u32[]{:S(2)}) collective-permute-start(bf16[45,16,128]{2,1,0:T(8,128)(2,1)} %get-tuple-element.134), channel_id=1, source_target_pairs={{0,8},{2,10},{4,12},{6,14},{8,0},{10,2},{12,4},{14,6},{1,9},{3,11}... | collective-permute-start | bytes 552968 | tf_op jit(solution)/shard_map/ppermute | solution.py:601
  118.0 35.4 %collective-permute-start.7 = (bf16[8,45,8,128]{3,2,1,0:T(8,128)(2,1)}, bf16[8,45,8,128]{3,2,1,0:T(8,128)(2,1)S(1)}, u32[]{:S(2)}, u32[]{:S(2)}) collective-permute-start(bf16[8,45,8,128]{3,2,1,0:T(8,128)(2,1)} %gather_halves.3), channel_id=1, source_target_pairs={{0,1},{1,0},{2,3},{3,2},{4,5},{5,4},{6,7},{7,6},{8,9},{9,8},{10,11... | collective-permute-start | bytes 2211848 | tf_op jit(solution)/shard_map/ppermute | solution.py:605
  120.8 17.3 %collective-permute-start.36 = (bf16[45,16,128]{2,1,0:T(8,128)(2,1)}, bf16[45,16,128]{2,1,0:T(8,128)(2,1)S(1)}, u32[]{:S(2)}, u32[]{:S(2)}) collective-permute-start(bf16[45,16,128]{2,1,0:T(8,128)(2,1)} %get-tuple-element.135), channel_id=1, source_target_pairs={{0,10},{2,8},{4,14},{6,12},{8,2},{10,0},{12,6},{14,4},{1,11},{3,9}... | collective-permute-start | bytes 552968 | tf_op jit(solution)/shard_map/ppermute | solution.py:601
  120.9 23.2 %collective-permute-start.37 = (bf16[45,16,128]{2,1,0:T(8,128)(2,1)}, bf16[45,16,128]{2,1,0:T(8,128)(2,1)S(1)}, u32[]{:S(2)}, u32[]{:S(2)}) collective-permute-start(bf16[45,16,128]{2,1,0:T(8,128)(2,1)} %get-tuple-element.136), channel_id=1, source_target_pairs={{0,12},{2,14},{4,8},{6,10},{8,4},{10,6},{12,0},{14,2},{1,13},{3,15... | collective-permute-start | bytes 552968 | tf_op jit(solution)/shard_map/ppermute | solution.py:601
  122.6 25.5 %collective-permute-start.38 = (bf16[45,16,128]{2,1,0:T(8,128)(2,1)}, bf16[45,16,128]{2,1,0:T(8,128)(2,1)S(1)}, u32[]{:S(2)}, u32[]{:S(2)}) collective-permute-start(bf16[45,16,128]{2,1,0:T(8,128)(2,1)} %get-tuple-element.137), channel_id=1, source_target_pairs={{0,14},{2,12},{4,10},{6,8},{8,6},{10,4},{12,2},{14,0},{1,15},{3,13... | collective-permute-start | bytes 552968 | tf_op jit(solution)/shard_map/ppermute | solution.py:601
  124.1 47.5 %collective-permute-start.23 = (bf16[8,45,8,128]{3,2,1,0:T(8,128)(2,1)}, bf16[8,45,8,128]{3,2,1,0:T(8,128)(2,1)S(1)}, u32[]{:S(2)}, u32[]{:S(2)}) collective-permute-start(bf16[8,45,8,128]{3,2,1,0:T(8,128)(2,1)} %gather_halves.4), channel_id=1, source_target_pairs={{0,1},{1,0},{2,3},{3,2},{4,5},{5,4},{6,7},{7,6},{8,9},{9,8},{10,11... | collective-permute-start | bytes 2211848 | tf_op jit(solution)/shard_map/ppermute | solution.py:605
  151.0 38.4 %collective-permute-start.39 = (bf16[8,45,8,128]{3,2,1,0:T(8,128)(2,1)}, bf16[8,45,8,128]{3,2,1,0:T(8,128)(2,1)S(1)}, u32[]{:S(2)}, u32[]{:S(2)}) collective-permute-start(bf16[8,45,8,128]{3,2,1,0:T(8,128)(2,1)} %gather_halves.5), channel_id=1, source_target_pairs={{0,1},{1,0},{2,3},{3,2},{4,5},{5,4},{6,7},{7,6},{8,9},{9,8},{10,11... | collective-permute-start | bytes 2211848 | tf_op jit(solution)/shard_map/ppermute | solution.py:605
  171.1 36.5 %collective-permute-start.8 = (bf16[8,45,8,128]{3,2,1,0:T(8,128)(2,1)}, bf16[8,45,8,128]{3,2,1,0:T(8,128)(2,1)S(1)}, u32[]{:S(2)}, u32[]{:S(2)}) collective-permute-start(bf16[8,45,8,128]{3,2,1,0:T(8,128)(2,1)} %get-tuple-element.88), channel_id=1, source_target_pairs={{0,1},{1,0},{2,3},{3,2},{4,5},{5,4},{6,7},{7,6},{8,9},{9,8},{10,11... | collective-permute-start | bytes 2211848 | tf_op jit(solution)/shard_map/ppermute | solution.py:605
  189.3 21.7 %collective-permute-start.24 = (bf16[8,45,8,128]{3,2,1,0:T(8,128)(2,1)}, bf16[8,45,8,128]{3,2,1,0:T(8,128)(2,1)S(1)}, u32[]{:S(2)}, u32[]{:S(2)}) collective-permute-start(bf16[8,45,8,128]{3,2,1,0:T(8,128)(2,1)} %get-tuple-element.113), channel_id=1, source_target_pairs={{0,1},{1,0},{2,3},{3,2},{4,5},{5,4},{6,7},{7,6},{8,9},{9,8},{10,11... | collective-permute-start | bytes 2211848 | tf_op jit(solution)/shard_map/ppermute | solution.py:605
  207.1 10.5 %collective-permute-start.40 = (bf16[8,45,8,128]{3,2,1,0:T(8,128)(2,1)}, bf16[8,45,8,128]{3,2,1,0:T(8,128)(2,1)S(1)}, u32[]{:S(2)}, u32[]{:S(2)}) collective-permute-start(bf16[8,45,8,128]{3,2,1,0:T(8,128)(2,1)} %get-tuple-element.138), channel_id=1, source_target_pairs={{0,1},{1,0},{2,3},{3,2},{4,5},{5,4},{6,7},{7,6},{8,9},{9,8},{10,11... | collective-permute-start | bytes 2211848 | tf_op jit(solution)/shard_map/ppermute | solution.py:605
  210.5 7.5 %collective-permute-start.9 = (bf16[45,16,128]{2,1,0:T(8,128)(2,1)}, bf16[45,16,128]{2,1,0:T(8,128)(2,1)S(1)}, u32[]{:S(2)}, u32[]{:S(2)}) collective-permute-start(bf16[45,16,128]{2,1,0:T(8,128)(2,1)} %get-tuple-element.98), channel_id=1, source_target_pairs={{0,2},{2,0},{4,6},{6,4},{8,10},{10,8},{12,14},{14,12},{1,3},{3,1},... | collective-permute-start | bytes 552968 | tf_op jit(solution)/shard_map/ppermute | solution.py:601
  211.0 10.3 %collective-permute-start.10 = (bf16[45,16,128]{2,1,0:T(8,128)(2,1)}, bf16[45,16,128]{2,1,0:T(8,128)(2,1)S(1)}, u32[]{:S(2)}, u32[]{:S(2)}) collective-permute-start(bf16[45,16,128]{2,1,0:T(8,128)(2,1)} %get-tuple-element.99), channel_id=1, source_target_pairs={{0,4},{2,6},{4,0},{6,2},{8,12},{10,14},{12,8},{14,10},{1,5},{3,7},... | collective-permute-start | bytes 552968 | tf_op jit(solution)/shard_map/ppermute | solution.py:601
  214.0 9.6 %collective-permute-start.25 = (bf16[45,16,128]{2,1,0:T(8,128)(2,1)}, bf16[45,16,128]{2,1,0:T(8,128)(2,1)S(1)}, u32[]{:S(2)}, u32[]{:S(2)}) collective-permute-start(bf16[45,16,128]{2,1,0:T(8,128)(2,1)} %get-tuple-element.123), channel_id=1, source_target_pairs={{0,2},{2,0},{4,6},{6,4},{8,10},{10,8},{12,14},{14,12},{1,3},{3,1},... | collective-permute-start | bytes 552968 | tf_op jit(solution)/shard_map/ppermute | solution.py:601
  215.5 12.3 %collective-permute-start.26 = (bf16[45,16,128]{2,1,0:T(8,128)(2,1)}, bf16[45,16,128]{2,1,0:T(8,128)(2,1)S(1)}, u32[]{:S(2)}, u32[]{:S(2)}) collective-permute-start(bf16[45,16,128]{2,1,0:T(8,128)(2,1)} %get-tuple-element.124), channel_id=1, source_target_pairs={{0,4},{2,6},{4,0},{6,2},{8,12},{10,14},{12,8},{14,10},{1,5},{3,7},... | collective-permute-start | bytes 552968 | tf_op jit(solution)/shard_map/ppermute | solution.py:601
  217.5 12.4 %collective-permute-start.27 = (bf16[45,16,128]{2,1,0:T(8,128)(2,1)}, bf16[45,16,128]{2,1,0:T(8,128)(2,1)S(1)}, u32[]{:S(2)}, u32[]{:S(2)}) collective-permute-start(bf16[45,16,128]{2,1,0:T(8,128)(2,1)} %get-tuple-element.125), channel_id=1, source_target_pairs={{0,6},{2,4},{4,2},{6,0},{8,14},{10,12},{12,10},{14,8},{1,7},{3,5},... | collective-permute-start | bytes 552968 | tf_op jit(solution)/shard_map/ppermute | solution.py:601
  218.0 13.2 %collective-permute-start.28 = (bf16[45,16,128]{2,1,0:T(8,128)(2,1)}, bf16[45,16,128]{2,1,0:T(8,128)(2,1)S(1)}, u32[]{:S(2)}, u32[]{:S(2)}) collective-permute-start(bf16[45,16,128]{2,1,0:T(8,128)(2,1)} %get-tuple-element.126), channel_id=1, source_target_pairs={{0,8},{2,10},{4,12},{6,14},{8,0},{10,2},{12,4},{14,6},{1,9},{3,11}... | collective-permute-start | bytes 552968 | tf_op jit(solution)/shard_map/ppermute | solution.py:601
  221.3 22.5 %collective-permute-start.29 = (bf16[45,16,128]{2,1,0:T(8,128)(2,1)}, bf16[45,16,128]{2,1,0:T(8,128)(2,1)S(1)}, u32[]{:S(2)}, u32[]{:S(2)}) collective-permute-start(bf16[45,16,128]{2,1,0:T(8,128)(2,1)} %get-tuple-element.127), channel_id=1, source_target_pairs={{0,10},{2,8},{4,14},{6,12},{8,2},{10,0},{12,6},{14,4},{1,11},{3,9}... | collective-permute-start | bytes 552968 | tf_op jit(solution)/shard_map/ppermute | solution.py:601
  223.6 26.1 %collective-permute-start.30 = (bf16[45,16,128]{2,1,0:T(8,128)(2,1)}, bf16[45,16,128]{2,1,0:T(8,128)(2,1)S(1)}, u32[]{:S(2)}, u32[]{:S(2)}) collective-permute-start(bf16[45,16,128]{2,1,0:T(8,128)(2,1)} %get-tuple-element.128), channel_id=1, source_target_pairs={{0,12},{2,14},{4,8},{6,10},{8,4},{10,6},{12,0},{14,2},{1,13},{3,15... | collective-permute-start | bytes 552968 | tf_op jit(solution)/shard_map/ppermute | solution.py:601
  227.8 38.0 %collective-permute-start.31 = (bf16[45,16,128]{2,1,0:T(8,128)(2,1)}, bf16[45,16,128]{2,1,0:T(8,128)(2,1)S(1)}, u32[]{:S(2)}, u32[]{:S(2)}) collective-permute-start(bf16[45,16,128]{2,1,0:T(8,128)(2,1)} %get-tuple-element.129), channel_id=1, source_target_pairs={{0,14},{2,12},{4,10},{6,8},{8,6},{10,4},{12,2},{14,0},{1,15},{3,13... | collective-permute-start | bytes 552968 | tf_op jit(solution)/shard_map/ppermute | solution.py:601
  230.0 35.8 %collective-permute-start.41 = (bf16[45,16,128]{2,1,0:T(8,128)(2,1)}, bf16[45,16,128]{2,1,0:T(8,128)(2,1)S(1)}, u32[]{:S(2)}, u32[]{:S(2)}) collective-permute-start(bf16[45,16,128]{2,1,0:T(8,128)(2,1)} %get-tuple-element.148), channel_id=1, source_target_pairs={{0,2},{2,0},{4,6},{6,4},{8,10},{10,8},{12,14},{14,12},{1,3},{3,1},... | collective-permute-start | bytes 552968 | tf_op jit(solution)/shard_map/ppermute | solution.py:601
  231.2 34.7 %collective-permute-start.42 = (bf16[45,16,128]{2,1,0:T(8,128)(2,1)}, bf16[45,16,128]{2,1,0:T(8,128)(2,1)S(1)}, u32[]{:S(2)}, u32[]{:S(2)}) collective-permute-start(bf16[45,16,128]{2,1,0:T(8,128)(2,1)} %get-tuple-element.149), channel_id=1, source_target_pairs={{0,4},{2,6},{4,0},{6,2},{8,12},{10,14},{12,8},{14,10},{1,5},{3,7},... | collective-permute-start | bytes 552968 | tf_op jit(solution)/shard_map/ppermute | solution.py:601
  243.9 23.2 %collective-permute-start.43 = (bf16[45,16,128]{2,1,0:T(8,128)(2,1)}, bf16[45,16,128]{2,1,0:T(8,128)(2,1)S(1)}, u32[]{:S(2)}, u32[]{:S(2)}) collective-permute-start(bf16[45,16,128]{2,1,0:T(8,128)(2,1)} %get-tuple-element.150), channel_id=1, source_target_pairs={{0,6},{2,4},{4,2},{6,0},{8,14},{10,12},{12,10},{14,8},{1,7},{3,5},... | collective-permute-start | bytes 552968 | tf_op jit(solution)/shard_map/ppermute | solution.py:601
  249.7 22.0 %collective-permute-start.44 = (bf16[45,16,128]{2,1,0:T(8,128)(2,1)}, bf16[45,16,128]{2,1,0:T(8,128)(2,1)S(1)}, u32[]{:S(2)}, u32[]{:S(2)}) collective-permute-start(bf16[45,16,128]{2,1,0:T(8,128)(2,1)} %get-tuple-element.151), channel_id=1, source_target_pairs={{0,8},{2,10},{4,12},{6,14},{8,0},{10,2},{12,4},{14,6},{1,9},{3,11}... | collective-permute-start | bytes 552968 | tf_op jit(solution)/shard_map/ppermute | solution.py:601
  265.8 20.9 %collective-permute-start.45 = (bf16[45,16,128]{2,1,0:T(8,128)(2,1)}, bf16[45,16,128]{2,1,0:T(8,128)(2,1)S(1)}, u32[]{:S(2)}, u32[]{:S(2)}) collective-permute-start(bf16[45,16,128]{2,1,0:T(8,128)(2,1)} %get-tuple-element.152), channel_id=1, source_target_pairs={{0,10},{2,8},{4,14},{6,12},{8,2},{10,0},{12,6},{14,4},{1,11},{3,9}... | collective-permute-start | bytes 552968 | tf_op jit(solution)/shard_map/ppermute | solution.py:601
  265.8 25.3 %collective-permute-start.46 = (bf16[45,16,128]{2,1,0:T(8,128)(2,1)}, bf16[45,16,128]{2,1,0:T(8,128)(2,1)S(1)}, u32[]{:S(2)}, u32[]{:S(2)}) collective-permute-start(bf16[45,16,128]{2,1,0:T(8,128)(2,1)} %get-tuple-element.153), channel_id=1, source_target_pairs={{0,12},{2,14},{4,8},{6,10},{8,4},{10,6},{12,0},{14,2},{1,13},{3,15... | collective-permute-start | bytes 552968 | tf_op jit(solution)/shard_map/ppermute | solution.py:601
  265.9 36.9 %collective-permute-start.47 = (bf16[45,16,128]{2,1,0:T(8,128)(2,1)}, bf16[45,16,128]{2,1,0:T(8,128)(2,1)S(1)}, u32[]{:S(2)}, u32[]{:S(2)}) collective-permute-start(bf16[45,16,128]{2,1,0:T(8,128)(2,1)} %get-tuple-element.154), channel_id=1, source_target_pairs={{0,14},{2,12},{4,10},{6,8},{8,6},{10,4},{12,2},{14,0},{1,15},{3,13... | collective-permute-start | bytes 552968 | tf_op jit(solution)/shard_map/ppermute | solution.py:601
  267.1 51.2 %collective-permute-start.11 = (bf16[45,16,128]{2,1,0:T(8,128)(2,1)}, bf16[45,16,128]{2,1,0:T(8,128)(2,1)S(1)}, u32[]{:S(2)}, u32[]{:S(2)}) collective-permute-start(bf16[45,16,128]{2,1,0:T(8,128)(2,1)} %get-tuple-element.100), channel_id=1, source_target_pairs={{0,6},{2,4},{4,2},{6,0},{8,14},{10,12},{12,10},{14,8},{1,7},{3,5},... | collective-permute-start | bytes 552968 | tf_op jit(solution)/shard_map/ppermute | solution.py:601
  271.7 46.6 %collective-permute-start.12 = (bf16[45,16,128]{2,1,0:T(8,128)(2,1)}, bf16[45,16,128]{2,1,0:T(8,128)(2,1)S(1)}, u32[]{:S(2)}, u32[]{:S(2)}) collective-permute-start(bf16[45,16,128]{2,1,0:T(8,128)(2,1)} %get-tuple-element.101), channel_id=1, source_target_pairs={{0,8},{2,10},{4,12},{6,14},{8,0},{10,2},{12,4},{14,6},{1,9},{3,11}... | collective-permute-start | bytes 552968 | tf_op jit(solution)/shard_map/ppermute | solution.py:601
  286.7 31.6 %collective-permute-start.13 = (bf16[45,16,128]{2,1,0:T(8,128)(2,1)}, bf16[45,16,128]{2,1,0:T(8,128)(2,1)S(1)}, u32[]{:S(2)}, u32[]{:S(2)}) collective-permute-start(bf16[45,16,128]{2,1,0:T(8,128)(2,1)} %get-tuple-element.102), channel_id=1, source_target_pairs={{0,10},{2,8},{4,14},{6,12},{8,2},{10,0},{12,6},{14,4},{1,11},{3,9}... | collective-permute-start | bytes 552968 | tf_op jit(solution)/shard_map/ppermute | solution.py:601
  291.2 27.1 %collective-permute-start.14 = (bf16[45,16,128]{2,1,0:T(8,128)(2,1)}, bf16[45,16,128]{2,1,0:T(8,128)(2,1)}, u32[]{:S(2)}, u32[]{:S(2)}) collective-permute-start(bf16[45,16,128]{2,1,0:T(8,128)(2,1)} %get-tuple-element.103), channel_id=1, source_target_pairs={{0,12},{2,14},{4,8},{6,10},{8,4},{10,6},{12,0},{14,2},{1,13},{3,15... | collective-permute-start | bytes 552968 | tf_op jit(solution)/shard_map/ppermute | solution.py:601
  302.8 15.5 %collective-permute-start.15 = (bf16[45,16,128]{2,1,0:T(8,128)(2,1)}, bf16[45,16,128]{2,1,0:T(8,128)(2,1)}, u32[]{:S(2)}, u32[]{:S(2)}) collective-permute-start(bf16[45,16,128]{2,1,0:T(8,128)(2,1)} %get-tuple-element.104), channel_id=1, source_target_pairs={{0,14},{2,12},{4,10},{6,8},{8,6},{10,4},{12,2},{14,0},{1,15},{3,13... | collective-permute-start | bytes 552968 | tf_op jit(solution)/shard_map/ppermute | solution.py:601
  (60 other events, 1662.1 us)

commit v5 on v4

--- a/solution.py
+++ b/solution.py
@@ -135,7 +135,7 @@
 
 LANES = 128
 LEVELS = 8
-SHARES = (1, 1, 1)
+SHARES = (1, 1)
 
 
 def xor_order(array, index, axis):
@@ -242,9 +242,9 @@
         else:
             parts.append((LEVELS + v, imag))
         for index, values in parts:
-            full = spare_lanes((index, values), last, latd).astype(BF16)
+            full = spare_lanes((index, values), last, latd)
             for g in range(groups):
-                outs[g][index] = full[g * per : (g + 1) * per]
+                outs[g][index] = full[g * per : (g + 1) * per].astype(BF16)
 
 
 def dft(x, table, lat_rows, wave_lanes, groups):
@@ -290,7 +290,7 @@
     outs = rest[groups + 1 : 2 * groups + 1]
     give = rest[2 * groups + 1]
     data, fresh_data = rest[2 * groups + 2 :]
-    slots = other.shape[2]
+    slots = outs[0].shape[1]
     lats = groups // levs
     nlev = levs * levd
     total = 4 * nlev
@@ -315,8 +315,8 @@
     def unpack(rel, field, dz, at, rows):
         values = []
         for i in range(packed):
-            value = own[rel][at + i, :slots] if field == 0 else other[rel, at + i]
-            values.append(value.astype(F32))
+            value = own[rel][at + i] if field == 0 else other[rel, at + i]
+            values.append(value.astype(F32)[:slots])
         values.append(last_row(values, latd))
         for row, value in zip(rows, values):
             data[dz, pl.ds(row, slots, stride=total), :] = value
@@ -329,7 +329,7 @@
             if field == 0:
                 outs[rel][at + i] = full
             else:
-                give[rel, at + i] = full
+                give[rel, at + i, :slots] = full
 
     @pl.when(t == 0)
     def _():
@@ -381,18 +381,20 @@
 
 
 def legendre_step(info, leg, perm, w1, w2, rates, own, other, levs, levd, latd):
-    groups, packed, count, _ = other.shape
+    groups, packed, rows, _ = other.shape
+    count = own[0].shape[1] // 2
     nmodes = leg.shape[2]
     lanes, nlat = perm.shape
     nlev = levs * levd
     const = lambda t, s: (0, 0)
     step = 2 if count % 2 == 0 else 1
-    piece = pl.BlockSpec((packed, count, LANES), lambda t, s: (0, 0, 0))
-    stack = pl.BlockSpec((groups, packed, count, LANES), lambda t, s: (0, 0, 0, 0))
+    piece = pl.BlockSpec((packed, 2 * count, LANES), lambda t, s: (0, 0, 0))
+    half = pl.BlockSpec((packed, count, LANES), lambda t, s: (0, 0, 0))
+    stack = pl.BlockSpec((groups, packed, rows, LANES), lambda t, s: (0, 0, 0, 0))
     flops = count * 2 * (2 * nlev * 2 * nmodes * lanes * 2 + nmodes * nlat * lanes)
     return pl.pallas_call(
         functools.partial(legendre_kernel, groups, levs, levd, latd, nmodes),
-        out_shape=[jax.ShapeDtypeStruct((packed, 2 * count, LANES), BF16)] * groups
+        out_shape=[jax.ShapeDtypeStruct((packed, count, LANES), BF16)] * groups
         + [jax.ShapeDtypeStruct(other.shape, BF16)],
         grid_spec=pltpu.PrefetchScalarGridSpec(
             num_scalar_prefetch=1,
@@ -406,7 +408,7 @@
             ]
             + [piece] * groups
             + [stack],
-            out_specs=[piece] * groups + [stack],
+            out_specs=[half] * groups + [stack],
             scratch_shapes=[pltpu.VMEM((groups // levs, count * 4 * nlev, LANES), F32)] * 2,
         ),
         cost_estimate=pl.CostEstimate(
@@ -420,40 +422,49 @@
 
 def gather_kernel(groups, *refs):
     ins, out = refs[:groups], refs[-1]
+    half = ins[0].shape[1] // 2
     for r in range(groups):
-        out[r] = ins[r][...]
+        out[r, :, :half] = ins[r][...].astype(F32)[:, half:].astype(BF16)
+
+
+def padded(rows):
+    return -(-rows // 8) * 8
 
 
 def gather_halves(blocks):
     groups = len(blocks)
     packed, count, _ = blocks[0].shape
-    half = count // 2
+    half = padded(count // 2)
+    group = packed_rows()
     return pl.pallas_call(
         functools.partial(gather_kernel, groups),
         out_shape=jax.ShapeDtypeStruct((groups, packed, half, LANES), BF16),
-        grid=(1,),
-        in_specs=[pl.BlockSpec((packed, half, LANES), lambda i: (0, 1, 0))] * groups,
-        out_specs=pl.BlockSpec((groups, packed, half, LANES), lambda i: (0, 0, 0, 0)),
+        grid=(packed // group,),
+        in_specs=[pl.BlockSpec((group, count, LANES), lambda i: (i, 0, 0))] * groups,
+        out_specs=pl.BlockSpec((groups, group, half, LANES), lambda i: (0, i, 0, 0)),
         name="gather_halves",
     )(*blocks)
 
 
 def fill_kernel(groups, got, *refs):
-    outs = refs[-groups:]
+    ins, outs = refs[:groups], refs[groups:]
+    half = ins[0].shape[1]
     for r in range(groups):
-        outs[r][...] = got[r]
+        both = [ins[r][...].astype(F32), got[r].astype(F32)[:, :half]]
+        outs[r][...] = jnp.concatenate(both, axis=1).astype(BF16)
 
 
 def fill_halves(blocks, got):
-    groups, packed, half, _ = got.shape
-    any_spec = pl.BlockSpec(memory_space=pl.ANY)
+    groups, packed, rows, _ = got.shape
+    half = blocks[0].shape[1]
+    group = packed_rows()
     return pl.pallas_call(
         functools.partial(fill_kernel, groups),
-        out_shape=[jax.ShapeDtypeStruct(b.shape, b.dtype) for b in blocks],
-        grid=(1,),
-        in_specs=[pl.BlockSpec(got.shape, lambda i: (0, 0, 0, 0))] + [any_spec] * groups,
-        out_specs=[pl.BlockSpec((packed, half, LANES), lambda i: (0, 1, 0))] * groups,
-        input_output_aliases={r + 1: r for r in range(groups)},
+        out_shape=[jax.ShapeDtypeStruct((packed, 2 * half, LANES), BF16)] * groups,
+        grid=(packed // group,),
+        in_specs=[pl.BlockSpec((groups, group, rows, LANES), lambda i: (0, i, 0, 0))]
+        + [pl.BlockSpec((group, half, LANES), lambda i: (i, 0, 0))] * groups,
+        out_specs=[pl.BlockSpec((group, 2 * half, LANES), lambda i: (i, 0, 0))] * groups,
         name="fill_halves",
     )(got, *blocks)
 
@@ -469,18 +480,13 @@
     for tab, number in zip(tabs, counts):
         half = tab.shape[0] // 2
         group = pieces[depth : depth + number]
-        for i in range(packed):
-            v, c = i % LEVELS, i // LEVELS
-            rows = jnp.concatenate([ref[i] for ref in group], axis=0)
-            at = base + c * half
-            lhs[v * LANES : (v + 1) * LANES, at : at + half] = rows.T
         rows = [
             jnp.concatenate([ref[i].astype(F32) for ref in group], axis=0) for i in range(packed)
         ]
-        v = LEVELS - 1
-        lhs[v * LANES : (v + 1) * LANES, base + half : base + 2 * half] = (
-            last_row(rows, latd).astype(BF16).T
-        )
+        rows.append(last_row(rows, latd))
+        for i, row in enumerate(rows):
+            v, at = i % LEVELS, base + i // LEVELS * half
+            lhs[v * LANES : (v + 1) * LANES, at : at + half] = row.astype(BF16).T
         base += 2 * half
         depth += number
     step = 3 * LANES
@@ -677,7 +683,7 @@
         levd, latd, nlon = grid_state.shape[1:]
         share = LANES - latd
         fits = (
-            legendre.shape[0] % (2 * 8 * sum(SHARES)) == 0
+            legendre.shape[0] % (4 * sum(SHARES)) == 0
             and levd % LEVELS == 0
             and latd % 8 == 0
             and share > 0

time: 335 us -> 323 us (0.964)
  starting transfers between devices: 66.6 us -> 41.4 us
  waiting for transfers between devices: 109 us -> 126 us
    ppermute x42 -> x28, starting transfers between devices: 65.6 us -> 40.9 us  [exchange(): out[r] = lax.ppermute(blocks[r], lat_lev, pairs)]
    ppermute x42 -> x28, waiting for transfers between devices: 109 us -> 126 us  [exchange(): out[r] = lax.ppermute(blocks[r], lat_lev, pairs)]
    pallas_call x3 -> x2, Pallas kernels: 39.2 us -> 32.4 us  [dft(): pl.pallas_call(functools.partial(dft_kernel, groups, latd), out_shape=[ja...]
    pallas_call x3 -> x2, Pallas kernels: 6.23 us -> 7.58 us  [fill_halves(): pl.pallas_call(functools.partial(fill_kernel, groups), out_shape=[jax.Sha...]
    pallas_call x3 -> x2, Pallas kernels: 8.61 us -> 7.3 us  [make_table(): pl.pallas_call(functools.partial(table_kernel, nlon), out_shape=jax.Shape...]
    pallas_call x3 -> x2, Pallas kernels: 6.33 us -> 7.53 us  [gather_halves(): pl.pallas_call(functools.partial(gather_kernel, groups), out_shape=jax.Sh...]
    pallas_call x3 -> x2, Pallas kernels: 50.6 us -> 51.2 us  [legendre_step(): pl.pallas_call(functools.partial(legendre_kernel, groups, levs, levd, lat...]
  transfers between devices with their start and end apart: 48 -> 32, of which waited for: 19 -> 14; matrix products, arithmetic and copies ran while one was open for 2% -> 2% of each run, Pallas kernels for 33% -> 31%
where the time goes in v5:
time: 323 us; the launch traced here: 322 us
  Pallas kernels  139 us (43%)
  waiting for transfers between devices  126 us (39%)
  starting transfers between devices  41.4 us (13%)
  local copies, waits for them, and re-layouts  11.2 us (3%)
  other arithmetic  4.49 us (1%)
    ppermute x28, waiting for transfers between devices, exchange(): out[r] = lax.ppermute(blocks[r], lat_lev, pairs)  126 us
    pallas_call x2, Pallas kernels, legendre_step(): pl.pallas_call(functools.partial(legendre_kernel, groups, levs, levd, lat...  51.2 us
    ppermute x28, starting transfers between devices, exchange(): out[r] = lax.ppermute(blocks[r], lat_lev, pairs)  40.9 us
    pallas_call x2, Pallas kernels, inverse_dft(): pl.pallas_call(functools.partial(inverse_kernel, counts, latd, scale, par...  32.5 us
    pallas_call x2, Pallas kernels, dft(): pl.pallas_call(functools.partial(dft_kernel, groups, latd), out_shape=[ja...  32.4 us
    pallas_call x2, Pallas kernels, fill_halves(): pl.pallas_call(functools.partial(fill_kernel, groups), out_shape=[jax.Sha...  7.58 us
    pallas_call x2, Pallas kernels, gather_halves(): pl.pallas_call(functools.partial(gather_kernel, groups), out_shape=jax.Sh...  7.53 us
    pallas_call x2, Pallas kernels, make_table(): pl.pallas_call(functools.partial(table_kernel, nlon), out_shape=jax.Shape...  7.3 us
  transfers between devices with their start and end apart: 32, of which 14 were waited for; matrix products, arithmetic and copies ran while one was open for 2% of the time, Pallas kernels for 31%

profile of v5, /device:TPU:12, one launch (start us, length us, event | category | flops | bytes accessed | tf_op | source)
XLA Modules:
  0.0 322.3 jit_solution(8744897628526466186)
XLA Ops:
  3.4 3.6 %table.2.t_ref.refs_0_ = bf16[384,1920]{1,0:T(8,128)(2,1)} custom-call(f32[192,128]{1,0:T(8,128)} %broadcast_in_dim.55.wave_ref), custom_call_target="tpu_custom_call" | custom-call | tf_op jit(solution)/shard_map/table/pallas_call | solution.py:198
  7.9 16.2 %dft.2 = (bf16[45,24,128]{2,1,0:T(8,128)(2,1)}, bf16[45,24,128]{2,1,0:T(8,128)(2,1)}, bf16[45,24,128]{2,1,0:T(8,128)(2,1)}, bf16[45,24,128]{2,1,0:T(8,128)(2,1)}...) custom-call(bf16[24,120,1920]{2,1,0:T(8,128)(2,1)} %bitcast.58, ...), custom_call_target="tpu_custom_call" | custom-call | flops 8493465600 | bytes 14745600 | tf_op jit(solution)/shard_map/dft/pallas_call | solution.py:258
  24.0 1.5 collective-permute-start
  26.0 1.5 collective-permute-start.2
  27.6 2.6 collective-permute-start.3
  30.2 1.3 collective-permute-start.4
  32.6 3.7 %table.3.t_ref.refs_0_ = bf16[384,1920]{1,0:T(8,128)(2,1)} custom-call(f32[192,128]{1,0:T(8,128)} %broadcast_in_dim.62.wave_ref), custom_call_target="tpu_custom_call" | custom-call | tf_op jit(solution)/shard_map/table/pallas_call | solution.py:198
  36.3 16.3 %dft.3 = (bf16[45,24,128]{2,1,0:T(8,128)(2,1)}, bf16[45,24,128]{2,1,0:T(8,128)(2,1)}, bf16[45,24,128]{2,1,0:T(8,128)(2,1)}, bf16[45,24,128]{2,1,0:T(8,128)(2,1)}...) custom-call(bf16[24,120,1920]{2,1,0:T(8,128)(2,1)} %bitcast.59, ...), custom_call_target="tpu_custom_call" | custom-call | flops 8493465600 | bytes 14745600 | tf_op jit(solution)/shard_map/dft/pallas_call | solution.py:258
  53.1 1.6 collective-permute-start.5
  55.2 1.5 collective-permute-start.16
  56.7 2.2 collective-permute-start.17
  59.7 13.3 %collective-permute-done.5.refs_6_.rest_6_ = bf16[45,24,128]{2,1,0:T(8,128)(2,1)S(1)} collective-permute-done((bf16[45,24,128]{2,1,0:T(8,128)(2,1)S(1)}, bf16[45,24,128]{2,1,0:T(8,128)(2,1)S(1)}, u32[]{:S(2)}, u32[]{:S(2)}) %collective-permute-start.5) | collective-permute-done | bytes 276512 | tf_op jit(solution)/shard_map/ppermute | solution.py:607
  73.1 13.5 %collective-permute-done.6.refs_7_.rest_7_ = bf16[45,24,128]{2,1,0:T(8,128)(2,1)S(1)} collective-permute-done((bf16[45,24,128]{2,1,0:T(8,128)(2,1)S(1)}, bf16[45,24,128]{2,1,0:T(8,128)(2,1)S(1)}, u32[]{:S(2)}, u32[]{:S(2)}) %collective-permute-start.6) | collective-permute-done | bytes 276512 | tf_op jit(solution)/shard_map/ppermute | solution.py:607
  87.3 3.8 %gather_halves.2 = bf16[8,45,16,128]{3,2,1,0:T(8,128)(2,1)} custom-call(bf16[45,24,128]{2,1,0:T(8,128)(2,1)} %get-tuple-element.55.refs_0_.rest_0_, bf16[45,24,128]{2,1,0:T(8,128)(2,1)} %copy-done.6, bf16[45,24,128]{2,1,0:T(8,128)(2,1)} %copy-done.7, bf16[45,24,128]{2,1,0:T(8,128)(2,1)} %copy-done.8, bf16[45,24,128]{2,1,0:T(8,128)(2,1)} %copy-done.9, ...), custom_call_target="tpu_custom_call" | custom-call | tf_op jit(solution)/shard_map/gather_halves/pallas_call | solution.py:439
  91.2 2.5 collective-permute-start.21
  95.6 20.5 %collective-permute-done.20.refs_5_.rest_5_ = bf16[45,24,128]{2,1,0:T(8,128)(2,1)S(1)} collective-permute-done((bf16[45,24,128]{2,1,0:T(8,128)(2,1)}, bf16[45,24,128]{2,1,0:T(8,128)(2,1)S(1)}, u32[]{:S(2)}, u32[]{:S(2)}) %collective-permute-start.20) | collective-permute-done | bytes 276512 | tf_op jit(solution)/shard_map/ppermute | solution.py:607
  116.1 8.9 %collective-permute-done.21.refs_6_.rest_6_ = bf16[45,24,128]{2,1,0:T(8,128)(2,1)S(1)} collective-permute-done((bf16[45,24,128]{2,1,0:T(8,128)(2,1)}, bf16[45,24,128]{2,1,0:T(8,128)(2,1)S(1)}, u32[]{:S(2)}, u32[]{:S(2)}) %collective-permute-start.21) | collective-permute-done | bytes 276512 | tf_op jit(solution)/shard_map/ppermute | solution.py:607
  125.0 2.8 collective-permute-done.22.refs_7_.rest_7_
  128.6 3.8 %gather_halves.3 = bf16[8,45,16,128]{3,2,1,0:T(8,128)(2,1)} custom-call(bf16[45,24,128]{2,1,0:T(8,128)(2,1)} %get-tuple-element.80.refs_0_.rest_0_, bf16[45,24,128]{2,1,0:T(8,128)(2,1)} %copy-done.11, bf16[45,24,128]{2,1,0:T(8,128)(2,1)} %copy-done.12, bf16[45,24,128]{2,1,0:T(8,128)(2,1)} %copy-done.14, bf16[45,24,128]{2,1,0:T(8,128)(2,1)} %copy-done.16, ...), custom_call_target="tpu_custom_call" | custom-call | tf_op jit(solution)/shard_map/gather_halves/pallas_call | solution.py:439
  133.2 1.0 fusion.perm_ref
  134.2 1.1 copy-done.2
  135.3 25.7 %legendre.2 = (bf16[45,12,128]{2,1,0:T(8,128)(2,1)}, bf16[45,12,128]{2,1,0:T(8,128)(2,1)}, bf16[45,12,128]{2,1,0:T(8,128)(2,1)}, bf16[45,12,128]{2,1,0:T(8,128)(...) custom-call(s32[4,12]{1,0:T(4,128)} %get-tuple-element.118.info, ...), custom_call_target="tpu_custom_call" | custom-call | flops 4076863488 | bytes 9142272 | tf_op jit(solution)/shard_map/legendre/pallas_call | solution.py:395
  161.5 1.1 copy-done.3
  162.6 25.5 %legendre.3 = (bf16[45,12,128]{2,1,0:T(8,128)(2,1)}, bf16[45,12,128]{2,1,0:T(8,128)(2,1)}, bf16[45,12,128]{2,1,0:T(8,128)(2,1)}, bf16[45,12,128]{2,1,0:T(8,128)(...) custom-call(s32[4,12]{1,0:T(4,128)} %get-tuple-element.117.info, ...), custom_call_target="tpu_custom_call" | custom-call | flops 4076863488 | bytes 9142272 | tf_op jit(solution)/shard_map/legendre/pallas_call | solution.py:395
  188.1 1.1 copy-done.4
  189.2 3.8 %fill_halves.2 = (bf16[45,24,128]{2,1,0:T(8,128)(2,1)}, bf16[45,24,128]{2,1,0:T(8,128)(2,1)}, bf16[45,24,128]{2,1,0:T(8,128)(2,1)}, bf16[45,24,128]{2,1,0:T(8,12...) custom-call(bf16[8,45,16,128]{3,2,1,0:T(8,128)(2,1)} %copy-done.4, ...), custom_call_target="tpu_custom_call" | custom-call | tf_op jit(solution)/shard_map/fill_halves/pallas_call | solution.py:461
  193.0 4.4 %collective-permute-start.9 = (bf16[45,24,128]{2,1,0:T(8,128)(2,1)}, bf16[45,24,128]{2,1,0:T(8,128)(2,1)S(1)}, u32[]{:S(2)}, u32[]{:S(2)}) collective-permute-start(bf16[45,24,128]{2,1,0:T(8,128)(2,1)} %get-tuple-element.73), channel_id=1, source_target_pairs={{0,2},{2,0},{4,6},{6,4},{8,10},{10,8},{12,14},{14,12},{1,3},{3,1},... | collective-permute-start | bytes 829448 | tf_op jit(solution)/shard_map/ppermute | solution.py:607
  197.4 1.1 copy-done.5
  198.5 3.8 %fill_halves.3 = (bf16[45,24,128]{2,1,0:T(8,128)(2,1)}, bf16[45,24,128]{2,1,0:T(8,128)(2,1)}, bf16[45,24,128]{2,1,0:T(8,128)(2,1)}, bf16[45,24,128]{2,1,0:T(8,12...) custom-call(bf16[8,45,16,128]{3,2,1,0:T(8,128)(2,1)} %copy-done.5, ...), custom_call_target="tpu_custom_call" | custom-call | tf_op jit(solution)/shard_map/fill_halves/pallas_call | solution.py:461
  202.4 2.0 collective-permute-start.26
  204.4 1.4 collective-permute-start.27
  205.8 1.0 collective-permute-start.28
  207.0 2.4 collective-permute-start.29
  209.4 1.9 collective-permute-done.25.refs_2_
  211.3 8.5 %collective-permute-done.26.refs_3_ = bf16[45,24,128]{2,1,0:T(8,128)(2,1)S(1)} collective-permute-done((bf16[45,24,128]{2,1,0:T(8,128)(2,1)}, bf16[45,24,128]{2,1,0:T(8,128)(2,1)S(1)}, u32[]{:S(2)}, u32[]{:S(2)}) %collective-permute-start.26) | collective-permute-done | bytes 276512 | tf_op jit(solution)/shard_map/ppermute | solution.py:607
  219.7 3.5 %collective-permute-start.31 = (bf16[45,24,128]{2,1,0:T(8,128)(2,1)}, bf16[45,24,128]{2,1,0:T(8,128)(2,1)S(1)}, u32[]{:S(2)}, u32[]{:S(2)}) collective-permute-start(bf16[45,24,128]{2,1,0:T(8,128)(2,1)} %get-tuple-element.104), channel_id=1, source_target_pairs={{0,14},{2,12},{4,10},{6,8},{8,6},{10,4},{12,2},{14,0},{1,15},{3,13... | collective-permute-start | bytes 829448 | tf_op jit(solution)/shard_map/ppermute | solution.py:607
  223.2 1.4 collective-permute-done.27.refs_4_
  224.6 3.3 %collective-permute-start.11 = (bf16[45,24,128]{2,1,0:T(8,128)(2,1)}, bf16[45,24,128]{2,1,0:T(8,128)(2,1)S(1)}, u32[]{:S(2)}, u32[]{:S(2)}) collective-permute-start(bf16[45,24,128]{2,1,0:T(8,128)(2,1)} %get-tuple-element.75), channel_id=1, source_target_pairs={{0,6},{2,4},{4,2},{6,0},{8,14},{10,12},{12,10},{14,8},{1,7},{3,5},... | collective-permute-start | bytes 829448 | tf_op jit(solution)/shard_map/ppermute | solution.py:607
  227.9 1.8 collective-permute-start.12
  229.7 14.1 %collective-permute-done.29.refs_6_ = bf16[45,24,128]{2,1,0:T(8,128)(2,1)S(1)} collective-permute-done((bf16[45,24,128]{2,1,0:T(8,128)(2,1)}, bf16[45,24,128]{2,1,0:T(8,128)(2,1)S(1)}, u32[]{:S(2)}, u32[]{:S(2)}) %collective-permute-start.29) | collective-permute-done | bytes 276512 | tf_op jit(solution)/shard_map/ppermute | solution.py:607
  243.8 4.2 %collective-permute-start.13 = (bf16[45,24,128]{2,1,0:T(8,128)(2,1)}, bf16[45,24,128]{2,1,0:T(8,128)(2,1)S(1)}, u32[]{:S(2)}, u32[]{:S(2)}) collective-permute-start(bf16[45,24,128]{2,1,0:T(8,128)(2,1)} %get-tuple-element.77), channel_id=1, source_target_pairs={{0,10},{2,8},{4,14},{6,12},{8,2},{10,0},{12,6},{14,4},{1,11},{3,9}... | collective-permute-start | bytes 829448 | tf_op jit(solution)/shard_map/ppermute | solution.py:607
  248.0 28.3 %collective-permute-done.30.refs_7_ = bf16[45,24,128]{2,1,0:T(8,128)(2,1)S(1)} collective-permute-done((bf16[45,24,128]{2,1,0:T(8,128)(2,1)}, bf16[45,24,128]{2,1,0:T(8,128)(2,1)S(1)}, u32[]{:S(2)}, u32[]{:S(2)}) %collective-permute-start.30) | collective-permute-done | bytes 276512 | tf_op jit(solution)/shard_map/ppermute | solution.py:607
  276.3 5.4 %collective-permute-done.31.refs_8_ = bf16[45,24,128]{2,1,0:T(8,128)(2,1)S(1)} collective-permute-done((bf16[45,24,128]{2,1,0:T(8,128)(2,1)}, bf16[45,24,128]{2,1,0:T(8,128)(2,1)S(1)}, u32[]{:S(2)}, u32[]{:S(2)}) %collective-permute-start.31) | collective-permute-done | bytes 276512 | tf_op jit(solution)/shard_map/ppermute | solution.py:607
  281.7 0.9 collective-permute-start.15
  282.7 14.4 %inverse_dft.2.refs_9_ = f32[24,120,1920]{2,1,0:T(8,128)} custom-call(bf16[384,1920]{1,0:T(8,128)(2,1)} %table.3.t_ref.refs_0_, bf16[45,24,128]{2,1,0:T(8,128)(2,1)} %get-tuple-element.97.refs_1_, bf16[45,24,128]{2,1,0:T(8,128)(2,1)} %copy-done.20, bf16[45,24,128]{2,1,0:T(8,128)(2,1)} %copy-done.21, bf16[45,24,128]{2,1,0:T(8,128)(2,1)} %copy-done.22, ...), custom_call_target="tpu_custom_call" | custom-call | flops 4246732800 | bytes 14745600 | tf_op jit(solution)/shard_map/inverse_dft/pallas_call | solution.py:526
  297.2 2.9 collective-permute-done.14.refs_7_
  300.1 3.9 %collective-permute-done.15.refs_8_ = bf16[45,24,128]{2,1,0:T(8,128)(2,1)} collective-permute-done((bf16[45,24,128]{2,1,0:T(8,128)(2,1)}, bf16[45,24,128]{2,1,0:T(8,128)(2,1)}, u32[]{:S(2)}, u32[]{:S(2)}) %collective-permute-start.15) | collective-permute-done | bytes 276512 | tf_op jit(solution)/shard_map/ppermute | solution.py:607
  304.0 18.1 %inverse_dft.3 = bf16[24,120,1920]{2,1,0:T(8,128)(2,1)} custom-call(bf16[384,1920]{1,0:T(8,128)(2,1)} %table.2.t_ref.refs_0_, bf16[45,24,128]{2,1,0:T(8,128)(2,1)} %get-tuple-element.72.refs_1_, bf16[45,24,128]{2,1,0:T(8,128)(2,1)} %copy-done.27, bf16[45,24,128]{2,1,0:T(8,128)(2,1)} %copy-done.28, bf16[45,24,128]{2,1,0:T(8,128)(2,1)} %copy-done.29, ...), custom_call_target="tpu_custom_call" | custom-call | flops 4246732800 | bytes 14745600 | tf_op jit(solution)/shard_map/inverse_dft/pallas_call | solution.py:526
  (155 shorter events, 12.6 us)
Async XLA Ops:
  0.0 31.5 %copy-start = (f32[48,48]{1,0:T(8,128)S(1)}, f32[48,48]{1,0:T(8,128)}, u32[]{:S(2)}) copy-start(f32[48,48]{1,0:T(8,128)} %param.24) | copy-start | bytes 27652
  24.0 29.0 %collective-permute-start = (bf16[45,24,128]{2,1,0:T(8,128)(2,1)}, bf16[45,24,128]{2,1,0:T(8,128)(2,1)S(1)}, u32[]{:S(2)}, u32[]{:S(2)}) collective-permute-start(bf16[45,24,128]{2,1,0:T(8,128)(2,1)} %get-tuple-element.56), channel_id=1, source_target_pairs={{0,2},{2,0},{4,6},{6,4},{8,10},{10,8},{12,14},{14,12},{1,3},{3,1},... | collective-permute-start | bytes 829448 | tf_op jit(solution)/shard_map/ppermute | solution.py:607
  25.6 29.2 %collective-permute-start.1 = (bf16[45,24,128]{2,1,0:T(8,128)(2,1)}, bf16[45,24,128]{2,1,0:T(8,128)(2,1)S(1)}, u32[]{:S(2)}, u32[]{:S(2)}) collective-permute-start(bf16[45,24,128]{2,1,0:T(8,128)(2,1)} %get-tuple-element.57), channel_id=1, source_target_pairs={{0,4},{2,6},{4,0},{6,2},{8,12},{10,14},{12,8},{14,10},{1,5},{3,7},... | collective-permute-start | bytes 829448 | tf_op jit(solution)/shard_map/ppermute | solution.py:607
  26.0 29.2 %collective-permute-start.2 = (bf16[45,24,128]{2,1,0:T(8,128)(2,1)}, bf16[45,24,128]{2,1,0:T(8,128)(2,1)S(1)}, u32[]{:S(2)}, u32[]{:S(2)}) collective-permute-start(bf16[45,24,128]{2,1,0:T(8,128)(2,1)} %get-tuple-element.58), channel_id=1, source_target_pairs={{0,6},{2,4},{4,2},{6,0},{8,14},{10,12},{12,10},{14,8},{1,7},{3,5},... | collective-permute-start | bytes 829448 | tf_op jit(solution)/shard_map/ppermute | solution.py:607
  27.6 29.2 %collective-permute-start.3 = (bf16[45,24,128]{2,1,0:T(8,128)(2,1)}, bf16[45,24,128]{2,1,0:T(8,128)(2,1)S(1)}, u32[]{:S(2)}, u32[]{:S(2)}) collective-permute-start(bf16[45,24,128]{2,1,0:T(8,128)(2,1)} %get-tuple-element.59), channel_id=1, source_target_pairs={{0,8},{2,10},{4,12},{6,14},{8,0},{10,2},{12,4},{14,6},{1,9},{3,11}... | collective-permute-start | bytes 829448 | tf_op jit(solution)/shard_map/ppermute | solution.py:607
  30.2 28.8 %collective-permute-start.4 = (bf16[45,24,128]{2,1,0:T(8,128)(2,1)}, bf16[45,24,128]{2,1,0:T(8,128)(2,1)S(1)}, u32[]{:S(2)}, u32[]{:S(2)}) collective-permute-start(bf16[45,24,128]{2,1,0:T(8,128)(2,1)} %get-tuple-element.60), channel_id=1, source_target_pairs={{0,10},{2,8},{4,14},{6,12},{8,2},{10,0},{12,6},{14,4},{1,11},{3,9}... | collective-permute-start | bytes 829448 | tf_op jit(solution)/shard_map/ppermute | solution.py:607
  53.1 33.5 %copy-start.6 = (bf16[45,24,128]{2,1,0:T(8,128)(2,1)}, bf16[45,24,128]{2,1,0:T(8,128)(2,1)S(1)}, u32[]{:S(2)}) copy-start(bf16[45,24,128]{2,1,0:T(8,128)(2,1)S(1)} %collective-permute-done.refs_1_.rest_1_) | copy-start | bytes 829444
  53.1 20.0 %collective-permute-start.5 = (bf16[45,24,128]{2,1,0:T(8,128)(2,1)S(1)}, bf16[45,24,128]{2,1,0:T(8,128)(2,1)S(1)}, u32[]{:S(2)}, u32[]{:S(2)}) collective-permute-start(bf16[45,24,128]{2,1,0:T(8,128)(2,1)S(1)} %copy-done.40), channel_id=1, source_target_pairs={{0,12},{2,14},{4,8},{6,10},{8,4},{10,6},{12,0},{14,2},{1,13},{3,15... | collective-permute-start | bytes 829448 | tf_op jit(solution)/shard_map/ppermute | solution.py:607
  54.7 31.9 %copy-start.7 = (bf16[45,24,128]{2,1,0:T(8,128)(2,1)}, bf16[45,24,128]{2,1,0:T(8,128)(2,1)S(1)}, u32[]{:S(2)}) copy-start(bf16[45,24,128]{2,1,0:T(8,128)(2,1)S(1)} %collective-permute-done.1.refs_2_.rest_2_) | copy-start | bytes 829444
  54.7 31.9 %collective-permute-start.6 = (bf16[45,24,128]{2,1,0:T(8,128)(2,1)S(1)}, bf16[45,24,128]{2,1,0:T(8,128)(2,1)S(1)}, u32[]{:S(2)}, u32[]{:S(2)}) collective-permute-start(bf16[45,24,128]{2,1,0:T(8,128)(2,1)S(1)} %copy-done.39), channel_id=1, source_target_pairs={{0,14},{2,12},{4,10},{6,8},{8,6},{10,4},{12,2},{14,0},{1,15},{3,13... | collective-permute-start | bytes 829448 | tf_op jit(solution)/shard_map/ppermute | solution.py:607
  55.2 31.4 %copy-start.8 = (bf16[45,24,128]{2,1,0:T(8,128)(2,1)}, bf16[45,24,128]{2,1,0:T(8,128)(2,1)S(1)}, u32[]{:S(2)}) copy-start(bf16[45,24,128]{2,1,0:T(8,128)(2,1)S(1)} %collective-permute-done.2.refs_3_.rest_3_) | copy-start | bytes 829444
  55.2 35.9 %collective-permute-start.16 = (bf16[45,24,128]{2,1,0:T(8,128)(2,1)}, bf16[45,24,128]{2,1,0:T(8,128)(2,1)S(1)}, u32[]{:S(2)}, u32[]{:S(2)}) collective-permute-start(bf16[45,24,128]{2,1,0:T(8,128)(2,1)} %get-tuple-element.81), channel_id=1, source_target_pairs={{0,2},{2,0},{4,6},{6,4},{8,10},{10,8},{12,14},{14,12},{1,3},{3,1},... | collective-permute-start | bytes 829448 | tf_op jit(solution)/shard_map/ppermute | solution.py:607
  56.7 29.9 %copy-start.9 = (bf16[45,24,128]{2,1,0:T(8,128)(2,1)}, bf16[45,24,128]{2,1,0:T(8,128)(2,1)S(1)}, u32[]{:S(2)}) copy-start(bf16[45,24,128]{2,1,0:T(8,128)(2,1)S(1)} %collective-permute-done.3.refs_4_.rest_4_) | copy-start | bytes 829444
  56.7 34.5 %collective-permute-start.17 = (bf16[45,24,128]{2,1,0:T(8,128)(2,1)}, bf16[45,24,128]{2,1,0:T(8,128)(2,1)S(1)}, u32[]{:S(2)}, u32[]{:S(2)}) collective-permute-start(bf16[45,24,128]{2,1,0:T(8,128)(2,1)} %get-tuple-element.82), channel_id=1, source_target_pairs={{0,4},{2,6},{4,0},{6,2},{8,12},{10,14},{12,8},{14,10},{1,5},{3,7},... | collective-permute-start | bytes 829448 | tf_op jit(solution)/shard_map/ppermute | solution.py:607
  59.0 34.8 %collective-permute-start.18 = (bf16[45,24,128]{2,1,0:T(8,128)(2,1)}, bf16[45,24,128]{2,1,0:T(8,128)(2,1)S(1)}, u32[]{:S(2)}, u32[]{:S(2)}) collective-permute-start(bf16[45,24,128]{2,1,0:T(8,128)(2,1)} %get-tuple-element.83), channel_id=1, source_target_pairs={{0,6},{2,4},{4,2},{6,0},{8,14},{10,12},{12,10},{14,8},{1,7},{3,5},... | collective-permute-start | bytes 829448 | tf_op jit(solution)/shard_map/ppermute | solution.py:607
  73.1 22.6 %collective-permute-start.19 = (bf16[45,24,128]{2,1,0:T(8,128)(2,1)}, bf16[45,24,128]{2,1,0:T(8,128)(2,1)S(1)}, u32[]{:S(2)}, u32[]{:S(2)}) collective-permute-start(bf16[45,24,128]{2,1,0:T(8,128)(2,1)} %get-tuple-element.84), channel_id=1, source_target_pairs={{0,8},{2,10},{4,12},{6,14},{8,0},{10,2},{12,4},{14,6},{1,9},{3,11}... | collective-permute-start | bytes 829448 | tf_op jit(solution)/shard_map/ppermute | solution.py:607
  91.1 43.1 %collective-permute-start.7 = (bf16[8,45,16,128]{3,2,1,0:T(8,128)(2,1)}, bf16[8,45,16,128]{3,2,1,0:T(8,128)(2,1)S(1)}, u32[]{:S(2)}, u32[]{:S(2)}) collective-permute-start(bf16[8,45,16,128]{3,2,1,0:T(8,128)(2,1)} %gather_halves.2), channel_id=1, source_target_pairs={{0,1},{1,0},{2,3},{3,2},{4,5},{5,4},{6,7},{7,6},{8,9},{9,8},{10,11... | collective-permute-start | bytes 4423688 | tf_op jit(solution)/shard_map/ppermute | solution.py:611
  91.1 36.8 %copy-start.11 = (bf16[45,24,128]{2,1,0:T(8,128)(2,1)}, bf16[45,24,128]{2,1,0:T(8,128)(2,1)S(1)}, u32[]{:S(2)}) copy-start(bf16[45,24,128]{2,1,0:T(8,128)(2,1)S(1)} %collective-permute-done.16.refs_1_.rest_1_) | copy-start | bytes 829444
  91.1 25.0 %collective-permute-start.20 = (bf16[45,24,128]{2,1,0:T(8,128)(2,1)}, bf16[45,24,128]{2,1,0:T(8,128)(2,1)S(1)}, u32[]{:S(2)}, u32[]{:S(2)}) collective-permute-start(bf16[45,24,128]{2,1,0:T(8,128)(2,1)} %get-tuple-element.85), channel_id=1, source_target_pairs={{0,10},{2,8},{4,14},{6,12},{8,2},{10,0},{12,6},{14,4},{1,11},{3,9}... | collective-permute-start | bytes 829448 | tf_op jit(solution)/shard_map/ppermute | solution.py:607
  91.2 36.7 %copy-start.12 = (bf16[45,24,128]{2,1,0:T(8,128)(2,1)}, bf16[45,24,128]{2,1,0:T(8,128)(2,1)S(1)}, u32[]{:S(2)}) copy-start(bf16[45,24,128]{2,1,0:T(8,128)(2,1)S(1)} %collective-permute-done.17.refs_2_.rest_2_) | copy-start | bytes 829444
  91.2 33.8 %collective-permute-start.21 = (bf16[45,24,128]{2,1,0:T(8,128)(2,1)}, bf16[45,24,128]{2,1,0:T(8,128)(2,1)S(1)}, u32[]{:S(2)}, u32[]{:S(2)}) collective-permute-start(bf16[45,24,128]{2,1,0:T(8,128)(2,1)} %get-tuple-element.86), channel_id=1, source_target_pairs={{0,12},{2,14},{4,8},{6,10},{8,4},{10,6},{12,0},{14,2},{1,13},{3,15... | collective-permute-start | bytes 829448 | tf_op jit(solution)/shard_map/ppermute | solution.py:607
  93.8 34.1 %copy-start.14 = (bf16[45,24,128]{2,1,0:T(8,128)(2,1)}, bf16[45,24,128]{2,1,0:T(8,128)(2,1)S(1)}, u32[]{:S(2)}) copy-start(bf16[45,24,128]{2,1,0:T(8,128)(2,1)S(1)} %collective-permute-done.18.refs_3_.rest_3_) | copy-start | bytes 829444
  93.8 34.1 %collective-permute-start.22 = (bf16[45,24,128]{2,1,0:T(8,128)(2,1)}, bf16[45,24,128]{2,1,0:T(8,128)(2,1)S(1)}, u32[]{:S(2)}, u32[]{:S(2)}) collective-permute-start(bf16[45,24,128]{2,1,0:T(8,128)(2,1)} %get-tuple-element.87), channel_id=1, source_target_pairs={{0,14},{2,12},{4,10},{6,8},{8,6},{10,4},{12,2},{14,0},{1,15},{3,13... | collective-permute-start | bytes 829448 | tf_op jit(solution)/shard_map/ppermute | solution.py:607
  95.6 32.3 %copy-start.16 = (bf16[45,24,128]{2,1,0:T(8,128)(2,1)}, bf16[45,24,128]{2,1,0:T(8,128)(2,1)S(1)}, u32[]{:S(2)}) copy-start(bf16[45,24,128]{2,1,0:T(8,128)(2,1)S(1)} %collective-permute-done.19.refs_4_.rest_4_) | copy-start | bytes 829444
  132.4 29.1 %collective-permute-start.23 = (bf16[8,45,16,128]{3,2,1,0:T(8,128)(2,1)}, bf16[8,45,16,128]{3,2,1,0:T(8,128)(2,1)S(1)}, u32[]{:S(2)}, u32[]{:S(2)}) collective-permute-start(bf16[8,45,16,128]{3,2,1,0:T(8,128)(2,1)} %gather_halves.3), channel_id=1, source_target_pairs={{0,1},{1,0},{2,3},{3,2},{4,5},{5,4},{6,7},{7,6},{8,9},{9,8},{10,11... | collective-permute-start | bytes 4423688 | tf_op jit(solution)/shard_map/ppermute | solution.py:611
  161.0 27.1 %collective-permute-start.8 = (bf16[8,45,16,128]{3,2,1,0:T(8,128)(2,1)}, bf16[8,45,16,128]{3,2,1,0:T(8,128)(2,1)S(1)}, u32[]{:S(2)}, u32[]{:S(2)}) collective-permute-start(bf16[8,45,16,128]{3,2,1,0:T(8,128)(2,1)} %get-tuple-element.63), channel_id=1, source_target_pairs={{0,1},{1,0},{2,3},{3,2},{4,5},{5,4},{6,7},{7,6},{8,9},{9,8},{10,11... | collective-permute-start | bytes 4423688 | tf_op jit(solution)/shard_map/ppermute | solution.py:611
  188.1 9.3 %collective-permute-start.24 = (bf16[8,45,16,128]{3,2,1,0:T(8,128)(2,1)}, bf16[8,45,16,128]{3,2,1,0:T(8,128)(2,1)S(1)}, u32[]{:S(2)}, u32[]{:S(2)}) collective-permute-start(bf16[8,45,16,128]{3,2,1,0:T(8,128)(2,1)} %get-tuple-element.88), channel_id=1, source_target_pairs={{0,1},{1,0},{2,3},{3,2},{4,5},{5,4},{6,7},{7,6},{8,9},{9,8},{10,11... | collective-permute-start | bytes 4423688 | tf_op jit(solution)/shard_map/ppermute | solution.py:611
  193.0 12.8 %collective-permute-start.9 = (bf16[45,24,128]{2,1,0:T(8,128)(2,1)}, bf16[45,24,128]{2,1,0:T(8,128)(2,1)S(1)}, u32[]{:S(2)}, u32[]{:S(2)}) collective-permute-start(bf16[45,24,128]{2,1,0:T(8,128)(2,1)} %get-tuple-element.73), channel_id=1, source_target_pairs={{0,2},{2,0},{4,6},{6,4},{8,10},{10,8},{12,14},{14,12},{1,3},{3,1},... | collective-permute-start | bytes 829448 | tf_op jit(solution)/shard_map/ppermute | solution.py:607
  197.3 9.7 %collective-permute-start.10 = (bf16[45,24,128]{2,1,0:T(8,128)(2,1)}, bf16[45,24,128]{2,1,0:T(8,128)(2,1)S(1)}, u32[]{:S(2)}, u32[]{:S(2)}) collective-permute-start(bf16[45,24,128]{2,1,0:T(8,128)(2,1)} %get-tuple-element.74), channel_id=1, source_target_pairs={{0,4},{2,6},{4,0},{6,2},{8,12},{10,14},{12,8},{14,10},{1,5},{3,7},... | collective-permute-start | bytes 829448 | tf_op jit(solution)/shard_map/ppermute | solution.py:607
  202.3 9.0 %collective-permute-start.25 = (bf16[45,24,128]{2,1,0:T(8,128)(2,1)}, bf16[45,24,128]{2,1,0:T(8,128)(2,1)S(1)}, u32[]{:S(2)}, u32[]{:S(2)}) collective-permute-start(bf16[45,24,128]{2,1,0:T(8,128)(2,1)} %get-tuple-element.98), channel_id=1, source_target_pairs={{0,2},{2,0},{4,6},{6,4},{8,10},{10,8},{12,14},{14,12},{1,3},{3,1},... | collective-permute-start | bytes 829448 | tf_op jit(solution)/shard_map/ppermute | solution.py:607
  202.4 17.3 %collective-permute-start.26 = (bf16[45,24,128]{2,1,0:T(8,128)(2,1)}, bf16[45,24,128]{2,1,0:T(8,128)(2,1)S(1)}, u32[]{:S(2)}, u32[]{:S(2)}) collective-permute-start(bf16[45,24,128]{2,1,0:T(8,128)(2,1)} %get-tuple-element.99), channel_id=1, source_target_pairs={{0,4},{2,6},{4,0},{6,2},{8,12},{10,14},{12,8},{14,10},{1,5},{3,7},... | collective-permute-start | bytes 829448 | tf_op jit(solution)/shard_map/ppermute | solution.py:607
  204.4 20.2 %collective-permute-start.27 = (bf16[45,24,128]{2,1,0:T(8,128)(2,1)}, bf16[45,24,128]{2,1,0:T(8,128)(2,1)S(1)}, u32[]{:S(2)}, u32[]{:S(2)}) collective-permute-start(bf16[45,24,128]{2,1,0:T(8,128)(2,1)} %get-tuple-element.100), channel_id=1, source_target_pairs={{0,6},{2,4},{4,2},{6,0},{8,14},{10,12},{12,10},{14,8},{1,7},{3,5},... | collective-permute-start | bytes 829448 | tf_op jit(solution)/shard_map/ppermute | solution.py:607
  205.8 91.3 %copy-start.27 = (bf16[45,24,128]{2,1,0:T(8,128)(2,1)}, bf16[45,24,128]{2,1,0:T(8,128)(2,1)S(1)}, u32[]{:S(2)}) copy-start(bf16[45,24,128]{2,1,0:T(8,128)(2,1)S(1)} %collective-permute-done.9.refs_2_) | copy-start | bytes 829444
  205.8 22.1 %collective-permute-start.28 = (bf16[45,24,128]{2,1,0:T(8,128)(2,1)}, bf16[45,24,128]{2,1,0:T(8,128)(2,1)S(1)}, u32[]{:S(2)}, u32[]{:S(2)}) collective-permute-start(bf16[45,24,128]{2,1,0:T(8,128)(2,1)} %get-tuple-element.101), channel_id=1, source_target_pairs={{0,8},{2,10},{4,12},{6,14},{8,0},{10,2},{12,4},{14,6},{1,9},{3,11}... | collective-permute-start | bytes 829448 | tf_op jit(solution)/shard_map/ppermute | solution.py:607
  207.0 90.1 %copy-start.28 = (bf16[45,24,128]{2,1,0:T(8,128)(2,1)}, bf16[45,24,128]{2,1,0:T(8,128)(2,1)S(1)}, u32[]{:S(2)}) copy-start(bf16[45,24,128]{2,1,0:T(8,128)(2,1)S(1)} %collective-permute-done.10.refs_3_) | copy-start | bytes 829444
  207.0 36.8 %collective-permute-start.29 = (bf16[45,24,128]{2,1,0:T(8,128)(2,1)}, bf16[45,24,128]{2,1,0:T(8,128)(2,1)S(1)}, u32[]{:S(2)}, u32[]{:S(2)}) collective-permute-start(bf16[45,24,128]{2,1,0:T(8,128)(2,1)} %get-tuple-element.102), channel_id=1, source_target_pairs={{0,10},{2,8},{4,14},{6,12},{8,2},{10,0},{12,6},{14,4},{1,11},{3,9}... | collective-permute-start | bytes 829448 | tf_op jit(solution)/shard_map/ppermute | solution.py:607
  211.3 71.4 %copy-start.20 = (bf16[45,24,128]{2,1,0:T(8,128)(2,1)}, bf16[45,24,128]{2,1,0:T(8,128)(2,1)S(1)}, u32[]{:S(2)}) copy-start(bf16[45,24,128]{2,1,0:T(8,128)(2,1)S(1)} %collective-permute-done.25.refs_2_) | copy-start | bytes 829444
  211.3 65.0 %collective-permute-start.30 = (bf16[45,24,128]{2,1,0:T(8,128)(2,1)}, bf16[45,24,128]{2,1,0:T(8,128)(2,1)S(1)}, u32[]{:S(2)}, u32[]{:S(2)}) collective-permute-start(bf16[45,24,128]{2,1,0:T(8,128)(2,1)} %get-tuple-element.103), channel_id=1, source_target_pairs={{0,12},{2,14},{4,8},{6,10},{8,4},{10,6},{12,0},{14,2},{1,13},{3,15... | collective-permute-start | bytes 829448 | tf_op jit(solution)/shard_map/ppermute | solution.py:607
  219.7 62.9 %copy-start.21 = (bf16[45,24,128]{2,1,0:T(8,128)(2,1)}, bf16[45,24,128]{2,1,0:T(8,128)(2,1)S(1)}, u32[]{:S(2)}) copy-start(bf16[45,24,128]{2,1,0:T(8,128)(2,1)S(1)} %collective-permute-done.26.refs_3_) | copy-start | bytes 829444
  219.7 62.0 %collective-permute-start.31 = (bf16[45,24,128]{2,1,0:T(8,128)(2,1)}, bf16[45,24,128]{2,1,0:T(8,128)(2,1)S(1)}, u32[]{:S(2)}, u32[]{:S(2)}) collective-permute-start(bf16[45,24,128]{2,1,0:T(8,128)(2,1)} %get-tuple-element.104), channel_id=1, source_target_pairs={{0,14},{2,12},{4,10},{6,8},{8,6},{10,4},{12,2},{14,0},{1,15},{3,13... | collective-permute-start | bytes 829448 | tf_op jit(solution)/shard_map/ppermute | solution.py:607
  224.6 58.0 %copy-start.22 = (bf16[45,24,128]{2,1,0:T(8,128)(2,1)}, bf16[45,24,128]{2,1,0:T(8,128)(2,1)S(1)}, u32[]{:S(2)}) copy-start(bf16[45,24,128]{2,1,0:T(8,128)(2,1)S(1)} %collective-permute-done.27.refs_4_) | copy-start | bytes 829444
  224.6 72.5 %collective-permute-start.11 = (bf16[45,24,128]{2,1,0:T(8,128)(2,1)}, bf16[45,24,128]{2,1,0:T(8,128)(2,1)S(1)}, u32[]{:S(2)}, u32[]{:S(2)}) collective-permute-start(bf16[45,24,128]{2,1,0:T(8,128)(2,1)} %get-tuple-element.75), channel_id=1, source_target_pairs={{0,6},{2,4},{4,2},{6,0},{8,14},{10,12},{12,10},{14,8},{1,7},{3,5},... | collective-permute-start | bytes 829448 | tf_op jit(solution)/shard_map/ppermute | solution.py:607
  227.9 54.8 %copy-start.23 = (bf16[45,24,128]{2,1,0:T(8,128)(2,1)}, bf16[45,24,128]{2,1,0:T(8,128)(2,1)S(1)}, u32[]{:S(2)}) copy-start(bf16[45,24,128]{2,1,0:T(8,128)(2,1)S(1)} %collective-permute-done.28.refs_5_) | copy-start | bytes 829444
  227.9 69.3 %collective-permute-start.12 = (bf16[45,24,128]{2,1,0:T(8,128)(2,1)}, bf16[45,24,128]{2,1,0:T(8,128)(2,1)S(1)}, u32[]{:S(2)}, u32[]{:S(2)}) collective-permute-start(bf16[45,24,128]{2,1,0:T(8,128)(2,1)} %get-tuple-element.76), channel_id=1, source_target_pairs={{0,8},{2,10},{4,12},{6,14},{8,0},{10,2},{12,4},{14,6},{1,9},{3,11}... | collective-permute-start | bytes 829448 | tf_op jit(solution)/shard_map/ppermute | solution.py:607
  243.8 38.8 %copy-start.24 = (bf16[45,24,128]{2,1,0:T(8,128)(2,1)}, bf16[45,24,128]{2,1,0:T(8,128)(2,1)S(1)}, u32[]{:S(2)}) copy-start(bf16[45,24,128]{2,1,0:T(8,128)(2,1)S(1)} %collective-permute-done.29.refs_6_) | copy-start | bytes 829444
  243.8 53.3 %collective-permute-start.13 = (bf16[45,24,128]{2,1,0:T(8,128)(2,1)}, bf16[45,24,128]{2,1,0:T(8,128)(2,1)S(1)}, u32[]{:S(2)}, u32[]{:S(2)}) collective-permute-start(bf16[45,24,128]{2,1,0:T(8,128)(2,1)} %get-tuple-element.77), channel_id=1, source_target_pairs={{0,10},{2,8},{4,14},{6,12},{8,2},{10,0},{12,6},{14,4},{1,11},{3,9}... | collective-permute-start | bytes 829448 | tf_op jit(solution)/shard_map/ppermute | solution.py:607
  276.3 23.8 %collective-permute-start.14 = (bf16[45,24,128]{2,1,0:T(8,128)(2,1)}, bf16[45,24,128]{2,1,0:T(8,128)(2,1)}, u32[]{:S(2)}, u32[]{:S(2)}) collective-permute-start(bf16[45,24,128]{2,1,0:T(8,128)(2,1)} %get-tuple-element.78), channel_id=1, source_target_pairs={{0,12},{2,14},{4,8},{6,10},{8,4},{10,6},{12,0},{14,2},{1,13},{3,15... | collective-permute-start | bytes 829448 | tf_op jit(solution)/shard_map/ppermute | solution.py:607
  281.7 22.2 %collective-permute-start.15 = (bf16[45,24,128]{2,1,0:T(8,128)(2,1)}, bf16[45,24,128]{2,1,0:T(8,128)(2,1)}, u32[]{:S(2)}, u32[]{:S(2)}) collective-permute-start(bf16[45,24,128]{2,1,0:T(8,128)(2,1)} %get-tuple-element.79), channel_id=1, source_target_pairs={{0,14},{2,12},{4,10},{6,8},{8,6},{10,4},{12,2},{14,0},{1,15},{3,13... | collective-permute-start | bytes 829448 | tf_op jit(solution)/shard_map/ppermute | solution.py:607
  (25 other events, 227.9 us)

commit v6 on v5

--- a/solution.py
+++ b/solution.py
@@ -164,10 +164,10 @@
 def last_row(rows, latd):
     share = LANES - latd
     lane = lax.broadcasted_iota(jnp.int32, rows[0].shape, 1)
-    out = jnp.zeros_like(rows[0])
-    for i, row in enumerate(rows):
+    out = pltpu.roll(rows[0], LANES - latd, 1)
+    for i, row in enumerate(rows[1:], 1):
         turned = pltpu.roll(row, (share * i - latd) % LANES, 1)
-        out = jnp.where((lane >= share * i) & (lane < share * (i + 1)), turned, out)
+        out = jnp.where(lane >= share * i, turned, out)
     return out
 
 
@@ -282,8 +282,38 @@
     return jnp.dot(w3, jnp.concatenate([hi, lo, hi], axis=0), preferred_element_type=F32)
 
 
+def permute_kernel(info, leg_ref, perm_ref, out):
+    for j in range(leg_ref.shape[0]):
+        out[j] = jnp.dot(perm_ref[...], leg_ref[j], preferred_element_type=F32).astype(BF16)
+
+
+def permute_legendre(first_slot, leg, perm, count):
+    _, nlat, nmodes = leg.shape
+    lanes = perm.shape[0]
+    step = 2 if count % 2 == 0 else 1
+    return pl.pallas_call(
+        permute_kernel,
+        out_shape=jax.ShapeDtypeStruct((count, lanes, nmodes), BF16),
+        grid_spec=pltpu.PrefetchScalarGridSpec(
+            num_scalar_prefetch=1,
+            grid=(count // step,),
+            in_specs=[
+                pl.BlockSpec((step, nlat, nmodes), lambda t, s: (s[0] // step + t, 0, 0)),
+                pl.BlockSpec((lanes, nlat), lambda t, s: (0, 0)),
+            ],
+            out_specs=pl.BlockSpec((step, lanes, nmodes), lambda t, s: (t, 0, 0)),
+        ),
+        cost_estimate=pl.CostEstimate(
+            flops=2 * count * lanes * nlat * nmodes,
+            bytes_accessed=2 * count * (lanes + nlat) * nmodes,
+            transcendentals=0,
+        ),
+        name="permute_legendre",
+    )(first_slot, leg, perm)
+
+
 def legendre_kernel(
-    groups, levs, levd, latd, nmodes, info, leg_ref, perm_ref, w1_ref, w2_ref, mr_ref, *rest
+    groups, levs, levd, latd, nmodes, info, leg_ref, w1_ref, w2_ref, mr_ref, *rest
 ):
     own = rest[:groups]
     other = rest[groups]
@@ -339,10 +369,7 @@
     first = info[2, 0] == 0
     keep_own = jnp.where(first, 0.0, 1.0)
     keep_other = jnp.where(first, 1.0, 0.0)
-    legs = [
-        jnp.dot(perm_ref[...], leg_ref[j], preferred_element_type=F32).astype(BF16)
-        for j in range(count)
-    ]
+    legs = [leg_ref[j] for j in range(count)]
     fresh = []
     for j in range(count):
         slot = t * count + j
@@ -380,18 +407,17 @@
         each_group(pack)
 
 
-def legendre_step(info, leg, perm, w1, w2, rates, own, other, levs, levd, latd):
+def legendre_step(info, leg, at, w1, w2, rates, own, other, levs, levd, latd):
     groups, packed, rows, _ = other.shape
     count = own[0].shape[1] // 2
-    nmodes = leg.shape[2]
-    lanes, nlat = perm.shape
+    lanes, nmodes = leg.shape[1:]
     nlev = levs * levd
     const = lambda t, s: (0, 0)
     step = 2 if count % 2 == 0 else 1
     piece = pl.BlockSpec((packed, 2 * count, LANES), lambda t, s: (0, 0, 0))
     half = pl.BlockSpec((packed, count, LANES), lambda t, s: (0, 0, 0))
     stack = pl.BlockSpec((groups, packed, rows, LANES), lambda t, s: (0, 0, 0, 0))
-    flops = count * 2 * (2 * nlev * 2 * nmodes * lanes * 2 + nmodes * nlat * lanes)
+    flops = count * 2 * 2 * nlev * 2 * nmodes * lanes * 2
     return pl.pallas_call(
         functools.partial(legendre_kernel, groups, levs, levd, latd, nmodes),
         out_shape=[jax.ShapeDtypeStruct((packed, count, LANES), BF16)] * groups
@@ -400,24 +426,23 @@
             num_scalar_prefetch=1,
             grid=(count // step,),
             in_specs=[
-                pl.BlockSpec((step, nlat, nmodes), lambda t, s: (s[3, 0] // step + t, 0, 0)),
-                pl.BlockSpec((lanes, nlat), const),
+                pl.BlockSpec((step, lanes, nmodes), lambda t, s: (at // step + t, 0, 0)),
                 pl.BlockSpec(w1.shape, const),
                 pl.BlockSpec(w2.shape, const),
                 pl.BlockSpec(rates.shape, const),
             ]
             + [piece] * groups
-            + [stack],
+            + [pl.BlockSpec(memory_space=pltpu.VMEM)],
             out_specs=[half] * groups + [stack],
             scratch_shapes=[pltpu.VMEM((groups // levs, count * 4 * nlev, LANES), F32)] * 2,
         ),
         cost_estimate=pl.CostEstimate(
             flops=flops,
-            bytes_accessed=count * 2 * (nmodes * nlat + 8 * nlev * lanes),
+            bytes_accessed=count * 2 * (nmodes * lanes + 8 * nlev * lanes),
             transcendentals=0,
         ),
         name="legendre",
-    )(info, leg, perm, w1, w2, rates, *own, other)
+    )(info, leg, w1, w2, rates, *own, other)
 
 
 def gather_kernel(groups, *refs):
@@ -448,21 +473,22 @@
 
 def fill_kernel(groups, got, *refs):
     ins, outs = refs[:groups], refs[groups:]
-    half = ins[0].shape[1]
+    rows, half = ins[0].shape[:2]
+    here = pl.ds(pl.program_id(0) * rows, rows)
     for r in range(groups):
-        both = [ins[r][...].astype(F32), got[r].astype(F32)[:, :half]]
+        both = [ins[r][...].astype(F32), got[r, here].astype(F32)[:, :half]]
         outs[r][...] = jnp.concatenate(both, axis=1).astype(BF16)
 
 
 def fill_halves(blocks, got):
-    groups, packed, rows, _ = got.shape
+    groups, packed, _, _ = got.shape
     half = blocks[0].shape[1]
     group = packed_rows()
     return pl.pallas_call(
         functools.partial(fill_kernel, groups),
         out_shape=[jax.ShapeDtypeStruct((packed, 2 * half, LANES), BF16)] * groups,
         grid=(packed // group,),
-        in_specs=[pl.BlockSpec((groups, group, rows, LANES), lambda i: (0, i, 0, 0))]
+        in_specs=[pl.BlockSpec(memory_space=pltpu.VMEM)]
         + [pl.BlockSpec((group, half, LANES), lambda i: (i, 0, 0))] * groups,
         out_specs=[pl.BlockSpec((group, 2 * half, LANES), lambda i: (i, 0, 0))] * groups,
         name="fill_halves",
@@ -618,7 +644,8 @@
         tables.append(make_table(lanes, nlon))
         blocks = dft(grid_state[0], tables[i], lat_rows, lanes, groups)
         arrived.append(exchange(blocks, far + near))
-    legendre = jnp.swapaxes(legendre, 1, 2)
+    first_slot = jnp.full((1,), f * (slots // 2), jnp.int32)
+    leg = permute_legendre(first_slot, jnp.swapaxes(legendre, 1, 2), perm, slots // 2)
     returned = []
     for i, (at, part) in enumerate(zip(starts, parts)):
         other = gather_halves(arrived[i])
@@ -628,11 +655,10 @@
                 my_waves[at : at + part],
                 counts[at : at + part],
                 jnp.full((part,), f, jnp.int32),
-                jnp.full((part,), f * (slots // 2) + at, jnp.int32),
             ]
         )
         res = legendre_step(
-            info, legendre, perm, w1, w2, rates, arrived[i], other, levs, levd, latd
+            info, leg, at, w1, w2, rates, arrived[i], other, levs, levd, latd
         )
         got = swap(res[groups])
         sent = fill_halves(res[:groups], got)

time: 323 us -> 325 us (level)
  waiting for transfers between devices: 126 us -> 115 us
  Pallas kernels: 139 us -> 147 us
  starting transfers between devices: 41.4 us -> 46.7 us
    pallas_call x0 -> x1, Pallas kernels: none -> 14.5 us  [permute_legendre(): pl.pallas_call(permute_kernel, out_shape=jax.ShapeDtypeStruct((count, lan...]
    ppermute x28, waiting for transfers between devices: 126 us -> 115 us  [exchange(): out[r] = lax.ppermute(blocks[r], lat_lev, pairs)]
    pallas_call x2, Pallas kernels: 51.2 us -> 44.2 us  [legendre_step(): pl.pallas_call(functools.partial(legendre_kernel, groups, levs, levd, lat...]
    ppermute x28, starting transfers between devices: 40.9 us -> 46.2 us  [exchange(): out[r] = lax.ppermute(blocks[r], lat_lev, pairs)]
  transfers between devices with their start and end apart: 32 -> 32, of which waited for: 14 -> 14; matrix products, arithmetic and copies ran while one was open for 2% -> 2% of each run, Pallas kernels for 31% -> 34%
where the time goes in v6:
time: 325 us; the launch traced here: 324 us
  Pallas kernels  147 us (45%)
  waiting for transfers between devices  115 us (35%)
  starting transfers between devices  46.7 us (14%)
  local copies, waits for them, and re-layouts  8.86 us (3%)
  other arithmetic  4.51 us (1%)
    ppermute x28, waiting for transfers between devices, exchange(): out[r] = lax.ppermute(blocks[r], lat_lev, pairs)  115 us
    ppermute x28, starting transfers between devices, exchange(): out[r] = lax.ppermute(blocks[r], lat_lev, pairs)  46.2 us
    pallas_call x2, Pallas kernels, legendre_step(): pl.pallas_call(functools.partial(legendre_kernel, groups, levs, levd, lat...  44.2 us
    pallas_call x2, Pallas kernels, inverse_dft(): pl.pallas_call(functools.partial(inverse_kernel, counts, latd, scale, par...  32.5 us
    pallas_call x2, Pallas kernels, dft(): pl.pallas_call(functools.partial(dft_kernel, groups, latd), out_shape=[ja...  32.4 us
    pallas_call x1, Pallas kernels, permute_legendre(): pl.pallas_call(permute_kernel, out_shape=jax.ShapeDtypeStruct((count, lan...  14.5 us
    pallas_call x2, Pallas kernels, fill_halves(): pl.pallas_call(functools.partial(fill_kernel, groups), out_shape=[jax.Sha...  8.88 us
    pallas_call x2, Pallas kernels, gather_halves(): pl.pallas_call(functools.partial(gather_kernel, groups), out_shape=jax.Sh...  7.57 us
  transfers between devices with their start and end apart: 32, of which 14 were waited for; matrix products, arithmetic and copies ran while one was open for 2% of the time, Pallas kernels for 34%

profile of v6, /device:TPU:12, one launch (start us, length us, event | category | flops | bytes accessed | tf_op | source)
XLA Modules:
  0.0 323.8 jit_solution(327447134322457840)
XLA Ops:
  3.4 3.7 %table.3.t_ref.refs_0_ = bf16[384,1920]{1,0:T(8,128)(2,1)} custom-call(f32[192,128]{1,0:T(8,128)} %broadcast_in_dim.66.wave_ref), custom_call_target="tpu_custom_call" | custom-call | tf_op jit(solution)/shard_map/table/pallas_call | solution.py:198
  8.0 16.2 %dft.3 = (bf16[45,24,128]{2,1,0:T(8,128)(2,1)}, bf16[45,24,128]{2,1,0:T(8,128)(2,1)}, bf16[45,24,128]{2,1,0:T(8,128)(2,1)}, bf16[45,24,128]{2,1,0:T(8,128)(2,1)}...) custom-call(bf16[24,120,1920]{2,1,0:T(8,128)(2,1)} %bitcast.56, ...), custom_call_target="tpu_custom_call" | custom-call | flops 8493465600 | bytes 14745600 | tf_op jit(solution)/shard_map/dft/pallas_call | solution.py:258
  24.2 1.5 collective-permute-start.16
  26.2 1.6 collective-permute-start.18
  27.7 2.6 collective-permute-start.19
  30.3 1.3 collective-permute-start.20
  32.7 3.6 %table.2.t_ref.refs_0_ = bf16[384,1920]{1,0:T(8,128)(2,1)} custom-call(f32[192,128]{1,0:T(8,128)} %broadcast_in_dim.58.wave_ref), custom_call_target="tpu_custom_call" | custom-call | tf_op jit(solution)/shard_map/table/pallas_call | solution.py:198
  36.4 16.2 %dft.2 = (bf16[45,24,128]{2,1,0:T(8,128)(2,1)}, bf16[45,24,128]{2,1,0:T(8,128)(2,1)}, bf16[45,24,128]{2,1,0:T(8,128)(2,1)}, bf16[45,24,128]{2,1,0:T(8,128)(2,1)}...) custom-call(bf16[24,120,1920]{2,1,0:T(8,128)(2,1)} %bitcast.57, ...), custom_call_target="tpu_custom_call" | custom-call | flops 8493465600 | bytes 14745600 | tf_op jit(solution)/shard_map/dft/pallas_call | solution.py:258
  55.0 2.5 collective-permute-start.2
  57.5 1.6 collective-permute-start.21
  59.7 8.1 %collective-permute-done.21.refs_6_.rest_6_ = bf16[45,24,128]{2,1,0:T(8,128)(2,1)S(1)} collective-permute-done((bf16[45,24,128]{2,1,0:T(8,128)(2,1)S(1)}, bf16[45,24,128]{2,1,0:T(8,128)(2,1)S(1)}, u32[]{:S(2)}, u32[]{:S(2)}) %collective-permute-start.21) | collective-permute-done | bytes 276512 | tf_op jit(solution)/shard_map/ppermute | solution.py:633
  67.8 10.7 %collective-permute-start.3 = (bf16[45,24,128]{2,1,0:T(8,128)(2,1)}, bf16[45,24,128]{2,1,0:T(8,128)(2,1)S(1)}, u32[]{:S(2)}, u32[]{:S(2)}) collective-permute-start(bf16[45,24,128]{2,1,0:T(8,128)(2,1)} %get-tuple-element.59), channel_id=1, source_target_pairs={{0,8},{2,10},{4,12},{6,14},{8,0},{10,2},{12,4},{14,6},{1,9},{3,11}... | collective-permute-start | bytes 829448 | tf_op jit(solution)/shard_map/ppermute | solution.py:633
  78.5 19.1 %collective-permute-done.22.refs_7_.rest_7_ = bf16[45,24,128]{2,1,0:T(8,128)(2,1)S(1)} collective-permute-done((bf16[45,24,128]{2,1,0:T(8,128)(2,1)S(1)}, bf16[45,24,128]{2,1,0:T(8,128)(2,1)S(1)}, u32[]{:S(2)}, u32[]{:S(2)}) %collective-permute-start.22) | collective-permute-done | bytes 276512 | tf_op jit(solution)/shard_map/ppermute | solution.py:633
  98.3 3.8 %gather_halves.3 = bf16[8,45,16,128]{3,2,1,0:T(8,128)(2,1)} custom-call(bf16[45,24,128]{2,1,0:T(8,128)(2,1)} %get-tuple-element.80.refs_0_.rest_0_, bf16[45,24,128]{2,1,0:T(8,128)(2,1)} %copy-done.5, bf16[45,24,128]{2,1,0:T(8,128)(2,1)} %copy-done.6, bf16[45,24,128]{2,1,0:T(8,128)(2,1)} %copy-done.7, bf16[45,24,128]{2,1,0:T(8,128)(2,1)} %copy-done.8, ...), custom_call_target="tpu_custom_call" | custom-call | tf_op jit(solution)/shard_map/gather_halves/pallas_call | solution.py:464
  102.1 1.6 collective-permute-start.5
  103.7 2.0 collective-permute-start.6
  107.2 11.2 %collective-permute-done.4.refs_5_.rest_5_ = bf16[45,24,128]{2,1,0:T(8,128)(2,1)} collective-permute-done((bf16[45,24,128]{2,1,0:T(8,128)(2,1)}, bf16[45,24,128]{2,1,0:T(8,128)(2,1)}, u32[]{:S(2)}, u32[]{:S(2)}) %collective-permute-start.4) | collective-permute-done | bytes 276512 | tf_op jit(solution)/shard_map/ppermute | solution.py:633
  118.4 5.9 %collective-permute-done.5.refs_6_.rest_6_ = bf16[45,24,128]{2,1,0:T(8,128)(2,1)S(1)} collective-permute-done((bf16[45,24,128]{2,1,0:T(8,128)(2,1)}, bf16[45,24,128]{2,1,0:T(8,128)(2,1)S(1)}, u32[]{:S(2)}, u32[]{:S(2)}) %collective-permute-start.5) | collective-permute-done | bytes 276512 | tf_op jit(solution)/shard_map/ppermute | solution.py:633
  124.4 4.4 %collective-permute-done.6.refs_7_.rest_7_ = bf16[45,24,128]{2,1,0:T(8,128)(2,1)S(1)} collective-permute-done((bf16[45,24,128]{2,1,0:T(8,128)(2,1)}, bf16[45,24,128]{2,1,0:T(8,128)(2,1)S(1)}, u32[]{:S(2)}, u32[]{:S(2)}) %collective-permute-start.6) | collective-permute-done | bytes 276512 | tf_op jit(solution)/shard_map/ppermute | solution.py:633
  129.5 3.8 %gather_halves.2 = bf16[8,45,16,128]{3,2,1,0:T(8,128)(2,1)} custom-call(bf16[45,24,128]{2,1,0:T(8,128)(2,1)} %get-tuple-element.55.refs_0_.rest_0_, bf16[45,24,128]{2,1,0:T(8,128)(2,1)} %copy-done.10, bf16[45,24,128]{2,1,0:T(8,128)(2,1)} %copy-done.11, bf16[45,24,128]{2,1,0:T(8,128)(2,1)} %copy-done.12, bf16[45,24,128]{2,1,0:T(8,128)(2,1)} %copy-done.13, ...), custom_call_target="tpu_custom_call" | custom-call | tf_op jit(solution)/shard_map/gather_halves/pallas_call | solution.py:464
  134.0 1.0 fusion.perm_ref
  135.0 14.5 %permute_legendre.1.leg_ref = bf16[24,512,384]{2,1,0:T(8,128)(2,1)} custom-call(s32[1]{0:T(128)} %bitcast.4.info, bf16[48,480,384]{2,1,0:T(8,128)(2,1)} %bitcast.40, bf16[512,480]{1,0:T(8,128)(2,1)} %fusion.perm_ref), custom_call_target="tpu_custom_call" | custom-call | flops 4529848320 | bytes 18284544 | tf_op jit(solution)/shard_map/permute_legendre/pallas_call | solution.py:294
  149.5 1.1 copy-done.2
  150.6 22.2 %legendre.3 = (bf16[45,12,128]{2,1,0:T(8,128)(2,1)}, bf16[45,12,128]{2,1,0:T(8,128)(2,1)}, bf16[45,12,128]{2,1,0:T(8,128)(2,1)}, bf16[45,12,128]{2,1,0:T(8,128)(...) custom-call(s32[3,12]{1,0:T(4,128)} %get-tuple-element.117.info, ...), custom_call_target="tpu_custom_call" | custom-call | flops 1811939328 | bytes 9437184 | tf_op jit(solution)/shard_map/legendre/pallas_call | solution.py:421
  173.3 1.1 copy-done.3
  174.4 22.0 %legendre.2 = (bf16[45,12,128]{2,1,0:T(8,128)(2,1)}, bf16[45,12,128]{2,1,0:T(8,128)(2,1)}, bf16[45,12,128]{2,1,0:T(8,128)(2,1)}, bf16[45,12,128]{2,1,0:T(8,128)(...) custom-call(s32[3,12]{1,0:T(4,128)} %get-tuple-element.118.info, ...), custom_call_target="tpu_custom_call" | custom-call | flops 1811939328 | bytes 9437184 | tf_op jit(solution)/shard_map/legendre/pallas_call | solution.py:421
  196.5 4.4 %fill_halves.3 = (bf16[45,24,128]{2,1,0:T(8,128)(2,1)}, bf16[45,24,128]{2,1,0:T(8,128)(2,1)}, bf16[45,24,128]{2,1,0:T(8,128)(2,1)}, bf16[45,24,128]{2,1,0:T(8,12...) custom-call(bf16[8,45,16,128]{3,2,1,0:T(8,128)(2,1)} %collective-per, ...), custom_call_target="tpu_custom_call" | custom-call | tf_op jit(solution)/shard_map/fill_halves/pallas_call | solution.py:487
  200.9 1.6 collective-permute-start.25
  202.5 2.0 collective-permute-start.27
  204.5 1.0 collective-permute-start.28
  205.5 2.8 collective-permute-start.29
  208.3 4.5 %fill_halves.2 = (bf16[45,24,128]{2,1,0:T(8,128)(2,1)}, bf16[45,24,128]{2,1,0:T(8,128)(2,1)}, bf16[45,24,128]{2,1,0:T(8,128)(2,1)}, bf16[45,24,128]{2,1,0:T(8,12...) custom-call(bf16[8,45,16,128]{3,2,1,0:T(8,128)(2,1)} %copy-done.4, ...), custom_call_target="tpu_custom_call" | custom-call | tf_op jit(solution)/shard_map/fill_halves/pallas_call | solution.py:487
  212.8 1.6 collective-permute-start.30
  214.5 6.6 %collective-permute-done.26.refs_3_ = bf16[45,24,128]{2,1,0:T(8,128)(2,1)S(1)} collective-permute-done((bf16[45,24,128]{2,1,0:T(8,128)(2,1)}, bf16[45,24,128]{2,1,0:T(8,128)(2,1)S(1)}, u32[]{:S(2)}, u32[]{:S(2)}) %collective-permute-start.26) | collective-permute-done | bytes 276512 | tf_op jit(solution)/shard_map/ppermute | solution.py:633
  221.0 5.4 %collective-permute-done.27.refs_4_ = bf16[45,24,128]{2,1,0:T(8,128)(2,1)S(1)} collective-permute-done((bf16[45,24,128]{2,1,0:T(8,128)(2,1)}, bf16[45,24,128]{2,1,0:T(8,128)(2,1)S(1)}, u32[]{:S(2)}, u32[]{:S(2)}) %collective-permute-start.27) | collective-permute-done | bytes 276512 | tf_op jit(solution)/shard_map/ppermute | solution.py:633
  226.5 3.8 %collective-permute-start.10 = (bf16[45,24,128]{2,1,0:T(8,128)(2,1)}, bf16[45,24,128]{2,1,0:T(8,128)(2,1)S(1)}, u32[]{:S(2)}, u32[]{:S(2)}) collective-permute-start(bf16[45,24,128]{2,1,0:T(8,128)(2,1)} %get-tuple-element.74), channel_id=1, source_target_pairs={{0,4},{2,6},{4,0},{6,2},{8,12},{10,14},{12,8},{14,10},{1,5},{3,7},... | collective-permute-start | bytes 829448 | tf_op jit(solution)/shard_map/ppermute | solution.py:633
  230.3 12.2 %collective-permute-done.29.refs_6_ = bf16[45,24,128]{2,1,0:T(8,128)(2,1)S(1)} collective-permute-done((bf16[45,24,128]{2,1,0:T(8,128)(2,1)}, bf16[45,24,128]{2,1,0:T(8,128)(2,1)S(1)}, u32[]{:S(2)}, u32[]{:S(2)}) %collective-permute-start.29) | collective-permute-done | bytes 276512 | tf_op jit(solution)/shard_map/ppermute | solution.py:633
  242.5 3.3 %collective-permute-start.11 = (bf16[45,24,128]{2,1,0:T(8,128)(2,1)}, bf16[45,24,128]{2,1,0:T(8,128)(2,1)S(1)}, u32[]{:S(2)}, u32[]{:S(2)}) collective-permute-start(bf16[45,24,128]{2,1,0:T(8,128)(2,1)} %get-tuple-element.75), channel_id=1, source_target_pairs={{0,6},{2,4},{4,2},{6,0},{8,14},{10,12},{12,10},{14,8},{1,7},{3,5},... | collective-permute-start | bytes 829448 | tf_op jit(solution)/shard_map/ppermute | solution.py:633
  245.8 3.6 %collective-permute-done.30.refs_7_ = bf16[45,24,128]{2,1,0:T(8,128)(2,1)S(1)} collective-permute-done((bf16[45,24,128]{2,1,0:T(8,128)(2,1)S(1)}, bf16[45,24,128]{2,1,0:T(8,128)(2,1)S(1)}, u32[]{:S(2)}, u32[]{:S(2)}) %collective-permute-start.30) | collective-permute-done | bytes 276512 | tf_op jit(solution)/shard_map/ppermute | solution.py:633
  249.3 15.3 %collective-permute-done.31.refs_8_ = bf16[45,24,128]{2,1,0:T(8,128)(2,1)S(1)} collective-permute-done((bf16[45,24,128]{2,1,0:T(8,128)(2,1)S(1)}, bf16[45,24,128]{2,1,0:T(8,128)(2,1)S(1)}, u32[]{:S(2)}, u32[]{:S(2)}) %collective-permute-start.31) | collective-permute-done | bytes 276512 | tf_op jit(solution)/shard_map/ppermute | solution.py:633
  264.7 1.0 collective-permute-start.14
  265.6 1.8 collective-permute-start.15
  267.5 14.2 %inverse_dft.2.refs_9_ = f32[24,120,1920]{2,1,0:T(8,128)} custom-call(bf16[384,1920]{1,0:T(8,128)(2,1)} %table.3.t_ref.refs_0_, bf16[45,24,128]{2,1,0:T(8,128)(2,1)} %get-tuple-element.97.refs_1_, bf16[45,24,128]{2,1,0:T(8,128)(2,1)} %copy-done.18, bf16[45,24,128]{2,1,0:T(8,128)(2,1)} %copy-done.19, bf16[45,24,128]{2,1,0:T(8,128)(2,1)} %copy-done.20, ...), custom_call_target="tpu_custom_call" | custom-call | flops 4246732800 | bytes 14745600 | tf_op jit(solution)/shard_map/inverse_dft/pallas_call | solution.py:552
  281.7 5.0 %collective-permute-done.12.refs_5_ = bf16[45,24,128]{2,1,0:T(8,128)(2,1)S(1)} collective-permute-done((bf16[45,24,128]{2,1,0:T(8,128)(2,1)}, bf16[45,24,128]{2,1,0:T(8,128)(2,1)S(1)}, u32[]{:S(2)}, u32[]{:S(2)}) %collective-permute-start.12) | collective-permute-done | bytes 276512 | tf_op jit(solution)/shard_map/ppermute | solution.py:633
  286.7 5.9 %collective-permute-done.13.refs_6_ = bf16[45,24,128]{2,1,0:T(8,128)(2,1)S(1)} collective-permute-done((bf16[45,24,128]{2,1,0:T(8,128)(2,1)}, bf16[45,24,128]{2,1,0:T(8,128)(2,1)S(1)}, u32[]{:S(2)}, u32[]{:S(2)}) %collective-permute-start.13) | collective-permute-done | bytes 276512 | tf_op jit(solution)/shard_map/ppermute | solution.py:633
  292.6 7.5 %collective-permute-done.14.refs_7_ = bf16[45,24,128]{2,1,0:T(8,128)(2,1)} collective-permute-done((bf16[45,24,128]{2,1,0:T(8,128)(2,1)}, bf16[45,24,128]{2,1,0:T(8,128)(2,1)}, u32[]{:S(2)}, u32[]{:S(2)}) %collective-permute-start.14) | collective-permute-done | bytes 276512 | tf_op jit(solution)/shard_map/ppermute | solution.py:633
  300.1 5.1 %collective-permute-done.15.refs_8_ = bf16[45,24,128]{2,1,0:T(8,128)(2,1)} collective-permute-done((bf16[45,24,128]{2,1,0:T(8,128)(2,1)}, bf16[45,24,128]{2,1,0:T(8,128)(2,1)}, u32[]{:S(2)}, u32[]{:S(2)}) %collective-permute-start.15) | collective-permute-done | bytes 276512 | tf_op jit(solution)/shard_map/ppermute | solution.py:633
  305.2 18.3 %inverse_dft.3 = bf16[24,120,1920]{2,1,0:T(8,128)(2,1)} custom-call(bf16[384,1920]{1,0:T(8,128)(2,1)} %table.2.t_ref.refs_0_, bf16[45,24,128]{2,1,0:T(8,128)(2,1)} %get-tuple-element.72.refs_1_, bf16[45,24,128]{2,1,0:T(8,128)(2,1)} %copy-done.25, bf16[45,24,128]{2,1,0:T(8,128)(2,1)} %copy-done.26, bf16[45,24,128]{2,1,0:T(8,128)(2,1)} %copy-done.27, ...), custom_call_target="tpu_custom_call" | custom-call | flops 4246732800 | bytes 14745600 | tf_op jit(solution)/shard_map/inverse_dft/pallas_call | solution.py:552
  (154 shorter events, 13.0 us)
Async XLA Ops:
  0.0 31.7 %copy-start = (f32[48,48]{1,0:T(8,128)S(1)}, f32[48,48]{1,0:T(8,128)}, u32[]{:S(2)}) copy-start(f32[48,48]{1,0:T(8,128)} %param.24) | copy-start | bytes 27652
  8.0 23.7 %copy-start.30 = (f32[48,48]{1,0:T(8,128)S(1)}, f32[48,48]{1,0:T(8,128)}, u32[]{:S(2)}) copy-start(f32[48,48]{1,0:T(8,128)} %param.22) | copy-start | bytes 27652
  24.2 29.7 %collective-permute-start.16 = (bf16[45,24,128]{2,1,0:T(8,128)(2,1)}, bf16[45,24,128]{2,1,0:T(8,128)(2,1)S(1)}, u32[]{:S(2)}, u32[]{:S(2)}) collective-permute-start(bf16[45,24,128]{2,1,0:T(8,128)(2,1)} %get-tuple-element.81), channel_id=1, source_target_pairs={{0,2},{2,0},{4,6},{6,4},{8,10},{10,8},{12,14},{14,12},{1,3},{3,1},... | collective-permute-start | bytes 829448 | tf_op jit(solution)/shard_map/ppermute | solution.py:633
  25.7 28.8 %collective-permute-start.17 = (bf16[45,24,128]{2,1,0:T(8,128)(2,1)}, bf16[45,24,128]{2,1,0:T(8,128)(2,1)S(1)}, u32[]{:S(2)}, u32[]{:S(2)}) collective-permute-start(bf16[45,24,128]{2,1,0:T(8,128)(2,1)} %get-tuple-element.82), channel_id=1, source_target_pairs={{0,4},{2,6},{4,0},{6,2},{8,12},{10,14},{12,8},{14,10},{1,5},{3,7},... | collective-permute-start | bytes 829448 | tf_op jit(solution)/shard_map/ppermute | solution.py:633
  26.2 28.8 %collective-permute-start.18 = (bf16[45,24,128]{2,1,0:T(8,128)(2,1)}, bf16[45,24,128]{2,1,0:T(8,128)(2,1)S(1)}, u32[]{:S(2)}, u32[]{:S(2)}) collective-permute-start(bf16[45,24,128]{2,1,0:T(8,128)(2,1)} %get-tuple-element.83), channel_id=1, source_target_pairs={{0,6},{2,4},{4,2},{6,0},{8,14},{10,12},{12,10},{14,8},{1,7},{3,5},... | collective-permute-start | bytes 829448 | tf_op jit(solution)/shard_map/ppermute | solution.py:633
  27.7 29.7 %collective-permute-start.19 = (bf16[45,24,128]{2,1,0:T(8,128)(2,1)}, bf16[45,24,128]{2,1,0:T(8,128)(2,1)S(1)}, u32[]{:S(2)}, u32[]{:S(2)}) collective-permute-start(bf16[45,24,128]{2,1,0:T(8,128)(2,1)} %get-tuple-element.84), channel_id=1, source_target_pairs={{0,8},{2,10},{4,12},{6,14},{8,0},{10,2},{12,4},{14,6},{1,9},{3,11}... | collective-permute-start | bytes 829448 | tf_op jit(solution)/shard_map/ppermute | solution.py:633
  30.3 28.8 %collective-permute-start.20 = (bf16[45,24,128]{2,1,0:T(8,128)(2,1)}, bf16[45,24,128]{2,1,0:T(8,128)(2,1)S(1)}, u32[]{:S(2)}, u32[]{:S(2)}) collective-permute-start(bf16[45,24,128]{2,1,0:T(8,128)(2,1)} %get-tuple-element.85), channel_id=1, source_target_pairs={{0,10},{2,8},{4,14},{6,12},{8,2},{10,0},{12,6},{14,4},{1,11},{3,9}... | collective-permute-start | bytes 829448 | tf_op jit(solution)/shard_map/ppermute | solution.py:633
  53.9 43.7 %copy-start.5 = (bf16[45,24,128]{2,1,0:T(8,128)(2,1)}, bf16[45,24,128]{2,1,0:T(8,128)(2,1)S(1)}, u32[]{:S(2)}) copy-start(bf16[45,24,128]{2,1,0:T(8,128)(2,1)S(1)} %collective-permute-done.16.refs_1_.rest_1_) | copy-start | bytes 829444
  53.9 48.2 %collective-permute-start = (bf16[45,24,128]{2,1,0:T(8,128)(2,1)}, bf16[45,24,128]{2,1,0:T(8,128)(2,1)S(1)}, u32[]{:S(2)}, u32[]{:S(2)}) collective-permute-start(bf16[45,24,128]{2,1,0:T(8,128)(2,1)} %get-tuple-element.56), channel_id=1, source_target_pairs={{0,2},{2,0},{4,6},{6,4},{8,10},{10,8},{12,14},{14,12},{1,3},{3,1},... | collective-permute-start | bytes 829448 | tf_op jit(solution)/shard_map/ppermute | solution.py:633
  54.5 43.1 %copy-start.6 = (bf16[45,24,128]{2,1,0:T(8,128)(2,1)}, bf16[45,24,128]{2,1,0:T(8,128)(2,1)S(1)}, u32[]{:S(2)}) copy-start(bf16[45,24,128]{2,1,0:T(8,128)(2,1)S(1)} %collective-permute-done.17.refs_2_.rest_2_) | copy-start | bytes 829444
  54.5 49.2 %collective-permute-start.1 = (bf16[45,24,128]{2,1,0:T(8,128)(2,1)}, bf16[45,24,128]{2,1,0:T(8,128)(2,1)S(1)}, u32[]{:S(2)}, u32[]{:S(2)}) collective-permute-start(bf16[45,24,128]{2,1,0:T(8,128)(2,1)} %get-tuple-element.57), channel_id=1, source_target_pairs={{0,4},{2,6},{4,0},{6,2},{8,12},{10,14},{12,8},{14,10},{1,5},{3,7},... | collective-permute-start | bytes 829448 | tf_op jit(solution)/shard_map/ppermute | solution.py:633
  54.9 42.7 %copy-start.7 = (bf16[45,24,128]{2,1,0:T(8,128)(2,1)}, bf16[45,24,128]{2,1,0:T(8,128)(2,1)S(1)}, u32[]{:S(2)}) copy-start(bf16[45,24,128]{2,1,0:T(8,128)(2,1)S(1)} %collective-permute-done.18.refs_3_.rest_3_) | copy-start | bytes 829444
  55.0 50.7 %collective-permute-start.2 = (bf16[45,24,128]{2,1,0:T(8,128)(2,1)}, bf16[45,24,128]{2,1,0:T(8,128)(2,1)S(1)}, u32[]{:S(2)}, u32[]{:S(2)}) collective-permute-start(bf16[45,24,128]{2,1,0:T(8,128)(2,1)} %get-tuple-element.58), channel_id=1, source_target_pairs={{0,6},{2,4},{4,2},{6,0},{8,14},{10,12},{12,10},{14,8},{1,7},{3,5},... | collective-permute-start | bytes 829448 | tf_op jit(solution)/shard_map/ppermute | solution.py:633
  57.5 40.2 %copy-start.8 = (bf16[45,24,128]{2,1,0:T(8,128)(2,1)}, bf16[45,24,128]{2,1,0:T(8,128)(2,1)S(1)}, u32[]{:S(2)}) copy-start(bf16[45,24,128]{2,1,0:T(8,128)(2,1)S(1)} %collective-permute-done.19.refs_4_.rest_4_) | copy-start | bytes 829444
  57.5 10.3 %collective-permute-start.21 = (bf16[45,24,128]{2,1,0:T(8,128)(2,1)S(1)}, bf16[45,24,128]{2,1,0:T(8,128)(2,1)S(1)}, u32[]{:S(2)}, u32[]{:S(2)}) collective-permute-start(bf16[45,24,128]{2,1,0:T(8,128)(2,1)S(1)} %copy-done.38), channel_id=1, source_target_pairs={{0,12},{2,14},{4,8},{6,10},{8,4},{10,6},{12,0},{14,2},{1,13},{3,15... | collective-permute-start | bytes 829448 | tf_op jit(solution)/shard_map/ppermute | solution.py:633
  59.1 38.5 %copy-start.9 = (bf16[45,24,128]{2,1,0:T(8,128)(2,1)}, bf16[45,24,128]{2,1,0:T(8,128)(2,1)S(1)}, u32[]{:S(2)}) copy-start(bf16[45,24,128]{2,1,0:T(8,128)(2,1)S(1)} %collective-permute-done.20.refs_5_.rest_5_) | copy-start | bytes 829444
  59.1 38.5 %collective-permute-start.22 = (bf16[45,24,128]{2,1,0:T(8,128)(2,1)S(1)}, bf16[45,24,128]{2,1,0:T(8,128)(2,1)S(1)}, u32[]{:S(2)}, u32[]{:S(2)}) collective-permute-start(bf16[45,24,128]{2,1,0:T(8,128)(2,1)S(1)} %copy-done.37), channel_id=1, source_target_pairs={{0,14},{2,12},{4,10},{6,8},{8,6},{10,4},{12,2},{14,0},{1,15},{3,13... | collective-permute-start | bytes 829448 | tf_op jit(solution)/shard_map/ppermute | solution.py:633
  67.8 29.9 %copy-start.14 = (bf16[45,24,128]{2,1,0:T(8,128)(2,1)}, bf16[45,24,128]{2,1,0:T(8,128)(2,1)S(1)}, u32[]{:S(2)}) copy-start(bf16[45,24,128]{2,1,0:T(8,128)(2,1)S(1)} %collective-permute-done.21.refs_6_.rest_6_) | copy-start | bytes 829444
  67.8 39.5 %collective-permute-start.3 = (bf16[45,24,128]{2,1,0:T(8,128)(2,1)}, bf16[45,24,128]{2,1,0:T(8,128)(2,1)S(1)}, u32[]{:S(2)}, u32[]{:S(2)}) collective-permute-start(bf16[45,24,128]{2,1,0:T(8,128)(2,1)} %get-tuple-element.59), channel_id=1, source_target_pairs={{0,8},{2,10},{4,12},{6,14},{8,0},{10,2},{12,4},{14,6},{1,9},{3,11}... | collective-permute-start | bytes 829448 | tf_op jit(solution)/shard_map/ppermute | solution.py:633
  97.6 20.8 %collective-permute-start.4 = (bf16[45,24,128]{2,1,0:T(8,128)(2,1)}, bf16[45,24,128]{2,1,0:T(8,128)(2,1)}, u32[]{:S(2)}, u32[]{:S(2)}) collective-permute-start(bf16[45,24,128]{2,1,0:T(8,128)(2,1)} %get-tuple-element.60), channel_id=1, source_target_pairs={{0,10},{2,8},{4,14},{6,12},{8,2},{10,0},{12,6},{14,4},{1,11},{3,9}... | collective-permute-start | bytes 829448 | tf_op jit(solution)/shard_map/ppermute | solution.py:633
  102.1 26.7 %copy-start.10 = (bf16[45,24,128]{2,1,0:T(8,128)(2,1)}, bf16[45,24,128]{2,1,0:T(8,128)(2,1)S(1)}, u32[]{:S(2)}) copy-start(bf16[45,24,128]{2,1,0:T(8,128)(2,1)S(1)} %collective-permute-done.refs_1_.rest_1_) | copy-start | bytes 829444
  102.1 22.3 %collective-permute-start.5 = (bf16[45,24,128]{2,1,0:T(8,128)(2,1)}, bf16[45,24,128]{2,1,0:T(8,128)(2,1)S(1)}, u32[]{:S(2)}, u32[]{:S(2)}) collective-permute-start(bf16[45,24,128]{2,1,0:T(8,128)(2,1)} %get-tuple-element.61), channel_id=1, source_target_pairs={{0,12},{2,14},{4,8},{6,10},{8,4},{10,6},{12,0},{14,2},{1,13},{3,15... | collective-permute-start | bytes 829448 | tf_op jit(solution)/shard_map/ppermute | solution.py:633
  103.7 25.1 %copy-start.11 = (bf16[45,24,128]{2,1,0:T(8,128)(2,1)}, bf16[45,24,128]{2,1,0:T(8,128)(2,1)S(1)}, u32[]{:S(2)}) copy-start(bf16[45,24,128]{2,1,0:T(8,128)(2,1)S(1)} %collective-permute-done.1.refs_2_.rest_2_) | copy-start | bytes 829444
  103.7 25.1 %collective-permute-start.6 = (bf16[45,24,128]{2,1,0:T(8,128)(2,1)}, bf16[45,24,128]{2,1,0:T(8,128)(2,1)S(1)}, u32[]{:S(2)}, u32[]{:S(2)}) collective-permute-start(bf16[45,24,128]{2,1,0:T(8,128)(2,1)} %get-tuple-element.62), channel_id=1, source_target_pairs={{0,14},{2,12},{4,10},{6,8},{8,6},{10,4},{12,2},{14,0},{1,15},{3,13... | collective-permute-start | bytes 829448 | tf_op jit(solution)/shard_map/ppermute | solution.py:633
  105.7 43.8 %collective-permute-start.23 = (bf16[8,45,16,128]{3,2,1,0:T(8,128)(2,1)}, bf16[8,45,16,128]{3,2,1,0:T(8,128)(2,1)S(1)}, u32[]{:S(2)}, u32[]{:S(2)}) collective-permute-start(bf16[8,45,16,128]{3,2,1,0:T(8,128)(2,1)} %gather_halves.3), channel_id=1, source_target_pairs={{0,1},{1,0},{2,3},{3,2},{4,5},{5,4},{6,7},{7,6},{8,9},{9,8},{10,11... | collective-permute-start | bytes 4423688 | tf_op jit(solution)/shard_map/ppermute | solution.py:637
  133.3 40.0 %collective-permute-start.7 = (bf16[8,45,16,128]{3,2,1,0:T(8,128)(2,1)}, bf16[8,45,16,128]{3,2,1,0:T(8,128)(2,1)S(1)}, u32[]{:S(2)}, u32[]{:S(2)}) collective-permute-start(bf16[8,45,16,128]{3,2,1,0:T(8,128)(2,1)} %gather_halves.2), channel_id=1, source_target_pairs={{0,1},{1,0},{2,3},{3,2},{4,5},{5,4},{6,7},{7,6},{8,9},{9,8},{10,11... | collective-permute-start | bytes 4423688 | tf_op jit(solution)/shard_map/ppermute | solution.py:637
  172.8 23.7 %collective-permute-start.24 = (bf16[8,45,16,128]{3,2,1,0:T(8,128)(2,1)}, bf16[8,45,16,128]{3,2,1,0:T(8,128)(2,1)}, u32[]{:S(2)}, u32[]{:S(2)}) collective-permute-start(bf16[8,45,16,128]{3,2,1,0:T(8,128)(2,1)} %get-tuple-element.88), channel_id=1, source_target_pairs={{0,1},{1,0},{2,3},{3,2},{4,5},{5,4},{6,7},{7,6},{8,9},{9,8},{10,11... | collective-permute-start | bytes 4423688 | tf_op jit(solution)/shard_map/ppermute | solution.py:637
  196.5 9.0 %collective-permute-start.8 = (bf16[8,45,16,128]{3,2,1,0:T(8,128)(2,1)}, bf16[8,45,16,128]{3,2,1,0:T(8,128)(2,1)S(1)}, u32[]{:S(2)}, u32[]{:S(2)}) collective-permute-start(bf16[8,45,16,128]{3,2,1,0:T(8,128)(2,1)} %get-tuple-element.63), channel_id=1, source_target_pairs={{0,1},{1,0},{2,3},{3,2},{4,5},{5,4},{6,7},{7,6},{8,9},{9,8},{10,11... | collective-permute-start | bytes 4423688 | tf_op jit(solution)/shard_map/ppermute | solution.py:637
  200.9 11.9 %collective-permute-start.25 = (bf16[45,24,128]{2,1,0:T(8,128)(2,1)}, bf16[45,24,128]{2,1,0:T(8,128)(2,1)S(1)}, u32[]{:S(2)}, u32[]{:S(2)}) collective-permute-start(bf16[45,24,128]{2,1,0:T(8,128)(2,1)} %get-tuple-element.98), channel_id=1, source_target_pairs={{0,2},{2,0},{4,6},{6,4},{8,10},{10,8},{12,14},{14,12},{1,3},{3,1},... | collective-permute-start | bytes 829448 | tf_op jit(solution)/shard_map/ppermute | solution.py:633
  202.5 18.6 %collective-permute-start.26 = (bf16[45,24,128]{2,1,0:T(8,128)(2,1)}, bf16[45,24,128]{2,1,0:T(8,128)(2,1)S(1)}, u32[]{:S(2)}, u32[]{:S(2)}) collective-permute-start(bf16[45,24,128]{2,1,0:T(8,128)(2,1)} %get-tuple-element.99), channel_id=1, source_target_pairs={{0,4},{2,6},{4,0},{6,2},{8,12},{10,14},{12,8},{14,10},{1,5},{3,7},... | collective-permute-start | bytes 829448 | tf_op jit(solution)/shard_map/ppermute | solution.py:633
  202.5 24.0 %collective-permute-start.27 = (bf16[45,24,128]{2,1,0:T(8,128)(2,1)}, bf16[45,24,128]{2,1,0:T(8,128)(2,1)S(1)}, u32[]{:S(2)}, u32[]{:S(2)}) collective-permute-start(bf16[45,24,128]{2,1,0:T(8,128)(2,1)} %get-tuple-element.100), channel_id=1, source_target_pairs={{0,6},{2,4},{4,2},{6,0},{8,14},{10,12},{12,10},{14,8},{1,7},{3,5},... | collective-permute-start | bytes 829448 | tf_op jit(solution)/shard_map/ppermute | solution.py:633
  204.5 22.0 %collective-permute-start.28 = (bf16[45,24,128]{2,1,0:T(8,128)(2,1)}, bf16[45,24,128]{2,1,0:T(8,128)(2,1)S(1)}, u32[]{:S(2)}, u32[]{:S(2)}) collective-permute-start(bf16[45,24,128]{2,1,0:T(8,128)(2,1)} %get-tuple-element.101), channel_id=1, source_target_pairs={{0,8},{2,10},{4,12},{6,14},{8,0},{10,2},{12,4},{14,6},{1,9},{3,11}... | collective-permute-start | bytes 829448 | tf_op jit(solution)/shard_map/ppermute | solution.py:633
  205.5 37.0 %collective-permute-start.29 = (bf16[45,24,128]{2,1,0:T(8,128)(2,1)}, bf16[45,24,128]{2,1,0:T(8,128)(2,1)S(1)}, u32[]{:S(2)}, u32[]{:S(2)}) collective-permute-start(bf16[45,24,128]{2,1,0:T(8,128)(2,1)} %get-tuple-element.102), channel_id=1, source_target_pairs={{0,10},{2,8},{4,14},{6,12},{8,2},{10,0},{12,6},{14,4},{1,11},{3,9}... | collective-permute-start | bytes 829448 | tf_op jit(solution)/shard_map/ppermute | solution.py:633
  212.8 54.6 %copy-start.18 = (bf16[45,24,128]{2,1,0:T(8,128)(2,1)}, bf16[45,24,128]{2,1,0:T(8,128)(2,1)S(1)}, u32[]{:S(2)}) copy-start(bf16[45,24,128]{2,1,0:T(8,128)(2,1)S(1)} %collective-permute-done.25.refs_2_) | copy-start | bytes 829444
  212.8 36.5 %collective-permute-start.30 = (bf16[45,24,128]{2,1,0:T(8,128)(2,1)S(1)}, bf16[45,24,128]{2,1,0:T(8,128)(2,1)S(1)}, u32[]{:S(2)}, u32[]{:S(2)}) collective-permute-start(bf16[45,24,128]{2,1,0:T(8,128)(2,1)S(1)} %copy-done.40), channel_id=1, source_target_pairs={{0,12},{2,14},{4,8},{6,10},{8,4},{10,6},{12,0},{14,2},{1,13},{3,15... | collective-permute-start | bytes 829448 | tf_op jit(solution)/shard_map/ppermute | solution.py:633
  221.0 46.4 %copy-start.19 = (bf16[45,24,128]{2,1,0:T(8,128)(2,1)}, bf16[45,24,128]{2,1,0:T(8,128)(2,1)S(1)}, u32[]{:S(2)}) copy-start(bf16[45,24,128]{2,1,0:T(8,128)(2,1)S(1)} %collective-permute-done.26.refs_3_) | copy-start | bytes 829444
  221.0 43.6 %collective-permute-start.31 = (bf16[45,24,128]{2,1,0:T(8,128)(2,1)S(1)}, bf16[45,24,128]{2,1,0:T(8,128)(2,1)S(1)}, u32[]{:S(2)}, u32[]{:S(2)}) collective-permute-start(bf16[45,24,128]{2,1,0:T(8,128)(2,1)S(1)} %copy-done.39), channel_id=1, source_target_pairs={{0,14},{2,12},{4,10},{6,8},{8,6},{10,4},{12,2},{14,0},{1,15},{3,13... | collective-permute-start | bytes 829448 | tf_op jit(solution)/shard_map/ppermute | solution.py:633
  226.5 41.0 %copy-start.20 = (bf16[45,24,128]{2,1,0:T(8,128)(2,1)}, bf16[45,24,128]{2,1,0:T(8,128)(2,1)S(1)}, u32[]{:S(2)}) copy-start(bf16[45,24,128]{2,1,0:T(8,128)(2,1)S(1)} %collective-permute-done.27.refs_4_) | copy-start | bytes 829444
  226.5 38.2 %collective-permute-start.9 = (bf16[45,24,128]{2,1,0:T(8,128)(2,1)}, bf16[45,24,128]{2,1,0:T(8,128)(2,1)S(1)}, u32[]{:S(2)}, u32[]{:S(2)}) collective-permute-start(bf16[45,24,128]{2,1,0:T(8,128)(2,1)} %get-tuple-element.73), channel_id=1, source_target_pairs={{0,2},{2,0},{4,6},{6,4},{8,10},{10,8},{12,14},{14,12},{1,3},{3,1},... | collective-permute-start | bytes 829448 | tf_op jit(solution)/shard_map/ppermute | solution.py:633
  226.5 41.0 %copy-start.21 = (bf16[45,24,128]{2,1,0:T(8,128)(2,1)}, bf16[45,24,128]{2,1,0:T(8,128)(2,1)S(1)}, u32[]{:S(2)}) copy-start(bf16[45,24,128]{2,1,0:T(8,128)(2,1)S(1)} %collective-permute-done.28.refs_5_) | copy-start | bytes 829444
  226.5 39.1 %collective-permute-start.10 = (bf16[45,24,128]{2,1,0:T(8,128)(2,1)}, bf16[45,24,128]{2,1,0:T(8,128)(2,1)S(1)}, u32[]{:S(2)}, u32[]{:S(2)}) collective-permute-start(bf16[45,24,128]{2,1,0:T(8,128)(2,1)} %get-tuple-element.74), channel_id=1, source_target_pairs={{0,4},{2,6},{4,0},{6,2},{8,12},{10,14},{12,8},{14,10},{1,5},{3,7},... | collective-permute-start | bytes 829448 | tf_op jit(solution)/shard_map/ppermute | solution.py:633
  242.5 25.0 %copy-start.22 = (bf16[45,24,128]{2,1,0:T(8,128)(2,1)}, bf16[45,24,128]{2,1,0:T(8,128)(2,1)S(1)}, u32[]{:S(2)}) copy-start(bf16[45,24,128]{2,1,0:T(8,128)(2,1)S(1)} %collective-permute-done.29.refs_6_) | copy-start | bytes 829444
  242.5 39.2 %collective-permute-start.11 = (bf16[45,24,128]{2,1,0:T(8,128)(2,1)}, bf16[45,24,128]{2,1,0:T(8,128)(2,1)S(1)}, u32[]{:S(2)}, u32[]{:S(2)}) collective-permute-start(bf16[45,24,128]{2,1,0:T(8,128)(2,1)} %get-tuple-element.75), channel_id=1, source_target_pairs={{0,6},{2,4},{4,2},{6,0},{8,14},{10,12},{12,10},{14,8},{1,7},{3,5},... | collective-permute-start | bytes 829448 | tf_op jit(solution)/shard_map/ppermute | solution.py:633
  249.3 37.4 %collective-permute-start.12 = (bf16[45,24,128]{2,1,0:T(8,128)(2,1)}, bf16[45,24,128]{2,1,0:T(8,128)(2,1)S(1)}, u32[]{:S(2)}, u32[]{:S(2)}) collective-permute-start(bf16[45,24,128]{2,1,0:T(8,128)(2,1)} %get-tuple-element.76), channel_id=1, source_target_pairs={{0,8},{2,10},{4,12},{6,14},{8,0},{10,2},{12,4},{14,6},{1,9},{3,11}... | collective-permute-start | bytes 829448 | tf_op jit(solution)/shard_map/ppermute | solution.py:633
  264.6 27.9 %collective-permute-start.13 = (bf16[45,24,128]{2,1,0:T(8,128)(2,1)}, bf16[45,24,128]{2,1,0:T(8,128)(2,1)S(1)}, u32[]{:S(2)}, u32[]{:S(2)}) collective-permute-start(bf16[45,24,128]{2,1,0:T(8,128)(2,1)} %get-tuple-element.77), channel_id=1, source_target_pairs={{0,10},{2,8},{4,14},{6,12},{8,2},{10,0},{12,6},{14,4},{1,11},{3,9}... | collective-permute-start | bytes 829448 | tf_op jit(solution)/shard_map/ppermute | solution.py:633
  264.7 35.4 %collective-permute-start.14 = (bf16[45,24,128]{2,1,0:T(8,128)(2,1)}, bf16[45,24,128]{2,1,0:T(8,128)(2,1)}, u32[]{:S(2)}, u32[]{:S(2)}) collective-permute-start(bf16[45,24,128]{2,1,0:T(8,128)(2,1)} %get-tuple-element.78), channel_id=1, source_target_pairs={{0,12},{2,14},{4,8},{6,10},{8,4},{10,6},{12,0},{14,2},{1,13},{3,15... | collective-permute-start | bytes 829448 | tf_op jit(solution)/shard_map/ppermute | solution.py:633
  265.6 39.6 %collective-permute-start.15 = (bf16[45,24,128]{2,1,0:T(8,128)(2,1)}, bf16[45,24,128]{2,1,0:T(8,128)(2,1)}, u32[]{:S(2)}, u32[]{:S(2)}) collective-permute-start(bf16[45,24,128]{2,1,0:T(8,128)(2,1)} %get-tuple-element.79), channel_id=1, source_target_pairs={{0,14},{2,12},{4,10},{6,8},{8,6},{10,4},{12,2},{14,0},{1,15},{3,13... | collective-permute-start | bytes 829448 | tf_op jit(solution)/shard_map/ppermute | solution.py:633
  281.7 23.5 %copy-start.27 = (bf16[45,24,128]{2,1,0:T(8,128)(2,1)}, bf16[45,24,128]{2,1,0:T(8,128)(2,1)S(1)}, u32[]{:S(2)}) copy-start(bf16[45,24,128]{2,1,0:T(8,128)(2,1)S(1)} %collective-permute-done.11.refs_4_) | copy-start | bytes 829444
  (25 other events, 292.5 us)

commit v7 on v6

--- a/solution.py
+++ b/solution.py
@@ -179,11 +179,18 @@
 
     def sincos(step):
         turns = (lane * step).astype(F32) * wave
-        turns = turns - nlon * jnp.floor(turns * (1.0 / nlon))
-        turns = jnp.where(turns < 0.0, turns + nlon, turns)
-        turns = jnp.where(turns >= nlon, turns - nlon, turns)
-        angle = turns * (2.0 * jnp.pi / nlon)
-        return jnp.cos(angle), jnp.sin(angle)
+        turns = turns - nlon * jnp.floor(turns * (1.0 / nlon) + 0.5)
+        quarter = jnp.floor(turns * (4.0 / nlon) + 0.5)
+        x = (turns - quarter * (nlon / 4.0)) * (2.0 * jnp.pi / nlon)
+        y = x * x
+        s = x * (1.0 + y * (-1 / 6 + y * (1 / 120 + y * (-1 / 5040 + y * (1 / 362880)))))
+        c = 1.0 + y * (-1 / 2 + y * (1 / 24 + y * (-1 / 720 + y * (1 / 40320))))
+        c = c - y * y * y * y * y * (1 / 3628800)
+        odd = jnp.abs(quarter) == 1.0
+        half = jnp.abs(quarter) == 2.0
+        sine = jnp.where(odd, c * quarter, jnp.where(half, -s, s))
+        cosine = jnp.where(odd, -s * quarter, jnp.where(half, -c, c))
+        return cosine, sine
 
     cl, sl = sincos(1)
     ch, sh = sincos(LANES)
@@ -460,7 +467,7 @@
     groups = len(blocks)
     packed, count, _ = blocks[0].shape
     half = padded(count // 2)
-    group = packed_rows()
+    group = packed
     return pl.pallas_call(
         functools.partial(gather_kernel, groups),
         out_shape=jax.ShapeDtypeStruct((groups, packed, half, LANES), BF16),
@@ -483,7 +490,7 @@
 def fill_halves(blocks, got):
     groups, packed, _, _ = got.shape
     half = blocks[0].shape[1]
-    group = packed_rows()
+    group = packed
     return pl.pallas_call(
         functools.partial(fill_kernel, groups),
         out_shape=[jax.ShapeDtypeStruct((packed, 2 * half, LANES), BF16)] * groups,
@@ -666,6 +673,11 @@
     sets = list(zip(tables, returned))
     scale = float(nmodes) ** (-0.5)
     shape = (levd, latd, nlon)
+    table, pieces = sets.pop()
+    table = table.reshape(2, groups, -1, nlon)
+    cut = groups // 2
+    for chosen in (slice(0, cut), slice(cut, groups)):
+        sets.append((table[:, chosen].reshape(-1, nlon), pieces[chosen]))
     total = inverse_dft(sets[:-1], shape, None, scale, F32)
     total = inverse_dft(sets[-1:], shape, total, scale, BF16)
     return total[None]

time: 325 us -> 339 us (1.043)
  waiting for transfers between devices: 115 us -> 130 us
    ppermute x28, waiting for transfers between devices: 115 us -> 130 us  [exchange(): out[r] = lax.ppermute(blocks[r], lat_lev, pairs)]
  transfers between devices with their start and end apart: 32 -> 32, of which waited for: 14 -> 18; matrix products, arithmetic and copies ran while one was open for 2% -> 2% of each run, Pallas kernels for 34% -> 33%
where the time goes in v7:
time: 339 us; the launch traced here: 338 us
  Pallas kernels  144 us (42%)
  waiting for transfers between devices  130 us (38%)
  starting transfers between devices  47.7 us (14%)
  local copies, waits for them, and re-layouts  11.3 us (3%)
  other arithmetic  4.46 us (1%)
    ppermute x28, waiting for transfers between devices, exchange(): out[r] = lax.ppermute(blocks[r], lat_lev, pairs)  130 us
    ppermute x28, starting transfers between devices, exchange(): out[r] = lax.ppermute(blocks[r], lat_lev, pairs)  47.1 us
    pallas_call x2, Pallas kernels, legendre_step(): pl.pallas_call(functools.partial(legendre_kernel, groups, levs, levd, lat...  44.2 us
    pallas_call x2, Pallas kernels, inverse_dft(): pl.pallas_call(functools.partial(inverse_kernel, counts, latd, scale, par...  34 us
    pallas_call x2, Pallas kernels, dft(): pl.pallas_call(functools.partial(dft_kernel, groups, latd), out_shape=[ja...  32.4 us
    pallas_call x1, Pallas kernels, permute_legendre(): pl.pallas_call(permute_kernel, out_shape=jax.ShapeDtypeStruct((count, lan...  14.5 us
    pallas_call x2, Pallas kernels, fill_halves(): pl.pallas_call(functools.partial(fill_kernel, groups), out_shape=[jax.Sha...  6.81 us
  transfers between devices with their start and end apart: 32, of which 18 were waited for; matrix products, arithmetic and copies ran while one was open for 2% of the time, Pallas kernels for 33%

profile of v7, /device:TPU:12, one launch (start us, length us, event | category | flops | bytes accessed | tf_op | source)
XLA Modules:
  0.0 337.9 jit_solution(2726778162712346934)
XLA Ops:
  3.4 3.1 table.2.t_ref
  7.4 16.2 %dft.2 = (bf16[45,24,128]{2,1,0:T(8,128)(2,1)}, bf16[45,24,128]{2,1,0:T(8,128)(2,1)}, bf16[45,24,128]{2,1,0:T(8,128)(2,1)}, bf16[45,24,128]{2,1,0:T(8,128)(2,1)}...) custom-call(bf16[24,120,1920]{2,1,0:T(8,128)(2,1)} %bitcast.62, ...), custom_call_target="tpu_custom_call" | custom-call | flops 8493465600 | bytes 14745600 | tf_op jit(solution)/shard_map/dft/pallas_call | solution.py:265
  23.6 1.5 collective-permute-start
  26.4 3.1 table.3.t_ref.refs_0_
  29.5 16.2 %dft.3 = (bf16[45,24,128]{2,1,0:T(8,128)(2,1)}, bf16[45,24,128]{2,1,0:T(8,128)(2,1)}, bf16[45,24,128]{2,1,0:T(8,128)(2,1)}, bf16[45,24,128]{2,1,0:T(8,128)(2,1)}...) custom-call(bf16[24,120,1920]{2,1,0:T(8,128)(2,1)} %bitcast.63, ...), custom_call_target="tpu_custom_call" | custom-call | flops 8493465600 | bytes 14745600 | tf_op jit(solution)/shard_map/dft/pallas_call | solution.py:265
  46.3 1.6 collective-permute-start.14
  50.0 2.6 collective-permute-start.16
  53.0 1.6 collective-permute-done.13.refs_1_.rest_1_
  54.6 2.7 collective-permute-start.18
  57.3 7.5 %collective-permute-done.14.refs_2_.rest_2_ = bf16[45,24,128]{2,1,0:T(8,128)(2,1)S(1)} collective-permute-done((bf16[45,24,128]{2,1,0:T(8,128)(2,1)}, bf16[45,24,128]{2,1,0:T(8,128)(2,1)S(1)}, u32[]{:S(2)}, u32[]{:S(2)}) %collective-permute-start.14) | collective-permute-done | bytes 276512 | tf_op jit(solution)/shard_map/ppermute | solution.py:640
  64.8 1.4 collective-permute-start.19
  66.4 2.4 collective-permute-done.15.refs_3_.rest_3_
  68.8 3.3 collective-permute-start.2
  72.1 10.0 %collective-permute-done.16.refs_4_.rest_4_ = bf16[45,24,128]{2,1,0:T(8,128)(2,1)S(1)} collective-permute-done((bf16[45,24,128]{2,1,0:T(8,128)(2,1)}, bf16[45,24,128]{2,1,0:T(8,128)(2,1)S(1)}, u32[]{:S(2)}, u32[]{:S(2)}) %collective-permute-start.16) | collective-permute-done | bytes 276512 | tf_op jit(solution)/shard_map/ppermute | solution.py:640
  82.2 3.8 %collective-permute-start.3 = (bf16[45,24,128]{2,1,0:T(8,128)(2,1)}, bf16[45,24,128]{2,1,0:T(8,128)(2,1)S(1)}, u32[]{:S(2)}, u32[]{:S(2)}) collective-permute-start(bf16[45,24,128]{2,1,0:T(8,128)(2,1)} %get-tuple-element.59), channel_id=1, source_target_pairs={{0,8},{2,10},{4,12},{6,14},{8,0},{10,2},{12,4},{14,6},{1,9},{3,11}... | collective-permute-start | bytes 829448 | tf_op jit(solution)/shard_map/ppermute | solution.py:640
  86.0 24.3 %collective-permute-done.17.refs_5_.rest_5_ = bf16[45,24,128]{2,1,0:T(8,128)(2,1)S(1)} collective-permute-done((bf16[45,24,128]{2,1,0:T(8,128)(2,1)}, bf16[45,24,128]{2,1,0:T(8,128)(2,1)S(1)}, u32[]{:S(2)}, u32[]{:S(2)}) %collective-permute-start.17) | collective-permute-done | bytes 276512 | tf_op jit(solution)/shard_map/ppermute | solution.py:640
  110.3 4.3 %collective-permute-start.4 = (bf16[45,24,128]{2,1,0:T(8,128)(2,1)}, bf16[45,24,128]{2,1,0:T(8,128)(2,1)S(1)}, u32[]{:S(2)}, u32[]{:S(2)}) collective-permute-start(bf16[45,24,128]{2,1,0:T(8,128)(2,1)} %get-tuple-element.60), channel_id=1, source_target_pairs={{0,10},{2,8},{4,14},{6,12},{8,2},{10,0},{12,6},{14,4},{1,11},{3,9}... | collective-permute-start | bytes 829448 | tf_op jit(solution)/shard_map/ppermute | solution.py:640
  114.6 2.6 collective-permute-done.18.refs_6_.rest_6_
  117.1 1.6 collective-permute-start.5
  118.7 7.3 %collective-permute-done.19.refs_7_.rest_7_ = bf16[45,24,128]{2,1,0:T(8,128)(2,1)S(1)} collective-permute-done((bf16[45,24,128]{2,1,0:T(8,128)(2,1)}, bf16[45,24,128]{2,1,0:T(8,128)(2,1)S(1)}, u32[]{:S(2)}, u32[]{:S(2)}) %collective-permute-start.19) | collective-permute-done | bytes 276512 | tf_op jit(solution)/shard_map/ppermute | solution.py:640
  126.0 2.5 collective-permute-start.6
  129.2 3.0 gather_halves.3
  133.9 3.2 collective-permute-done.4.refs_5_.rest_5_
  137.1 6.8 %collective-permute-done.5.refs_6_.rest_6_ = bf16[45,24,128]{2,1,0:T(8,128)(2,1)} collective-permute-done((bf16[45,24,128]{2,1,0:T(8,128)(2,1)}, bf16[45,24,128]{2,1,0:T(8,128)(2,1)}, u32[]{:S(2)}, u32[]{:S(2)}) %collective-permute-start.5) | collective-permute-done | bytes 276512 | tf_op jit(solution)/shard_map/ppermute | solution.py:640
  143.9 3.4 %collective-permute-done.6.refs_7_.rest_7_ = bf16[45,24,128]{2,1,0:T(8,128)(2,1)} collective-permute-done((bf16[45,24,128]{2,1,0:T(8,128)(2,1)}, bf16[45,24,128]{2,1,0:T(8,128)(2,1)}, u32[]{:S(2)}, u32[]{:S(2)}) %collective-permute-start.6) | collective-permute-done | bytes 276512 | tf_op jit(solution)/shard_map/ppermute | solution.py:640
  147.3 3.1 gather_halves.2
  152.1 14.5 %permute_legendre.1.leg_ref = bf16[24,512,384]{2,1,0:T(8,128)(2,1)} custom-call(s32[1]{0:T(128)} %bitcast.6.info, bf16[48,480,384]{2,1,0:T(8,128)(2,1)} %bitcast.43, bf16[512,480]{1,0:T(8,128)(2,1)} %fusion.perm_ref), custom_call_target="tpu_custom_call" | custom-call | flops 4529848320 | bytes 18284544 | tf_op jit(solution)/shard_map/permute_legendre/pallas_call | solution.py:301
  167.7 22.2 %legendre.3 = (bf16[45,12,128]{2,1,0:T(8,128)(2,1)}, bf16[45,12,128]{2,1,0:T(8,128)(2,1)}, bf16[45,12,128]{2,1,0:T(8,128)(2,1)}, bf16[45,12,128]{2,1,0:T(8,128)(...) custom-call(s32[3,12]{1,0:T(4,128)} %get-tuple-element.119.info, ...), custom_call_target="tpu_custom_call" | custom-call | flops 1811939328 | bytes 9437184 | tf_op jit(solution)/shard_map/legendre/pallas_call | solution.py:428
  191.6 22.0 %legendre.2 = (bf16[45,12,128]{2,1,0:T(8,128)(2,1)}, bf16[45,12,128]{2,1,0:T(8,128)(2,1)}, bf16[45,12,128]{2,1,0:T(8,128)(2,1)}, bf16[45,12,128]{2,1,0:T(8,128)(...) custom-call(s32[3,12]{1,0:T(4,128)} %get-tuple-element.120.info, ...), custom_call_target="tpu_custom_call" | custom-call | flops 1811939328 | bytes 9437184 | tf_op jit(solution)/shard_map/legendre/pallas_call | solution.py:428
  214.7 3.4 %fill_halves.3 = (bf16[45,24,128]{2,1,0:T(8,128)(2,1)}, bf16[45,24,128]{2,1,0:T(8,128)(2,1)}, bf16[45,24,128]{2,1,0:T(8,128)(2,1)}, bf16[45,24,128]{2,1,0:T(8,12...) custom-call(bf16[8,45,16,128]{3,2,1,0:T(8,128)(2,1)} %copy-done.6, ...), custom_call_target="tpu_custom_call" | custom-call | tf_op jit(solution)/shard_map/fill_halves/pallas_call | solution.py:494
  218.1 1.5 collective-permute-start.22
  219.6 2.0 collective-permute-start.24
  222.7 2.8 collective-permute-start.26
  225.5 3.4 %fill_halves.2 = (bf16[45,24,128]{2,1,0:T(8,128)(2,1)}, bf16[45,24,128]{2,1,0:T(8,128)(2,1)}, bf16[45,24,128]{2,1,0:T(8,128)(2,1)}, bf16[45,24,128]{2,1,0:T(8,12...) custom-call(bf16[8,45,16,128]{3,2,1,0:T(8,128)(2,1)} %copy-done.5, ...), custom_call_target="tpu_custom_call" | custom-call | tf_op jit(solution)/shard_map/fill_halves/pallas_call | solution.py:494
  228.9 1.7 collective-permute-start.27
  230.6 7.6 %collective-permute-done.23.refs_4_ = bf16[45,24,128]{2,1,0:T(8,128)(2,1)S(1)} collective-permute-done((bf16[45,24,128]{2,1,0:T(8,128)(2,1)}, bf16[45,24,128]{2,1,0:T(8,128)(2,1)S(1)}, u32[]{:S(2)}, u32[]{:S(2)}) %collective-permute-start.23) | collective-permute-done | bytes 276512 | tf_op jit(solution)/shard_map/ppermute | solution.py:640
  238.2 5.4 %collective-permute-done.24.refs_5_ = bf16[45,24,128]{2,1,0:T(8,128)(2,1)} collective-permute-done((bf16[45,24,128]{2,1,0:T(8,128)(2,1)}, bf16[45,24,128]{2,1,0:T(8,128)(2,1)}, u32[]{:S(2)}, u32[]{:S(2)}) %collective-permute-start.24) | collective-permute-done | bytes 276512 | tf_op jit(solution)/shard_map/ppermute | solution.py:640
  243.7 3.9 %collective-permute-start.30 = (bf16[45,24,128]{2,1,0:T(8,128)(2,1)}, bf16[45,24,128]{2,1,0:T(8,128)(2,1)S(1)}, u32[]{:S(2)}, u32[]{:S(2)}) collective-permute-start(bf16[45,24,128]{2,1,0:T(8,128)(2,1)} %get-tuple-element.103), channel_id=1, source_target_pairs={{0,4},{2,6},{4,0},{6,2},{8,12},{10,14},{12,8},{14,10},{1,5},{3,7},... | collective-permute-start | bytes 829448 | tf_op jit(solution)/shard_map/ppermute | solution.py:640
  247.6 12.1 %collective-permute-done.26.refs_7_ = bf16[45,24,128]{2,1,0:T(8,128)(2,1)} collective-permute-done((bf16[45,24,128]{2,1,0:T(8,128)(2,1)}, bf16[45,24,128]{2,1,0:T(8,128)(2,1)}, u32[]{:S(2)}, u32[]{:S(2)}) %collective-permute-start.26) | collective-permute-done | bytes 276512 | tf_op jit(solution)/shard_map/ppermute | solution.py:640
  259.7 3.3 collective-permute-start.31
  264.3 2.1 collective-permute-done.27.refs_8_
  266.5 15.3 %collective-permute-done.28.refs_9_ = bf16[45,24,128]{2,1,0:T(8,128)(2,1)S(1)} collective-permute-done((bf16[45,24,128]{2,1,0:T(8,128)(2,1)}, bf16[45,24,128]{2,1,0:T(8,128)(2,1)S(1)}, u32[]{:S(2)}, u32[]{:S(2)}) %collective-permute-start.28) | collective-permute-done | bytes 276512 | tf_op jit(solution)/shard_map/ppermute | solution.py:640
  282.8 1.8 collective-permute-start.12
  285.3 19.1 %inverse_dft.2.refs_5_ = f32[24,120,1920]{2,1,0:T(8,128)} custom-call(bf16[384,1920]{1,0:T(8,128)(2,1)} %table.3.t_ref.refs_0_, bf16[192,1920]{1,0:T(8,128)(2,1)} %bitcast.46, bf16[45,24,128]{2,1,0:T(8,128)(2,1)} %get-tuple-element.93.refs_2_, bf16[45,24,128]{2,1,0:T(8,128)(2,1)} %copy-done.19, bf16[45,24,128]{2,1,0:T(8,128)(2,1)} %copy-done.20, ...), custom_call_target="tpu_custom_call" | custom-call | flops 6370099200 | bytes 16588800 | tf_op jit(solution)/shard_map/inverse_dft/pallas_call | solution.py:559
  304.4 5.4 %collective-permute-done.10.refs_2_ = bf16[45,24,128]{2,1,0:T(8,128)(2,1)S(1)} collective-permute-done((bf16[45,24,128]{2,1,0:T(8,128)(2,1)}, bf16[45,24,128]{2,1,0:T(8,128)(2,1)S(1)}, u32[]{:S(2)}, u32[]{:S(2)}) %collective-permute-start.10) | collective-permute-done | bytes 276512 | tf_op jit(solution)/shard_map/ppermute | solution.py:640
  309.8 7.4 %collective-permute-done.11.refs_3_ = bf16[45,24,128]{2,1,0:T(8,128)(2,1)S(1)} collective-permute-done((bf16[45,24,128]{2,1,0:T(8,128)(2,1)}, bf16[45,24,128]{2,1,0:T(8,128)(2,1)S(1)}, u32[]{:S(2)}, u32[]{:S(2)}) %collective-permute-start.11) | collective-permute-done | bytes 276512 | tf_op jit(solution)/shard_map/ppermute | solution.py:640
  317.1 5.1 %collective-permute-done.12.refs_4_ = bf16[45,24,128]{2,1,0:T(8,128)(2,1)S(1)} collective-permute-done((bf16[45,24,128]{2,1,0:T(8,128)(2,1)}, bf16[45,24,128]{2,1,0:T(8,128)(2,1)S(1)}, u32[]{:S(2)}, u32[]{:S(2)}) %collective-permute-start.12) | collective-permute-done | bytes 276512 | tf_op jit(solution)/shard_map/ppermute | solution.py:640
  323.0 14.9 %inverse_dft.3 = bf16[24,120,1920]{2,1,0:T(8,128)(2,1)} custom-call(bf16[192,1920]{1,0:T(8,128)(2,1)} %bitcast.45, bf16[45,24,128]{2,1,0:T(8,128)(2,1)} %copy-done.26, bf16[45,24,128]{2,1,0:T(8,128)(2,1)} %copy-done.27, bf16[45,24,128]{2,1,0:T(8,128)(2,1)} %copy-done.28, bf16[45,24,128]{2,1,0:T(8,128)(2,1)} %copy-done.29, f32[24,120,1920]{2,1,0:T(8,128)} %inverse_dft.2.refs_5_), custom_call_target="tpu_custom_call" | custom-call | flops 2123366400 | bytes 12902400 | tf_op jit(solution)/shard_map/inverse_dft/pallas_call | solution.py:559
  (147 shorter events, 21.4 us)
Async XLA Ops:
  0.0 49.3 %copy-start = (f32[48,48]{1,0:T(8,128)S(1)}, f32[48,48]{1,0:T(8,128)}, u32[]{:S(2)}) copy-start(f32[48,48]{1,0:T(8,128)} %param.24) | copy-start | bytes 27652
  23.6 26.4 %collective-permute-start = (bf16[45,24,128]{2,1,0:T(8,128)(2,1)}, bf16[45,24,128]{2,1,0:T(8,128)(2,1)S(1)}, u32[]{:S(2)}, u32[]{:S(2)}) collective-permute-start(bf16[45,24,128]{2,1,0:T(8,128)(2,1)} %get-tuple-element.56), channel_id=1, source_target_pairs={{0,2},{2,0},{4,6},{6,4},{8,10},{10,8},{12,14},{14,12},{1,3},{3,1},... | collective-permute-start | bytes 829448 | tf_op jit(solution)/shard_map/ppermute | solution.py:640
  25.1 27.6 %collective-permute-start.1 = (bf16[45,24,128]{2,1,0:T(8,128)(2,1)}, bf16[45,24,128]{2,1,0:T(8,128)(2,1)S(1)}, u32[]{:S(2)}, u32[]{:S(2)}) collective-permute-start(bf16[45,24,128]{2,1,0:T(8,128)(2,1)} %get-tuple-element.57), channel_id=1, source_target_pairs={{0,4},{2,6},{4,0},{6,2},{8,12},{10,14},{12,8},{14,10},{1,5},{3,7},... | collective-permute-start | bytes 829448 | tf_op jit(solution)/shard_map/ppermute | solution.py:640
  29.5 19.8 %copy-start.30 = (f32[48,48]{1,0:T(8,128)S(1)}, f32[48,48]{1,0:T(8,128)}, u32[]{:S(2)}) copy-start(f32[48,48]{1,0:T(8,128)} %param.22) | copy-start | bytes 27652
  29.5 20.1 %copy-start.31 = (f32[48,48]{1,0:T(8,128)S(1)}, f32[48,48]{1,0:T(8,128)}, u32[]{:S(2)}) copy-start(f32[48,48]{1,0:T(8,128)} %param.21) | copy-start | bytes 27652
  29.5 20.1 %copy-start.32 = (f32[48,48]{1,0:T(8,128)S(1)}, f32[48,48]{1,0:T(8,128)}, u32[]{:S(2)}) copy-start(f32[48,48]{1,0:T(8,128)} %param.25) | copy-start | bytes 27652
  29.5 20.3 %copy-start.35 = (s32[384]{0:T(512)S(1)}, s32[384]{0:T(512)}, u32[]{:S(2)}) copy-start(s32[384]{0:T(512)} %param.16) | copy-start | bytes 4612
  45.8 8.8 %collective-permute-start.13 = (bf16[45,24,128]{2,1,0:T(8,128)(2,1)}, bf16[45,24,128]{2,1,0:T(8,128)(2,1)S(1)}, u32[]{:S(2)}, u32[]{:S(2)}) collective-permute-start(bf16[45,24,128]{2,1,0:T(8,128)(2,1)} %get-tuple-element.77), channel_id=1, source_target_pairs={{0,2},{2,0},{4,6},{6,4},{8,10},{10,8},{12,14},{14,12},{1,3},{3,1},... | collective-permute-start | bytes 829448 | tf_op jit(solution)/shard_map/ppermute | solution.py:640
  46.3 18.5 %collective-permute-start.14 = (bf16[45,24,128]{2,1,0:T(8,128)(2,1)}, bf16[45,24,128]{2,1,0:T(8,128)(2,1)S(1)}, u32[]{:S(2)}, u32[]{:S(2)}) collective-permute-start(bf16[45,24,128]{2,1,0:T(8,128)(2,1)} %get-tuple-element.78), channel_id=1, source_target_pairs={{0,4},{2,6},{4,0},{6,2},{8,12},{10,14},{12,8},{14,10},{1,5},{3,7},... | collective-permute-start | bytes 829448 | tf_op jit(solution)/shard_map/ppermute | solution.py:640
  47.9 20.9 %collective-permute-start.15 = (bf16[45,24,128]{2,1,0:T(8,128)(2,1)}, bf16[45,24,128]{2,1,0:T(8,128)(2,1)S(1)}, u32[]{:S(2)}, u32[]{:S(2)}) collective-permute-start(bf16[45,24,128]{2,1,0:T(8,128)(2,1)} %get-tuple-element.79), channel_id=1, source_target_pairs={{0,6},{2,4},{4,2},{6,0},{8,14},{10,12},{12,10},{14,8},{1,7},{3,5},... | collective-permute-start | bytes 829448 | tf_op jit(solution)/shard_map/ppermute | solution.py:640
  50.0 82.3 %copy-start.7 = (bf16[45,24,128]{2,1,0:T(8,128)(2,1)}, bf16[45,24,128]{2,1,0:T(8,128)(2,1)S(1)}, u32[]{:S(2)}) copy-start(bf16[45,24,128]{2,1,0:T(8,128)(2,1)S(1)} %collective-permute-done.refs_1_.rest_1_) | copy-start | bytes 829444
  50.0 32.1 %collective-permute-start.16 = (bf16[45,24,128]{2,1,0:T(8,128)(2,1)}, bf16[45,24,128]{2,1,0:T(8,128)(2,1)S(1)}, u32[]{:S(2)}, u32[]{:S(2)}) collective-permute-start(bf16[45,24,128]{2,1,0:T(8,128)(2,1)} %get-tuple-element.80), channel_id=1, source_target_pairs={{0,8},{2,10},{4,12},{6,14},{8,0},{10,2},{12,4},{14,6},{1,9},{3,11}... | collective-permute-start | bytes 829448 | tf_op jit(solution)/shard_map/ppermute | solution.py:640
  52.7 79.6 %copy-start.8 = (bf16[45,24,128]{2,1,0:T(8,128)(2,1)}, bf16[45,24,128]{2,1,0:T(8,128)(2,1)S(1)}, u32[]{:S(2)}) copy-start(bf16[45,24,128]{2,1,0:T(8,128)(2,1)S(1)} %collective-permute-done.1.refs_2_.rest_2_) | copy-start | bytes 829444
  52.7 57.6 %collective-permute-start.17 = (bf16[45,24,128]{2,1,0:T(8,128)(2,1)}, bf16[45,24,128]{2,1,0:T(8,128)(2,1)S(1)}, u32[]{:S(2)}, u32[]{:S(2)}) collective-permute-start(bf16[45,24,128]{2,1,0:T(8,128)(2,1)} %get-tuple-element.81), channel_id=1, source_target_pairs={{0,10},{2,8},{4,14},{6,12},{8,2},{10,0},{12,6},{14,4},{1,11},{3,9}... | collective-permute-start | bytes 829448 | tf_op jit(solution)/shard_map/ppermute | solution.py:640
  54.6 74.6 %copy-start.9 = (bf16[45,24,128]{2,1,0:T(8,128)(2,1)}, bf16[45,24,128]{2,1,0:T(8,128)(2,1)S(1)}, u32[]{:S(2)}) copy-start(bf16[45,24,128]{2,1,0:T(8,128)(2,1)S(1)} %collective-permute-done.13.refs_1_.rest_1_) | copy-start | bytes 829444
  54.6 62.5 %collective-permute-start.18 = (bf16[45,24,128]{2,1,0:T(8,128)(2,1)}, bf16[45,24,128]{2,1,0:T(8,128)(2,1)S(1)}, u32[]{:S(2)}, u32[]{:S(2)}) collective-permute-start(bf16[45,24,128]{2,1,0:T(8,128)(2,1)} %get-tuple-element.82), channel_id=1, source_target_pairs={{0,12},{2,14},{4,8},{6,10},{8,4},{10,6},{12,0},{14,2},{1,13},{3,15... | collective-permute-start | bytes 829448 | tf_op jit(solution)/shard_map/ppermute | solution.py:640
  64.8 64.4 %copy-start.10 = (bf16[45,24,128]{2,1,0:T(8,128)(2,1)}, bf16[45,24,128]{2,1,0:T(8,128)(2,1)S(1)}, u32[]{:S(2)}) copy-start(bf16[45,24,128]{2,1,0:T(8,128)(2,1)S(1)} %collective-permute-done.14.refs_2_.rest_2_) | copy-start | bytes 829444
  64.8 61.2 %collective-permute-start.19 = (bf16[45,24,128]{2,1,0:T(8,128)(2,1)}, bf16[45,24,128]{2,1,0:T(8,128)(2,1)S(1)}, u32[]{:S(2)}, u32[]{:S(2)}) collective-permute-start(bf16[45,24,128]{2,1,0:T(8,128)(2,1)} %get-tuple-element.83), channel_id=1, source_target_pairs={{0,14},{2,12},{4,10},{6,8},{8,6},{10,4},{12,2},{14,0},{1,15},{3,13... | collective-permute-start | bytes 829448 | tf_op jit(solution)/shard_map/ppermute | solution.py:640
  68.8 60.4 %copy-start.11 = (bf16[45,24,128]{2,1,0:T(8,128)(2,1)}, bf16[45,24,128]{2,1,0:T(8,128)(2,1)S(1)}, u32[]{:S(2)}) copy-start(bf16[45,24,128]{2,1,0:T(8,128)(2,1)S(1)} %collective-permute-done.15.refs_3_.rest_3_) | copy-start | bytes 829444
  68.8 63.5 %collective-permute-start.2 = (bf16[45,24,128]{2,1,0:T(8,128)(2,1)}, bf16[45,24,128]{2,1,0:T(8,128)(2,1)S(1)}, u32[]{:S(2)}, u32[]{:S(2)}) collective-permute-start(bf16[45,24,128]{2,1,0:T(8,128)(2,1)} %get-tuple-element.58), channel_id=1, source_target_pairs={{0,6},{2,4},{4,2},{6,0},{8,14},{10,12},{12,10},{14,8},{1,7},{3,5},... | collective-permute-start | bytes 829448 | tf_op jit(solution)/shard_map/ppermute | solution.py:640
  82.2 47.0 %copy-start.12 = (bf16[45,24,128]{2,1,0:T(8,128)(2,1)}, bf16[45,24,128]{2,1,0:T(8,128)(2,1)S(1)}, u32[]{:S(2)}) copy-start(bf16[45,24,128]{2,1,0:T(8,128)(2,1)S(1)} %collective-permute-done.16.refs_4_.rest_4_) | copy-start | bytes 829444
  82.2 51.7 %collective-permute-start.3 = (bf16[45,24,128]{2,1,0:T(8,128)(2,1)}, bf16[45,24,128]{2,1,0:T(8,128)(2,1)S(1)}, u32[]{:S(2)}, u32[]{:S(2)}) collective-permute-start(bf16[45,24,128]{2,1,0:T(8,128)(2,1)} %get-tuple-element.59), channel_id=1, source_target_pairs={{0,8},{2,10},{4,12},{6,14},{8,0},{10,2},{12,4},{14,6},{1,9},{3,11}... | collective-permute-start | bytes 829448 | tf_op jit(solution)/shard_map/ppermute | solution.py:640
  110.3 18.9 %copy-start.13 = (bf16[45,24,128]{2,1,0:T(8,128)(2,1)}, bf16[45,24,128]{2,1,0:T(8,128)(2,1)S(1)}, u32[]{:S(2)}) copy-start(bf16[45,24,128]{2,1,0:T(8,128)(2,1)S(1)} %collective-permute-done.17.refs_5_.rest_5_) | copy-start | bytes 829444
  110.3 26.8 %collective-permute-start.4 = (bf16[45,24,128]{2,1,0:T(8,128)(2,1)}, bf16[45,24,128]{2,1,0:T(8,128)(2,1)S(1)}, u32[]{:S(2)}, u32[]{:S(2)}) collective-permute-start(bf16[45,24,128]{2,1,0:T(8,128)(2,1)} %get-tuple-element.60), channel_id=1, source_target_pairs={{0,10},{2,8},{4,14},{6,12},{8,2},{10,0},{12,6},{14,4},{1,11},{3,9}... | collective-permute-start | bytes 829448 | tf_op jit(solution)/shard_map/ppermute | solution.py:640
  117.1 26.8 %collective-permute-start.5 = (bf16[45,24,128]{2,1,0:T(8,128)(2,1)}, bf16[45,24,128]{2,1,0:T(8,128)(2,1)}, u32[]{:S(2)}, u32[]{:S(2)}) collective-permute-start(bf16[45,24,128]{2,1,0:T(8,128)(2,1)} %get-tuple-element.61), channel_id=1, source_target_pairs={{0,12},{2,14},{4,8},{6,10},{8,4},{10,6},{12,0},{14,2},{1,13},{3,15... | collective-permute-start | bytes 829448 | tf_op jit(solution)/shard_map/ppermute | solution.py:640
  126.0 21.3 %collective-permute-start.6 = (bf16[45,24,128]{2,1,0:T(8,128)(2,1)}, bf16[45,24,128]{2,1,0:T(8,128)(2,1)}, u32[]{:S(2)}, u32[]{:S(2)}) collective-permute-start(bf16[45,24,128]{2,1,0:T(8,128)(2,1)} %get-tuple-element.62), channel_id=1, source_target_pairs={{0,14},{2,12},{4,10},{6,8},{8,6},{10,4},{12,2},{14,0},{1,15},{3,13... | collective-permute-start | bytes 829448 | tf_op jit(solution)/shard_map/ppermute | solution.py:640
  132.3 34.3 %collective-permute-start.20 = (bf16[8,45,16,128]{3,2,1,0:T(8,128)(2,1)}, bf16[8,45,16,128]{3,2,1,0:T(8,128)(2,1)S(1)}, u32[]{:S(2)}, u32[]{:S(2)}) collective-permute-start(bf16[8,45,16,128]{3,2,1,0:T(8,128)(2,1)} %gather_halves.3), channel_id=1, source_target_pairs={{0,1},{1,0},{2,3},{3,2},{4,5},{5,4},{6,7},{7,6},{8,9},{9,8},{10,11... | collective-permute-start | bytes 4423688 | tf_op jit(solution)/shard_map/ppermute | solution.py:644
  150.4 40.1 %collective-permute-start.7 = (bf16[8,45,16,128]{3,2,1,0:T(8,128)(2,1)}, bf16[8,45,16,128]{3,2,1,0:T(8,128)(2,1)S(1)}, u32[]{:S(2)}, u32[]{:S(2)}) collective-permute-start(bf16[8,45,16,128]{3,2,1,0:T(8,128)(2,1)} %gather_halves.2), channel_id=1, source_target_pairs={{0,1},{1,0},{2,3},{3,2},{4,5},{5,4},{6,7},{7,6},{8,9},{9,8},{10,11... | collective-permute-start | bytes 4423688 | tf_op jit(solution)/shard_map/ppermute | solution.py:644
  189.9 23.7 %collective-permute-start.21 = (bf16[8,45,16,128]{3,2,1,0:T(8,128)(2,1)}, bf16[8,45,16,128]{3,2,1,0:T(8,128)(2,1)S(1)}, u32[]{:S(2)}, u32[]{:S(2)}) collective-permute-start(bf16[8,45,16,128]{3,2,1,0:T(8,128)(2,1)} %get-tuple-element.84), channel_id=1, source_target_pairs={{0,1},{1,0},{2,3},{3,2},{4,5},{5,4},{6,7},{7,6},{8,9},{9,8},{10,11... | collective-permute-start | bytes 4423688 | tf_op jit(solution)/shard_map/ppermute | solution.py:644
  213.6 9.1 %collective-permute-start.8 = (bf16[8,45,16,128]{3,2,1,0:T(8,128)(2,1)}, bf16[8,45,16,128]{3,2,1,0:T(8,128)(2,1)S(1)}, u32[]{:S(2)}, u32[]{:S(2)}) collective-permute-start(bf16[8,45,16,128]{3,2,1,0:T(8,128)(2,1)} %get-tuple-element.63), channel_id=1, source_target_pairs={{0,1},{1,0},{2,3},{3,2},{4,5},{5,4},{6,7},{7,6},{8,9},{9,8},{10,11... | collective-permute-start | bytes 4423688 | tf_op jit(solution)/shard_map/ppermute | solution.py:644
  218.1 10.8 %collective-permute-start.22 = (bf16[45,24,128]{2,1,0:T(8,128)(2,1)}, bf16[45,24,128]{2,1,0:T(8,128)(2,1)S(1)}, u32[]{:S(2)}, u32[]{:S(2)}) collective-permute-start(bf16[45,24,128]{2,1,0:T(8,128)(2,1)} %get-tuple-element.94), channel_id=1, source_target_pairs={{0,2},{2,0},{4,6},{6,4},{8,10},{10,8},{12,14},{14,12},{1,3},{3,1},... | collective-permute-start | bytes 829448 | tf_op jit(solution)/shard_map/ppermute | solution.py:640
  219.6 18.6 %collective-permute-start.23 = (bf16[45,24,128]{2,1,0:T(8,128)(2,1)}, bf16[45,24,128]{2,1,0:T(8,128)(2,1)S(1)}, u32[]{:S(2)}, u32[]{:S(2)}) collective-permute-start(bf16[45,24,128]{2,1,0:T(8,128)(2,1)} %get-tuple-element.95), channel_id=1, source_target_pairs={{0,4},{2,6},{4,0},{6,2},{8,12},{10,14},{12,8},{14,10},{1,5},{3,7},... | collective-permute-start | bytes 829448 | tf_op jit(solution)/shard_map/ppermute | solution.py:640
  219.6 24.0 %collective-permute-start.24 = (bf16[45,24,128]{2,1,0:T(8,128)(2,1)}, bf16[45,24,128]{2,1,0:T(8,128)(2,1)}, u32[]{:S(2)}, u32[]{:S(2)}) collective-permute-start(bf16[45,24,128]{2,1,0:T(8,128)(2,1)} %get-tuple-element.96), channel_id=1, source_target_pairs={{0,6},{2,4},{4,2},{6,0},{8,14},{10,12},{12,10},{14,8},{1,7},{3,5},... | collective-permute-start | bytes 829448 | tf_op jit(solution)/shard_map/ppermute | solution.py:640
  221.6 22.0 %collective-permute-start.25 = (bf16[45,24,128]{2,1,0:T(8,128)(2,1)}, bf16[45,24,128]{2,1,0:T(8,128)(2,1)}, u32[]{:S(2)}, u32[]{:S(2)}) collective-permute-start(bf16[45,24,128]{2,1,0:T(8,128)(2,1)} %get-tuple-element.97), channel_id=1, source_target_pairs={{0,8},{2,10},{4,12},{6,14},{8,0},{10,2},{12,4},{14,6},{1,9},{3,11}... | collective-permute-start | bytes 829448 | tf_op jit(solution)/shard_map/ppermute | solution.py:640
  222.7 37.0 %collective-permute-start.26 = (bf16[45,24,128]{2,1,0:T(8,128)(2,1)}, bf16[45,24,128]{2,1,0:T(8,128)(2,1)}, u32[]{:S(2)}, u32[]{:S(2)}) collective-permute-start(bf16[45,24,128]{2,1,0:T(8,128)(2,1)} %get-tuple-element.98), channel_id=1, source_target_pairs={{0,10},{2,8},{4,14},{6,12},{8,2},{10,0},{12,6},{14,4},{1,11},{3,9}... | collective-permute-start | bytes 829448 | tf_op jit(solution)/shard_map/ppermute | solution.py:640
  225.5 37.5 %copy-start.2 = (bf16[384,1920]{1,0:T(8,128)(2,1)S(1)}, bf16[384,1920]{1,0:T(8,128)(2,1)}, u32[]{:S(2)}) copy-start(bf16[384,1920]{1,0:T(8,128)(2,1)} %table.2.t_ref) | copy-start | bytes 4423684
  228.9 35.4 %copy-start.19 = (bf16[45,24,128]{2,1,0:T(8,128)(2,1)}, bf16[45,24,128]{2,1,0:T(8,128)(2,1)S(1)}, u32[]{:S(2)}) copy-start(bf16[45,24,128]{2,1,0:T(8,128)(2,1)S(1)} %collective-permute-done.22.refs_3_) | copy-start | bytes 829444
  228.9 37.5 %collective-permute-start.27 = (bf16[45,24,128]{2,1,0:T(8,128)(2,1)}, bf16[45,24,128]{2,1,0:T(8,128)(2,1)S(1)}, u32[]{:S(2)}, u32[]{:S(2)}) collective-permute-start(bf16[45,24,128]{2,1,0:T(8,128)(2,1)} %get-tuple-element.99), channel_id=1, source_target_pairs={{0,12},{2,14},{4,8},{6,10},{8,4},{10,6},{12,0},{14,2},{1,13},{3,15... | collective-permute-start | bytes 829448 | tf_op jit(solution)/shard_map/ppermute | solution.py:640
  238.2 26.1 %copy-start.20 = (bf16[45,24,128]{2,1,0:T(8,128)(2,1)}, bf16[45,24,128]{2,1,0:T(8,128)(2,1)S(1)}, u32[]{:S(2)}) copy-start(bf16[45,24,128]{2,1,0:T(8,128)(2,1)S(1)} %collective-permute-done.23.refs_4_) | copy-start | bytes 829444
  238.2 43.6 %collective-permute-start.28 = (bf16[45,24,128]{2,1,0:T(8,128)(2,1)}, bf16[45,24,128]{2,1,0:T(8,128)(2,1)S(1)}, u32[]{:S(2)}, u32[]{:S(2)}) collective-permute-start(bf16[45,24,128]{2,1,0:T(8,128)(2,1)} %get-tuple-element.100), channel_id=1, source_target_pairs={{0,14},{2,12},{4,10},{6,8},{8,6},{10,4},{12,2},{14,0},{1,15},{3,13... | collective-permute-start | bytes 829448 | tf_op jit(solution)/shard_map/ppermute | solution.py:640
  243.7 38.1 %collective-permute-start.29 = (bf16[45,24,128]{2,1,0:T(8,128)(2,1)}, bf16[45,24,128]{2,1,0:T(8,128)(2,1)S(1)}, u32[]{:S(2)}, u32[]{:S(2)}) collective-permute-start(bf16[45,24,128]{2,1,0:T(8,128)(2,1)} %get-tuple-element.102), channel_id=1, source_target_pairs={{0,2},{2,0},{4,6},{6,4},{8,10},{10,8},{12,14},{14,12},{1,3},{3,1},... | collective-permute-start | bytes 829448 | tf_op jit(solution)/shard_map/ppermute | solution.py:640
  243.7 39.1 %collective-permute-start.30 = (bf16[45,24,128]{2,1,0:T(8,128)(2,1)}, bf16[45,24,128]{2,1,0:T(8,128)(2,1)S(1)}, u32[]{:S(2)}, u32[]{:S(2)}) collective-permute-start(bf16[45,24,128]{2,1,0:T(8,128)(2,1)} %get-tuple-element.103), channel_id=1, source_target_pairs={{0,4},{2,6},{4,0},{6,2},{8,12},{10,14},{12,8},{14,10},{1,5},{3,7},... | collective-permute-start | bytes 829448 | tf_op jit(solution)/shard_map/ppermute | solution.py:640
  259.7 24.9 %collective-permute-start.31 = (bf16[45,24,128]{2,1,0:T(8,128)(2,1)}, bf16[45,24,128]{2,1,0:T(8,128)(2,1)S(1)}, u32[]{:S(2)}, u32[]{:S(2)}) collective-permute-start(bf16[45,24,128]{2,1,0:T(8,128)(2,1)} %get-tuple-element.104), channel_id=1, source_target_pairs={{0,6},{2,4},{4,2},{6,0},{8,14},{10,12},{12,10},{14,8},{1,7},{3,5},... | collective-permute-start | bytes 829448 | tf_op jit(solution)/shard_map/ppermute | solution.py:640
  266.4 18.2 %copy-start.21 = (bf16[45,24,128]{2,1,0:T(8,128)(2,1)}, bf16[45,24,128]{2,1,0:T(8,128)(2,1)S(1)}, u32[]{:S(2)}) copy-start(bf16[45,24,128]{2,1,0:T(8,128)(2,1)S(1)} %collective-permute-done.27.refs_8_) | copy-start | bytes 829444
  266.4 38.0 %collective-permute-start.9 = (bf16[45,24,128]{2,1,0:T(8,128)(2,1)}, bf16[45,24,128]{2,1,0:T(8,128)(2,1)S(1)}, u32[]{:S(2)}, u32[]{:S(2)}) collective-permute-start(bf16[45,24,128]{2,1,0:T(8,128)(2,1)} %get-tuple-element.72), channel_id=1, source_target_pairs={{0,8},{2,10},{4,12},{6,14},{8,0},{10,2},{12,4},{14,6},{1,9},{3,11}... | collective-permute-start | bytes 829448 | tf_op jit(solution)/shard_map/ppermute | solution.py:640
  281.8 28.0 %collective-permute-start.10 = (bf16[45,24,128]{2,1,0:T(8,128)(2,1)}, bf16[45,24,128]{2,1,0:T(8,128)(2,1)S(1)}, u32[]{:S(2)}, u32[]{:S(2)}) collective-permute-start(bf16[45,24,128]{2,1,0:T(8,128)(2,1)} %get-tuple-element.73), channel_id=1, source_target_pairs={{0,10},{2,8},{4,14},{6,12},{8,2},{10,0},{12,6},{14,4},{1,11},{3,9}... | collective-permute-start | bytes 829448 | tf_op jit(solution)/shard_map/ppermute | solution.py:640
  281.8 35.3 %collective-permute-start.11 = (bf16[45,24,128]{2,1,0:T(8,128)(2,1)}, bf16[45,24,128]{2,1,0:T(8,128)(2,1)S(1)}, u32[]{:S(2)}, u32[]{:S(2)}) collective-permute-start(bf16[45,24,128]{2,1,0:T(8,128)(2,1)} %get-tuple-element.74), channel_id=1, source_target_pairs={{0,12},{2,14},{4,8},{6,10},{8,4},{10,6},{12,0},{14,2},{1,13},{3,15... | collective-permute-start | bytes 829448 | tf_op jit(solution)/shard_map/ppermute | solution.py:640
  282.8 39.5 %collective-permute-start.12 = (bf16[45,24,128]{2,1,0:T(8,128)(2,1)}, bf16[45,24,128]{2,1,0:T(8,128)(2,1)S(1)}, u32[]{:S(2)}, u32[]{:S(2)}) collective-permute-start(bf16[45,24,128]{2,1,0:T(8,128)(2,1)} %get-tuple-element.75), channel_id=1, source_target_pairs={{0,14},{2,12},{4,10},{6,8},{8,6},{10,4},{12,2},{14,0},{1,15},{3,13... | collective-permute-start | bytes 829448 | tf_op jit(solution)/shard_map/ppermute | solution.py:640
  (21 other events, 135.8 us)

commit v8 on v7

--- a/solution.py
+++ b/solution.py
@@ -537,7 +537,7 @@
         for v in range(LEVELS):
             piece = grid[v * LANES : v * LANES + latd]
             if partial is not None:
-                piece = piece + partial[v, :, cols]
+                piece = piece + partial[v, :, cols].astype(F32)
             out[v, :, cols] = piece.astype(out.dtype)
 
 
@@ -673,12 +673,7 @@
     sets = list(zip(tables, returned))
     scale = float(nmodes) ** (-0.5)
     shape = (levd, latd, nlon)
-    table, pieces = sets.pop()
-    table = table.reshape(2, groups, -1, nlon)
-    cut = groups // 2
-    for chosen in (slice(0, cut), slice(cut, groups)):
-        sets.append((table[:, chosen].reshape(-1, nlon), pieces[chosen]))
-    total = inverse_dft(sets[:-1], shape, None, scale, F32)
+    total = inverse_dft(sets[:-1], shape, None, scale, BF16)
     total = inverse_dft(sets[-1:], shape, total, scale, BF16)
     return total[None]
 

time: 339 us -> 319 us (0.941)
  waiting for transfers between devices: 130 us -> 117 us
  Pallas kernels: 144 us -> 138 us
    ppermute x28, waiting for transfers between devices: 130 us -> 117 us  [exchange(): out[r] = lax.ppermute(blocks[r], lat_lev, pairs)]
    pallas_call x2, Pallas kernels: 34 us -> 28 us  [inverse_dft(): pl.pallas_call(functools.partial(inverse_kernel, counts, latd, scale, par...]
  transfers between devices with their start and end apart: 32 -> 32, of which waited for: 18 -> 14; matrix products, arithmetic and copies ran while one was open for 2% -> 2% of each run, Pallas kernels for 33% -> 33%
where the time goes in v8:
time: 319 us; the launch traced here: 318 us
  Pallas kernels  138 us (43%)
  waiting for transfers between devices  117 us (37%)
  starting transfers between devices  46.7 us (15%)
  local copies, waits for them, and re-layouts  10.9 us (3%)
  other arithmetic  4.5 us (1%)
    ppermute x28, waiting for transfers between devices, exchange(): out[r] = lax.ppermute(blocks[r], lat_lev, pairs)  117 us
    ppermute x28, starting transfers between devices, exchange(): out[r] = lax.ppermute(blocks[r], lat_lev, pairs)  46.2 us
    pallas_call x2, Pallas kernels, legendre_step(): pl.pallas_call(functools.partial(legendre_kernel, groups, levs, levd, lat...  44.3 us
    pallas_call x2, Pallas kernels, dft(): pl.pallas_call(functools.partial(dft_kernel, groups, latd), out_shape=[ja...  32.4 us
    pallas_call x2, Pallas kernels, inverse_dft(): pl.pallas_call(functools.partial(inverse_kernel, counts, latd, scale, par...  28 us
    pallas_call x1, Pallas kernels, permute_legendre(): pl.pallas_call(permute_kernel, out_shape=jax.ShapeDtypeStruct((count, lan...  14.5 us
    pallas_call x2, Pallas kernels, fill_halves(): pl.pallas_call(functools.partial(fill_kernel, groups), out_shape=[jax.Sha...  6.68 us
  transfers between devices with their start and end apart: 32, of which 14 were waited for; matrix products, arithmetic and copies ran while one was open for 2% of the time, Pallas kernels for 33%

profile of v8, /device:TPU:12, one launch (start us, length us, event | category | flops | bytes accessed | tf_op | source)
XLA Modules:
  0.0 318.1 jit_solution(12980415221997086045)
XLA Ops:
  3.4 3.1 table.3.t_ref.refs_0_
  7.4 16.2 %dft.3 = (bf16[45,24,128]{2,1,0:T(8,128)(2,1)}, bf16[45,24,128]{2,1,0:T(8,128)(2,1)}, bf16[45,24,128]{2,1,0:T(8,128)(2,1)}, bf16[45,24,128]{2,1,0:T(8,128)(2,1)}...) custom-call(bf16[24,120,1920]{2,1,0:T(8,128)(2,1)} %bitcast.56, ...), custom_call_target="tpu_custom_call" | custom-call | flops 8493465600 | bytes 14745600 | tf_op jit(solution)/shard_map/dft/pallas_call | solution.py:265
  23.6 1.5 collective-permute-start.16
  25.6 1.5 collective-permute-start.18
  27.1 2.6 collective-permute-start.19
  29.7 1.3 collective-permute-start.20
  32.1 3.2 %table.2.t_ref.refs_0_ = bf16[384,1920]{1,0:T(8,128)(2,1)} custom-call(f32[192,128]{1,0:T(8,128)} %broadcast_in_dim.58.wave_ref), custom_call_target="tpu_custom_call" | custom-call | tf_op jit(solution)/shard_map/table/pallas_call | solution.py:205
  35.3 16.2 %dft.2 = (bf16[45,24,128]{2,1,0:T(8,128)(2,1)}, bf16[45,24,128]{2,1,0:T(8,128)(2,1)}, bf16[45,24,128]{2,1,0:T(8,128)(2,1)}, bf16[45,24,128]{2,1,0:T(8,128)(2,1)}...) custom-call(bf16[24,120,1920]{2,1,0:T(8,128)(2,1)} %bitcast.57, ...), custom_call_target="tpu_custom_call" | custom-call | flops 8493465600 | bytes 14745600 | tf_op jit(solution)/shard_map/dft/pallas_call | solution.py:265
  53.9 2.5 collective-permute-start.2
  56.4 1.6 collective-permute-start.21
  58.7 8.1 %collective-permute-done.21.refs_6_.rest_6_ = bf16[45,24,128]{2,1,0:T(8,128)(2,1)S(1)} collective-permute-done((bf16[45,24,128]{2,1,0:T(8,128)(2,1)S(1)}, bf16[45,24,128]{2,1,0:T(8,128)(2,1)S(1)}, u32[]{:S(2)}, u32[]{:S(2)}) %collective-permute-start.21) | collective-permute-done | bytes 276512 | tf_op jit(solution)/shard_map/ppermute | solution.py:640
  66.7 10.7 %collective-permute-start.3 = (bf16[45,24,128]{2,1,0:T(8,128)(2,1)}, bf16[45,24,128]{2,1,0:T(8,128)(2,1)S(1)}, u32[]{:S(2)}, u32[]{:S(2)}) collective-permute-start(bf16[45,24,128]{2,1,0:T(8,128)(2,1)} %get-tuple-element.59), channel_id=1, source_target_pairs={{0,8},{2,10},{4,12},{6,14},{8,0},{10,2},{12,4},{14,6},{1,9},{3,11}... | collective-permute-start | bytes 829448 | tf_op jit(solution)/shard_map/ppermute | solution.py:640
  77.5 19.1 %collective-permute-done.22.refs_7_.rest_7_ = bf16[45,24,128]{2,1,0:T(8,128)(2,1)S(1)} collective-permute-done((bf16[45,24,128]{2,1,0:T(8,128)(2,1)S(1)}, bf16[45,24,128]{2,1,0:T(8,128)(2,1)S(1)}, u32[]{:S(2)}, u32[]{:S(2)}) %collective-permute-start.22) | collective-permute-done | bytes 276512 | tf_op jit(solution)/shard_map/ppermute | solution.py:640
  97.3 3.0 gather_halves.3
  100.3 1.6 collective-permute-start.5
  101.9 2.0 collective-permute-start.6
  105.4 12.0 %collective-permute-done.4.refs_5_.rest_5_ = bf16[45,24,128]{2,1,0:T(8,128)(2,1)} collective-permute-done((bf16[45,24,128]{2,1,0:T(8,128)(2,1)}, bf16[45,24,128]{2,1,0:T(8,128)(2,1)}, u32[]{:S(2)}, u32[]{:S(2)}) %collective-permute-start.4) | collective-permute-done | bytes 276512 | tf_op jit(solution)/shard_map/ppermute | solution.py:640
  117.4 5.9 %collective-permute-done.5.refs_6_.rest_6_ = bf16[45,24,128]{2,1,0:T(8,128)(2,1)S(1)} collective-permute-done((bf16[45,24,128]{2,1,0:T(8,128)(2,1)}, bf16[45,24,128]{2,1,0:T(8,128)(2,1)S(1)}, u32[]{:S(2)}, u32[]{:S(2)}) %collective-permute-start.5) | collective-permute-done | bytes 276512 | tf_op jit(solution)/shard_map/ppermute | solution.py:640
  123.3 4.4 %collective-permute-done.6.refs_7_.rest_7_ = bf16[45,24,128]{2,1,0:T(8,128)(2,1)S(1)} collective-permute-done((bf16[45,24,128]{2,1,0:T(8,128)(2,1)}, bf16[45,24,128]{2,1,0:T(8,128)(2,1)S(1)}, u32[]{:S(2)}, u32[]{:S(2)}) %collective-permute-start.6) | collective-permute-done | bytes 276512 | tf_op jit(solution)/shard_map/ppermute | solution.py:640
  128.5 3.1 gather_halves.2
  132.3 1.0 fusion.perm_ref
  133.3 14.5 %permute_legendre.1.leg_ref = bf16[24,512,384]{2,1,0:T(8,128)(2,1)} custom-call(s32[1]{0:T(128)} %bitcast.4.info, bf16[48,480,384]{2,1,0:T(8,128)(2,1)} %bitcast.40, bf16[512,480]{1,0:T(8,128)(2,1)} %fusion.perm_ref), custom_call_target="tpu_custom_call" | custom-call | flops 4529848320 | bytes 18284544 | tf_op jit(solution)/shard_map/permute_legendre/pallas_call | solution.py:301
  147.7 1.1 copy-done.2
  148.9 22.2 %legendre.3 = (bf16[45,12,128]{2,1,0:T(8,128)(2,1)}, bf16[45,12,128]{2,1,0:T(8,128)(2,1)}, bf16[45,12,128]{2,1,0:T(8,128)(2,1)}, bf16[45,12,128]{2,1,0:T(8,128)(...) custom-call(s32[3,12]{1,0:T(4,128)} %get-tuple-element.117.info, ...), custom_call_target="tpu_custom_call" | custom-call | flops 1811939328 | bytes 9437184 | tf_op jit(solution)/shard_map/legendre/pallas_call | solution.py:428
  171.5 1.2 copy-done.3
  172.7 22.1 %legendre.2 = (bf16[45,12,128]{2,1,0:T(8,128)(2,1)}, bf16[45,12,128]{2,1,0:T(8,128)(2,1)}, bf16[45,12,128]{2,1,0:T(8,128)(2,1)}, bf16[45,12,128]{2,1,0:T(8,128)(...) custom-call(s32[3,12]{1,0:T(4,128)} %get-tuple-element.118.info, ...), custom_call_target="tpu_custom_call" | custom-call | flops 1811939328 | bytes 9437184 | tf_op jit(solution)/shard_map/legendre/pallas_call | solution.py:428
  194.8 3.3 %fill_halves.3 = (bf16[45,24,128]{2,1,0:T(8,128)(2,1)}, bf16[45,24,128]{2,1,0:T(8,128)(2,1)}, bf16[45,24,128]{2,1,0:T(8,128)(2,1)}, bf16[45,24,128]{2,1,0:T(8,12...) custom-call(bf16[8,45,16,128]{3,2,1,0:T(8,128)(2,1)} %collective-per, ...), custom_call_target="tpu_custom_call" | custom-call | tf_op jit(solution)/shard_map/fill_halves/pallas_call | solution.py:494
  198.1 1.5 collective-permute-start.25
  199.6 2.0 collective-permute-start.27
  201.6 1.0 collective-permute-start.28
  202.7 2.8 collective-permute-start.29
  205.5 3.4 %fill_halves.2 = (bf16[45,24,128]{2,1,0:T(8,128)(2,1)}, bf16[45,24,128]{2,1,0:T(8,128)(2,1)}, bf16[45,24,128]{2,1,0:T(8,128)(2,1)}, bf16[45,24,128]{2,1,0:T(8,12...) custom-call(bf16[8,45,16,128]{3,2,1,0:T(8,128)(2,1)} %copy-done.4, ...), custom_call_target="tpu_custom_call" | custom-call | tf_op jit(solution)/shard_map/fill_halves/pallas_call | solution.py:494
  208.8 1.6 collective-permute-start.30
  210.5 7.7 %collective-permute-done.26.refs_3_ = bf16[45,24,128]{2,1,0:T(8,128)(2,1)S(1)} collective-permute-done((bf16[45,24,128]{2,1,0:T(8,128)(2,1)}, bf16[45,24,128]{2,1,0:T(8,128)(2,1)S(1)}, u32[]{:S(2)}, u32[]{:S(2)}) %collective-permute-start.26) | collective-permute-done | bytes 276512 | tf_op jit(solution)/shard_map/ppermute | solution.py:640
  218.2 5.4 %collective-permute-done.27.refs_4_ = bf16[45,24,128]{2,1,0:T(8,128)(2,1)S(1)} collective-permute-done((bf16[45,24,128]{2,1,0:T(8,128)(2,1)}, bf16[45,24,128]{2,1,0:T(8,128)(2,1)S(1)}, u32[]{:S(2)}, u32[]{:S(2)}) %collective-permute-start.27) | collective-permute-done | bytes 276512 | tf_op jit(solution)/shard_map/ppermute | solution.py:640
  223.6 3.8 %collective-permute-start.10 = (bf16[45,24,128]{2,1,0:T(8,128)(2,1)}, bf16[45,24,128]{2,1,0:T(8,128)(2,1)S(1)}, u32[]{:S(2)}, u32[]{:S(2)}) collective-permute-start(bf16[45,24,128]{2,1,0:T(8,128)(2,1)} %get-tuple-element.74), channel_id=1, source_target_pairs={{0,4},{2,6},{4,0},{6,2},{8,12},{10,14},{12,8},{14,10},{1,5},{3,7},... | collective-permute-start | bytes 829448 | tf_op jit(solution)/shard_map/ppermute | solution.py:640
  227.5 12.2 %collective-permute-done.29.refs_6_ = bf16[45,24,128]{2,1,0:T(8,128)(2,1)S(1)} collective-permute-done((bf16[45,24,128]{2,1,0:T(8,128)(2,1)}, bf16[45,24,128]{2,1,0:T(8,128)(2,1)S(1)}, u32[]{:S(2)}, u32[]{:S(2)}) %collective-permute-start.29) | collective-permute-done | bytes 276512 | tf_op jit(solution)/shard_map/ppermute | solution.py:640
  239.6 3.3 %collective-permute-start.11 = (bf16[45,24,128]{2,1,0:T(8,128)(2,1)}, bf16[45,24,128]{2,1,0:T(8,128)(2,1)S(1)}, u32[]{:S(2)}, u32[]{:S(2)}) collective-permute-start(bf16[45,24,128]{2,1,0:T(8,128)(2,1)} %get-tuple-element.75), channel_id=1, source_target_pairs={{0,6},{2,4},{4,2},{6,0},{8,14},{10,12},{12,10},{14,8},{1,7},{3,5},... | collective-permute-start | bytes 829448 | tf_op jit(solution)/shard_map/ppermute | solution.py:640
  242.9 3.6 %collective-permute-done.30.refs_7_ = bf16[45,24,128]{2,1,0:T(8,128)(2,1)S(1)} collective-permute-done((bf16[45,24,128]{2,1,0:T(8,128)(2,1)}, bf16[45,24,128]{2,1,0:T(8,128)(2,1)S(1)}, u32[]{:S(2)}, u32[]{:S(2)}) %collective-permute-start.30) | collective-permute-done | bytes 276512 | tf_op jit(solution)/shard_map/ppermute | solution.py:640
  247.2 14.6 %collective-permute-done.31.refs_8_ = bf16[45,24,128]{2,1,0:T(8,128)(2,1)S(1)} collective-permute-done((bf16[45,24,128]{2,1,0:T(8,128)(2,1)S(1)}, bf16[45,24,128]{2,1,0:T(8,128)(2,1)S(1)}, u32[]{:S(2)}, u32[]{:S(2)}) %collective-permute-start.31) | collective-permute-done | bytes 276512 | tf_op jit(solution)/shard_map/ppermute | solution.py:640
  262.5 1.0 collective-permute-start.14
  263.5 1.8 collective-permute-start.15
  265.3 13.0 %inverse_dft.2.refs_9_ = bf16[24,120,1920]{2,1,0:T(8,128)(2,1)} custom-call(bf16[384,1920]{1,0:T(8,128)(2,1)} %table.3.t_ref.refs_0_, bf16[45,24,128]{2,1,0:T(8,128)(2,1)} %get-tuple-element.97.refs_1_, bf16[45,24,128]{2,1,0:T(8,128)(2,1)} %copy-done.34, bf16[45,24,128]{2,1,0:T(8,128)(2,1)} %copy-done.35, bf16[45,24,128]{2,1,0:T(8,128)(2,1)} %copy-done.36, ...), custom_call_target="tpu_custom_call" | custom-call | flops 4246732800 | bytes 14745600 | tf_op jit(solution)/shard_map/inverse_dft/pallas_call | solution.py:559
  278.4 5.4 %collective-permute-done.12.refs_5_ = bf16[45,24,128]{2,1,0:T(8,128)(2,1)S(1)} collective-permute-done((bf16[45,24,128]{2,1,0:T(8,128)(2,1)}, bf16[45,24,128]{2,1,0:T(8,128)(2,1)S(1)}, u32[]{:S(2)}, u32[]{:S(2)}) %collective-permute-start.12) | collective-permute-done | bytes 276512 | tf_op jit(solution)/shard_map/ppermute | solution.py:640
  283.8 5.9 %collective-permute-done.13.refs_6_ = bf16[45,24,128]{2,1,0:T(8,128)(2,1)S(1)} collective-permute-done((bf16[45,24,128]{2,1,0:T(8,128)(2,1)}, bf16[45,24,128]{2,1,0:T(8,128)(2,1)S(1)}, u32[]{:S(2)}, u32[]{:S(2)}) %collective-permute-start.13) | collective-permute-done | bytes 276512 | tf_op jit(solution)/shard_map/ppermute | solution.py:640
  289.8 7.4 %collective-permute-done.14.refs_7_ = bf16[45,24,128]{2,1,0:T(8,128)(2,1)S(1)} collective-permute-done((bf16[45,24,128]{2,1,0:T(8,128)(2,1)}, bf16[45,24,128]{2,1,0:T(8,128)(2,1)S(1)}, u32[]{:S(2)}, u32[]{:S(2)}) %collective-permute-start.14) | collective-permute-done | bytes 276512 | tf_op jit(solution)/shard_map/ppermute | solution.py:640
  297.1 5.1 %collective-permute-done.15.refs_8_ = bf16[45,24,128]{2,1,0:T(8,128)(2,1)S(1)} collective-permute-done((bf16[45,24,128]{2,1,0:T(8,128)(2,1)}, bf16[45,24,128]{2,1,0:T(8,128)(2,1)S(1)}, u32[]{:S(2)}, u32[]{:S(2)}) %collective-permute-start.15) | collective-permute-done | bytes 276512 | tf_op jit(solution)/shard_map/ppermute | solution.py:640
  303.0 15.0 %inverse_dft.3 = bf16[24,120,1920]{2,1,0:T(8,128)(2,1)} custom-call(bf16[384,1920]{1,0:T(8,128)(2,1)} %table.2.t_ref.refs_0_, bf16[45,24,128]{2,1,0:T(8,128)(2,1)} %get-tuple-element.72.refs_1_, bf16[45,24,128]{2,1,0:T(8,128)(2,1)} %copy-done.18, bf16[45,24,128]{2,1,0:T(8,128)(2,1)} %copy-done.19, bf16[45,24,128]{2,1,0:T(8,128)(2,1)} %copy-done.20, ...), custom_call_target="tpu_custom_call" | custom-call | flops 4246732800 | bytes 14745600 | tf_op jit(solution)/shard_map/inverse_dft/pallas_call | solution.py:559
  (156 shorter events, 15.1 us)
Async XLA Ops:
  0.0 31.1 %copy-start = (f32[48,48]{1,0:T(8,128)S(1)}, f32[48,48]{1,0:T(8,128)}, u32[]{:S(2)}) copy-start(f32[48,48]{1,0:T(8,128)} %param.24) | copy-start | bytes 27652
  23.6 29.3 %collective-permute-start.16 = (bf16[45,24,128]{2,1,0:T(8,128)(2,1)}, bf16[45,24,128]{2,1,0:T(8,128)(2,1)S(1)}, u32[]{:S(2)}, u32[]{:S(2)}) collective-permute-start(bf16[45,24,128]{2,1,0:T(8,128)(2,1)} %get-tuple-element.81), channel_id=1, source_target_pairs={{0,2},{2,0},{4,6},{6,4},{8,10},{10,8},{12,14},{14,12},{1,3},{3,1},... | collective-permute-start | bytes 829448 | tf_op jit(solution)/shard_map/ppermute | solution.py:640
  25.1 28.4 %collective-permute-start.17 = (bf16[45,24,128]{2,1,0:T(8,128)(2,1)}, bf16[45,24,128]{2,1,0:T(8,128)(2,1)S(1)}, u32[]{:S(2)}, u32[]{:S(2)}) collective-permute-start(bf16[45,24,128]{2,1,0:T(8,128)(2,1)} %get-tuple-element.82), channel_id=1, source_target_pairs={{0,4},{2,6},{4,0},{6,2},{8,12},{10,14},{12,8},{14,10},{1,5},{3,7},... | collective-permute-start | bytes 829448 | tf_op jit(solution)/shard_map/ppermute | solution.py:640
  25.6 28.4 %collective-permute-start.18 = (bf16[45,24,128]{2,1,0:T(8,128)(2,1)}, bf16[45,24,128]{2,1,0:T(8,128)(2,1)S(1)}, u32[]{:S(2)}, u32[]{:S(2)}) collective-permute-start(bf16[45,24,128]{2,1,0:T(8,128)(2,1)} %get-tuple-element.83), channel_id=1, source_target_pairs={{0,6},{2,4},{4,2},{6,0},{8,14},{10,12},{12,10},{14,8},{1,7},{3,5},... | collective-permute-start | bytes 829448 | tf_op jit(solution)/shard_map/ppermute | solution.py:640
  27.1 29.3 %collective-permute-start.19 = (bf16[45,24,128]{2,1,0:T(8,128)(2,1)}, bf16[45,24,128]{2,1,0:T(8,128)(2,1)S(1)}, u32[]{:S(2)}, u32[]{:S(2)}) collective-permute-start(bf16[45,24,128]{2,1,0:T(8,128)(2,1)} %get-tuple-element.84), channel_id=1, source_target_pairs={{0,8},{2,10},{4,12},{6,14},{8,0},{10,2},{12,4},{14,6},{1,9},{3,11}... | collective-permute-start | bytes 829448 | tf_op jit(solution)/shard_map/ppermute | solution.py:640
  29.7 28.4 %collective-permute-start.20 = (bf16[45,24,128]{2,1,0:T(8,128)(2,1)}, bf16[45,24,128]{2,1,0:T(8,128)(2,1)S(1)}, u32[]{:S(2)}, u32[]{:S(2)}) collective-permute-start(bf16[45,24,128]{2,1,0:T(8,128)(2,1)} %get-tuple-element.85), channel_id=1, source_target_pairs={{0,10},{2,8},{4,14},{6,12},{8,2},{10,0},{12,6},{14,4},{1,11},{3,9}... | collective-permute-start | bytes 829448 | tf_op jit(solution)/shard_map/ppermute | solution.py:640
  52.9 43.7 %copy-start.5 = (bf16[45,24,128]{2,1,0:T(8,128)(2,1)}, bf16[45,24,128]{2,1,0:T(8,128)(2,1)S(1)}, u32[]{:S(2)}) copy-start(bf16[45,24,128]{2,1,0:T(8,128)(2,1)S(1)} %collective-permute-done.16.refs_1_.rest_1_) | copy-start | bytes 829444
  52.9 47.4 %collective-permute-start = (bf16[45,24,128]{2,1,0:T(8,128)(2,1)}, bf16[45,24,128]{2,1,0:T(8,128)(2,1)S(1)}, u32[]{:S(2)}, u32[]{:S(2)}) collective-permute-start(bf16[45,24,128]{2,1,0:T(8,128)(2,1)} %get-tuple-element.56), channel_id=1, source_target_pairs={{0,2},{2,0},{4,6},{6,4},{8,10},{10,8},{12,14},{14,12},{1,3},{3,1},... | collective-permute-start | bytes 829448 | tf_op jit(solution)/shard_map/ppermute | solution.py:640
  53.5 43.1 %copy-start.6 = (bf16[45,24,128]{2,1,0:T(8,128)(2,1)}, bf16[45,24,128]{2,1,0:T(8,128)(2,1)S(1)}, u32[]{:S(2)}) copy-start(bf16[45,24,128]{2,1,0:T(8,128)(2,1)S(1)} %collective-permute-done.17.refs_2_.rest_2_) | copy-start | bytes 829444
  53.5 48.4 %collective-permute-start.1 = (bf16[45,24,128]{2,1,0:T(8,128)(2,1)}, bf16[45,24,128]{2,1,0:T(8,128)(2,1)S(1)}, u32[]{:S(2)}, u32[]{:S(2)}) collective-permute-start(bf16[45,24,128]{2,1,0:T(8,128)(2,1)} %get-tuple-element.57), channel_id=1, source_target_pairs={{0,4},{2,6},{4,0},{6,2},{8,12},{10,14},{12,8},{14,10},{1,5},{3,7},... | collective-permute-start | bytes 829448 | tf_op jit(solution)/shard_map/ppermute | solution.py:640
  53.9 42.7 %copy-start.7 = (bf16[45,24,128]{2,1,0:T(8,128)(2,1)}, bf16[45,24,128]{2,1,0:T(8,128)(2,1)S(1)}, u32[]{:S(2)}) copy-start(bf16[45,24,128]{2,1,0:T(8,128)(2,1)S(1)} %collective-permute-done.18.refs_3_.rest_3_) | copy-start | bytes 829444
  53.9 49.9 %collective-permute-start.2 = (bf16[45,24,128]{2,1,0:T(8,128)(2,1)}, bf16[45,24,128]{2,1,0:T(8,128)(2,1)S(1)}, u32[]{:S(2)}, u32[]{:S(2)}) collective-permute-start(bf16[45,24,128]{2,1,0:T(8,128)(2,1)} %get-tuple-element.58), channel_id=1, source_target_pairs={{0,6},{2,4},{4,2},{6,0},{8,14},{10,12},{12,10},{14,8},{1,7},{3,5},... | collective-permute-start | bytes 829448 | tf_op jit(solution)/shard_map/ppermute | solution.py:640
  56.4 40.2 %copy-start.8 = (bf16[45,24,128]{2,1,0:T(8,128)(2,1)}, bf16[45,24,128]{2,1,0:T(8,128)(2,1)S(1)}, u32[]{:S(2)}) copy-start(bf16[45,24,128]{2,1,0:T(8,128)(2,1)S(1)} %collective-permute-done.19.refs_4_.rest_4_) | copy-start | bytes 829444
  56.4 10.3 %collective-permute-start.21 = (bf16[45,24,128]{2,1,0:T(8,128)(2,1)S(1)}, bf16[45,24,128]{2,1,0:T(8,128)(2,1)S(1)}, u32[]{:S(2)}, u32[]{:S(2)}) collective-permute-start(bf16[45,24,128]{2,1,0:T(8,128)(2,1)S(1)} %copy-done.33), channel_id=1, source_target_pairs={{0,12},{2,14},{4,8},{6,10},{8,4},{10,6},{12,0},{14,2},{1,13},{3,15... | collective-permute-start | bytes 829448 | tf_op jit(solution)/shard_map/ppermute | solution.py:640
  58.1 38.5 %copy-start.9 = (bf16[45,24,128]{2,1,0:T(8,128)(2,1)}, bf16[45,24,128]{2,1,0:T(8,128)(2,1)S(1)}, u32[]{:S(2)}) copy-start(bf16[45,24,128]{2,1,0:T(8,128)(2,1)S(1)} %collective-permute-done.20.refs_5_.rest_5_) | copy-start | bytes 829444
  58.1 38.5 %collective-permute-start.22 = (bf16[45,24,128]{2,1,0:T(8,128)(2,1)S(1)}, bf16[45,24,128]{2,1,0:T(8,128)(2,1)S(1)}, u32[]{:S(2)}, u32[]{:S(2)}) collective-permute-start(bf16[45,24,128]{2,1,0:T(8,128)(2,1)S(1)} %copy-done.32), channel_id=1, source_target_pairs={{0,14},{2,12},{4,10},{6,8},{8,6},{10,4},{12,2},{14,0},{1,15},{3,13... | collective-permute-start | bytes 829448 | tf_op jit(solution)/shard_map/ppermute | solution.py:640
  66.7 29.9 %copy-start.14 = (bf16[45,24,128]{2,1,0:T(8,128)(2,1)}, bf16[45,24,128]{2,1,0:T(8,128)(2,1)S(1)}, u32[]{:S(2)}) copy-start(bf16[45,24,128]{2,1,0:T(8,128)(2,1)S(1)} %collective-permute-done.21.refs_6_.rest_6_) | copy-start | bytes 829444
  66.7 38.7 %collective-permute-start.3 = (bf16[45,24,128]{2,1,0:T(8,128)(2,1)}, bf16[45,24,128]{2,1,0:T(8,128)(2,1)S(1)}, u32[]{:S(2)}, u32[]{:S(2)}) collective-permute-start(bf16[45,24,128]{2,1,0:T(8,128)(2,1)} %get-tuple-element.59), channel_id=1, source_target_pairs={{0,8},{2,10},{4,12},{6,14},{8,0},{10,2},{12,4},{14,6},{1,9},{3,11}... | collective-permute-start | bytes 829448 | tf_op jit(solution)/shard_map/ppermute | solution.py:640
  96.6 20.8 %collective-permute-start.4 = (bf16[45,24,128]{2,1,0:T(8,128)(2,1)}, bf16[45,24,128]{2,1,0:T(8,128)(2,1)}, u32[]{:S(2)}, u32[]{:S(2)}) collective-permute-start(bf16[45,24,128]{2,1,0:T(8,128)(2,1)} %get-tuple-element.60), channel_id=1, source_target_pairs={{0,10},{2,8},{4,14},{6,12},{8,2},{10,0},{12,6},{14,4},{1,11},{3,9}... | collective-permute-start | bytes 829448 | tf_op jit(solution)/shard_map/ppermute | solution.py:640
  100.3 27.5 %copy-start.10 = (bf16[45,24,128]{2,1,0:T(8,128)(2,1)}, bf16[45,24,128]{2,1,0:T(8,128)(2,1)S(1)}, u32[]{:S(2)}) copy-start(bf16[45,24,128]{2,1,0:T(8,128)(2,1)S(1)} %collective-permute-done.refs_1_.rest_1_) | copy-start | bytes 829444
  100.3 23.0 %collective-permute-start.5 = (bf16[45,24,128]{2,1,0:T(8,128)(2,1)}, bf16[45,24,128]{2,1,0:T(8,128)(2,1)S(1)}, u32[]{:S(2)}, u32[]{:S(2)}) collective-permute-start(bf16[45,24,128]{2,1,0:T(8,128)(2,1)} %get-tuple-element.61), channel_id=1, source_target_pairs={{0,12},{2,14},{4,8},{6,10},{8,4},{10,6},{12,0},{14,2},{1,13},{3,15... | collective-permute-start | bytes 829448 | tf_op jit(solution)/shard_map/ppermute | solution.py:640
  101.9 25.9 %copy-start.11 = (bf16[45,24,128]{2,1,0:T(8,128)(2,1)}, bf16[45,24,128]{2,1,0:T(8,128)(2,1)S(1)}, u32[]{:S(2)}) copy-start(bf16[45,24,128]{2,1,0:T(8,128)(2,1)S(1)} %collective-permute-done.1.refs_2_.rest_2_) | copy-start | bytes 829444
  101.9 25.9 %collective-permute-start.6 = (bf16[45,24,128]{2,1,0:T(8,128)(2,1)}, bf16[45,24,128]{2,1,0:T(8,128)(2,1)S(1)}, u32[]{:S(2)}, u32[]{:S(2)}) collective-permute-start(bf16[45,24,128]{2,1,0:T(8,128)(2,1)} %get-tuple-element.62), channel_id=1, source_target_pairs={{0,14},{2,12},{4,10},{6,8},{8,6},{10,4},{12,2},{14,0},{1,15},{3,13... | collective-permute-start | bytes 829448 | tf_op jit(solution)/shard_map/ppermute | solution.py:640
  103.9 23.9 %copy-start.12 = (bf16[45,24,128]{2,1,0:T(8,128)(2,1)}, bf16[45,24,128]{2,1,0:T(8,128)(2,1)S(1)}, u32[]{:S(2)}) copy-start(bf16[45,24,128]{2,1,0:T(8,128)(2,1)S(1)} %collective-permute-done.2.refs_3_.rest_3_) | copy-start | bytes 829444
  103.9 43.9 %collective-permute-start.23 = (bf16[8,45,16,128]{3,2,1,0:T(8,128)(2,1)}, bf16[8,45,16,128]{3,2,1,0:T(8,128)(2,1)S(1)}, u32[]{:S(2)}, u32[]{:S(2)}) collective-permute-start(bf16[8,45,16,128]{3,2,1,0:T(8,128)(2,1)} %gather_halves.3), channel_id=1, source_target_pairs={{0,1},{1,0},{2,3},{3,2},{4,5},{5,4},{6,7},{7,6},{8,9},{9,8},{10,11... | collective-permute-start | bytes 4423688 | tf_op jit(solution)/shard_map/ppermute | solution.py:644
  131.6 40.0 %collective-permute-start.7 = (bf16[8,45,16,128]{3,2,1,0:T(8,128)(2,1)}, bf16[8,45,16,128]{3,2,1,0:T(8,128)(2,1)S(1)}, u32[]{:S(2)}, u32[]{:S(2)}) collective-permute-start(bf16[8,45,16,128]{3,2,1,0:T(8,128)(2,1)} %gather_halves.2), channel_id=1, source_target_pairs={{0,1},{1,0},{2,3},{3,2},{4,5},{5,4},{6,7},{7,6},{8,9},{9,8},{10,11... | collective-permute-start | bytes 4423688 | tf_op jit(solution)/shard_map/ppermute | solution.py:644
  171.0 23.8 %collective-permute-start.24 = (bf16[8,45,16,128]{3,2,1,0:T(8,128)(2,1)}, bf16[8,45,16,128]{3,2,1,0:T(8,128)(2,1)}, u32[]{:S(2)}, u32[]{:S(2)}) collective-permute-start(bf16[8,45,16,128]{3,2,1,0:T(8,128)(2,1)} %get-tuple-element.88), channel_id=1, source_target_pairs={{0,1},{1,0},{2,3},{3,2},{4,5},{5,4},{6,7},{7,6},{8,9},{9,8},{10,11... | collective-permute-start | bytes 4423688 | tf_op jit(solution)/shard_map/ppermute | solution.py:644
  194.8 7.9 %collective-permute-start.8 = (bf16[8,45,16,128]{3,2,1,0:T(8,128)(2,1)}, bf16[8,45,16,128]{3,2,1,0:T(8,128)(2,1)S(1)}, u32[]{:S(2)}, u32[]{:S(2)}) collective-permute-start(bf16[8,45,16,128]{3,2,1,0:T(8,128)(2,1)} %get-tuple-element.63), channel_id=1, source_target_pairs={{0,1},{1,0},{2,3},{3,2},{4,5},{5,4},{6,7},{7,6},{8,9},{9,8},{10,11... | collective-permute-start | bytes 4423688 | tf_op jit(solution)/shard_map/ppermute | solution.py:644
  198.1 10.7 %collective-permute-start.25 = (bf16[45,24,128]{2,1,0:T(8,128)(2,1)}, bf16[45,24,128]{2,1,0:T(8,128)(2,1)S(1)}, u32[]{:S(2)}, u32[]{:S(2)}) collective-permute-start(bf16[45,24,128]{2,1,0:T(8,128)(2,1)} %get-tuple-element.98), channel_id=1, source_target_pairs={{0,2},{2,0},{4,6},{6,4},{8,10},{10,8},{12,14},{14,12},{1,3},{3,1},... | collective-permute-start | bytes 829448 | tf_op jit(solution)/shard_map/ppermute | solution.py:640
  199.6 18.6 %collective-permute-start.26 = (bf16[45,24,128]{2,1,0:T(8,128)(2,1)}, bf16[45,24,128]{2,1,0:T(8,128)(2,1)S(1)}, u32[]{:S(2)}, u32[]{:S(2)}) collective-permute-start(bf16[45,24,128]{2,1,0:T(8,128)(2,1)} %get-tuple-element.99), channel_id=1, source_target_pairs={{0,4},{2,6},{4,0},{6,2},{8,12},{10,14},{12,8},{14,10},{1,5},{3,7},... | collective-permute-start | bytes 829448 | tf_op jit(solution)/shard_map/ppermute | solution.py:640
  199.6 24.0 %collective-permute-start.27 = (bf16[45,24,128]{2,1,0:T(8,128)(2,1)}, bf16[45,24,128]{2,1,0:T(8,128)(2,1)S(1)}, u32[]{:S(2)}, u32[]{:S(2)}) collective-permute-start(bf16[45,24,128]{2,1,0:T(8,128)(2,1)} %get-tuple-element.100), channel_id=1, source_target_pairs={{0,6},{2,4},{4,2},{6,0},{8,14},{10,12},{12,10},{14,8},{1,7},{3,5},... | collective-permute-start | bytes 829448 | tf_op jit(solution)/shard_map/ppermute | solution.py:640
  201.6 22.0 %collective-permute-start.28 = (bf16[45,24,128]{2,1,0:T(8,128)(2,1)}, bf16[45,24,128]{2,1,0:T(8,128)(2,1)S(1)}, u32[]{:S(2)}, u32[]{:S(2)}) collective-permute-start(bf16[45,24,128]{2,1,0:T(8,128)(2,1)} %get-tuple-element.101), channel_id=1, source_target_pairs={{0,8},{2,10},{4,12},{6,14},{8,0},{10,2},{12,4},{14,6},{1,9},{3,11}... | collective-permute-start | bytes 829448 | tf_op jit(solution)/shard_map/ppermute | solution.py:640
  202.7 37.0 %collective-permute-start.29 = (bf16[45,24,128]{2,1,0:T(8,128)(2,1)}, bf16[45,24,128]{2,1,0:T(8,128)(2,1)S(1)}, u32[]{:S(2)}, u32[]{:S(2)}) collective-permute-start(bf16[45,24,128]{2,1,0:T(8,128)(2,1)} %get-tuple-element.102), channel_id=1, source_target_pairs={{0,10},{2,8},{4,14},{6,12},{8,2},{10,0},{12,6},{14,4},{1,11},{3,9}... | collective-permute-start | bytes 829448 | tf_op jit(solution)/shard_map/ppermute | solution.py:640
  208.8 56.5 %copy-start.34 = (bf16[45,24,128]{2,1,0:T(8,128)(2,1)}, bf16[45,24,128]{2,1,0:T(8,128)(2,1)S(1)}, u32[]{:S(2)}) copy-start(bf16[45,24,128]{2,1,0:T(8,128)(2,1)S(1)} %collective-permute-done.25.refs_2_) | copy-start | bytes 829444
  208.8 37.6 %collective-permute-start.30 = (bf16[45,24,128]{2,1,0:T(8,128)(2,1)}, bf16[45,24,128]{2,1,0:T(8,128)(2,1)S(1)}, u32[]{:S(2)}, u32[]{:S(2)}) collective-permute-start(bf16[45,24,128]{2,1,0:T(8,128)(2,1)} %get-tuple-element.103), channel_id=1, source_target_pairs={{0,12},{2,14},{4,8},{6,10},{8,4},{10,6},{12,0},{14,2},{1,13},{3,15... | collective-permute-start | bytes 829448 | tf_op jit(solution)/shard_map/ppermute | solution.py:640
  218.2 47.1 %copy-start.35 = (bf16[45,24,128]{2,1,0:T(8,128)(2,1)}, bf16[45,24,128]{2,1,0:T(8,128)(2,1)S(1)}, u32[]{:S(2)}) copy-start(bf16[45,24,128]{2,1,0:T(8,128)(2,1)S(1)} %collective-permute-done.26.refs_3_) | copy-start | bytes 829444
  218.2 43.6 %collective-permute-start.31 = (bf16[45,24,128]{2,1,0:T(8,128)(2,1)S(1)}, bf16[45,24,128]{2,1,0:T(8,128)(2,1)S(1)}, u32[]{:S(2)}, u32[]{:S(2)}) collective-permute-start(bf16[45,24,128]{2,1,0:T(8,128)(2,1)S(1)} %copy-done.38), channel_id=1, source_target_pairs={{0,14},{2,12},{4,10},{6,8},{8,6},{10,4},{12,2},{14,0},{1,15},{3,13... | collective-permute-start | bytes 829448 | tf_op jit(solution)/shard_map/ppermute | solution.py:640
  223.6 41.7 %copy-start.36 = (bf16[45,24,128]{2,1,0:T(8,128)(2,1)}, bf16[45,24,128]{2,1,0:T(8,128)(2,1)S(1)}, u32[]{:S(2)}) copy-start(bf16[45,24,128]{2,1,0:T(8,128)(2,1)S(1)} %collective-permute-done.27.refs_4_) | copy-start | bytes 829444
  223.6 38.9 %collective-permute-start.9 = (bf16[45,24,128]{2,1,0:T(8,128)(2,1)}, bf16[45,24,128]{2,1,0:T(8,128)(2,1)S(1)}, u32[]{:S(2)}, u32[]{:S(2)}) collective-permute-start(bf16[45,24,128]{2,1,0:T(8,128)(2,1)} %get-tuple-element.73), channel_id=1, source_target_pairs={{0,2},{2,0},{4,6},{6,4},{8,10},{10,8},{12,14},{14,12},{1,3},{3,1},... | collective-permute-start | bytes 829448 | tf_op jit(solution)/shard_map/ppermute | solution.py:640
  223.6 41.7 %copy-start.37 = (bf16[45,24,128]{2,1,0:T(8,128)(2,1)}, bf16[45,24,128]{2,1,0:T(8,128)(2,1)S(1)}, u32[]{:S(2)}) copy-start(bf16[45,24,128]{2,1,0:T(8,128)(2,1)S(1)} %collective-permute-done.28.refs_5_) | copy-start | bytes 829444
  223.6 39.9 %collective-permute-start.10 = (bf16[45,24,128]{2,1,0:T(8,128)(2,1)}, bf16[45,24,128]{2,1,0:T(8,128)(2,1)S(1)}, u32[]{:S(2)}, u32[]{:S(2)}) collective-permute-start(bf16[45,24,128]{2,1,0:T(8,128)(2,1)} %get-tuple-element.74), channel_id=1, source_target_pairs={{0,4},{2,6},{4,0},{6,2},{8,12},{10,14},{12,8},{14,10},{1,5},{3,7},... | collective-permute-start | bytes 829448 | tf_op jit(solution)/shard_map/ppermute | solution.py:640
  239.6 25.7 %copy-start.39 = (bf16[45,24,128]{2,1,0:T(8,128)(2,1)}, bf16[45,24,128]{2,1,0:T(8,128)(2,1)S(1)}, u32[]{:S(2)}) copy-start(bf16[45,24,128]{2,1,0:T(8,128)(2,1)S(1)} %collective-permute-done.29.refs_6_) | copy-start | bytes 829444
  239.6 38.7 %collective-permute-start.11 = (bf16[45,24,128]{2,1,0:T(8,128)(2,1)}, bf16[45,24,128]{2,1,0:T(8,128)(2,1)S(1)}, u32[]{:S(2)}, u32[]{:S(2)}) collective-permute-start(bf16[45,24,128]{2,1,0:T(8,128)(2,1)} %get-tuple-element.75), channel_id=1, source_target_pairs={{0,6},{2,4},{4,2},{6,0},{8,14},{10,12},{12,10},{14,8},{1,7},{3,5},... | collective-permute-start | bytes 829448 | tf_op jit(solution)/shard_map/ppermute | solution.py:640
  247.2 36.7 %collective-permute-start.12 = (bf16[45,24,128]{2,1,0:T(8,128)(2,1)}, bf16[45,24,128]{2,1,0:T(8,128)(2,1)S(1)}, u32[]{:S(2)}, u32[]{:S(2)}) collective-permute-start(bf16[45,24,128]{2,1,0:T(8,128)(2,1)} %get-tuple-element.76), channel_id=1, source_target_pairs={{0,8},{2,10},{4,12},{6,14},{8,0},{10,2},{12,4},{14,6},{1,9},{3,11}... | collective-permute-start | bytes 829448 | tf_op jit(solution)/shard_map/ppermute | solution.py:640
  262.5 27.3 %collective-permute-start.13 = (bf16[45,24,128]{2,1,0:T(8,128)(2,1)}, bf16[45,24,128]{2,1,0:T(8,128)(2,1)S(1)}, u32[]{:S(2)}, u32[]{:S(2)}) collective-permute-start(bf16[45,24,128]{2,1,0:T(8,128)(2,1)} %get-tuple-element.77), channel_id=1, source_target_pairs={{0,10},{2,8},{4,14},{6,12},{8,2},{10,0},{12,6},{14,4},{1,11},{3,9}... | collective-permute-start | bytes 829448 | tf_op jit(solution)/shard_map/ppermute | solution.py:640
  262.5 34.6 %collective-permute-start.14 = (bf16[45,24,128]{2,1,0:T(8,128)(2,1)}, bf16[45,24,128]{2,1,0:T(8,128)(2,1)S(1)}, u32[]{:S(2)}, u32[]{:S(2)}) collective-permute-start(bf16[45,24,128]{2,1,0:T(8,128)(2,1)} %get-tuple-element.78), channel_id=1, source_target_pairs={{0,12},{2,14},{4,8},{6,10},{8,4},{10,6},{12,0},{14,2},{1,13},{3,15... | collective-permute-start | bytes 829448 | tf_op jit(solution)/shard_map/ppermute | solution.py:640
  263.5 38.8 %collective-permute-start.15 = (bf16[45,24,128]{2,1,0:T(8,128)(2,1)}, bf16[45,24,128]{2,1,0:T(8,128)(2,1)S(1)}, u32[]{:S(2)}, u32[]{:S(2)}) collective-permute-start(bf16[45,24,128]{2,1,0:T(8,128)(2,1)} %get-tuple-element.79), channel_id=1, source_target_pairs={{0,14},{2,12},{4,10},{6,8},{8,6},{10,4},{12,2},{14,0},{1,15},{3,13... | collective-permute-start | bytes 829448 | tf_op jit(solution)/shard_map/ppermute | solution.py:640
  278.4 23.9 %copy-start.20 = (bf16[45,24,128]{2,1,0:T(8,128)(2,1)}, bf16[45,24,128]{2,1,0:T(8,128)(2,1)S(1)}, u32[]{:S(2)}) copy-start(bf16[45,24,128]{2,1,0:T(8,128)(2,1)S(1)} %collective-permute-done.11.refs_4_) | copy-start | bytes 829444
  (26 other events, 267.8 us)

commit v9 on v8

--- a/solution.py
+++ b/solution.py
@@ -222,7 +222,7 @@
 
     wind = jnp.broadcast_to(lat_ref[...].T[:latd, 0:1], (latd, LANES))
     wind = jnp.concatenate([wind] * nblk, axis=1)
-    weight = lat_ref[2:3, :]
+    weight = lat_ref[2:3, :] * float(x_ref.shape[2]) ** (-0.5)
     factor = wave_ref[...] * lat_ref[1:2, :]
 
     def load(v):
@@ -441,7 +441,7 @@
             + [piece] * groups
             + [pl.BlockSpec(memory_space=pltpu.VMEM)],
             out_specs=[half] * groups + [stack],
-            scratch_shapes=[pltpu.VMEM((groups // levs, count * 4 * nlev, LANES), F32)] * 2,
+            scratch_shapes=[pltpu.VMEM((lanes // LANES, padded(count) * 4 * nlev, LANES), F32)] * 2,
         ),
         cost_estimate=pl.CostEstimate(
             flops=flops,
@@ -604,9 +604,9 @@
     lat_rel = xor_order(lat_order.reshape(lats, latd), z, 0)
     lat_rel = jnp.pad(lat_rel, ((0, 0), (0, LANES - latd)), constant_values=-1)
     hits = lat_rel[0][None, :, None] == jnp.arange(nlat, dtype=jnp.int32)[None, None, :]
-    zonal = jnp.stack([zonal_wind, zonal_rate, quad_weight * nlon ** (-0.5)], axis=0)
+    blank = jnp.zeros_like(quad_weight)
+    zonal = jnp.stack([zonal_wind, zonal_rate, quad_weight] + [blank] * 5, axis=0)
     lat_rows = jnp.sum(jnp.where(hits, zonal[:, None, :], 0.0), axis=2)
-    lat_rows = jnp.pad(lat_rows, ((0, 5), (0, 0)))
 
     first = f == 0
     mix = jnp.dot(vert_project, thermal_matrix, precision=PRECISE)

time: 319 us -> 319 us (level)
  no operation moved by 1% of the time
where the time goes in v9:
time: 319 us; the launch traced here: 318 us
  Pallas kernels  138 us (43%)
  waiting for transfers between devices  117 us (37%)
  starting transfers between devices  46.7 us (15%)
  local copies, waits for them, and re-layouts  10.4 us (3%)
  other arithmetic  4.73 us (1%)
    ppermute x28, waiting for transfers between devices, exchange(): out[r] = lax.ppermute(blocks[r], lat_lev, pairs)  117 us
    ppermute x28, starting transfers between devices, exchange(): out[r] = lax.ppermute(blocks[r], lat_lev, pairs)  46.2 us
    pallas_call x2, Pallas kernels, legendre_step(): pl.pallas_call(functools.partial(legendre_kernel, groups, levs, levd, lat...  44.2 us
    pallas_call x2, Pallas kernels, dft(): pl.pallas_call(functools.partial(dft_kernel, groups, latd), out_shape=[ja...  32.4 us
    pallas_call x2, Pallas kernels, inverse_dft(): pl.pallas_call(functools.partial(inverse_kernel, counts, latd, scale, par...  28 us
    pallas_call x1, Pallas kernels, permute_legendre(): pl.pallas_call(permute_kernel, out_shape=jax.ShapeDtypeStruct((count, lan...  14.5 us
    pallas_call x2, Pallas kernels, fill_halves(): pl.pallas_call(functools.partial(fill_kernel, groups), out_shape=[jax.Sha...  6.63 us
  transfers between devices with their start and end apart: 32, of which 14 were waited for; matrix products, arithmetic and copies ran while one was open for 2% of the time, Pallas kernels for 33%

profile of v9, /device:TPU:12, one launch (start us, length us, event | category | flops | bytes accessed | tf_op | source)
XLA Modules:
  0.0 317.7 jit_solution(10269020949120327723)
XLA Ops:
  2.7 3.1 table.3.t_ref.refs_0_
  5.9 1.2 select_reduce_fusion.lat_ref
  7.1 16.2 %dft.3 = (bf16[45,24,128]{2,1,0:T(8,128)(2,1)}, bf16[45,24,128]{2,1,0:T(8,128)(2,1)}, bf16[45,24,128]{2,1,0:T(8,128)(2,1)}, bf16[45,24,128]{2,1,0:T(8,128)(2,1)}...) custom-call(bf16[24,120,1920]{2,1,0:T(8,128)(2,1)} %bitcast.56, ...), custom_call_target="tpu_custom_call" | custom-call | flops 8493465600 | bytes 14745600 | tf_op jit(solution)/shard_map/dft/pallas_call | solution.py:265
  23.2 1.5 collective-permute-start.16
  25.2 1.5 collective-permute-start.18
  26.7 2.6 collective-permute-start.19
  29.3 1.3 collective-permute-start.20
  31.8 3.2 %table.2.t_ref.refs_0_ = bf16[384,1920]{1,0:T(8,128)(2,1)} custom-call(f32[192,128]{1,0:T(8,128)} %broadcast_in_dim.58.wave_ref), custom_call_target="tpu_custom_call" | custom-call | tf_op jit(solution)/shard_map/table/pallas_call | solution.py:205
  35.0 16.2 %dft.2 = (bf16[45,24,128]{2,1,0:T(8,128)(2,1)}, bf16[45,24,128]{2,1,0:T(8,128)(2,1)}, bf16[45,24,128]{2,1,0:T(8,128)(2,1)}, bf16[45,24,128]{2,1,0:T(8,128)(2,1)}...) custom-call(bf16[24,120,1920]{2,1,0:T(8,128)(2,1)} %bitcast.57, ...), custom_call_target="tpu_custom_call" | custom-call | flops 8493465600 | bytes 14745600 | tf_op jit(solution)/shard_map/dft/pallas_call | solution.py:265
  53.6 2.5 collective-permute-start.2
  56.1 1.6 collective-permute-start.21
  58.3 8.1 %collective-permute-done.21.refs_6_.rest_6_ = bf16[45,24,128]{2,1,0:T(8,128)(2,1)S(1)} collective-permute-done((bf16[45,24,128]{2,1,0:T(8,128)(2,1)S(1)}, bf16[45,24,128]{2,1,0:T(8,128)(2,1)S(1)}, u32[]{:S(2)}, u32[]{:S(2)}) %collective-permute-start.21) | collective-permute-done | bytes 276512 | tf_op jit(solution)/shard_map/ppermute | solution.py:640
  66.4 10.8 %collective-permute-start.3 = (bf16[45,24,128]{2,1,0:T(8,128)(2,1)}, bf16[45,24,128]{2,1,0:T(8,128)(2,1)S(1)}, u32[]{:S(2)}, u32[]{:S(2)}) collective-permute-start(bf16[45,24,128]{2,1,0:T(8,128)(2,1)} %get-tuple-element.59), channel_id=1, source_target_pairs={{0,8},{2,10},{4,12},{6,14},{8,0},{10,2},{12,4},{14,6},{1,9},{3,11}... | collective-permute-start | bytes 829448 | tf_op jit(solution)/shard_map/ppermute | solution.py:640
  77.1 19.1 %collective-permute-done.22.refs_7_.rest_7_ = bf16[45,24,128]{2,1,0:T(8,128)(2,1)S(1)} collective-permute-done((bf16[45,24,128]{2,1,0:T(8,128)(2,1)S(1)}, bf16[45,24,128]{2,1,0:T(8,128)(2,1)S(1)}, u32[]{:S(2)}, u32[]{:S(2)}) %collective-permute-start.22) | collective-permute-done | bytes 276512 | tf_op jit(solution)/shard_map/ppermute | solution.py:640
  96.9 3.0 gather_halves.3
  100.0 1.6 collective-permute-start.5
  101.5 2.0 collective-permute-start.6
  105.1 11.9 %collective-permute-done.4.refs_5_.rest_5_ = bf16[45,24,128]{2,1,0:T(8,128)(2,1)} collective-permute-done((bf16[45,24,128]{2,1,0:T(8,128)(2,1)}, bf16[45,24,128]{2,1,0:T(8,128)(2,1)}, u32[]{:S(2)}, u32[]{:S(2)}) %collective-permute-start.4) | collective-permute-done | bytes 276512 | tf_op jit(solution)/shard_map/ppermute | solution.py:640
  117.0 5.9 %collective-permute-done.5.refs_6_.rest_6_ = bf16[45,24,128]{2,1,0:T(8,128)(2,1)S(1)} collective-permute-done((bf16[45,24,128]{2,1,0:T(8,128)(2,1)}, bf16[45,24,128]{2,1,0:T(8,128)(2,1)S(1)}, u32[]{:S(2)}, u32[]{:S(2)}) %collective-permute-start.5) | collective-permute-done | bytes 276512 | tf_op jit(solution)/shard_map/ppermute | solution.py:640
  123.0 4.4 %collective-permute-done.6.refs_7_.rest_7_ = bf16[45,24,128]{2,1,0:T(8,128)(2,1)S(1)} collective-permute-done((bf16[45,24,128]{2,1,0:T(8,128)(2,1)}, bf16[45,24,128]{2,1,0:T(8,128)(2,1)S(1)}, u32[]{:S(2)}, u32[]{:S(2)}) %collective-permute-start.6) | collective-permute-done | bytes 276512 | tf_op jit(solution)/shard_map/ppermute | solution.py:640
  128.1 3.1 gather_halves.2
  132.9 14.5 %permute_legendre.1.leg_ref = bf16[24,512,384]{2,1,0:T(8,128)(2,1)} custom-call(s32[1]{0:T(128)} %bitcast.4.info, bf16[48,480,384]{2,1,0:T(8,128)(2,1)} %bitcast.40, bf16[512,480]{1,0:T(8,128)(2,1)} %fusion.perm_ref), custom_call_target="tpu_custom_call" | custom-call | flops 4529848320 | bytes 18284544 | tf_op jit(solution)/shard_map/permute_legendre/pallas_call | solution.py:301
  147.4 1.1 copy-done.2
  148.5 22.2 %legendre.3 = (bf16[45,12,128]{2,1,0:T(8,128)(2,1)}, bf16[45,12,128]{2,1,0:T(8,128)(2,1)}, bf16[45,12,128]{2,1,0:T(8,128)(2,1)}, bf16[45,12,128]{2,1,0:T(8,128)(...) custom-call(s32[3,12]{1,0:T(4,128)} %get-tuple-element.117.info, ...), custom_call_target="tpu_custom_call" | custom-call | flops 1811939328 | bytes 9437184 | tf_op jit(solution)/shard_map/legendre/pallas_call | solution.py:428
  171.2 1.2 copy-done.3
  172.4 22.0 %legendre.2 = (bf16[45,12,128]{2,1,0:T(8,128)(2,1)}, bf16[45,12,128]{2,1,0:T(8,128)(2,1)}, bf16[45,12,128]{2,1,0:T(8,128)(2,1)}, bf16[45,12,128]{2,1,0:T(8,128)(...) custom-call(s32[3,12]{1,0:T(4,128)} %get-tuple-element.118.info, ...), custom_call_target="tpu_custom_call" | custom-call | flops 1811939328 | bytes 9437184 | tf_op jit(solution)/shard_map/legendre/pallas_call | solution.py:428
  194.5 3.3 %fill_halves.3 = (bf16[45,24,128]{2,1,0:T(8,128)(2,1)}, bf16[45,24,128]{2,1,0:T(8,128)(2,1)}, bf16[45,24,128]{2,1,0:T(8,128)(2,1)}, bf16[45,24,128]{2,1,0:T(8,12...) custom-call(bf16[8,45,16,128]{3,2,1,0:T(8,128)(2,1)} %collective-per, ...), custom_call_target="tpu_custom_call" | custom-call | tf_op jit(solution)/shard_map/fill_halves/pallas_call | solution.py:494
  197.8 1.5 collective-permute-start.25
  199.2 2.0 collective-permute-start.27
  201.2 1.0 collective-permute-start.28
  202.3 2.8 collective-permute-start.29
  205.1 3.3 %fill_halves.2 = (bf16[45,24,128]{2,1,0:T(8,128)(2,1)}, bf16[45,24,128]{2,1,0:T(8,128)(2,1)}, bf16[45,24,128]{2,1,0:T(8,128)(2,1)}, bf16[45,24,128]{2,1,0:T(8,12...) custom-call(bf16[8,45,16,128]{3,2,1,0:T(8,128)(2,1)} %copy-done.4, ...), custom_call_target="tpu_custom_call" | custom-call | tf_op jit(solution)/shard_map/fill_halves/pallas_call | solution.py:494
  208.4 1.6 collective-permute-start.30
  210.1 7.7 %collective-permute-done.26.refs_3_ = bf16[45,24,128]{2,1,0:T(8,128)(2,1)S(1)} collective-permute-done((bf16[45,24,128]{2,1,0:T(8,128)(2,1)}, bf16[45,24,128]{2,1,0:T(8,128)(2,1)S(1)}, u32[]{:S(2)}, u32[]{:S(2)}) %collective-permute-start.26) | collective-permute-done | bytes 276512 | tf_op jit(solution)/shard_map/ppermute | solution.py:640
  217.8 5.4 %collective-permute-done.27.refs_4_ = bf16[45,24,128]{2,1,0:T(8,128)(2,1)S(1)} collective-permute-done((bf16[45,24,128]{2,1,0:T(8,128)(2,1)}, bf16[45,24,128]{2,1,0:T(8,128)(2,1)S(1)}, u32[]{:S(2)}, u32[]{:S(2)}) %collective-permute-start.27) | collective-permute-done | bytes 276512 | tf_op jit(solution)/shard_map/ppermute | solution.py:640
  223.3 3.8 %collective-permute-start.10 = (bf16[45,24,128]{2,1,0:T(8,128)(2,1)}, bf16[45,24,128]{2,1,0:T(8,128)(2,1)S(1)}, u32[]{:S(2)}, u32[]{:S(2)}) collective-permute-start(bf16[45,24,128]{2,1,0:T(8,128)(2,1)} %get-tuple-element.74), channel_id=1, source_target_pairs={{0,4},{2,6},{4,0},{6,2},{8,12},{10,14},{12,8},{14,10},{1,5},{3,7},... | collective-permute-start | bytes 829448 | tf_op jit(solution)/shard_map/ppermute | solution.py:640
  227.1 12.2 %collective-permute-done.29.refs_6_ = bf16[45,24,128]{2,1,0:T(8,128)(2,1)S(1)} collective-permute-done((bf16[45,24,128]{2,1,0:T(8,128)(2,1)}, bf16[45,24,128]{2,1,0:T(8,128)(2,1)S(1)}, u32[]{:S(2)}, u32[]{:S(2)}) %collective-permute-start.29) | collective-permute-done | bytes 276512 | tf_op jit(solution)/shard_map/ppermute | solution.py:640
  239.3 3.3 %collective-permute-start.11 = (bf16[45,24,128]{2,1,0:T(8,128)(2,1)}, bf16[45,24,128]{2,1,0:T(8,128)(2,1)S(1)}, u32[]{:S(2)}, u32[]{:S(2)}) collective-permute-start(bf16[45,24,128]{2,1,0:T(8,128)(2,1)} %get-tuple-element.75), channel_id=1, source_target_pairs={{0,6},{2,4},{4,2},{6,0},{8,14},{10,12},{12,10},{14,8},{1,7},{3,5},... | collective-permute-start | bytes 829448 | tf_op jit(solution)/shard_map/ppermute | solution.py:640
  242.5 3.6 %collective-permute-done.30.refs_7_ = bf16[45,24,128]{2,1,0:T(8,128)(2,1)S(1)} collective-permute-done((bf16[45,24,128]{2,1,0:T(8,128)(2,1)}, bf16[45,24,128]{2,1,0:T(8,128)(2,1)S(1)}, u32[]{:S(2)}, u32[]{:S(2)}) %collective-permute-start.30) | collective-permute-done | bytes 276512 | tf_op jit(solution)/shard_map/ppermute | solution.py:640
  246.8 14.6 %collective-permute-done.31.refs_8_ = bf16[45,24,128]{2,1,0:T(8,128)(2,1)S(1)} collective-permute-done((bf16[45,24,128]{2,1,0:T(8,128)(2,1)S(1)}, bf16[45,24,128]{2,1,0:T(8,128)(2,1)S(1)}, u32[]{:S(2)}, u32[]{:S(2)}) %collective-permute-start.31) | collective-permute-done | bytes 276512 | tf_op jit(solution)/shard_map/ppermute | solution.py:640
  262.1 1.0 collective-permute-start.14
  263.1 1.8 collective-permute-start.15
  264.9 13.0 %inverse_dft.2.refs_9_ = bf16[24,120,1920]{2,1,0:T(8,128)(2,1)} custom-call(bf16[384,1920]{1,0:T(8,128)(2,1)} %table.3.t_ref.refs_0_, bf16[45,24,128]{2,1,0:T(8,128)(2,1)} %get-tuple-element.97.refs_1_, bf16[45,24,128]{2,1,0:T(8,128)(2,1)} %copy-done.35, bf16[45,24,128]{2,1,0:T(8,128)(2,1)} %copy-done.36, bf16[45,24,128]{2,1,0:T(8,128)(2,1)} %copy-done.37, ...), custom_call_target="tpu_custom_call" | custom-call | flops 4246732800 | bytes 14745600 | tf_op jit(solution)/shard_map/inverse_dft/pallas_call | solution.py:559
  278.0 5.5 %collective-permute-done.12.refs_5_ = bf16[45,24,128]{2,1,0:T(8,128)(2,1)S(1)} collective-permute-done((bf16[45,24,128]{2,1,0:T(8,128)(2,1)}, bf16[45,24,128]{2,1,0:T(8,128)(2,1)S(1)}, u32[]{:S(2)}, u32[]{:S(2)}) %collective-permute-start.12) | collective-permute-done | bytes 276512 | tf_op jit(solution)/shard_map/ppermute | solution.py:640
  283.5 5.9 %collective-permute-done.13.refs_6_ = bf16[45,24,128]{2,1,0:T(8,128)(2,1)S(1)} collective-permute-done((bf16[45,24,128]{2,1,0:T(8,128)(2,1)}, bf16[45,24,128]{2,1,0:T(8,128)(2,1)S(1)}, u32[]{:S(2)}, u32[]{:S(2)}) %collective-permute-start.13) | collective-permute-done | bytes 276512 | tf_op jit(solution)/shard_map/ppermute | solution.py:640
  289.4 7.4 %collective-permute-done.14.refs_7_ = bf16[45,24,128]{2,1,0:T(8,128)(2,1)S(1)} collective-permute-done((bf16[45,24,128]{2,1,0:T(8,128)(2,1)}, bf16[45,24,128]{2,1,0:T(8,128)(2,1)S(1)}, u32[]{:S(2)}, u32[]{:S(2)}) %collective-permute-start.14) | collective-permute-done | bytes 276512 | tf_op jit(solution)/shard_map/ppermute | solution.py:640
  296.7 5.1 %collective-permute-done.15.refs_8_ = bf16[45,24,128]{2,1,0:T(8,128)(2,1)S(1)} collective-permute-done((bf16[45,24,128]{2,1,0:T(8,128)(2,1)}, bf16[45,24,128]{2,1,0:T(8,128)(2,1)S(1)}, u32[]{:S(2)}, u32[]{:S(2)}) %collective-permute-start.15) | collective-permute-done | bytes 276512 | tf_op jit(solution)/shard_map/ppermute | solution.py:640
  302.6 15.0 %inverse_dft.3 = bf16[24,120,1920]{2,1,0:T(8,128)(2,1)} custom-call(bf16[384,1920]{1,0:T(8,128)(2,1)} %table.2.t_ref.refs_0_, bf16[45,24,128]{2,1,0:T(8,128)(2,1)} %get-tuple-element.72.refs_1_, bf16[45,24,128]{2,1,0:T(8,128)(2,1)} %copy-done.18, bf16[45,24,128]{2,1,0:T(8,128)(2,1)} %copy-done.19, bf16[45,24,128]{2,1,0:T(8,128)(2,1)} %copy-done.20, ...), custom_call_target="tpu_custom_call" | custom-call | flops 4246732800 | bytes 14745600 | tf_op jit(solution)/shard_map/inverse_dft/pallas_call | solution.py:559
  (158 shorter events, 14.6 us)
Async XLA Ops:
  0.0 30.7 %copy-start = (f32[48,48]{1,0:T(8,128)S(1)}, f32[48,48]{1,0:T(8,128)}, u32[]{:S(2)}) copy-start(f32[48,48]{1,0:T(8,128)} %param.24) | copy-start | bytes 27652
  23.2 29.3 %collective-permute-start.16 = (bf16[45,24,128]{2,1,0:T(8,128)(2,1)}, bf16[45,24,128]{2,1,0:T(8,128)(2,1)S(1)}, u32[]{:S(2)}, u32[]{:S(2)}) collective-permute-start(bf16[45,24,128]{2,1,0:T(8,128)(2,1)} %get-tuple-element.81), channel_id=1, source_target_pairs={{0,2},{2,0},{4,6},{6,4},{8,10},{10,8},{12,14},{14,12},{1,3},{3,1},... | collective-permute-start | bytes 829448 | tf_op jit(solution)/shard_map/ppermute | solution.py:640
  24.7 28.4 %collective-permute-start.17 = (bf16[45,24,128]{2,1,0:T(8,128)(2,1)}, bf16[45,24,128]{2,1,0:T(8,128)(2,1)S(1)}, u32[]{:S(2)}, u32[]{:S(2)}) collective-permute-start(bf16[45,24,128]{2,1,0:T(8,128)(2,1)} %get-tuple-element.82), channel_id=1, source_target_pairs={{0,4},{2,6},{4,0},{6,2},{8,12},{10,14},{12,8},{14,10},{1,5},{3,7},... | collective-permute-start | bytes 829448 | tf_op jit(solution)/shard_map/ppermute | solution.py:640
  25.2 28.4 %collective-permute-start.18 = (bf16[45,24,128]{2,1,0:T(8,128)(2,1)}, bf16[45,24,128]{2,1,0:T(8,128)(2,1)S(1)}, u32[]{:S(2)}, u32[]{:S(2)}) collective-permute-start(bf16[45,24,128]{2,1,0:T(8,128)(2,1)} %get-tuple-element.83), channel_id=1, source_target_pairs={{0,6},{2,4},{4,2},{6,0},{8,14},{10,12},{12,10},{14,8},{1,7},{3,5},... | collective-permute-start | bytes 829448 | tf_op jit(solution)/shard_map/ppermute | solution.py:640
  26.7 29.3 %collective-permute-start.19 = (bf16[45,24,128]{2,1,0:T(8,128)(2,1)}, bf16[45,24,128]{2,1,0:T(8,128)(2,1)S(1)}, u32[]{:S(2)}, u32[]{:S(2)}) collective-permute-start(bf16[45,24,128]{2,1,0:T(8,128)(2,1)} %get-tuple-element.84), channel_id=1, source_target_pairs={{0,8},{2,10},{4,12},{6,14},{8,0},{10,2},{12,4},{14,6},{1,9},{3,11}... | collective-permute-start | bytes 829448 | tf_op jit(solution)/shard_map/ppermute | solution.py:640
  29.3 28.4 %collective-permute-start.20 = (bf16[45,24,128]{2,1,0:T(8,128)(2,1)}, bf16[45,24,128]{2,1,0:T(8,128)(2,1)S(1)}, u32[]{:S(2)}, u32[]{:S(2)}) collective-permute-start(bf16[45,24,128]{2,1,0:T(8,128)(2,1)} %get-tuple-element.85), channel_id=1, source_target_pairs={{0,10},{2,8},{4,14},{6,12},{8,2},{10,0},{12,6},{14,4},{1,11},{3,9}... | collective-permute-start | bytes 829448 | tf_op jit(solution)/shard_map/ppermute | solution.py:640
  52.5 43.7 %copy-start.5 = (bf16[45,24,128]{2,1,0:T(8,128)(2,1)}, bf16[45,24,128]{2,1,0:T(8,128)(2,1)S(1)}, u32[]{:S(2)}) copy-start(bf16[45,24,128]{2,1,0:T(8,128)(2,1)S(1)} %collective-permute-done.16.refs_1_.rest_1_) | copy-start | bytes 829444
  52.5 47.4 %collective-permute-start = (bf16[45,24,128]{2,1,0:T(8,128)(2,1)}, bf16[45,24,128]{2,1,0:T(8,128)(2,1)S(1)}, u32[]{:S(2)}, u32[]{:S(2)}) collective-permute-start(bf16[45,24,128]{2,1,0:T(8,128)(2,1)} %get-tuple-element.56), channel_id=1, source_target_pairs={{0,2},{2,0},{4,6},{6,4},{8,10},{10,8},{12,14},{14,12},{1,3},{3,1},... | collective-permute-start | bytes 829448 | tf_op jit(solution)/shard_map/ppermute | solution.py:640
  53.1 43.1 %copy-start.6 = (bf16[45,24,128]{2,1,0:T(8,128)(2,1)}, bf16[45,24,128]{2,1,0:T(8,128)(2,1)S(1)}, u32[]{:S(2)}) copy-start(bf16[45,24,128]{2,1,0:T(8,128)(2,1)S(1)} %collective-permute-done.17.refs_2_.rest_2_) | copy-start | bytes 829444
  53.1 48.4 %collective-permute-start.1 = (bf16[45,24,128]{2,1,0:T(8,128)(2,1)}, bf16[45,24,128]{2,1,0:T(8,128)(2,1)S(1)}, u32[]{:S(2)}, u32[]{:S(2)}) collective-permute-start(bf16[45,24,128]{2,1,0:T(8,128)(2,1)} %get-tuple-element.57), channel_id=1, source_target_pairs={{0,4},{2,6},{4,0},{6,2},{8,12},{10,14},{12,8},{14,10},{1,5},{3,7},... | collective-permute-start | bytes 829448 | tf_op jit(solution)/shard_map/ppermute | solution.py:640
  53.6 42.6 %copy-start.7 = (bf16[45,24,128]{2,1,0:T(8,128)(2,1)}, bf16[45,24,128]{2,1,0:T(8,128)(2,1)S(1)}, u32[]{:S(2)}) copy-start(bf16[45,24,128]{2,1,0:T(8,128)(2,1)S(1)} %collective-permute-done.18.refs_3_.rest_3_) | copy-start | bytes 829444
  53.6 49.9 %collective-permute-start.2 = (bf16[45,24,128]{2,1,0:T(8,128)(2,1)}, bf16[45,24,128]{2,1,0:T(8,128)(2,1)S(1)}, u32[]{:S(2)}, u32[]{:S(2)}) collective-permute-start(bf16[45,24,128]{2,1,0:T(8,128)(2,1)} %get-tuple-element.58), channel_id=1, source_target_pairs={{0,6},{2,4},{4,2},{6,0},{8,14},{10,12},{12,10},{14,8},{1,7},{3,5},... | collective-permute-start | bytes 829448 | tf_op jit(solution)/shard_map/ppermute | solution.py:640
  56.1 40.1 %copy-start.8 = (bf16[45,24,128]{2,1,0:T(8,128)(2,1)}, bf16[45,24,128]{2,1,0:T(8,128)(2,1)S(1)}, u32[]{:S(2)}) copy-start(bf16[45,24,128]{2,1,0:T(8,128)(2,1)S(1)} %collective-permute-done.19.refs_4_.rest_4_) | copy-start | bytes 829444
  56.1 10.3 %collective-permute-start.21 = (bf16[45,24,128]{2,1,0:T(8,128)(2,1)S(1)}, bf16[45,24,128]{2,1,0:T(8,128)(2,1)S(1)}, u32[]{:S(2)}, u32[]{:S(2)}) collective-permute-start(bf16[45,24,128]{2,1,0:T(8,128)(2,1)S(1)} %copy-done.34), channel_id=1, source_target_pairs={{0,12},{2,14},{4,8},{6,10},{8,4},{10,6},{12,0},{14,2},{1,13},{3,15... | collective-permute-start | bytes 829448 | tf_op jit(solution)/shard_map/ppermute | solution.py:640
  57.7 38.5 %copy-start.9 = (bf16[45,24,128]{2,1,0:T(8,128)(2,1)}, bf16[45,24,128]{2,1,0:T(8,128)(2,1)S(1)}, u32[]{:S(2)}) copy-start(bf16[45,24,128]{2,1,0:T(8,128)(2,1)S(1)} %collective-permute-done.20.refs_5_.rest_5_) | copy-start | bytes 829444
  57.7 38.5 %collective-permute-start.22 = (bf16[45,24,128]{2,1,0:T(8,128)(2,1)S(1)}, bf16[45,24,128]{2,1,0:T(8,128)(2,1)S(1)}, u32[]{:S(2)}, u32[]{:S(2)}) collective-permute-start(bf16[45,24,128]{2,1,0:T(8,128)(2,1)S(1)} %copy-done.33), channel_id=1, source_target_pairs={{0,14},{2,12},{4,10},{6,8},{8,6},{10,4},{12,2},{14,0},{1,15},{3,13... | collective-permute-start | bytes 829448 | tf_op jit(solution)/shard_map/ppermute | solution.py:640
  66.4 29.9 %copy-start.14 = (bf16[45,24,128]{2,1,0:T(8,128)(2,1)}, bf16[45,24,128]{2,1,0:T(8,128)(2,1)S(1)}, u32[]{:S(2)}) copy-start(bf16[45,24,128]{2,1,0:T(8,128)(2,1)S(1)} %collective-permute-done.21.refs_6_.rest_6_) | copy-start | bytes 829444
  66.4 38.7 %collective-permute-start.3 = (bf16[45,24,128]{2,1,0:T(8,128)(2,1)}, bf16[45,24,128]{2,1,0:T(8,128)(2,1)S(1)}, u32[]{:S(2)}, u32[]{:S(2)}) collective-permute-start(bf16[45,24,128]{2,1,0:T(8,128)(2,1)} %get-tuple-element.59), channel_id=1, source_target_pairs={{0,8},{2,10},{4,12},{6,14},{8,0},{10,2},{12,4},{14,6},{1,9},{3,11}... | collective-permute-start | bytes 829448 | tf_op jit(solution)/shard_map/ppermute | solution.py:640
  96.2 20.8 %collective-permute-start.4 = (bf16[45,24,128]{2,1,0:T(8,128)(2,1)}, bf16[45,24,128]{2,1,0:T(8,128)(2,1)}, u32[]{:S(2)}, u32[]{:S(2)}) collective-permute-start(bf16[45,24,128]{2,1,0:T(8,128)(2,1)} %get-tuple-element.60), channel_id=1, source_target_pairs={{0,10},{2,8},{4,14},{6,12},{8,2},{10,0},{12,6},{14,4},{1,11},{3,9}... | collective-permute-start | bytes 829448 | tf_op jit(solution)/shard_map/ppermute | solution.py:640
  99.9 27.5 %copy-start.10 = (bf16[45,24,128]{2,1,0:T(8,128)(2,1)}, bf16[45,24,128]{2,1,0:T(8,128)(2,1)S(1)}, u32[]{:S(2)}) copy-start(bf16[45,24,128]{2,1,0:T(8,128)(2,1)S(1)} %collective-permute-done.refs_1_.rest_1_) | copy-start | bytes 829444
  100.0 23.0 %collective-permute-start.5 = (bf16[45,24,128]{2,1,0:T(8,128)(2,1)}, bf16[45,24,128]{2,1,0:T(8,128)(2,1)S(1)}, u32[]{:S(2)}, u32[]{:S(2)}) collective-permute-start(bf16[45,24,128]{2,1,0:T(8,128)(2,1)} %get-tuple-element.61), channel_id=1, source_target_pairs={{0,12},{2,14},{4,8},{6,10},{8,4},{10,6},{12,0},{14,2},{1,13},{3,15... | collective-permute-start | bytes 829448 | tf_op jit(solution)/shard_map/ppermute | solution.py:640
  101.5 25.9 %copy-start.11 = (bf16[45,24,128]{2,1,0:T(8,128)(2,1)}, bf16[45,24,128]{2,1,0:T(8,128)(2,1)S(1)}, u32[]{:S(2)}) copy-start(bf16[45,24,128]{2,1,0:T(8,128)(2,1)S(1)} %collective-permute-done.1.refs_2_.rest_2_) | copy-start | bytes 829444
  101.5 25.9 %collective-permute-start.6 = (bf16[45,24,128]{2,1,0:T(8,128)(2,1)}, bf16[45,24,128]{2,1,0:T(8,128)(2,1)S(1)}, u32[]{:S(2)}, u32[]{:S(2)}) collective-permute-start(bf16[45,24,128]{2,1,0:T(8,128)(2,1)} %get-tuple-element.62), channel_id=1, source_target_pairs={{0,14},{2,12},{4,10},{6,8},{8,6},{10,4},{12,2},{14,0},{1,15},{3,13... | collective-permute-start | bytes 829448 | tf_op jit(solution)/shard_map/ppermute | solution.py:640
  103.5 23.9 %copy-start.12 = (bf16[45,24,128]{2,1,0:T(8,128)(2,1)}, bf16[45,24,128]{2,1,0:T(8,128)(2,1)S(1)}, u32[]{:S(2)}) copy-start(bf16[45,24,128]{2,1,0:T(8,128)(2,1)S(1)} %collective-permute-done.2.refs_3_.rest_3_) | copy-start | bytes 829444
  103.5 43.9 %collective-permute-start.23 = (bf16[8,45,16,128]{3,2,1,0:T(8,128)(2,1)}, bf16[8,45,16,128]{3,2,1,0:T(8,128)(2,1)S(1)}, u32[]{:S(2)}, u32[]{:S(2)}) collective-permute-start(bf16[8,45,16,128]{3,2,1,0:T(8,128)(2,1)} %gather_halves.3), channel_id=1, source_target_pairs={{0,1},{1,0},{2,3},{3,2},{4,5},{5,4},{6,7},{7,6},{8,9},{9,8},{10,11... | collective-permute-start | bytes 4423688 | tf_op jit(solution)/shard_map/ppermute | solution.py:644
  131.2 40.0 %collective-permute-start.7 = (bf16[8,45,16,128]{3,2,1,0:T(8,128)(2,1)}, bf16[8,45,16,128]{3,2,1,0:T(8,128)(2,1)S(1)}, u32[]{:S(2)}, u32[]{:S(2)}) collective-permute-start(bf16[8,45,16,128]{3,2,1,0:T(8,128)(2,1)} %gather_halves.2), channel_id=1, source_target_pairs={{0,1},{1,0},{2,3},{3,2},{4,5},{5,4},{6,7},{7,6},{8,9},{9,8},{10,11... | collective-permute-start | bytes 4423688 | tf_op jit(solution)/shard_map/ppermute | solution.py:644
  170.7 23.7 %collective-permute-start.24 = (bf16[8,45,16,128]{3,2,1,0:T(8,128)(2,1)}, bf16[8,45,16,128]{3,2,1,0:T(8,128)(2,1)}, u32[]{:S(2)}, u32[]{:S(2)}) collective-permute-start(bf16[8,45,16,128]{3,2,1,0:T(8,128)(2,1)} %get-tuple-element.88), channel_id=1, source_target_pairs={{0,1},{1,0},{2,3},{3,2},{4,5},{5,4},{6,7},{7,6},{8,9},{9,8},{10,11... | collective-permute-start | bytes 4423688 | tf_op jit(solution)/shard_map/ppermute | solution.py:644
  194.4 7.8 %collective-permute-start.8 = (bf16[8,45,16,128]{3,2,1,0:T(8,128)(2,1)}, bf16[8,45,16,128]{3,2,1,0:T(8,128)(2,1)S(1)}, u32[]{:S(2)}, u32[]{:S(2)}) collective-permute-start(bf16[8,45,16,128]{3,2,1,0:T(8,128)(2,1)} %get-tuple-element.63), channel_id=1, source_target_pairs={{0,1},{1,0},{2,3},{3,2},{4,5},{5,4},{6,7},{7,6},{8,9},{9,8},{10,11... | collective-permute-start | bytes 4423688 | tf_op jit(solution)/shard_map/ppermute | solution.py:644
  197.8 10.7 %collective-permute-start.25 = (bf16[45,24,128]{2,1,0:T(8,128)(2,1)}, bf16[45,24,128]{2,1,0:T(8,128)(2,1)S(1)}, u32[]{:S(2)}, u32[]{:S(2)}) collective-permute-start(bf16[45,24,128]{2,1,0:T(8,128)(2,1)} %get-tuple-element.98), channel_id=1, source_target_pairs={{0,2},{2,0},{4,6},{6,4},{8,10},{10,8},{12,14},{14,12},{1,3},{3,1},... | collective-permute-start | bytes 829448 | tf_op jit(solution)/shard_map/ppermute | solution.py:640
  199.2 18.6 %collective-permute-start.26 = (bf16[45,24,128]{2,1,0:T(8,128)(2,1)}, bf16[45,24,128]{2,1,0:T(8,128)(2,1)S(1)}, u32[]{:S(2)}, u32[]{:S(2)}) collective-permute-start(bf16[45,24,128]{2,1,0:T(8,128)(2,1)} %get-tuple-element.99), channel_id=1, source_target_pairs={{0,4},{2,6},{4,0},{6,2},{8,12},{10,14},{12,8},{14,10},{1,5},{3,7},... | collective-permute-start | bytes 829448 | tf_op jit(solution)/shard_map/ppermute | solution.py:640
  199.2 24.0 %collective-permute-start.27 = (bf16[45,24,128]{2,1,0:T(8,128)(2,1)}, bf16[45,24,128]{2,1,0:T(8,128)(2,1)S(1)}, u32[]{:S(2)}, u32[]{:S(2)}) collective-permute-start(bf16[45,24,128]{2,1,0:T(8,128)(2,1)} %get-tuple-element.100), channel_id=1, source_target_pairs={{0,6},{2,4},{4,2},{6,0},{8,14},{10,12},{12,10},{14,8},{1,7},{3,5},... | collective-permute-start | bytes 829448 | tf_op jit(solution)/shard_map/ppermute | solution.py:640
  201.2 22.0 %collective-permute-start.28 = (bf16[45,24,128]{2,1,0:T(8,128)(2,1)}, bf16[45,24,128]{2,1,0:T(8,128)(2,1)S(1)}, u32[]{:S(2)}, u32[]{:S(2)}) collective-permute-start(bf16[45,24,128]{2,1,0:T(8,128)(2,1)} %get-tuple-element.101), channel_id=1, source_target_pairs={{0,8},{2,10},{4,12},{6,14},{8,0},{10,2},{12,4},{14,6},{1,9},{3,11}... | collective-permute-start | bytes 829448 | tf_op jit(solution)/shard_map/ppermute | solution.py:640
  202.3 37.0 %collective-permute-start.29 = (bf16[45,24,128]{2,1,0:T(8,128)(2,1)}, bf16[45,24,128]{2,1,0:T(8,128)(2,1)S(1)}, u32[]{:S(2)}, u32[]{:S(2)}) collective-permute-start(bf16[45,24,128]{2,1,0:T(8,128)(2,1)} %get-tuple-element.102), channel_id=1, source_target_pairs={{0,10},{2,8},{4,14},{6,12},{8,2},{10,0},{12,6},{14,4},{1,11},{3,9}... | collective-permute-start | bytes 829448 | tf_op jit(solution)/shard_map/ppermute | solution.py:640
  208.4 56.5 %copy-start.35 = (bf16[45,24,128]{2,1,0:T(8,128)(2,1)}, bf16[45,24,128]{2,1,0:T(8,128)(2,1)S(1)}, u32[]{:S(2)}) copy-start(bf16[45,24,128]{2,1,0:T(8,128)(2,1)S(1)} %collective-permute-done.25.refs_2_) | copy-start | bytes 829444
  208.4 37.6 %collective-permute-start.30 = (bf16[45,24,128]{2,1,0:T(8,128)(2,1)}, bf16[45,24,128]{2,1,0:T(8,128)(2,1)S(1)}, u32[]{:S(2)}, u32[]{:S(2)}) collective-permute-start(bf16[45,24,128]{2,1,0:T(8,128)(2,1)} %get-tuple-element.103), channel_id=1, source_target_pairs={{0,12},{2,14},{4,8},{6,10},{8,4},{10,6},{12,0},{14,2},{1,13},{3,15... | collective-permute-start | bytes 829448 | tf_op jit(solution)/shard_map/ppermute | solution.py:640
  217.8 47.1 %copy-start.36 = (bf16[45,24,128]{2,1,0:T(8,128)(2,1)}, bf16[45,24,128]{2,1,0:T(8,128)(2,1)S(1)}, u32[]{:S(2)}) copy-start(bf16[45,24,128]{2,1,0:T(8,128)(2,1)S(1)} %collective-permute-done.26.refs_3_) | copy-start | bytes 829444
  217.8 43.6 %collective-permute-start.31 = (bf16[45,24,128]{2,1,0:T(8,128)(2,1)S(1)}, bf16[45,24,128]{2,1,0:T(8,128)(2,1)S(1)}, u32[]{:S(2)}, u32[]{:S(2)}) collective-permute-start(bf16[45,24,128]{2,1,0:T(8,128)(2,1)S(1)} %copy-done.39), channel_id=1, source_target_pairs={{0,14},{2,12},{4,10},{6,8},{8,6},{10,4},{12,2},{14,0},{1,15},{3,13... | collective-permute-start | bytes 829448 | tf_op jit(solution)/shard_map/ppermute | solution.py:640
  223.2 41.7 %copy-start.37 = (bf16[45,24,128]{2,1,0:T(8,128)(2,1)}, bf16[45,24,128]{2,1,0:T(8,128)(2,1)S(1)}, u32[]{:S(2)}) copy-start(bf16[45,24,128]{2,1,0:T(8,128)(2,1)S(1)} %collective-permute-done.27.refs_4_) | copy-start | bytes 829444
  223.2 38.9 %collective-permute-start.9 = (bf16[45,24,128]{2,1,0:T(8,128)(2,1)}, bf16[45,24,128]{2,1,0:T(8,128)(2,1)S(1)}, u32[]{:S(2)}, u32[]{:S(2)}) collective-permute-start(bf16[45,24,128]{2,1,0:T(8,128)(2,1)} %get-tuple-element.73), channel_id=1, source_target_pairs={{0,2},{2,0},{4,6},{6,4},{8,10},{10,8},{12,14},{14,12},{1,3},{3,1},... | collective-permute-start | bytes 829448 | tf_op jit(solution)/shard_map/ppermute | solution.py:640
  223.3 41.7 %copy-start.38 = (bf16[45,24,128]{2,1,0:T(8,128)(2,1)}, bf16[45,24,128]{2,1,0:T(8,128)(2,1)S(1)}, u32[]{:S(2)}) copy-start(bf16[45,24,128]{2,1,0:T(8,128)(2,1)S(1)} %collective-permute-done.28.refs_5_) | copy-start | bytes 829444
  223.3 39.9 %collective-permute-start.10 = (bf16[45,24,128]{2,1,0:T(8,128)(2,1)}, bf16[45,24,128]{2,1,0:T(8,128)(2,1)S(1)}, u32[]{:S(2)}, u32[]{:S(2)}) collective-permute-start(bf16[45,24,128]{2,1,0:T(8,128)(2,1)} %get-tuple-element.74), channel_id=1, source_target_pairs={{0,4},{2,6},{4,0},{6,2},{8,12},{10,14},{12,8},{14,10},{1,5},{3,7},... | collective-permute-start | bytes 829448 | tf_op jit(solution)/shard_map/ppermute | solution.py:640
  239.3 25.7 %copy-start.40 = (bf16[45,24,128]{2,1,0:T(8,128)(2,1)}, bf16[45,24,128]{2,1,0:T(8,128)(2,1)S(1)}, u32[]{:S(2)}) copy-start(bf16[45,24,128]{2,1,0:T(8,128)(2,1)S(1)} %collective-permute-done.29.refs_6_) | copy-start | bytes 829444
  239.3 38.7 %collective-permute-start.11 = (bf16[45,24,128]{2,1,0:T(8,128)(2,1)}, bf16[45,24,128]{2,1,0:T(8,128)(2,1)S(1)}, u32[]{:S(2)}, u32[]{:S(2)}) collective-permute-start(bf16[45,24,128]{2,1,0:T(8,128)(2,1)} %get-tuple-element.75), channel_id=1, source_target_pairs={{0,6},{2,4},{4,2},{6,0},{8,14},{10,12},{12,10},{14,8},{1,7},{3,5},... | collective-permute-start | bytes 829448 | tf_op jit(solution)/shard_map/ppermute | solution.py:640
  246.8 36.7 %collective-permute-start.12 = (bf16[45,24,128]{2,1,0:T(8,128)(2,1)}, bf16[45,24,128]{2,1,0:T(8,128)(2,1)S(1)}, u32[]{:S(2)}, u32[]{:S(2)}) collective-permute-start(bf16[45,24,128]{2,1,0:T(8,128)(2,1)} %get-tuple-element.76), channel_id=1, source_target_pairs={{0,8},{2,10},{4,12},{6,14},{8,0},{10,2},{12,4},{14,6},{1,9},{3,11}... | collective-permute-start | bytes 829448 | tf_op jit(solution)/shard_map/ppermute | solution.py:640
  262.1 27.3 %collective-permute-start.13 = (bf16[45,24,128]{2,1,0:T(8,128)(2,1)}, bf16[45,24,128]{2,1,0:T(8,128)(2,1)S(1)}, u32[]{:S(2)}, u32[]{:S(2)}) collective-permute-start(bf16[45,24,128]{2,1,0:T(8,128)(2,1)} %get-tuple-element.77), channel_id=1, source_target_pairs={{0,10},{2,8},{4,14},{6,12},{8,2},{10,0},{12,6},{14,4},{1,11},{3,9}... | collective-permute-start | bytes 829448 | tf_op jit(solution)/shard_map/ppermute | solution.py:640
  262.1 34.6 %collective-permute-start.14 = (bf16[45,24,128]{2,1,0:T(8,128)(2,1)}, bf16[45,24,128]{2,1,0:T(8,128)(2,1)S(1)}, u32[]{:S(2)}, u32[]{:S(2)}) collective-permute-start(bf16[45,24,128]{2,1,0:T(8,128)(2,1)} %get-tuple-element.78), channel_id=1, source_target_pairs={{0,12},{2,14},{4,8},{6,10},{8,4},{10,6},{12,0},{14,2},{1,13},{3,15... | collective-permute-start | bytes 829448 | tf_op jit(solution)/shard_map/ppermute | solution.py:640
  263.1 38.8 %collective-permute-start.15 = (bf16[45,24,128]{2,1,0:T(8,128)(2,1)}, bf16[45,24,128]{2,1,0:T(8,128)(2,1)S(1)}, u32[]{:S(2)}, u32[]{:S(2)}) collective-permute-start(bf16[45,24,128]{2,1,0:T(8,128)(2,1)} %get-tuple-element.79), channel_id=1, source_target_pairs={{0,14},{2,12},{4,10},{6,8},{8,6},{10,4},{12,2},{14,0},{1,15},{3,13... | collective-permute-start | bytes 829448 | tf_op jit(solution)/shard_map/ppermute | solution.py:640
  278.0 23.9 %copy-start.20 = (bf16[45,24,128]{2,1,0:T(8,128)(2,1)}, bf16[45,24,128]{2,1,0:T(8,128)(2,1)S(1)}, u32[]{:S(2)}) copy-start(bf16[45,24,128]{2,1,0:T(8,128)(2,1)S(1)} %collective-permute-done.11.refs_4_) | copy-start | bytes 829444
  (27 other events, 272.1 us)
